TPU v7x, 512 devices: a whole 4x8x8 slice. The times are simulated.
512 devices in a mesh: dp: 64 (over y, z_hi, core), section: 8 (over x, z_lo).
Axes of the slice: x: 4, y: 8, z: 8 (z_hi: 4, z_lo: 2; z = z_hi * 2 + z_lo), core: 2. Of those that a mesh axis runs over, the one named last changes fastest.
Arguments:
- features: bfloat16 [256, 64, 512], P('dp'), may hold values from -6 to 6
- lengths: int32 [256], P('dp'), may hold values from 32 to 64
- front_weight: bfloat16 [512, 768], replicated, may hold values from -0.25 to 0.25
- pointwise: bfloat16 [8, 768, 768], P('section'), may hold values from -0.21875 to 0.21875
- kernel: float32 [8, 5, 768], P('section'), may hold values from -2.5 to 2.5
- targets: bfloat16 [256, 64, 768], P('dp'), may hold values from -6 to 6
Outputs:
- grad_pointwise: bfloat16 [8, 768, 768], P('section')
- grad_kernel: float32 [8, 5, 768], P('section')
All inputs are finite; a program needn't handle non-finite values.
Results may differ from a plain program's by a relative error of at most 0.005.
Values may be sent and summed in bfloat16 or wider, within the bound.
No kernel may reach another device: no remote copies, remote signals or barrier semaphores. Data moves between devices by JAX's collectives and lax.ppermute only.
A program may use at most 64 MiB of HBM per device.

v0:
```python
import jax
import jax.numpy as jnp
from jax import lax
from jax.sharding import PartitionSpec as P

EPS = 1e-06


def from_behind(block, axis, distance):
    devices = range(lax.axis_size(axis))
    route = [((i - distance) % len(devices), i) for i in devices]
    return lax.ppermute(block, axis, route)


def depthwise(signal, taps):
    half_span = taps.shape[0] // 2
    frames = signal.shape[-2]
    padding = [(0, 0)] * (signal.ndim - 2) + [(half_span, half_span), (0, 0)]
    padded = jnp.pad(signal, padding)
    summed = jnp.zeros_like(signal)
    for offset in range(taps.shape[0]):
        summed = summed + taps[offset] * lax.slice_in_dim(
            padded, offset, offset + frames, axis=signal.ndim - 2
        )
    return summed


def depthwise_transpose(signal, taps):
    half_span = taps.shape[0] // 2
    frames = signal.shape[-2]
    padding = [(0, 0)] * (signal.ndim - 2) + [(half_span, half_span), (0, 0)]
    padded = jnp.pad(signal, padding)
    summed = jnp.zeros_like(signal)
    for offset in range(taps.shape[0]):
        begin = 2 * half_span - offset
        summed = summed + taps[offset] * lax.slice_in_dim(
            padded, begin, begin + frames, axis=signal.ndim - 2
        )
    return summed


def taps_gradient(normed, grad_conv, count):
    half_span = count // 2
    frames = normed.shape[-2]
    padding = [(0, 0)] * (normed.ndim - 2) + [(half_span, half_span), (0, 0)]
    padded = jnp.pad(normed, padding)
    rows = []
    for offset in range(count):
        window = lax.slice_in_dim(padded, offset, offset + frames, axis=normed.ndim - 2)
        rows.append(jnp.sum(grad_conv * window, axis=0))
    return jnp.stack(rows)


def block_inner(block_input, taps, frame_mask):
    values = block_input.astype(jnp.float32)
    scale_inv = lax.rsqrt(jnp.mean(values * values, axis=-1, keepdims=True) + EPS)
    normed = values * scale_inv * frame_mask[..., None]
    conv_out = depthwise(normed, taps)
    sigmoid_out = jax.nn.sigmoid(conv_out)
    activated = (conv_out * sigmoid_out).astype(jnp.bfloat16)
    return (values, scale_inv, normed, conv_out, sigmoid_out, activated)


def block_forward(block_input, weight, taps, frame_mask):
    values, scale_inv, normed, conv_out, sigmoid_out, activated = block_inner(
        block_input, taps, frame_mask
    )
    update = jnp.dot(activated, weight, preferred_element_type=jnp.float32)
    return (values + update).astype(jnp.bfloat16)


def block_backward(block_input, weight, taps, frame_mask, cotangent):
    values, scale_inv, normed, conv_out, sigmoid_out, activated = block_inner(
        block_input, taps, frame_mask
    )
    grad_weight = jnp.dot(activated.T, cotangent, preferred_element_type=jnp.float32)
    grad_act = jnp.dot(cotangent, weight.T, preferred_element_type=jnp.float32)
    grad_conv = grad_act * sigmoid_out * (1.0 + conv_out * (1.0 - sigmoid_out))
    grad_taps = taps_gradient(normed, grad_conv, taps.shape[0])
    grad_normed = depthwise_transpose(grad_conv, taps) * frame_mask[..., None]
    grad_values = scale_inv * grad_normed - values * scale_inv * scale_inv * scale_inv * jnp.mean(
        grad_normed * values, axis=-1, keepdims=True
    )
    grad_input = (cotangent.astype(jnp.float32) + grad_values).astype(jnp.bfloat16)
    return (grad_input, grad_weight, grad_taps)


def head_gradient(outputs, targets, frame_mask, lengths):
    differ = (outputs.astype(jnp.float32) - targets.astype(jnp.float32)) * frame_mask[..., None]
    return (differ / lengths.astype(jnp.float32)[:, None, None]).astype(jnp.bfloat16)


def body(features, lengths, front_weight, pointwise, kernel, targets):
    sections = lax.axis_size("section")
    section_index = lax.axis_index("section")
    micro_count = features.shape[0]
    frames = features.shape[1]
    width = front_weight.shape[1]
    frame_mask = (jnp.arange(frames, dtype=jnp.int32)[None, :] < lengths[:, None]).astype(
        jnp.float32
    )
    front_out = jnp.dot(
        features.reshape(-1, features.shape[2]), front_weight, preferred_element_type=jnp.float32
    )
    front_out = front_out.reshape(micro_count, frames, width).astype(jnp.bfloat16)
    weight = pointwise[0]
    taps = kernel[0]
    blank = jnp.zeros((frames, width), jnp.bfloat16)
    ticks = micro_count + sections

    def send_forward(payload):
        return from_behind(payload, "section", 1)

    def send_backward(grad_input, tick_index, head_grads):
        opening = jnp.clip(tick_index, 0, micro_count - 1)
        started = jnp.where(tick_index < micro_count, head_grads[opening], blank)
        payload = jnp.where(section_index == 0, started, grad_input)
        return from_behind(payload, "section", -1)

    def forward_tick(state, tick_index):
        incoming, saved = state
        micro = tick_index - section_index
        valid = (micro >= 0) & (micro < micro_count)
        picked = jnp.clip(micro, 0, micro_count - 1)
        block_input = jnp.where(section_index == 0, front_out[picked], incoming)
        block_output = block_forward(block_input, weight, taps, frame_mask[picked])
        saved = saved.at[picked].set(jnp.where(valid, block_input, saved[picked]))
        outgoing = send_forward(block_output)
        return ((outgoing, saved), incoming)

    saved_start = jnp.zeros((micro_count, frames, width), jnp.bfloat16)
    (unused_carry, saved), recorded = lax.scan(
        forward_tick, (blank, saved_start), jnp.arange(ticks, dtype=jnp.int32)
    )
    finals = recorded[sections : sections + micro_count]
    head_grads = head_gradient(finals, targets, frame_mask, lengths)

    def backward_tick(state, tick_index):
        incoming, grad_weight, grad_taps = state
        micro = tick_index - sections + section_index
        valid = (micro >= 0) & (micro < micro_count)
        picked = jnp.clip(micro, 0, micro_count - 1)
        grad_input, step_weight, step_taps = block_backward(
            saved[picked], weight, taps, frame_mask[picked], incoming
        )
        grad_weight = grad_weight + jnp.where(valid, step_weight, 0.0)
        grad_taps = grad_taps + jnp.where(valid, step_taps, 0.0)
        outgoing = send_backward(grad_input, tick_index, head_grads)
        return ((outgoing, grad_weight, grad_taps), None)

    start_state = (
        blank,
        jnp.zeros((width, width), jnp.float32),
        jnp.zeros(taps.shape, jnp.float32),
    )
    (unused_back, grad_weight, grad_taps), unused_out = lax.scan(
        backward_tick, start_state, jnp.arange(ticks, dtype=jnp.int32)
    )
    summed_weight, summed_taps = lax.psum((grad_weight, grad_taps), "dp")
    return (summed_weight.astype(jnp.bfloat16)[None], summed_taps[None])


def solution(mesh):
    placed = (
        P("dp", None, None),
        P("dp"),
        P(),
        P("section", None, None),
        P("section", None, None),
        P("dp", None, None),
    )
    return jax.shard_map(
        body,
        mesh=mesh,
        in_specs=placed,
        out_specs=(P("section", None, None), P("section", None, None)),
        check_vma=False,
    )
```

profile of v0, /device:TPU:66, one launch (start us, length us, event | category | flops | bytes accessed | tf_op | source)
XLA Modules:
  0.0 756.6 jit_solution(13514638791243117145)
XLA Ops:
  5.3 163.8 %while.34 = (s32[]{:T(128)}, bf16[64,768]{1,0:T(8,128)(2,1)S(1)}, bf16[4,64,768]{2,1,0:T(8,128)(2,1)S(1)}, bf16[12,64,768]{2,1,0:T(8,128)(2,1)S(1)}, pred[]{:T(5...) while((s32[]{:T(128)}, bf16[64,768]{1,0:T(8,128)(2,1)S(1)}, ...), condition=%wide.region_3.4_spmd, body=%wide.region_0.3_spmd.sunk | while | flops 76775512 | bytes 3193906 | solution.py:132
  10.8 2.5 collective-permute-start
  13.2 4.0 collective-permute-done
  22.6 3.4 collective-permute-start
  26.0 3.1 collective-permute-done
  32.9 1.7 fusion.71
  34.5 4.3 collective-permute-start
  38.8 3.2 collective-permute-done
  47.4 4.2 collective-permute-start
  51.6 4.4 collective-permute-done
  61.4 3.0 collective-permute-start
  64.4 5.6 collective-permute-done
  75.4 1.9 collective-permute-start
  77.4 6.7 collective-permute-done
  89.4 1.9 collective-permute-start
  91.4 6.7 collective-permute-done
  103.5 1.9 collective-permute-start
  105.4 7.9 %collective-permute-done = bf16[64,768]{1,0:T(8,128)(2,1)S(1)} collective-permute-done((bf16[64,768]{1,0:T(8,128)(2,1)S(1)}, bf16[64,768]{1,0:T(8,128)(2,1)S(1)}, u32[]{:S(2)}, u32[]{:S(2)}) %collective-permute-start) | collective-permute-done | bytes 98336 | tf_op jit(solution)/shard_map/while/body/eval_jaxpr/ppermute | solution.py:12
  118.7 1.9 collective-permute-start
  120.6 6.7 collective-permute-done
  132.7 1.9 collective-permute-start
  134.7 6.8 collective-permute-done
  146.8 1.9 collective-permute-start
  148.7 6.4 collective-permute-done
  160.5 1.9 collective-permute-start
  162.4 6.7 collective-permute-done
  172.0 273.6 %while.35 = (s32[]{:T(128)}, bf16[64,768]{1,0:T(8,128)(2,1)}, f32[768,768]{1,0:T(8,128)S(1)}, f32[5,768]{1,0:T(8,128)}, pred[]{:T(512)}, /*index=5*/s32[12]{0:T(...) while((s32[]{:T(128)}, bf16[64,768]{1,0:T(8,128)(2,1)}, ...), condition=%wide.region_12.13_spmd.clone, body=%wide.region_4.12_spmd.clone.sunk | while | flops 155967040 | bytes 10731494 | solution.py:156
  177.8 1.9 fusion.78
  182.2 6.0 collective-permute-start.1
  190.8 2.0 select_add_fusion.4
  202.1 1.9 fusion.78
  206.5 6.0 collective-permute-start.1
  215.0 2.0 select_add_fusion.4
  227.1 1.9 fusion.78
  231.5 6.0 collective-permute-start.1
  240.0 2.0 select_add_fusion.4
  252.1 1.9 fusion.78
  256.6 1.9 collective-permute-start.1
  261.0 2.0 select_add_fusion.4
  273.0 1.9 fusion.78
  277.5 2.5 collective-permute-start.1
  282.4 2.0 select_add_fusion.4
  294.5 1.9 fusion.78
  298.9 1.9 collective-permute-start.1
  303.3 2.0 select_add_fusion.4
  315.4 1.9 fusion.78
  319.9 1.9 collective-permute-start.1
  324.3 2.0 select_add_fusion.4
  336.3 1.9 fusion.78
  340.8 1.9 collective-permute-start.1
  345.2 2.0 select_add_fusion.4
  357.3 1.9 fusion.78
  361.7 3.5 collective-permute-start.1
  367.7 2.0 select_add_fusion.4
  379.8 1.9 fusion.78
  384.2 6.0 collective-permute-start.1
  392.8 2.0 select_add_fusion.4
  404.8 1.9 fusion.78
  409.3 6.0 collective-permute-start.1
  417.8 2.0 select_add_fusion.4
  429.8 1.9 fusion.78
  434.3 2.6 collective-permute-start.1
  439.4 2.0 select_add_fusion.4
  446.4 310.2 %all-reduce.5 = (bf16[768,768]{1,0:T(8,128)(2,1)}, f32[1,5,768]{2,0,1:T(1,128)}) all-reduce(f32[768,768]{1,0:T(8,128)S(1)} %get-tuple-element.293, f32[1,5,768]{2,0,1:T(1,128)S(1)} %broadcast_in_dim.62), channel_id=1, replica_groups=mesh['dp'=64,'section'=8] {'dp'}, use_global_device_ids=true, to_apply=%region_13.14 | all-reduce | flops 593664 | bytes 3569664 | tf_op jit(solution)/shard_map/psum | solution.py:159
  (465 shorter events, 219.2 us)
Async XLA Ops:
  0.6 3.3 copy-start
  0.6 4.7 copy-start.7
  5.3 164.4 %copy-start.4 = (bf16[4,64,768]{2,1,0:T(8,128)(2,1)S(1)}, bf16[4,64,768]{2,1,0:T(8,128)(2,1)}, u32[]{:S(2)}) copy-start(bf16[4,64,768]{2,1,0:T(8,128)(2,1)} %param.17) | copy-start | bytes 1179652
  10.8 6.5 collective-permute-start
  22.6 6.5 collective-permute-start
  34.5 7.5 collective-permute-start
  47.4 8.6 %collective-permute-start = (bf16[64,768]{1,0:T(8,128)(2,1)S(1)}, bf16[64,768]{1,0:T(8,128)(2,1)S(1)}, u32[]{:S(2)}, u32[]{:S(2)}) collective-permute-start(bf16[64,768]{1,0:T(8,128)(2,1)S(1)} %fusion.71), channel_id=1, source_target_pairs={{7,0},{0,1},{1,2},{2,3},{3,4},{4,5},{5,6},{6,7},{15,8},{8,9},{9,10... | collective-permute-start | bytes 294920 | tf_op jit(solution)/shard_map/while/body/eval_jaxpr/ppermute | solution.py:12
  61.4 8.6 %collective-permute-start = (bf16[64,768]{1,0:T(8,128)(2,1)S(1)}, bf16[64,768]{1,0:T(8,128)(2,1)S(1)}, u32[]{:S(2)}, u32[]{:S(2)}) collective-permute-start(bf16[64,768]{1,0:T(8,128)(2,1)S(1)} %fusion.71), channel_id=1, source_target_pairs={{7,0},{0,1},{1,2},{2,3},{3,4},{4,5},{5,6},{6,7},{15,8},{8,9},{9,10... | collective-permute-start | bytes 294920 | tf_op jit(solution)/shard_map/while/body/eval_jaxpr/ppermute | solution.py:12
  75.4 8.6 %collective-permute-start = (bf16[64,768]{1,0:T(8,128)(2,1)S(1)}, bf16[64,768]{1,0:T(8,128)(2,1)S(1)}, u32[]{:S(2)}, u32[]{:S(2)}) collective-permute-start(bf16[64,768]{1,0:T(8,128)(2,1)S(1)} %fusion.71), channel_id=1, source_target_pairs={{7,0},{0,1},{1,2},{2,3},{3,4},{4,5},{5,6},{6,7},{15,8},{8,9},{9,10... | collective-permute-start | bytes 294920 | tf_op jit(solution)/shard_map/while/body/eval_jaxpr/ppermute | solution.py:12
  89.4 8.7 %collective-permute-start = (bf16[64,768]{1,0:T(8,128)(2,1)S(1)}, bf16[64,768]{1,0:T(8,128)(2,1)S(1)}, u32[]{:S(2)}, u32[]{:S(2)}) collective-permute-start(bf16[64,768]{1,0:T(8,128)(2,1)S(1)} %fusion.71), channel_id=1, source_target_pairs={{7,0},{0,1},{1,2},{2,3},{3,4},{4,5},{5,6},{6,7},{15,8},{8,9},{9,10... | collective-permute-start | bytes 294920 | tf_op jit(solution)/shard_map/while/body/eval_jaxpr/ppermute | solution.py:12
  103.5 9.8 %collective-permute-start = (bf16[64,768]{1,0:T(8,128)(2,1)S(1)}, bf16[64,768]{1,0:T(8,128)(2,1)S(1)}, u32[]{:S(2)}, u32[]{:S(2)}) collective-permute-start(bf16[64,768]{1,0:T(8,128)(2,1)S(1)} %fusion.71), channel_id=1, source_target_pairs={{7,0},{0,1},{1,2},{2,3},{3,4},{4,5},{5,6},{6,7},{15,8},{8,9},{9,10... | collective-permute-start | bytes 294920 | tf_op jit(solution)/shard_map/while/body/eval_jaxpr/ppermute | solution.py:12
  118.7 8.7 %collective-permute-start = (bf16[64,768]{1,0:T(8,128)(2,1)S(1)}, bf16[64,768]{1,0:T(8,128)(2,1)S(1)}, u32[]{:S(2)}, u32[]{:S(2)}) collective-permute-start(bf16[64,768]{1,0:T(8,128)(2,1)S(1)} %fusion.71), channel_id=1, source_target_pairs={{7,0},{0,1},{1,2},{2,3},{3,4},{4,5},{5,6},{6,7},{15,8},{8,9},{9,10... | collective-permute-start | bytes 294920 | tf_op jit(solution)/shard_map/while/body/eval_jaxpr/ppermute | solution.py:12
  132.7 8.7 %collective-permute-start = (bf16[64,768]{1,0:T(8,128)(2,1)S(1)}, bf16[64,768]{1,0:T(8,128)(2,1)S(1)}, u32[]{:S(2)}, u32[]{:S(2)}) collective-permute-start(bf16[64,768]{1,0:T(8,128)(2,1)S(1)} %fusion.71), channel_id=1, source_target_pairs={{7,0},{0,1},{1,2},{2,3},{3,4},{4,5},{5,6},{6,7},{15,8},{8,9},{9,10... | collective-permute-start | bytes 294920 | tf_op jit(solution)/shard_map/while/body/eval_jaxpr/ppermute | solution.py:12
  146.8 8.3 %collective-permute-start = (bf16[64,768]{1,0:T(8,128)(2,1)S(1)}, bf16[64,768]{1,0:T(8,128)(2,1)S(1)}, u32[]{:S(2)}, u32[]{:S(2)}) collective-permute-start(bf16[64,768]{1,0:T(8,128)(2,1)S(1)} %fusion.71), channel_id=1, source_target_pairs={{7,0},{0,1},{1,2},{2,3},{3,4},{4,5},{5,6},{6,7},{15,8},{8,9},{9,10... | collective-permute-start | bytes 294920 | tf_op jit(solution)/shard_map/while/body/eval_jaxpr/ppermute | solution.py:12
  160.5 8.6 %collective-permute-start = (bf16[64,768]{1,0:T(8,128)(2,1)S(1)}, bf16[64,768]{1,0:T(8,128)(2,1)S(1)}, u32[]{:S(2)}, u32[]{:S(2)}) collective-permute-start(bf16[64,768]{1,0:T(8,128)(2,1)S(1)} %fusion.71), channel_id=1, source_target_pairs={{7,0},{0,1},{1,2},{2,3},{3,4},{4,5},{5,6},{6,7},{15,8},{8,9},{9,10... | collective-permute-start | bytes 294920 | tf_op jit(solution)/shard_map/while/body/eval_jaxpr/ppermute | solution.py:12
  177.1 0.7 copy-start.1
  177.8 2.8 copy-start.2
  182.2 12.5 %collective-permute-start.1 = (bf16[64,768]{1,0:T(8,128)(2,1)}, bf16[64,768]{1,0:T(8,128)(2,1)}, u32[]{:S(2)}, u32[]{:S(2)}) collective-permute-start(bf16[64,768]{1,0:T(8,128)(2,1)} %fusion.79), channel_id=1, source_target_pairs={{1,0},{2,1},{3,2},{4,3},{5,4},{6,5},{7,6},{0,7},{9,8},{10,9},{11,1... | collective-permute-start | bytes 294920 | tf_op jit(solution)/shard_map/while/body/eval_jaxpr/ppermute | solution.py:12
  190.7 2.0 copy-start.5
  190.7 2.0 copy-start.6
  202.1 2.8 copy-start.2
  206.5 13.2 %collective-permute-start.1 = (bf16[64,768]{1,0:T(8,128)(2,1)}, bf16[64,768]{1,0:T(8,128)(2,1)}, u32[]{:S(2)}, u32[]{:S(2)}) collective-permute-start(bf16[64,768]{1,0:T(8,128)(2,1)} %fusion.79), channel_id=1, source_target_pairs={{1,0},{2,1},{3,2},{4,3},{5,4},{6,5},{7,6},{0,7},{9,8},{10,9},{11,1... | collective-permute-start | bytes 294920 | tf_op jit(solution)/shard_map/while/body/eval_jaxpr/ppermute | solution.py:12
  215.0 2.0 copy-start.5
  215.0 2.0 copy-start.6
  227.1 2.8 copy-start.2
  231.5 13.2 %collective-permute-start.1 = (bf16[64,768]{1,0:T(8,128)(2,1)}, bf16[64,768]{1,0:T(8,128)(2,1)}, u32[]{:S(2)}, u32[]{:S(2)}) collective-permute-start(bf16[64,768]{1,0:T(8,128)(2,1)} %fusion.79), channel_id=1, source_target_pairs={{1,0},{2,1},{3,2},{4,3},{5,4},{6,5},{7,6},{0,7},{9,8},{10,9},{11,1... | collective-permute-start | bytes 294920 | tf_op jit(solution)/shard_map/while/body/eval_jaxpr/ppermute | solution.py:12
  240.0 2.0 copy-start.5
  240.0 2.0 copy-start.6
  252.1 2.8 copy-start.2
  256.6 9.1 %collective-permute-start.1 = (bf16[64,768]{1,0:T(8,128)(2,1)}, bf16[64,768]{1,0:T(8,128)(2,1)}, u32[]{:S(2)}, u32[]{:S(2)}) collective-permute-start(bf16[64,768]{1,0:T(8,128)(2,1)} %fusion.79), channel_id=1, source_target_pairs={{1,0},{2,1},{3,2},{4,3},{5,4},{6,5},{7,6},{0,7},{9,8},{10,9},{11,1... | collective-permute-start | bytes 294920 | tf_op jit(solution)/shard_map/while/body/eval_jaxpr/ppermute | solution.py:12
  261.0 2.0 copy-start.5
  261.0 2.0 copy-start.6
  273.0 2.8 copy-start.2
  277.5 9.7 %collective-permute-start.1 = (bf16[64,768]{1,0:T(8,128)(2,1)}, bf16[64,768]{1,0:T(8,128)(2,1)}, u32[]{:S(2)}, u32[]{:S(2)}) collective-permute-start(bf16[64,768]{1,0:T(8,128)(2,1)} %fusion.79), channel_id=1, source_target_pairs={{1,0},{2,1},{3,2},{4,3},{5,4},{6,5},{7,6},{0,7},{9,8},{10,9},{11,1... | collective-permute-start | bytes 294920 | tf_op jit(solution)/shard_map/while/body/eval_jaxpr/ppermute | solution.py:12
  282.4 2.0 copy-start.5
  282.4 2.0 copy-start.6
  294.5 2.8 copy-start.2
  298.9 9.1 %collective-permute-start.1 = (bf16[64,768]{1,0:T(8,128)(2,1)}, bf16[64,768]{1,0:T(8,128)(2,1)}, u32[]{:S(2)}, u32[]{:S(2)}) collective-permute-start(bf16[64,768]{1,0:T(8,128)(2,1)} %fusion.79), channel_id=1, source_target_pairs={{1,0},{2,1},{3,2},{4,3},{5,4},{6,5},{7,6},{0,7},{9,8},{10,9},{11,1... | collective-permute-start | bytes 294920 | tf_op jit(solution)/shard_map/while/body/eval_jaxpr/ppermute | solution.py:12
  303.3 2.0 copy-start.5
  303.3 2.0 copy-start.6
  315.4 2.8 copy-start.2
  319.9 9.1 %collective-permute-start.1 = (bf16[64,768]{1,0:T(8,128)(2,1)}, bf16[64,768]{1,0:T(8,128)(2,1)}, u32[]{:S(2)}, u32[]{:S(2)}) collective-permute-start(bf16[64,768]{1,0:T(8,128)(2,1)} %fusion.79), channel_id=1, source_target_pairs={{1,0},{2,1},{3,2},{4,3},{5,4},{6,5},{7,6},{0,7},{9,8},{10,9},{11,1... | collective-permute-start | bytes 294920 | tf_op jit(solution)/shard_map/while/body/eval_jaxpr/ppermute | solution.py:12
  324.3 2.0 copy-start.5
  324.3 2.0 copy-start.6
  336.3 2.8 copy-start.2
  340.8 9.1 %collective-permute-start.1 = (bf16[64,768]{1,0:T(8,128)(2,1)}, bf16[64,768]{1,0:T(8,128)(2,1)}, u32[]{:S(2)}, u32[]{:S(2)}) collective-permute-start(bf16[64,768]{1,0:T(8,128)(2,1)} %fusion.79), channel_id=1, source_target_pairs={{1,0},{2,1},{3,2},{4,3},{5,4},{6,5},{7,6},{0,7},{9,8},{10,9},{11,1... | collective-permute-start | bytes 294920 | tf_op jit(solution)/shard_map/while/body/eval_jaxpr/ppermute | solution.py:12
  345.2 2.0 copy-start.5
  345.2 2.0 copy-start.6
  357.3 2.8 copy-start.2
  361.7 10.7 %collective-permute-start.1 = (bf16[64,768]{1,0:T(8,128)(2,1)}, bf16[64,768]{1,0:T(8,128)(2,1)}, u32[]{:S(2)}, u32[]{:S(2)}) collective-permute-start(bf16[64,768]{1,0:T(8,128)(2,1)} %fusion.79), channel_id=1, source_target_pairs={{1,0},{2,1},{3,2},{4,3},{5,4},{6,5},{7,6},{0,7},{9,8},{10,9},{11,1... | collective-permute-start | bytes 294920 | tf_op jit(solution)/shard_map/while/body/eval_jaxpr/ppermute | solution.py:12
  367.7 2.0 copy-start.5
  367.7 2.0 copy-start.6
  379.8 2.8 copy-start.2
  384.2 13.2 %collective-permute-start.1 = (bf16[64,768]{1,0:T(8,128)(2,1)}, bf16[64,768]{1,0:T(8,128)(2,1)}, u32[]{:S(2)}, u32[]{:S(2)}) collective-permute-start(bf16[64,768]{1,0:T(8,128)(2,1)} %fusion.79), channel_id=1, source_target_pairs={{1,0},{2,1},{3,2},{4,3},{5,4},{6,5},{7,6},{0,7},{9,8},{10,9},{11,1... | collective-permute-start | bytes 294920 | tf_op jit(solution)/shard_map/while/body/eval_jaxpr/ppermute | solution.py:12
  392.7 2.0 copy-start.5
  392.8 2.0 copy-start.6
  404.8 2.8 copy-start.2
  409.3 13.2 %collective-permute-start.1 = (bf16[64,768]{1,0:T(8,128)(2,1)}, bf16[64,768]{1,0:T(8,128)(2,1)}, u32[]{:S(2)}, u32[]{:S(2)}) collective-permute-start(bf16[64,768]{1,0:T(8,128)(2,1)} %fusion.79), channel_id=1, source_target_pairs={{1,0},{2,1},{3,2},{4,3},{5,4},{6,5},{7,6},{0,7},{9,8},{10,9},{11,1... | collective-permute-start | bytes 294920 | tf_op jit(solution)/shard_map/while/body/eval_jaxpr/ppermute | solution.py:12
  417.8 2.0 copy-start.5
  417.8 2.0 copy-start.6
  429.8 2.8 copy-start.2
  434.3 9.8 %collective-permute-start.1 = (bf16[64,768]{1,0:T(8,128)(2,1)}, bf16[64,768]{1,0:T(8,128)(2,1)}, u32[]{:S(2)}, u32[]{:S(2)}) collective-permute-start(bf16[64,768]{1,0:T(8,128)(2,1)} %fusion.79), channel_id=1, source_target_pairs={{1,0},{2,1},{3,2},{4,3},{5,4},{6,5},{7,6},{0,7},{9,8},{10,9},{11,1... | collective-permute-start | bytes 294920 | tf_op jit(solution)/shard_map/while/body/eval_jaxpr/ppermute | solution.py:12
  439.4 2.0 copy-start.5
  439.4 2.0 copy-start.6
  (12 other events, 8.0 us)
where the time goes:
time: 763 us; the launch traced here: 757 us
  blocking collectives  310 us (41%)
  local copies, waits for them, and re-layouts  125 us (16%)
  starting transfers between devices  77.1 us (10%)
  other arithmetic  74.4 us (10%)
  waiting for transfers between devices  68.3 us (9%)
  matrix products  67.8 us (9%)
  loops' own time  33 us (4%)
    psum x1, blocking collectives, body(): summed_weight, summed_taps = lax.psum((grad_weight, grad_taps), 'dp')  310 us
    ppermute x24, starting transfers between devices, from_behind(): return lax.ppermute(block, axis, route)  77.1 us
    ppermute x24, waiting for transfers between devices, from_behind(): return lax.ppermute(block, axis, route)  68.3 us
    another operation x72, local copies, waits for them, and re-layouts, taps_gradient(): return jnp.stack(rows)  45.3 us
    while x108, local copies, waits for them, and re-layouts  26.5 us
    another operation x1, loops' own time, body(): lax.scan(backward_tick, start_state, jnp.arange(ticks, dtype=jnp.int32))  24.5 us
    dot_general x12, matrix products, block_backward(): jnp.dot(activated.T, cotangent, preferred_element_type=jnp.float32)  24.2 us
    dot_general x12, matrix products, block_backward(): grad_act = jnp.dot(cotangent, weight.T, preferred_element_type=jnp.float32)  22.2 us
  transfers between devices with their start and end apart: 24, of which 12 were waited for; matrix products, arithmetic and copies ran while one was open for 11% of the time, Pallas kernels for 0%

commit v1 on v0

v1 whole, which is shorter than its diff:
```python
import itertools

import jax
import jax.numpy as jnp
from jax import lax
from jax.experimental import pallas as pl
from jax.experimental.pallas import tpu as pltpu
from jax.sharding import Mesh, PartitionSpec as P

EPS = 1e-06
BF = jnp.bfloat16
F32 = jnp.float32

D = 768
H = 384
KER = 5
FEAT = 512
T = 64
L = 8
TAPS = 16
PIECE = H + TAPS
INROWS = T + 16
PAY = T + T // 2 + TAPS
PEERS = 32
CHUNK = 72
CROWS = 80
MIB = 1024 * 1024

VMEM = pl.BlockSpec(memory_space=pltpu.VMEM)
ANY = pl.BlockSpec(memory_space=pl.ANY)
SMEM = pl.BlockSpec(memory_space=pltpu.SMEM)


def route(shape, step):
    spots = list(itertools.product(*map(range, shape)))
    place = {spot: i for i, spot in enumerate(spots)}
    return [(place[spot], place[step(*spot)]) for spot in spots]


def split3(x):
    hi = x.astype(BF).astype(F32)
    rest = x - hi
    mid = rest.astype(BF).astype(F32)
    return hi, mid, rest - mid


def where_am_i():
    section = 2 * lax.axis_index("x") + lax.axis_index("zl")
    return section, lax.axis_index("c")


def prep_kernel(w_ref, taps_ref, feat_ref, targ_ref, len_ref, near_ref, far_ref, io_ref):
    section, core = where_am_i()
    utt = lax.rem(section, 4)
    hi, mid, low = split3(taps_ref[0])
    packed = jnp.concatenate([hi, mid, low, jnp.zeros((1, D), F32)], axis=0).astype(BF)
    mine = pl.multiple_of(core * H, H)
    theirs = pl.multiple_of((1 - core) * H, H)
    near_ref[0:H, :] = w_ref[0, pl.ds(mine, H), :]
    near_ref[H:PIECE, :] = packed
    far_ref[...] = w_ref[0, pl.ds(theirs, H), :]
    io_ref[0:T, 0:FEAT] = feat_ref[utt]
    io_ref[0:T, FEAT:] = targ_ref[utt]
    count = len_ref[utt].astype(F32)
    io_ref[T:, :] = jnp.full((INROWS - T, FEAT + D), count, F32).astype(BF)


def model_kernel(
    io_a_ref, io_b_ref, front_ref,
    n0, f0, n1, f1, n2, n3, n4, f4, n5, m1, g1, m2, m3, m4, g4, m5,
    pay_ref,
    w_ref, traw_ref, taps_ref, vals_ref, inv_ref, norm_ref, slope_ref, act_ref, gpad_ref, g_ref,
    sem,
):
    section, core = where_am_i()
    col = lax.div(section, 2)
    row = lax.rem(section, 2)
    other = 1 - core
    side = lax.rem(col + 3 + 2 * core, 4)
    anti = lax.rem(col + 1 + 2 * core, 4)
    across = lax.rem(col + 2, 4)
    copies = []

    def bring(piece, c, r, part, with_taps):
        layer = 2 * c + r
        k = len(copies)
        start = pl.multiple_of(part * H, H)
        copies.append(pltpu.make_async_copy(
            piece.at[pl.ds(0, H)], w_ref.at[layer, pl.ds(start, H)], sem.at[k]))
        if with_taps:
            copies.append(pltpu.make_async_copy(
                piece.at[pl.ds(H, TAPS)], traw_ref.at[layer], sem.at[k + 1]))

    flip = 1 - row
    bring(n0, col, row, core, True)
    bring(f0, col, row, other, False)
    bring(n1, side, row, core, True)
    bring(f1, side, row, other, False)
    bring(n2, across, row, core, True)
    bring(n3, col, flip, core, True)
    bring(n4, side, flip, core, True)
    bring(f4, side, flip, other, False)
    bring(n5, across, flip, core, True)
    bring(m1, anti, row, other, True)
    bring(g1, anti, row, core, False)
    bring(m2, across, row, other, False)
    bring(m3, col, flip, other, False)
    bring(m4, anti, flip, other, True)
    bring(g4, anti, flip, core, False)
    bring(m5, across, flip, other, False)
    for copy in copies:
        copy.start()

    own = core == lax.div(section, 4)
    pick = jnp.where(own, 1.0, 0.0).astype(F32)
    io = io_a_ref[...].astype(F32) * pick + io_b_ref[...].astype(F32) * (1.0 - pick)
    count = io[T:T + 1, 0:1]
    target = io[0:T, FEAT:]
    frame = lax.broadcasted_iota(jnp.int32, (T, 1), 0).astype(F32)
    mask = jnp.where(frame < count, 1.0, 0.0).astype(F32)
    hidden = jnp.dot(io[0:T, 0:FEAT].astype(BF), front_ref[...], preferred_element_type=F32)
    g_ref[...] = hidden.astype(BF).astype(F32)

    edge = jnp.zeros((8, D), F32)
    gpad_ref[0:8, :] = edge
    gpad_ref[T + 8:, :] = edge
    for copy in copies:
        copy.wait()

    def forward(l, carry):
        raw = traw_ref[l].astype(F32)
        taps = raw[0:KER] + raw[KER:2 * KER] + raw[2 * KER:3 * KER]
        taps_ref[l, 0:KER, :] = taps
        vals = g_ref[...]
        inv = lax.rsqrt(jnp.mean(vals * vals, axis=-1, keepdims=True) + EPS)
        norm = vals * inv * mask
        vals_ref[l] = vals
        inv_ref[l] = jnp.broadcast_to(inv, (T, 128))
        norm_ref[l, 0:8, :] = edge
        norm_ref[l, T + 8:, :] = edge
        norm_ref[l, 8:T + 8, :] = norm
        conv = taps[0:1] * norm_ref[l, 6:T + 6, :]
        for k in range(1, KER):
            conv = conv + taps[k:k + 1] * norm_ref[l, 6 + k:T + 6 + k, :]
        sig = jax.nn.sigmoid(conv)
        act = (conv * sig).astype(BF)
        slope_ref[l] = sig * (1.0 + conv * (1.0 - sig))
        act_ref[l] = act
        out = vals + jnp.dot(act, w_ref[l], preferred_element_type=F32)
        g_ref[...] = out.astype(BF).astype(F32)
        return carry

    lax.fori_loop(0, L, forward, 0)

    g_ref[...] = ((g_ref[...] - target) * mask / count).astype(BF).astype(F32)

    def backward(i, carry):
        l = L - 1 - i
        g = g_ref[...]
        gb = g.astype(BF)
        pay_ref[l, 0:T, :] = gb
        act = act_ref[l].astype(F32)
        share = jnp.where(core == 0, act[:, 0:H], act[:, H:])
        pay_ref[l, T:T + T // 2, 0:H] = share[0:T // 2].astype(BF)
        pay_ref[l, T:T + T // 2, H:] = share[T // 2:].astype(BF)
        grad_act = lax.dot_general(
            gb, w_ref[l], (((1,), (1,)), ((), ())), preferred_element_type=F32)
        grad_conv = grad_act * slope_ref[l]
        gpad_ref[8:T + 8, :] = grad_conv
        taps = taps_ref[l, 0:KER, :]
        rows = []
        for k in range(KER):
            rows.append(jnp.sum(grad_conv * norm_ref[l, 6 + k:T + 6 + k, :], axis=0, keepdims=True))
        total = jnp.concatenate(rows, axis=0)
        hi = total.astype(BF).astype(F32)
        packed = jnp.concatenate([hi, total - hi, jnp.zeros((TAPS - 2 * KER, D), F32)], axis=0)
        pay_ref[l, T + T // 2:, :] = packed.astype(BF)
        grad_norm = taps[0:1] * gpad_ref[10:T + 10, :]
        for k in range(1, KER):
            grad_norm = grad_norm + taps[k:k + 1] * gpad_ref[10 - k:T + 10 - k, :]
        grad_norm = grad_norm * mask
        vals = vals_ref[l]
        inv = inv_ref[l][:, 0:1]
        mean = jnp.mean(grad_norm * vals, axis=-1, keepdims=True)
        g_ref[...] = (g + (inv * grad_norm - vals * (inv * inv * inv * mean))).astype(BF).astype(F32)
        return carry

    lax.fori_loop(0, L, backward, 0)


def grad_kernel(recv_ref, out_ref, act_ref, flat_ref, row_ref, chunk_ref):
    half = T // 2
    for i in range(L):
        act_ref[i * T:i * T + half, :] = recv_ref[i, T:T + half, 0:H]
        act_ref[i * T + half:(i + 1) * T, :] = recv_ref[i, T:T + half, H:]
    g = recv_ref[:, 0:T, :].reshape(L * T, D)
    grad = lax.dot_general(
        act_ref[...], g, (((0,), (0,)), ((), ())), preferred_element_type=F32)
    for b in range(D // 128):
        flat_ref[b * H:(b + 1) * H, :] = grad[:, b * 128:(b + 1) * 128]
    taps = recv_ref[0, T + half:, :].astype(F32)
    for i in range(1, L):
        taps = taps + recv_ref[i, T + half:, :].astype(F32)
    total = taps[0:KER] + taps[KER:2 * KER]
    hi = total.astype(BF).astype(F32)
    low = total - hi
    chunk_ref[CHUNK:, :] = jnp.zeros((CROWS - CHUNK, 128), F32)
    for j in range(PEERS):
        chunk_ref[0:CHUNK, :] = flat_ref[j * CHUNK:(j + 1) * CHUNK, :]
        if j < KER * 6:
            k, b = divmod(j, 6)
            chunk_ref[CHUNK:CHUNK + 1, :] = hi[k:k + 1, b * 128:(b + 1) * 128]
            chunk_ref[CHUNK + 1:CHUNK + 2, :] = low[k:k + 1, b * 128:(b + 1) * 128]
        out_ref[j] = chunk_ref[...].astype(BF)


def sum_kernel(parts_ref, out_ref, chunk_ref):
    total = parts_ref[0].astype(F32)
    for j in range(1, PEERS):
        total = total + parts_ref[j].astype(F32)
    chunk_ref[...] = total
    tap = total[CHUNK:CHUNK + 1] + total[CHUNK + 1:CHUNK + 2]
    hi = tap.astype(BF).astype(F32)
    chunk_ref[CHUNK:CHUNK + 1, :] = hi
    chunk_ref[CHUNK + 1:CHUNK + 2, :] = tap - hi
    mine = chunk_ref[...].astype(BF)
    for j in range(PEERS):
        out_ref[j] = mine


def place_kernel(mine_ref, theirs_ref, grad_ref, taps_ref, flat_ref):
    core = lax.axis_index("c")
    for ref, which in ((mine_ref, core), (theirs_ref, 1 - core)):
        start = pl.multiple_of(which * H, H)
        for j in range(PEERS):
            flat_ref[j * CHUNK:(j + 1) * CHUNK, :] = ref[j, 0:CHUNK, :].astype(F32)
        for b in range(D // 128):
            grad_ref[0, pl.ds(start, H), b * 128:(b + 1) * 128] = (
                flat_ref[b * H:(b + 1) * H, :].astype(BF))
    for j in range(KER * 6):
        k, b = divmod(j, 6)
        pair = mine_ref[j, CHUNK:, :].astype(F32)
        taps_ref[0, k:k + 1, b * 128:(b + 1) * 128] = pair[0:1] + pair[1:2]


def params(mib):
    return pltpu.CompilerParams(vmem_limit_bytes=mib * MIB)


def body(features, lengths, front_weight, pointwise, kernel, targets):
    ring = route((2, 4), lambda c, x: (c, (x + 1 if c == 0 else x - 1) % 4))
    pair = route(
        (4, 2, 2),
        lambda h, c, z: (h, c, 1 - z) if c == 0 else ((h + 2 * z - 1) % 4, c, 1 - z),
    )

    def along_x(a):
        return lax.ppermute(a, ("c", "x"), ring)

    def along_z(a):
        return lax.ppermute(a, ("zh", "c", "zl"), pair)

    def to_core(a):
        return lax.ppermute(a, "c", [(0, 1), (1, 0)])

    near, far, io = pl.pallas_call(
        prep_kernel,
        name="prep",
        out_shape=(
            jax.ShapeDtypeStruct((PIECE, D), BF),
            jax.ShapeDtypeStruct((H, D), BF),
            jax.ShapeDtypeStruct((INROWS, FEAT + D), BF),
        ),
        in_specs=[VMEM, VMEM, VMEM, VMEM, SMEM],
        out_specs=(VMEM, VMEM, VMEM),
    )(pointwise, kernel, features, targets, lengths)

    n1 = along_x(near)
    n3 = along_z(near)
    f1 = along_x(far)
    io_other = to_core(io)
    n2 = along_x(n1)
    n4 = along_z(n1)
    f4 = along_z(f1)
    n5 = along_z(n2)
    here = [near, far, n1, f1, n2, n3, n4, f4, n5]
    there = [to_core(a) for a in (n1, f1, n2, n3, n4, f4, n5)]

    payload = pl.pallas_call(
        model_kernel,
        name="model",
        out_shape=jax.ShapeDtypeStruct((L, PAY, D), BF),
        in_specs=[VMEM, VMEM, VMEM] + [ANY] * 16,
        out_specs=VMEM,
        scratch_shapes=[
            pltpu.VMEM((L, D, D), BF),
            pltpu.VMEM((L, TAPS, D), BF),
            pltpu.VMEM((L, 8, D), F32),
            pltpu.VMEM((L, T, D), F32),
            pltpu.VMEM((L, T, 128), F32),
            pltpu.VMEM((L, T + 16, D), F32),
            pltpu.VMEM((L, T, D), F32),
            pltpu.VMEM((L, T, D), BF),
            pltpu.VMEM((T + 16, D), F32),
            pltpu.VMEM((T, D), F32),
            pltpu.SemaphoreType.DMA((32,)),
        ],
        compiler_params=params(40),
    )(io, io_other, front_weight, *here, *there)

    received = lax.all_to_all(payload, ("x", "zl"), 0, 0)

    parts = pl.pallas_call(
        grad_kernel,
        name="grad",
        out_shape=jax.ShapeDtypeStruct((PEERS, CROWS, 128), BF),
        in_specs=[VMEM],
        out_specs=VMEM,
        scratch_shapes=[
            pltpu.VMEM((L * T, H), BF),
            pltpu.VMEM((H * 6, 128), F32),
            pltpu.VMEM((8, D), F32),
            pltpu.VMEM((CROWS, 128), F32),
        ],
        compiler_params=params(24),
    )(received)

    scattered = lax.all_to_all(parts, ("y", "zh"), 0, 0)

    mine = pl.pallas_call(
        sum_kernel,
        name="total",
        out_shape=jax.ShapeDtypeStruct((PEERS, CROWS, 128), BF),
        in_specs=[VMEM],
        out_specs=VMEM,
        scratch_shapes=[pltpu.VMEM((CROWS, 128), F32)],
        compiler_params=params(16),
    )(scattered)

    half = lax.all_to_all(mine, ("y", "zh"), 0, 0)
    other_half = to_core(half)

    return pl.pallas_call(
        place_kernel,
        name="place",
        out_shape=(
            jax.ShapeDtypeStruct((1, D, D), BF),
            jax.ShapeDtypeStruct((1, KER, D), F32),
        ),
        in_specs=[VMEM, VMEM],
        out_specs=(VMEM, VMEM),
        scratch_shapes=[pltpu.VMEM((H * 6, 128), F32)],
        compiler_params=params(16),
    )(half, other_half)


def solution(mesh):
    fine = Mesh(mesh.devices.reshape(8, 4, 2, 4, 2), ("y", "zh", "c", "x", "zl"))
    dp = ("y", "zh", "c")
    section = ("x", "zl")
    return jax.shard_map(
        body,
        mesh=fine,
        in_specs=(
            P(dp, None, None),
            P(dp),
            P(),
            P(section, None, None),
            P(section, None, None),
            P(dp, None, None),
        ),
        out_specs=(P(section, None, None), P(section, None, None)),
        check_vma=False,
    )
```

time: 763 us -> 177 us (0.23)
  the two profiles are of different devices: /device:TPU:66 before, /device:TPU:9 now
where the time goes in v1:
time: 177 us; the launch traced here: 176 us
  blocking collectives  77.6 us (44%)
  starting transfers between devices  56.6 us (32%)
  Pallas kernels  18.9 us (11%)
  waiting for transfers between devices  17.4 us (10%)
  local copies, waits for them, and re-layouts  5.08 us (3%)
    all_to_all x1, blocking collectives, body(): scattered = lax.all_to_all(parts, ('y', 'zh'), 0, 0)  28.7 us
    all_to_all x1, blocking collectives, body(): half = lax.all_to_all(mine, ('y', 'zh'), 0, 0)  27.6 us
    ppermute x4, starting transfers between devices, along_z(): return lax.ppermute(a, ('zh', 'c', 'zl'), pair)  23 us
    ppermute x9, starting transfers between devices, to_core(): return lax.ppermute(a, 'c', [(0, 1), (1, 0)])  22.4 us
    all_to_all x1, blocking collectives, body(): received = lax.all_to_all(payload, ('x', 'zl'), 0, 0)  21.3 us
    pallas_call x1, Pallas kernels, body(): pl.pallas_call(model_kernel, name='model', out_shape=jax.ShapeDtypeStruct...  14.4 us
    ppermute x3, starting transfers between devices, along_x(): return lax.ppermute(a, ('c', 'x'), ring)  11.2 us
    ppermute x3, waiting for transfers between devices, along_x(): return lax.ppermute(a, ('c', 'x'), ring)  8.14 us
  transfers between devices with their start and end apart: 16, of which 5 were waited for; matrix products, arithmetic and copies ran while one was open for 0% of the time, Pallas kernels for 0%

profile of v1, /device:TPU:9, one launch (start us, length us, event | category | flops | bytes accessed | tf_op | source)
XLA Modules:
  0.0 176.4 jit_solution(7486572106666803755)
XLA Ops:
  0.6 0.0 copy-start
  0.6 1.4 copy.8.taps_ref
  2.0 2.6 %prep.1 = (bf16[400,768]{1,0:T(8,128)(2,1)}, bf16[384,768]{1,0:T(8,128)(2,1)}, bf16[80,1280]{1,0:T(8,128)(2,1)}) custom-call(bf16[1,768,768]{2,1,0:T(8,128)(2,1)} %w_ref.1, f32[1,5,768]{2,1,0:T(8,128)} %copy.8.taps_ref, bf16[4,64,512]{2,1,0:T(8,128)(2,1)} %feat_ref.1, bf16[4,64,768]{2,1,0:T(8,128)(2,1)} %targ_ref.1, s32[4]{0:T(128)} %len_ref.1), custom_call_target="tpu_custom_call" | custom-call | tf_op jit(solution)/shard_map/prep/pallas_call | solution.py:266
  4.7 4.4 %collective-permute-start.1 = (bf16[400,768]{1,0:T(8,128)(2,1)}, bf16[400,768]{1,0:T(8,128)(2,1)S(1)}, u32[]{:S(2)}, u32[]{:S(2)}) collective-permute-start(bf16[400,768]{1,0:T(8,128)(2,1)} %get-tuple-element.6.n0), channel_id=1, source_target_pairs={{0,2},{2,4},{4,6},{6,0},{8,14},{10,8},{12,10},{14,12},{1,3},{3,5},... | collective-permute-start | bytes 1843208 | tf_op jit(solution)/shard_map/ppermute | solution.py:258
  9.1 7.4 %collective-permute-done.1.n1 = bf16[400,768]{1,0:T(8,128)(2,1)S(1)} collective-permute-done((bf16[400,768]{1,0:T(8,128)(2,1)}, bf16[400,768]{1,0:T(8,128)(2,1)S(1)}, u32[]{:S(2)}, u32[]{:S(2)}) %collective-permute-start.1) | collective-permute-done | bytes 614432 | tf_op jit(solution)/shard_map/ppermute | solution.py:258
  16.4 4.9 %collective-permute-start.3 = (bf16[400,768]{1,0:T(8,128)(2,1)S(1)}, bf16[400,768]{1,0:T(8,128)(2,1)S(1)}, u32[]{:S(2)}, u32[]{:S(2)}) collective-permute-start(bf16[400,768]{1,0:T(8,128)(2,1)S(1)} %collective-permute-done.1.n1), channel_id=1, source_target_pairs={{0,2},{2,4},{4,6},{6,0},{8,14},{10,8},{12,10},{14,12},{1,3},{3,5},... | collective-permute-start | bytes 1843208 | tf_op jit(solution)/shard_map/ppermute | solution.py:258
  21.4 10.7 %collective-permute-start.4 = (bf16[400,768]{1,0:T(8,128)(2,1)}, bf16[400,768]{1,0:T(8,128)(2,1)S(1)}, u32[]{:S(2)}, u32[]{:S(2)}) collective-permute-start(bf16[400,768]{1,0:T(8,128)(2,1)} %get-tuple-element.6.n0), channel_id=1, source_target_pairs={{0,1},{1,0},{8,57},{9,24},{16,17},{17,16},{24,9},{25,40},{32,33},{... | collective-permute-start | bytes 1843208 | tf_op jit(solution)/shard_map/ppermute | solution.py:261
  32.0 1.9 %collective-permute-start.2 = (bf16[384,768]{1,0:T(8,128)(2,1)}, bf16[384,768]{1,0:T(8,128)(2,1)S(1)}, u32[]{:S(2)}, u32[]{:S(2)}) collective-permute-start(bf16[384,768]{1,0:T(8,128)(2,1)} %get-tuple-element.7.f0), channel_id=1, source_target_pairs={{0,2},{2,4},{4,6},{6,0},{8,14},{10,8},{12,10},{14,12},{1,3},{3,5},... | collective-permute-start | bytes 1769480 | tf_op jit(solution)/shard_map/ppermute | solution.py:258
  34.0 1.9 %collective-permute-start = (bf16[80,1280]{1,0:T(8,128)(2,1)}, bf16[80,1280]{1,0:T(8,128)(2,1)S(1)}, u32[]{:S(2)}, u32[]{:S(2)}) collective-permute-start(bf16[80,1280]{1,0:T(8,128)(2,1)} %get-tuple-element.5.io_a_ref), channel_id=1, source_target_pairs={{0,8},{8,0},{1,9},{9,1},{2,10},{10,2},{3,11},{11,3},{4,12},{12,4},... | collective-permute-start | bytes 614408 | tf_op jit(solution)/shard_map/ppermute | solution.py:264
  35.9 3.6 %collective-permute-start.5 = (bf16[400,768]{1,0:T(8,128)(2,1)S(1)}, bf16[400,768]{1,0:T(8,128)(2,1)S(1)}, u32[]{:S(2)}, u32[]{:S(2)}) collective-permute-start(bf16[400,768]{1,0:T(8,128)(2,1)S(1)} %collective-permute-done.1.n1), channel_id=1, source_target_pairs={{0,1},{1,0},{8,57},{9,24},{16,17},{17,16},{24,9},{25,40},{32,33},{... | collective-permute-start | bytes 1843208 | tf_op jit(solution)/shard_map/ppermute | solution.py:261
  39.4 0.0 collective-permute-done.3.n2
  39.5 2.9 %collective-permute-start.7 = (bf16[400,768]{1,0:T(8,128)(2,1)S(1)}, bf16[400,768]{1,0:T(8,128)(2,1)S(1)}, u32[]{:S(2)}, u32[]{:S(2)}) collective-permute-start(bf16[400,768]{1,0:T(8,128)(2,1)S(1)} %collective-permute-done.3.n2), channel_id=1, source_target_pairs={{0,1},{1,0},{8,57},{9,24},{16,17},{17,16},{24,9},{25,40},{32,33},{... | collective-permute-start | bytes 1843208 | tf_op jit(solution)/shard_map/ppermute | solution.py:261
  42.4 0.8 collective-permute-done.2.f1
  43.2 1.9 %collective-permute-start.9 = (bf16[384,768]{1,0:T(8,128)(2,1)S(1)}, bf16[384,768]{1,0:T(8,128)(2,1)S(1)}, u32[]{:S(2)}, u32[]{:S(2)}) collective-permute-start(bf16[384,768]{1,0:T(8,128)(2,1)S(1)} %collective-permute-done.2.f1), channel_id=1, source_target_pairs={{0,8},{8,0},{1,9},{9,1},{2,10},{10,2},{3,11},{11,3},{4,12},{12,4},... | collective-permute-start | bytes 1769480 | tf_op jit(solution)/shard_map/ppermute | solution.py:264
  45.1 0.0 collective-permute-done.io_b_ref
  45.1 5.8 %collective-permute-start.6 = (bf16[384,768]{1,0:T(8,128)(2,1)S(1)}, bf16[384,768]{1,0:T(8,128)(2,1)S(1)}, u32[]{:S(2)}, u32[]{:S(2)}) collective-permute-start(bf16[384,768]{1,0:T(8,128)(2,1)S(1)} %collective-permute-done.2.f1), channel_id=1, source_target_pairs={{0,1},{1,0},{8,57},{9,24},{16,17},{17,16},{24,9},{25,40},{32,33},{... | collective-permute-start | bytes 1769480 | tf_op jit(solution)/shard_map/ppermute | solution.py:261
  50.9 0.0 collective-permute-done.4.n3
  51.0 1.9 %collective-permute-start.11 = (bf16[400,768]{1,0:T(8,128)(2,1)S(1)}, bf16[400,768]{1,0:T(8,128)(2,1)S(1)}, u32[]{:S(2)}, u32[]{:S(2)}) collective-permute-start(bf16[400,768]{1,0:T(8,128)(2,1)S(1)} %collective-permute-done.4.n3), channel_id=1, source_target_pairs={{0,8},{8,0},{1,9},{9,1},{2,10},{10,2},{3,11},{11,3},{4,12},{12,4},... | collective-permute-start | bytes 1843208 | tf_op jit(solution)/shard_map/ppermute | solution.py:264
  52.9 0.0 collective-permute-done.9.g1
  52.9 2.4 %collective-permute-start.8 = (bf16[400,768]{1,0:T(8,128)(2,1)S(1)}, bf16[400,768]{1,0:T(8,128)(2,1)S(1)}, u32[]{:S(2)}, u32[]{:S(2)}) collective-permute-start(bf16[400,768]{1,0:T(8,128)(2,1)S(1)} %collective-permute-done.1.n1), channel_id=1, source_target_pairs={{0,8},{8,0},{1,9},{9,1},{2,10},{10,2},{3,11},{11,3},{4,12},{12,4},... | collective-permute-start | bytes 1843208 | tf_op jit(solution)/shard_map/ppermute | solution.py:264
  55.3 5.6 %collective-permute-done.6.f4 = bf16[384,768]{1,0:T(8,128)(2,1)S(1)} collective-permute-done((bf16[384,768]{1,0:T(8,128)(2,1)S(1)}, bf16[384,768]{1,0:T(8,128)(2,1)S(1)}, u32[]{:S(2)}, u32[]{:S(2)}) %collective-permute-start.6) | collective-permute-done | bytes 589856 | tf_op jit(solution)/shard_map/ppermute | solution.py:261
  60.9 2.3 %collective-permute-start.10 = (bf16[400,768]{1,0:T(8,128)(2,1)S(1)}, bf16[400,768]{1,0:T(8,128)(2,1)S(1)}, u32[]{:S(2)}, u32[]{:S(2)}) collective-permute-start(bf16[400,768]{1,0:T(8,128)(2,1)S(1)} %collective-permute-done.3.n2), channel_id=1, source_target_pairs={{0,8},{8,0},{1,9},{9,1},{2,10},{10,2},{3,11},{11,3},{4,12},{12,4},... | collective-permute-start | bytes 1843208 | tf_op jit(solution)/shard_map/ppermute | solution.py:264
  63.2 0.0 collective-permute-done.5.n4
  63.2 2.0 %collective-permute-start.12 = (bf16[400,768]{1,0:T(8,128)(2,1)S(1)}, bf16[400,768]{1,0:T(8,128)(2,1)S(1)}, u32[]{:S(2)}, u32[]{:S(2)}) collective-permute-start(bf16[400,768]{1,0:T(8,128)(2,1)S(1)} %collective-permute-done.5.n4), channel_id=1, source_target_pairs={{0,8},{8,0},{1,9},{9,1},{2,10},{10,2},{3,11},{11,3},{4,12},{12,4},... | collective-permute-start | bytes 1843208 | tf_op jit(solution)/shard_map/ppermute | solution.py:264
  65.2 0.0 collective-permute-done.7.n5
  65.2 2.3 %collective-permute-start.14 = (bf16[400,768]{1,0:T(8,128)(2,1)S(1)}, bf16[400,768]{1,0:T(8,128)(2,1)S(1)}, u32[]{:S(2)}, u32[]{:S(2)}) collective-permute-start(bf16[400,768]{1,0:T(8,128)(2,1)S(1)} %collective-permute-done.7.n5), channel_id=1, source_target_pairs={{0,8},{8,0},{1,9},{9,1},{2,10},{10,2},{3,11},{11,3},{4,12},{12,4},... | collective-permute-start | bytes 1843208 | tf_op jit(solution)/shard_map/ppermute | solution.py:264
  67.6 0.0 collective-permute-done.11.m3
  67.6 2.0 %collective-permute-start.13 = (bf16[384,768]{1,0:T(8,128)(2,1)S(1)}, bf16[384,768]{1,0:T(8,128)(2,1)S(1)}, u32[]{:S(2)}, u32[]{:S(2)}) collective-permute-start(bf16[384,768]{1,0:T(8,128)(2,1)S(1)} %collective-permute-done.6.f4), channel_id=1, source_target_pairs={{0,8},{8,0},{1,9},{9,1},{2,10},{10,2},{3,11},{11,3},{4,12},{12,4},... | collective-permute-start | bytes 1769480 | tf_op jit(solution)/shard_map/ppermute | solution.py:264
  69.6 0.0 collective-permute-done.8.m1
  69.6 1.9 %collective-permute-done.13.g4 = bf16[384,768]{1,0:T(8,128)(2,1)S(1)} collective-permute-done((bf16[384,768]{1,0:T(8,128)(2,1)S(1)}, bf16[384,768]{1,0:T(8,128)(2,1)S(1)}, u32[]{:S(2)}, u32[]{:S(2)}) %collective-permute-start.13) | collective-permute-done | bytes 589856 | tf_op jit(solution)/shard_map/ppermute | solution.py:264
  71.5 0.0 collective-permute-done.12.m4
  71.5 0.0 collective-permute-done.10.m2
  71.5 0.0 collective-permute-done.14.m5
  71.5 0.0 copy-done
  71.5 0.0 copy-start.1
  71.5 1.1 copy-done.1
  72.6 0.0 copy-start.2
  72.6 1.1 copy-done.2
  73.7 0.0 copy-start.3
  73.7 0.9 copy-done.3
  74.6 14.4 %model.1 = bf16[8,112,768]{2,1,0:T(8,128)(2,1)S(1)} custom-call(bf16[80,1280]{1,0:T(8,128)(2,1)S(1)} %copy-done.3, bf16[80,1280]{1,0:T(8,128)(2,1)S(1)} %collective-permute-done.io_b_ref, bf16[512,768]{1,0:T(8,128)(2,1)S(1)} %copy-done, bf16[400,768]{1,0:T(8,128)(2,1)S(1)} %copy-done.1, bf16[384,768]{1,0:T(8,128)(2,1)S(1)} %copy-done.2, ...), custom_call_target="tpu_custom_call" | custom-call | tf_op jit(solution)/shard_map/model/pallas_call | solution.py:289
  89.0 21.3 %all_to_all.15.recv_ref = bf16[8,112,768]{2,1,0:T(8,128)(2,1)S(1)} all-to-all(bf16[8,112,768]{2,1,0:T(8,128)(2,1)S(1)} %model.1), channel_id=1, replica_groups=mesh['y'=8,'zh'=4,'c'=2,'x'=4,'zl'=2] {'x','zl'}, dimensions={0} | all-to-all | bytes 2752512 | tf_op jit(solution)/shard_map/all_to_all | solution.py:311
  110.3 0.6 grad.1
  110.9 28.7 %all_to_all.16.parts_ref = bf16[32,80,128]{2,1,0:T(8,128)(2,1)S(1)} all-to-all(bf16[32,80,128]{2,1,0:T(8,128)(2,1)S(1)} %grad.1), channel_id=1, replica_groups=mesh['y'=8,'zh'=4,'c'=2,'x'=4,'zl'=2] {'y','zh'}, dimensions={0} | all-to-all | bytes 1310720 | tf_op jit(solution)/shard_map/all_to_all | solution.py:328
  139.6 0.1 total.1
  139.7 27.6 %all_to_all.17.mine_ref = bf16[32,80,128]{2,1,0:T(8,128)(2,1)S(1)} all-to-all(bf16[32,80,128]{2,1,0:T(8,128)(2,1)S(1)} %total.1), channel_id=1, replica_groups=mesh['y'=8,'zh'=4,'c'=2,'x'=4,'zl'=2] {'y','zh'}, dimensions={0} | all-to-all | bytes 1310720 | tf_op jit(solution)/shard_map/all_to_all | solution.py:340
  167.3 5.6 %collective-permute-start.15 = (bf16[32,80,128]{2,1,0:T(8,128)(2,1)S(1)}, bf16[32,80,128]{2,1,0:T(8,128)(2,1)S(1)}, u32[]{:S(2)}, u32[]{:S(2)}) collective-permute-start(bf16[32,80,128]{2,1,0:T(8,128)(2,1)S(1)} %all_to_all.17.mine_ref), channel_id=1, source_target_pairs={{0,8},{8,0},{1,9},{9,1},{2,10},{10,2},{3,11},{11,3},{4,12},{12,4},... | collective-permute-start | bytes 1966088 | tf_op jit(solution)/shard_map/ppermute | solution.py:264
  172.9 1.7 collective-permute-done.15.theirs_ref
  174.6 1.2 place.1
  175.8 0.6 copy.9
Async XLA Ops:
  0.6 70.9 %copy-start = (bf16[512,768]{1,0:T(8,128)(2,1)S(1)}, bf16[512,768]{1,0:T(8,128)(2,1)}, u32[]{:S(2)}) copy-start(bf16[512,768]{1,0:T(8,128)(2,1)} %front_ref.1) | copy-start | bytes 2359300
  4.7 11.8 %collective-permute-start.1 = (bf16[400,768]{1,0:T(8,128)(2,1)}, bf16[400,768]{1,0:T(8,128)(2,1)S(1)}, u32[]{:S(2)}, u32[]{:S(2)}) collective-permute-start(bf16[400,768]{1,0:T(8,128)(2,1)} %get-tuple-element.6.n0), channel_id=1, source_target_pairs={{0,2},{2,4},{4,6},{6,0},{8,14},{10,8},{12,10},{14,12},{1,3},{3,5},... | collective-permute-start | bytes 1843208 | tf_op jit(solution)/shard_map/ppermute | solution.py:258
  16.4 23.0 %collective-permute-start.3 = (bf16[400,768]{1,0:T(8,128)(2,1)S(1)}, bf16[400,768]{1,0:T(8,128)(2,1)S(1)}, u32[]{:S(2)}, u32[]{:S(2)}) collective-permute-start(bf16[400,768]{1,0:T(8,128)(2,1)S(1)} %collective-permute-done.1.n1), channel_id=1, source_target_pairs={{0,2},{2,4},{4,6},{6,0},{8,14},{10,8},{12,10},{14,12},{1,3},{3,5},... | collective-permute-start | bytes 1843208 | tf_op jit(solution)/shard_map/ppermute | solution.py:258
  21.4 29.6 %collective-permute-start.4 = (bf16[400,768]{1,0:T(8,128)(2,1)}, bf16[400,768]{1,0:T(8,128)(2,1)S(1)}, u32[]{:S(2)}, u32[]{:S(2)}) collective-permute-start(bf16[400,768]{1,0:T(8,128)(2,1)} %get-tuple-element.6.n0), channel_id=1, source_target_pairs={{0,1},{1,0},{8,57},{9,24},{16,17},{17,16},{24,9},{25,40},{32,33},{... | collective-permute-start | bytes 1843208 | tf_op jit(solution)/shard_map/ppermute | solution.py:261
  32.0 11.1 %collective-permute-start.2 = (bf16[384,768]{1,0:T(8,128)(2,1)}, bf16[384,768]{1,0:T(8,128)(2,1)S(1)}, u32[]{:S(2)}, u32[]{:S(2)}) collective-permute-start(bf16[384,768]{1,0:T(8,128)(2,1)} %get-tuple-element.7.f0), channel_id=1, source_target_pairs={{0,2},{2,4},{4,6},{6,0},{8,14},{10,8},{12,10},{14,12},{1,3},{3,5},... | collective-permute-start | bytes 1769480 | tf_op jit(solution)/shard_map/ppermute | solution.py:258
  34.0 11.1 %collective-permute-start = (bf16[80,1280]{1,0:T(8,128)(2,1)}, bf16[80,1280]{1,0:T(8,128)(2,1)S(1)}, u32[]{:S(2)}, u32[]{:S(2)}) collective-permute-start(bf16[80,1280]{1,0:T(8,128)(2,1)} %get-tuple-element.5.io_a_ref), channel_id=1, source_target_pairs={{0,8},{8,0},{1,9},{9,1},{2,10},{10,2},{3,11},{11,3},{4,12},{12,4},... | collective-permute-start | bytes 614408 | tf_op jit(solution)/shard_map/ppermute | solution.py:264
  35.9 27.3 %collective-permute-start.5 = (bf16[400,768]{1,0:T(8,128)(2,1)S(1)}, bf16[400,768]{1,0:T(8,128)(2,1)S(1)}, u32[]{:S(2)}, u32[]{:S(2)}) collective-permute-start(bf16[400,768]{1,0:T(8,128)(2,1)S(1)} %collective-permute-done.1.n1), channel_id=1, source_target_pairs={{0,1},{1,0},{8,57},{9,24},{16,17},{17,16},{24,9},{25,40},{32,33},{... | collective-permute-start | bytes 1843208 | tf_op jit(solution)/shard_map/ppermute | solution.py:261
  39.5 25.8 %collective-permute-start.7 = (bf16[400,768]{1,0:T(8,128)(2,1)S(1)}, bf16[400,768]{1,0:T(8,128)(2,1)S(1)}, u32[]{:S(2)}, u32[]{:S(2)}) collective-permute-start(bf16[400,768]{1,0:T(8,128)(2,1)S(1)} %collective-permute-done.3.n2), channel_id=1, source_target_pairs={{0,1},{1,0},{8,57},{9,24},{16,17},{17,16},{24,9},{25,40},{32,33},{... | collective-permute-start | bytes 1843208 | tf_op jit(solution)/shard_map/ppermute | solution.py:261
  43.2 9.7 %collective-permute-start.9 = (bf16[384,768]{1,0:T(8,128)(2,1)S(1)}, bf16[384,768]{1,0:T(8,128)(2,1)S(1)}, u32[]{:S(2)}, u32[]{:S(2)}) collective-permute-start(bf16[384,768]{1,0:T(8,128)(2,1)S(1)} %collective-permute-done.2.f1), channel_id=1, source_target_pairs={{0,8},{8,0},{1,9},{9,1},{2,10},{10,2},{3,11},{11,3},{4,12},{12,4},... | collective-permute-start | bytes 1769480 | tf_op jit(solution)/shard_map/ppermute | solution.py:264
  45.1 15.8 %collective-permute-start.6 = (bf16[384,768]{1,0:T(8,128)(2,1)S(1)}, bf16[384,768]{1,0:T(8,128)(2,1)S(1)}, u32[]{:S(2)}, u32[]{:S(2)}) collective-permute-start(bf16[384,768]{1,0:T(8,128)(2,1)S(1)} %collective-permute-done.2.f1), channel_id=1, source_target_pairs={{0,1},{1,0},{8,57},{9,24},{16,17},{17,16},{24,9},{25,40},{32,33},{... | collective-permute-start | bytes 1769480 | tf_op jit(solution)/shard_map/ppermute | solution.py:261
  51.0 16.6 %collective-permute-start.11 = (bf16[400,768]{1,0:T(8,128)(2,1)S(1)}, bf16[400,768]{1,0:T(8,128)(2,1)S(1)}, u32[]{:S(2)}, u32[]{:S(2)}) collective-permute-start(bf16[400,768]{1,0:T(8,128)(2,1)S(1)} %collective-permute-done.4.n3), channel_id=1, source_target_pairs={{0,8},{8,0},{1,9},{9,1},{2,10},{10,2},{3,11},{11,3},{4,12},{12,4},... | collective-permute-start | bytes 1843208 | tf_op jit(solution)/shard_map/ppermute | solution.py:264
  52.9 16.7 %collective-permute-start.8 = (bf16[400,768]{1,0:T(8,128)(2,1)S(1)}, bf16[400,768]{1,0:T(8,128)(2,1)S(1)}, u32[]{:S(2)}, u32[]{:S(2)}) collective-permute-start(bf16[400,768]{1,0:T(8,128)(2,1)S(1)} %collective-permute-done.1.n1), channel_id=1, source_target_pairs={{0,8},{8,0},{1,9},{9,1},{2,10},{10,2},{3,11},{11,3},{4,12},{12,4},... | collective-permute-start | bytes 1843208 | tf_op jit(solution)/shard_map/ppermute | solution.py:264
  60.9 10.6 %collective-permute-start.10 = (bf16[400,768]{1,0:T(8,128)(2,1)S(1)}, bf16[400,768]{1,0:T(8,128)(2,1)S(1)}, u32[]{:S(2)}, u32[]{:S(2)}) collective-permute-start(bf16[400,768]{1,0:T(8,128)(2,1)S(1)} %collective-permute-done.3.n2), channel_id=1, source_target_pairs={{0,8},{8,0},{1,9},{9,1},{2,10},{10,2},{3,11},{11,3},{4,12},{12,4},... | collective-permute-start | bytes 1843208 | tf_op jit(solution)/shard_map/ppermute | solution.py:264
  63.2 8.3 %collective-permute-start.12 = (bf16[400,768]{1,0:T(8,128)(2,1)S(1)}, bf16[400,768]{1,0:T(8,128)(2,1)S(1)}, u32[]{:S(2)}, u32[]{:S(2)}) collective-permute-start(bf16[400,768]{1,0:T(8,128)(2,1)S(1)} %collective-permute-done.5.n4), channel_id=1, source_target_pairs={{0,8},{8,0},{1,9},{9,1},{2,10},{10,2},{3,11},{11,3},{4,12},{12,4},... | collective-permute-start | bytes 1843208 | tf_op jit(solution)/shard_map/ppermute | solution.py:264
  65.2 6.3 %collective-permute-start.14 = (bf16[400,768]{1,0:T(8,128)(2,1)S(1)}, bf16[400,768]{1,0:T(8,128)(2,1)S(1)}, u32[]{:S(2)}, u32[]{:S(2)}) collective-permute-start(bf16[400,768]{1,0:T(8,128)(2,1)S(1)} %collective-permute-done.7.n5), channel_id=1, source_target_pairs={{0,8},{8,0},{1,9},{9,1},{2,10},{10,2},{3,11},{11,3},{4,12},{12,4},... | collective-permute-start | bytes 1843208 | tf_op jit(solution)/shard_map/ppermute | solution.py:264
  67.6 3.9 %collective-permute-start.13 = (bf16[384,768]{1,0:T(8,128)(2,1)S(1)}, bf16[384,768]{1,0:T(8,128)(2,1)S(1)}, u32[]{:S(2)}, u32[]{:S(2)}) collective-permute-start(bf16[384,768]{1,0:T(8,128)(2,1)S(1)} %collective-permute-done.6.f4), channel_id=1, source_target_pairs={{0,8},{8,0},{1,9},{9,1},{2,10},{10,2},{3,11},{11,3},{4,12},{12,4},... | collective-permute-start | bytes 1769480 | tf_op jit(solution)/shard_map/ppermute | solution.py:264
  71.5 1.1 copy-start.1
  72.6 1.1 copy-start.2
  73.7 0.9 copy-start.3
  167.3 7.3 %collective-permute-start.15 = (bf16[32,80,128]{2,1,0:T(8,128)(2,1)S(1)}, bf16[32,80,128]{2,1,0:T(8,128)(2,1)S(1)}, u32[]{:S(2)}, u32[]{:S(2)}) collective-permute-start(bf16[32,80,128]{2,1,0:T(8,128)(2,1)S(1)} %all_to_all.17.mine_ref), channel_id=1, source_target_pairs={{0,8},{8,0},{1,9},{9,1},{2,10},{10,2},{3,11},{11,3},{4,12},{12,4},... | collective-permute-start | bytes 1966088 | tf_op jit(solution)/shard_map/ppermute | solution.py:264

commit v2 on v1

--- a/solution.py
+++ b/solution.py
@@ -49,28 +49,48 @@
     return section, lax.axis_index("c")
 
 
-def prep_kernel(w_ref, taps_ref, feat_ref, targ_ref, len_ref, near_ref, far_ref, io_ref):
+def prep_kernel(
+    w_ref, taps_ref, feat_ref, targ_ref, len_ref, both_ref, near_ref, io_ref,
+    packed_ref, count_ref, sem,
+):
     section, core = where_am_i()
     utt = lax.rem(section, 4)
-    hi, mid, low = split3(taps_ref[0])
-    packed = jnp.concatenate([hi, mid, low, jnp.zeros((1, D), F32)], axis=0).astype(BF)
     mine = pl.multiple_of(core * H, H)
     theirs = pl.multiple_of((1 - core) * H, H)
-    near_ref[0:H, :] = w_ref[0, pl.ds(mine, H), :]
-    near_ref[H:PIECE, :] = packed
-    far_ref[...] = w_ref[0, pl.ds(theirs, H), :]
-    io_ref[0:T, 0:FEAT] = feat_ref[utt]
-    io_ref[0:T, FEAT:] = targ_ref[utt]
+    copies = [
+        pltpu.make_async_copy(w_ref.at[0, pl.ds(mine, H)], both_ref.at[pl.ds(0, H)], sem.at[0]),
+        pltpu.make_async_copy(w_ref.at[0, pl.ds(theirs, H)], both_ref.at[pl.ds(PIECE, H)], sem.at[1]),
+        pltpu.make_async_copy(
+            feat_ref.at[utt], io_ref.at[pl.ds(0, T), pl.ds(0, FEAT)], sem.at[2]),
+        pltpu.make_async_copy(w_ref.at[0, pl.ds(mine, H)], near_ref.at[pl.ds(0, H)], sem.at[6]),
+        pltpu.make_async_copy(
+            targ_ref.at[utt], io_ref.at[pl.ds(0, T), pl.ds(FEAT, D)], sem.at[3]),
+    ]
+    for copy in copies:
+        copy.start()
+    taps = jnp.concatenate([taps_ref[k] for k in range(KER)], axis=0)
+    hi, mid, low = split3(taps)
+    packed = jnp.concatenate([hi, mid, low, jnp.zeros((1, D), F32)], axis=0)
+    packed_ref[...] = packed.astype(BF)
     count = len_ref[utt].astype(F32)
-    io_ref[T:, :] = jnp.full((INROWS - T, FEAT + D), count, F32).astype(BF)
+    count_ref[...] = jnp.full((INROWS - T, FEAT + D), count, F32).astype(BF)
+    late = [
+        pltpu.make_async_copy(packed_ref, both_ref.at[pl.ds(H, TAPS)], sem.at[4]),
+        pltpu.make_async_copy(packed_ref, near_ref.at[pl.ds(H, TAPS)], sem.at[7]),
+        pltpu.make_async_copy(count_ref, io_ref.at[pl.ds(T, INROWS - T)], sem.at[5]),
+    ]
+    for copy in late:
+        copy.start()
+    for copy in copies + late:
+        copy.wait()
 
 
 def model_kernel(
     io_a_ref, io_b_ref, front_ref,
-    n0, f0, n1, f1, n2, n3, n4, f4, n5, m1, g1, m2, m3, m4, g4, m5,
+    own_w, near_w, n3, n2, slant_w, n5, anti_w, m3, m2, far_w, m5,
     pay_ref,
     w_ref, traw_ref, taps_ref, vals_ref, inv_ref, norm_ref, slope_ref, act_ref, gpad_ref, g_ref,
-    sem,
+    io_ref, wsem, tsem, isem,
 ):
     section, core = where_am_i()
     col = lax.div(section, 2)
@@ -79,41 +99,40 @@
     side = lax.rem(col + 3 + 2 * core, 4)
     anti = lax.rem(col + 1 + 2 * core, 4)
     across = lax.rem(col + 2, 4)
-    copies = []
-
-    def bring(piece, c, r, part, with_taps):
+    flip = 1 - row
+    inputs = [
+        pltpu.make_async_copy(ref, io_ref.at[i], isem.at[i])
+        for i, ref in enumerate((io_a_ref, io_b_ref))
+    ]
+    for copy in inputs:
+        copy.start()
+
+    def bring(piece, first, c, r, part, taps_at):
         layer = 2 * c + r
-        k = len(copies)
         start = pl.multiple_of(part * H, H)
-        copies.append(pltpu.make_async_copy(
-            piece.at[pl.ds(0, H)], w_ref.at[layer, pl.ds(start, H)], sem.at[k]))
-        if with_taps:
-            copies.append(pltpu.make_async_copy(
-                piece.at[pl.ds(H, TAPS)], traw_ref.at[layer], sem.at[k + 1]))
-
-    flip = 1 - row
-    bring(n0, col, row, core, True)
-    bring(f0, col, row, other, False)
-    bring(n1, side, row, core, True)
-    bring(f1, side, row, other, False)
-    bring(n2, across, row, core, True)
-    bring(n3, col, flip, core, True)
-    bring(n4, side, flip, core, True)
-    bring(f4, side, flip, other, False)
-    bring(n5, across, flip, core, True)
-    bring(m1, anti, row, other, True)
-    bring(g1, anti, row, core, False)
-    bring(m2, across, row, other, False)
-    bring(m3, col, flip, other, False)
-    bring(m4, anti, flip, other, True)
-    bring(g4, anti, flip, core, False)
-    bring(m5, across, flip, other, False)
-    for copy in copies:
-        copy.start()
-
+        pltpu.make_async_copy(
+            piece.at[pl.ds(first, H)], w_ref.at[layer, pl.ds(start, H)], wsem.at[layer]).start()
+        if taps_at is not None:
+            pltpu.make_async_copy(
+                piece.at[pl.ds(taps_at, TAPS)], traw_ref.at[layer], tsem.at[layer]).start()
+
+    for piece, c, r, part in (
+        (own_w, col, row, core), (near_w, side, row, core), (slant_w, side, flip, core),
+        (anti_w, anti, row, other), (far_w, anti, flip, other),
+    ):
+        bring(piece, 0, c, r, part, H)
+        bring(piece, PIECE, c, r, 1 - part, None)
+    for piece, mirror, c, r in (
+        (n3, m3, col, flip), (n2, m2, across, row), (n5, m5, across, flip),
+    ):
+        bring(piece, 0, c, r, core, H)
+        bring(mirror, 0, c, r, other, None)
+
+    for copy in inputs:
+        copy.wait()
     own = core == lax.div(section, 4)
     pick = jnp.where(own, 1.0, 0.0).astype(F32)
-    io = io_a_ref[...].astype(F32) * pick + io_b_ref[...].astype(F32) * (1.0 - pick)
+    io = io_ref[0].astype(F32) * pick + io_ref[1].astype(F32) * (1.0 - pick)
     count = io[T:T + 1, 0:1]
     target = io[0:T, FEAT:]
     frame = lax.broadcasted_iota(jnp.int32, (T, 1), 0).astype(F32)
@@ -124,10 +143,10 @@
     edge = jnp.zeros((8, D), F32)
     gpad_ref[0:8, :] = edge
     gpad_ref[T + 8:, :] = edge
-    for copy in copies:
-        copy.wait()
 
     def forward(l, carry):
+        pltpu.make_async_copy(traw_ref.at[l], traw_ref.at[l], tsem.at[l]).wait()
+        pltpu.make_async_copy(w_ref.at[l], w_ref.at[l], wsem.at[l]).wait()
         raw = traw_ref[l].astype(F32)
         taps = raw[0:KER] + raw[KER:2 * KER] + raw[2 * KER:3 * KER]
         taps_ref[l, 0:KER, :] = taps
@@ -240,7 +259,7 @@
     for j in range(KER * 6):
         k, b = divmod(j, 6)
         pair = mine_ref[j, CHUNK:, :].astype(F32)
-        taps_ref[0, k:k + 1, b * 128:(b + 1) * 128] = pair[0:1] + pair[1:2]
+        taps_ref[k, :, b * 128:(b + 1) * 128] = pair[0:1] + pair[1:2]
 
 
 def params(mib):
@@ -263,34 +282,36 @@
     def to_core(a):
         return lax.ppermute(a, "c", [(0, 1), (1, 0)])
 
-    near, far, io = pl.pallas_call(
+    both, near, io = pl.pallas_call(
         prep_kernel,
         name="prep",
         out_shape=(
+            jax.ShapeDtypeStruct((PIECE + H, D), BF),
             jax.ShapeDtypeStruct((PIECE, D), BF),
-            jax.ShapeDtypeStruct((H, D), BF),
             jax.ShapeDtypeStruct((INROWS, FEAT + D), BF),
         ),
-        in_specs=[VMEM, VMEM, VMEM, VMEM, SMEM],
-        out_specs=(VMEM, VMEM, VMEM),
-    )(pointwise, kernel, features, targets, lengths)
-
-    n1 = along_x(near)
-    n3 = along_z(near)
-    f1 = along_x(far)
+        in_specs=[ANY, VMEM, ANY, ANY, SMEM],
+        out_specs=(ANY, ANY, ANY),
+        scratch_shapes=[
+            pltpu.VMEM((TAPS, D), BF),
+            pltpu.VMEM((INROWS - T, FEAT + D), BF),
+            pltpu.SemaphoreType.DMA((8,)),
+        ],
+    )(pointwise, jnp.transpose(kernel, (1, 0, 2)), features, targets, lengths)
+
+    beside, n3 = lax.optimization_barrier((along_x(both), along_z(near)))
     io_other = to_core(io)
-    n2 = along_x(n1)
-    n4 = along_z(n1)
-    f4 = along_z(f1)
+    n2 = along_x(beside[:PIECE])
+    slant = along_z(beside)
     n5 = along_z(n2)
-    here = [near, far, n1, f1, n2, n3, n4, f4, n5]
-    there = [to_core(a) for a in (n1, f1, n2, n3, n4, f4, n5)]
+    here = [both, beside, n3, n2, slant, n5]
+    there = [to_core(a) for a in (beside, n3, n2, slant, n5)]
 
     payload = pl.pallas_call(
         model_kernel,
         name="model",
         out_shape=jax.ShapeDtypeStruct((L, PAY, D), BF),
-        in_specs=[VMEM, VMEM, VMEM] + [ANY] * 16,
+        in_specs=[ANY, ANY, VMEM] + [ANY] * 11,
         out_specs=VMEM,
         scratch_shapes=[
             pltpu.VMEM((L, D, D), BF),
@@ -303,9 +324,12 @@
             pltpu.VMEM((L, T, D), BF),
             pltpu.VMEM((T + 16, D), F32),
             pltpu.VMEM((T, D), F32),
-            pltpu.SemaphoreType.DMA((32,)),
+            pltpu.VMEM((2, INROWS, FEAT + D), BF),
+            pltpu.SemaphoreType.DMA((L,)),
+            pltpu.SemaphoreType.DMA((L,)),
+            pltpu.SemaphoreType.DMA((2,)),
         ],
-        compiler_params=params(40),
+        compiler_params=params(28),
     )(io, io_other, front_weight, *here, *there)
 
     received = lax.all_to_all(payload, ("x", "zl"), 0, 0)
@@ -340,18 +364,19 @@
     half = lax.all_to_all(mine, ("y", "zh"), 0, 0)
     other_half = to_core(half)
 
-    return pl.pallas_call(
+    grads, tap_grads = pl.pallas_call(
         place_kernel,
         name="place",
         out_shape=(
             jax.ShapeDtypeStruct((1, D, D), BF),
-            jax.ShapeDtypeStruct((1, KER, D), F32),
+            jax.ShapeDtypeStruct((KER, 1, D), F32),
         ),
         in_specs=[VMEM, VMEM],
         out_specs=(VMEM, VMEM),
         scratch_shapes=[pltpu.VMEM((H * 6, 128), F32)],
         compiler_params=params(16),
     )(half, other_half)
+    return grads, jnp.transpose(tap_grads, (1, 0, 2))
 
 
 def solution(mesh):

time: 177 us -> 224 us (1.27)
  Pallas kernels: 18.9 us -> 77 us
  starting transfers between devices: 56.6 us -> 46.7 us
  local copies, waits for them, and re-layouts: 5.08 us -> 0.98 us
    pallas_call x1, Pallas kernels: 2.63 us -> 60.6 us  [body(): pl.pallas_call(prep_kernel, name='prep', out_shape=(jax.ShapeDtypeStruct(...]
    ppermute x4 -> x3, starting transfers between devices: 23 us -> 18.5 us  [along_z(): return lax.ppermute(a, ('zh', 'c', 'zl'), pair)]
    ppermute x9 -> x7, starting transfers between devices: 22.4 us -> 18.8 us  [to_core(): return lax.ppermute(a, 'c', [(0, 1), (1, 0)])]
    unnamed x9 -> x6, local copies, waits for them, and re-layouts: 4.46 us -> 0.94 us
    ppermute x4 -> x3, waiting for transfers between devices: 5.59 us -> 7.74 us  [along_z(): return lax.ppermute(a, ('zh', 'c', 'zl'), pair)]
    ppermute x3 -> x2, starting transfers between devices: 11.2 us -> 9.44 us  [along_x(): return lax.ppermute(a, ('c', 'x'), ring)]
    ppermute x3 -> x2, waiting for transfers between devices: 8.14 us -> 7.07 us  [along_x(): return lax.ppermute(a, ('c', 'x'), ring)]
  transfers between devices with their start and end apart: 16 -> 12, of which waited for: 5 -> 4; matrix products, arithmetic and copies ran while one was open for 0% -> 0% of each run, Pallas kernels for 0% -> 0%
where the time goes in v2:
time: 224 us; the launch traced here: 223 us
  blocking collectives  79.4 us (35%)
  Pallas kernels  77 us (34%)
  starting transfers between devices  46.7 us (21%)
  waiting for transfers between devices  18.1 us (8%)
    pallas_call x1, Pallas kernels, body(): pl.pallas_call(prep_kernel, name='prep', out_shape=(jax.ShapeDtypeStruct(...  60.6 us
    all_to_all x1, blocking collectives, body(): scattered = lax.all_to_all(parts, ('y', 'zh'), 0, 0)  29.3 us
    all_to_all x1, blocking collectives, body(): half = lax.all_to_all(mine, ('y', 'zh'), 0, 0)  27.3 us
    all_to_all x1, blocking collectives, body(): received = lax.all_to_all(payload, ('x', 'zl'), 0, 0)  22.8 us
    ppermute x7, starting transfers between devices, to_core(): return lax.ppermute(a, 'c', [(0, 1), (1, 0)])  18.8 us
    ppermute x3, starting transfers between devices, along_z(): return lax.ppermute(a, ('zh', 'c', 'zl'), pair)  18.5 us
    pallas_call x1, Pallas kernels, body(): pl.pallas_call(model_kernel, name='model', out_shape=jax.ShapeDtypeStruct...  14.6 us
    ppermute x2, starting transfers between devices, along_x(): return lax.ppermute(a, ('c', 'x'), ring)  9.44 us
  transfers between devices with their start and end apart: 12, of which 4 were waited for; matrix products, arithmetic and copies ran while one was open for 0% of the time, Pallas kernels for 0%

profile of v2, /device:TPU:9, one launch (start us, length us, event | category | flops | bytes accessed | tf_op | source)
XLA Modules:
  0.0 223.1 jit_solution(9407940254187576402)
XLA Ops:
  0.6 0.0 copy-start.1
  0.6 60.6 %prep.1 = (bf16[784,768]{1,0:T(8,128)(2,1)}, bf16[400,768]{1,0:T(8,128)(2,1)}, bf16[80,1280]{1,0:T(8,128)(2,1)}) custom-call(bf16[1,768,768]{2,1,0:T(8,128)(2,1)} %w_ref.1, f32[5,1,768]{2,1,0:T(1,128)} %bitcast.2, bf16[4,64,512]{2,1,0:T(8,128)(2,1)} %feat_ref.1, bf16[4,64,768]{2,1,0:T(8,128)(2,1)} %targ_ref.1, s32[4]{0:T(128)} %len_ref.1), custom_call_target="tpu_custom_call" | custom-call | tf_op jit(solution)/shard_map/prep/pallas_call | solution.py:285
  61.2 0.0 copy-start
  61.2 4.5 %collective-permute-start.1 = (bf16[784,768]{1,0:T(8,128)(2,1)}, bf16[784,768]{1,0:T(8,128)(2,1)S(1)}, u32[]{:S(2)}, u32[]{:S(2)}) collective-permute-start(bf16[784,768]{1,0:T(8,128)(2,1)} %get-tuple-element.10.own_w), channel_id=1, source_target_pairs={{0,2},{2,4},{4,6},{6,0},{8,14},{10,8},{12,10},{14,12},{1,3},{3,5},... | collective-permute-start | bytes 3612680 | tf_op jit(solution)/shard_map/ppermute | solution.py:277
  65.7 10.7 %collective-permute-start.2 = (bf16[400,768]{1,0:T(8,128)(2,1)}, bf16[400,768]{1,0:T(8,128)(2,1)S(1)}, u32[]{:S(2)}, u32[]{:S(2)}) collective-permute-start(bf16[400,768]{1,0:T(8,128)(2,1)} %get-tuple-element.11), channel_id=1, source_target_pairs={{0,1},{1,0},{8,57},{9,24},{16,17},{17,16},{24,9},{25,40},{32,33},{... | collective-permute-start | bytes 1843208 | tf_op jit(solution)/shard_map/ppermute | solution.py:280
  76.4 7.7 %collective-permute-done.2.n3 = bf16[400,768]{1,0:T(8,128)(2,1)S(1)} collective-permute-done((bf16[400,768]{1,0:T(8,128)(2,1)}, bf16[400,768]{1,0:T(8,128)(2,1)S(1)}, u32[]{:S(2)}, u32[]{:S(2)}) %collective-permute-start.2) | collective-permute-done | bytes 614432 | tf_op jit(solution)/shard_map/ppermute | solution.py:280
  84.1 0.0 collective-permute-done.1.near_w
  84.1 6.0 %collective-permute-start.4 = (bf16[784,768]{1,0:T(8,128)(2,1)S(1)}, bf16[784,768]{1,0:T(8,128)(2,1)S(1)}, u32[]{:S(2)}, u32[]{:S(2)}) collective-permute-start(bf16[784,768]{1,0:T(8,128)(2,1)S(1)} %collective-permute-done.1.near_w), channel_id=1, source_target_pairs={{0,1},{1,0},{8,57},{9,24},{16,17},{17,16},{24,9},{25,40},{32,33},{... | collective-permute-start | bytes 3612680 | tf_op jit(solution)/shard_map/ppermute | solution.py:280
  90.2 4.9 %collective-permute-start.3 = (bf16[400,768]{1,0:T(8,128)(2,1)S(1)}, bf16[400,768]{1,0:T(8,128)(2,1)S(1)}, u32[]{:S(2)}, u32[]{:S(2)}) collective-permute-start(bf16[400,768]{1,0:T(8,128)(2,1)S(1)} %slice.3), channel_id=1, source_target_pairs={{0,2},{2,4},{4,6},{6,0},{8,14},{10,8},{12,10},{14,12},{1,3},{3,5},... | collective-permute-start | bytes 1843208 | tf_op jit(solution)/shard_map/ppermute | solution.py:277
  95.1 7.1 %collective-permute-done.3.n2 = bf16[400,768]{1,0:T(8,128)(2,1)S(1)} collective-permute-done((bf16[400,768]{1,0:T(8,128)(2,1)S(1)}, bf16[400,768]{1,0:T(8,128)(2,1)S(1)}, u32[]{:S(2)}, u32[]{:S(2)}) %collective-permute-start.3) | collective-permute-done | bytes 614432 | tf_op jit(solution)/shard_map/ppermute | solution.py:277
  102.2 1.9 collective-permute-start.5
  104.1 1.9 collective-permute-start.6
  106.0 0.0 collective-permute-done.4.slant_w
  106.0 2.4 %collective-permute-start.9 = (bf16[784,768]{1,0:T(8,128)(2,1)S(1)}, bf16[784,768]{1,0:T(8,128)(2,1)S(1)}, u32[]{:S(2)}, u32[]{:S(2)}) collective-permute-start(bf16[784,768]{1,0:T(8,128)(2,1)S(1)} %collective-permute-done.4.slant_w), channel_id=1, source_target_pairs={{0,8},{8,0},{1,9},{9,1},{2,10},{10,2},{3,11},{11,3},{4,12},{12,4},... | collective-permute-start | bytes 3612680 | tf_op jit(solution)/shard_map/ppermute | solution.py:283
  108.4 1.9 collective-permute-start
  110.4 2.4 %collective-permute-start.7 = (bf16[400,768]{1,0:T(8,128)(2,1)S(1)}, bf16[400,768]{1,0:T(8,128)(2,1)S(1)}, u32[]{:S(2)}, u32[]{:S(2)}) collective-permute-start(bf16[400,768]{1,0:T(8,128)(2,1)S(1)} %collective-permute-done.2.n3), channel_id=1, source_target_pairs={{0,8},{8,0},{1,9},{9,1},{2,10},{10,2},{3,11},{11,3},{4,12},{12,4},... | collective-permute-start | bytes 1843208 | tf_op jit(solution)/shard_map/ppermute | solution.py:283
  112.8 0.0 collective-permute-done.io_b_ref
  112.8 1.9 collective-permute-start.8
  114.7 0.0 collective-permute-done.5.n5
  114.7 2.4 %collective-permute-start.10 = (bf16[400,768]{1,0:T(8,128)(2,1)S(1)}, bf16[400,768]{1,0:T(8,128)(2,1)S(1)}, u32[]{:S(2)}, u32[]{:S(2)}) collective-permute-start(bf16[400,768]{1,0:T(8,128)(2,1)S(1)} %collective-permute-done.5.n5), channel_id=1, source_target_pairs={{0,8},{8,0},{1,9},{9,1},{2,10},{10,2},{3,11},{11,3},{4,12},{12,4},... | collective-permute-start | bytes 1843208 | tf_op jit(solution)/shard_map/ppermute | solution.py:283
  117.1 0.0 collective-permute-done.7.m3
  117.1 0.0 collective-permute-done.6.anti_w
  117.2 0.0 collective-permute-done.8.m2
  117.2 1.6 collective-permute-done.10.m5
  118.8 0.0 collective-permute-done.9.far_w
  118.8 0.0 copy-done.1
  118.8 0.0 copy-done
  118.8 0.0 copy-start.2
  118.8 0.9 copy-done.2
  119.7 14.6 %model.1 = bf16[8,112,768]{2,1,0:T(8,128)(2,1)S(1)} custom-call(bf16[80,1280]{1,0:T(8,128)(2,1)S(1)} %copy-done.2, bf16[80,1280]{1,0:T(8,128)(2,1)S(1)} %collective-permute-done.io_b_ref, bf16[512,768]{1,0:T(8,128)(2,1)S(1)} %copy-done.1, bf16[784,768]{1,0:T(8,128)(2,1)S(1)} %copy-done, bf16[784,768]{1,0:T(8,128)(2,1)S(1)} %collective-permute-done.1.near_w, ...), custom_call_target="tpu_custom_call" | custom-call | tf_op jit(solution)/shard_map/model/pallas_call | solution.py:310
  134.3 22.8 %all_to_all.15.recv_ref = bf16[8,112,768]{2,1,0:T(8,128)(2,1)S(1)} all-to-all(bf16[8,112,768]{2,1,0:T(8,128)(2,1)S(1)} %model.1), channel_id=1, replica_groups=mesh['y'=8,'zh'=4,'c'=2,'x'=4,'zl'=2] {'x','zl'}, dimensions={0} | all-to-all | bytes 2752512 | tf_op jit(solution)/shard_map/all_to_all | solution.py:335
  157.2 0.6 grad.1
  157.7 29.3 %all_to_all.16.parts_ref = bf16[32,80,128]{2,1,0:T(8,128)(2,1)S(1)} all-to-all(bf16[32,80,128]{2,1,0:T(8,128)(2,1)S(1)} %grad.1), channel_id=1, replica_groups=mesh['y'=8,'zh'=4,'c'=2,'x'=4,'zl'=2] {'y','zh'}, dimensions={0} | all-to-all | bytes 1310720 | tf_op jit(solution)/shard_map/all_to_all | solution.py:352
  187.0 0.1 total.1
  187.1 27.3 %all_to_all.17.mine_ref = bf16[32,80,128]{2,1,0:T(8,128)(2,1)S(1)} all-to-all(bf16[32,80,128]{2,1,0:T(8,128)(2,1)S(1)} %total.1), channel_id=1, replica_groups=mesh['y'=8,'zh'=4,'c'=2,'x'=4,'zl'=2] {'y','zh'}, dimensions={0} | all-to-all | bytes 1310720 | tf_op jit(solution)/shard_map/all_to_all | solution.py:364
  214.4 5.8 %collective-permute-start.11 = (bf16[32,80,128]{2,1,0:T(8,128)(2,1)S(1)}, bf16[32,80,128]{2,1,0:T(8,128)(2,1)S(1)}, u32[]{:S(2)}, u32[]{:S(2)}) collective-permute-start(bf16[32,80,128]{2,1,0:T(8,128)(2,1)S(1)} %all_to_all.17.mine_ref), channel_id=1, source_target_pairs={{0,8},{8,0},{1,9},{9,1},{2,10},{10,2},{3,11},{11,3},{4,12},{12,4},... | collective-permute-start | bytes 1966088 | tf_op jit(solution)/shard_map/ppermute | solution.py:283
  220.2 1.7 collective-permute-done.11.theirs_ref
  221.9 1.2 place.1
  (1 shorter events, 0.0 us)
Async XLA Ops:
  0.6 118.1 %copy-start.1 = (bf16[512,768]{1,0:T(8,128)(2,1)S(1)}, bf16[512,768]{1,0:T(8,128)(2,1)}, u32[]{:S(2)}) copy-start(bf16[512,768]{1,0:T(8,128)(2,1)} %front_ref.1) | copy-start | bytes 2359300
  61.2 57.6 %copy-start = (bf16[784,768]{1,0:T(8,128)(2,1)S(1)}, bf16[784,768]{1,0:T(8,128)(2,1)}, u32[]{:S(2)}) copy-start(bf16[784,768]{1,0:T(8,128)(2,1)} %get-tuple-element.10.own_w) | copy-start | bytes 3612676
  61.2 22.9 %collective-permute-start.1 = (bf16[784,768]{1,0:T(8,128)(2,1)}, bf16[784,768]{1,0:T(8,128)(2,1)S(1)}, u32[]{:S(2)}, u32[]{:S(2)}) collective-permute-start(bf16[784,768]{1,0:T(8,128)(2,1)} %get-tuple-element.10.own_w), channel_id=1, source_target_pairs={{0,2},{2,4},{4,6},{6,0},{8,14},{10,8},{12,10},{14,12},{1,3},{3,5},... | collective-permute-start | bytes 3612680 | tf_op jit(solution)/shard_map/ppermute | solution.py:277
  65.7 18.4 %collective-permute-start.2 = (bf16[400,768]{1,0:T(8,128)(2,1)}, bf16[400,768]{1,0:T(8,128)(2,1)S(1)}, u32[]{:S(2)}, u32[]{:S(2)}) collective-permute-start(bf16[400,768]{1,0:T(8,128)(2,1)} %get-tuple-element.11), channel_id=1, source_target_pairs={{0,1},{1,0},{8,57},{9,24},{16,17},{17,16},{24,9},{25,40},{32,33},{... | collective-permute-start | bytes 1843208 | tf_op jit(solution)/shard_map/ppermute | solution.py:280
  84.1 21.9 %collective-permute-start.4 = (bf16[784,768]{1,0:T(8,128)(2,1)S(1)}, bf16[784,768]{1,0:T(8,128)(2,1)S(1)}, u32[]{:S(2)}, u32[]{:S(2)}) collective-permute-start(bf16[784,768]{1,0:T(8,128)(2,1)S(1)} %collective-permute-done.1.near_w), channel_id=1, source_target_pairs={{0,1},{1,0},{8,57},{9,24},{16,17},{17,16},{24,9},{25,40},{32,33},{... | collective-permute-start | bytes 3612680 | tf_op jit(solution)/shard_map/ppermute | solution.py:280
  90.2 12.0 %collective-permute-start.3 = (bf16[400,768]{1,0:T(8,128)(2,1)S(1)}, bf16[400,768]{1,0:T(8,128)(2,1)S(1)}, u32[]{:S(2)}, u32[]{:S(2)}) collective-permute-start(bf16[400,768]{1,0:T(8,128)(2,1)S(1)} %slice.3), channel_id=1, source_target_pairs={{0,2},{2,4},{4,6},{6,0},{8,14},{10,8},{12,10},{14,12},{1,3},{3,5},... | collective-permute-start | bytes 1843208 | tf_op jit(solution)/shard_map/ppermute | solution.py:277
  102.2 12.6 %collective-permute-start.5 = (bf16[400,768]{1,0:T(8,128)(2,1)S(1)}, bf16[400,768]{1,0:T(8,128)(2,1)S(1)}, u32[]{:S(2)}, u32[]{:S(2)}) collective-permute-start(bf16[400,768]{1,0:T(8,128)(2,1)S(1)} %collective-permute-done.3.n2), channel_id=1, source_target_pairs={{0,1},{1,0},{8,57},{9,24},{16,17},{17,16},{24,9},{25,40},{32,33},{... | collective-permute-start | bytes 1843208 | tf_op jit(solution)/shard_map/ppermute | solution.py:280
  104.1 13.1 %collective-permute-start.6 = (bf16[784,768]{1,0:T(8,128)(2,1)S(1)}, bf16[784,768]{1,0:T(8,128)(2,1)S(1)}, u32[]{:S(2)}, u32[]{:S(2)}) collective-permute-start(bf16[784,768]{1,0:T(8,128)(2,1)S(1)} %collective-permute-done.1.near_w), channel_id=1, source_target_pairs={{0,8},{8,0},{1,9},{9,1},{2,10},{10,2},{3,11},{11,3},{4,12},{12,4},... | collective-permute-start | bytes 3612680 | tf_op jit(solution)/shard_map/ppermute | solution.py:283
  106.0 12.8 %collective-permute-start.9 = (bf16[784,768]{1,0:T(8,128)(2,1)S(1)}, bf16[784,768]{1,0:T(8,128)(2,1)S(1)}, u32[]{:S(2)}, u32[]{:S(2)}) collective-permute-start(bf16[784,768]{1,0:T(8,128)(2,1)S(1)} %collective-permute-done.4.slant_w), channel_id=1, source_target_pairs={{0,8},{8,0},{1,9},{9,1},{2,10},{10,2},{3,11},{11,3},{4,12},{12,4},... | collective-permute-start | bytes 3612680 | tf_op jit(solution)/shard_map/ppermute | solution.py:283
  108.4 4.3 %collective-permute-start = (bf16[80,1280]{1,0:T(8,128)(2,1)}, bf16[80,1280]{1,0:T(8,128)(2,1)S(1)}, u32[]{:S(2)}, u32[]{:S(2)}) collective-permute-start(bf16[80,1280]{1,0:T(8,128)(2,1)} %get-tuple-element.9.io_a_ref), channel_id=1, source_target_pairs={{0,8},{8,0},{1,9},{9,1},{2,10},{10,2},{3,11},{11,3},{4,12},{12,4},... | collective-permute-start | bytes 614408 | tf_op jit(solution)/shard_map/ppermute | solution.py:283
  110.4 6.8 %collective-permute-start.7 = (bf16[400,768]{1,0:T(8,128)(2,1)S(1)}, bf16[400,768]{1,0:T(8,128)(2,1)S(1)}, u32[]{:S(2)}, u32[]{:S(2)}) collective-permute-start(bf16[400,768]{1,0:T(8,128)(2,1)S(1)} %collective-permute-done.2.n3), channel_id=1, source_target_pairs={{0,8},{8,0},{1,9},{9,1},{2,10},{10,2},{3,11},{11,3},{4,12},{12,4},... | collective-permute-start | bytes 1843208 | tf_op jit(solution)/shard_map/ppermute | solution.py:283
  112.8 4.4 %collective-permute-start.8 = (bf16[400,768]{1,0:T(8,128)(2,1)S(1)}, bf16[400,768]{1,0:T(8,128)(2,1)S(1)}, u32[]{:S(2)}, u32[]{:S(2)}) collective-permute-start(bf16[400,768]{1,0:T(8,128)(2,1)S(1)} %collective-permute-done.3.n2), channel_id=1, source_target_pairs={{0,8},{8,0},{1,9},{9,1},{2,10},{10,2},{3,11},{11,3},{4,12},{12,4},... | collective-permute-start | bytes 1843208 | tf_op jit(solution)/shard_map/ppermute | solution.py:283
  114.7 4.1 %collective-permute-start.10 = (bf16[400,768]{1,0:T(8,128)(2,1)S(1)}, bf16[400,768]{1,0:T(8,128)(2,1)S(1)}, u32[]{:S(2)}, u32[]{:S(2)}) collective-permute-start(bf16[400,768]{1,0:T(8,128)(2,1)S(1)} %collective-permute-done.5.n5), channel_id=1, source_target_pairs={{0,8},{8,0},{1,9},{9,1},{2,10},{10,2},{3,11},{11,3},{4,12},{12,4},... | collective-permute-start | bytes 1843208 | tf_op jit(solution)/shard_map/ppermute | solution.py:283
  118.8 0.9 copy-start.2
  214.4 7.5 %collective-permute-start.11 = (bf16[32,80,128]{2,1,0:T(8,128)(2,1)S(1)}, bf16[32,80,128]{2,1,0:T(8,128)(2,1)S(1)}, u32[]{:S(2)}, u32[]{:S(2)}) collective-permute-start(bf16[32,80,128]{2,1,0:T(8,128)(2,1)S(1)} %all_to_all.17.mine_ref), channel_id=1, source_target_pairs={{0,8},{8,0},{1,9},{9,1},{2,10},{10,2},{3,11},{11,3},{4,12},{12,4},... | collective-permute-start | bytes 1966088 | tf_op jit(solution)/shard_map/ppermute | solution.py:283

commit v3 on v2

--- a/solution.py
+++ b/solution.py
@@ -18,9 +18,9 @@
 T = 64
 L = 8
 TAPS = 16
-PIECE = H + TAPS
 INROWS = T + 16
-PAY = T + T // 2 + TAPS
+HT = T // 2
+PAY = T + HT + TAPS
 PEERS = 32
 CHUNK = 72
 CROWS = 80
@@ -49,48 +49,30 @@
     return section, lax.axis_index("c")
 
 
-def prep_kernel(
-    w_ref, taps_ref, feat_ref, targ_ref, len_ref, both_ref, near_ref, io_ref,
-    packed_ref, count_ref, sem,
-):
-    section, core = where_am_i()
+def prep_kernel(taps_ref, feat_ref, targ_ref, len_ref, packed_ref, io_ref):
+    section, _ = where_am_i()
     utt = lax.rem(section, 4)
-    mine = pl.multiple_of(core * H, H)
-    theirs = pl.multiple_of((1 - core) * H, H)
-    copies = [
-        pltpu.make_async_copy(w_ref.at[0, pl.ds(mine, H)], both_ref.at[pl.ds(0, H)], sem.at[0]),
-        pltpu.make_async_copy(w_ref.at[0, pl.ds(theirs, H)], both_ref.at[pl.ds(PIECE, H)], sem.at[1]),
-        pltpu.make_async_copy(
-            feat_ref.at[utt], io_ref.at[pl.ds(0, T), pl.ds(0, FEAT)], sem.at[2]),
-        pltpu.make_async_copy(w_ref.at[0, pl.ds(mine, H)], near_ref.at[pl.ds(0, H)], sem.at[6]),
-        pltpu.make_async_copy(
-            targ_ref.at[utt], io_ref.at[pl.ds(0, T), pl.ds(FEAT, D)], sem.at[3]),
-    ]
-    for copy in copies:
-        copy.start()
     taps = jnp.concatenate([taps_ref[k] for k in range(KER)], axis=0)
     hi, mid, low = split3(taps)
-    packed = jnp.concatenate([hi, mid, low, jnp.zeros((1, D), F32)], axis=0)
-    packed_ref[...] = packed.astype(BF)
+    packed = jnp.concatenate([hi, mid, low, jnp.zeros((1, D), F32)], axis=0).astype(BF)
+    for i in range(L):
+        packed_ref[i] = packed
+    io_ref[0:T, 0:FEAT] = feat_ref[utt]
+    io_ref[0:T, FEAT:] = targ_ref[utt]
     count = len_ref[utt].astype(F32)
-    count_ref[...] = jnp.full((INROWS - T, FEAT + D), count, F32).astype(BF)
-    late = [
-        pltpu.make_async_copy(packed_ref, both_ref.at[pl.ds(H, TAPS)], sem.at[4]),
-        pltpu.make_async_copy(packed_ref, near_ref.at[pl.ds(H, TAPS)], sem.at[7]),
-        pltpu.make_async_copy(count_ref, io_ref.at[pl.ds(T, INROWS - T)], sem.at[5]),
-    ]
-    for copy in late:
-        copy.start()
-    for copy in copies + late:
-        copy.wait()
+    io_ref[T:, :] = jnp.full((INROWS - T, FEAT + D), count, F32).astype(BF)
+
+
+def fold(x):
+    return jnp.concatenate([x[0:HT], x[HT:]], axis=1)
 
 
 def model_kernel(
-    io_a_ref, io_b_ref, front_ref,
-    own_w, near_w, n3, n2, slant_w, n5, anti_w, m3, m2, far_w, m5,
+    io_a_ref, io_b_ref, front_ref, traw_ref,
+    own_w, near_w, flip_w, n2, slant_w, n5, anti_w, m2, far_w, m5,
     pay_ref,
-    w_ref, traw_ref, taps_ref, vals_ref, inv_ref, norm_ref, slope_ref, act_ref, gpad_ref, g_ref,
-    io_ref, wsem, tsem, isem,
+    w_ref, taps_ref, vals_ref, inv_ref, norm_ref, slope_ref, act_ref, gpad_ref, g_ref,
+    io_ref, wsem, isem,
 ):
     section, core = where_am_i()
     col = lax.div(section, 2)
@@ -107,26 +89,19 @@
     for copy in inputs:
         copy.start()
 
-    def bring(piece, first, c, r, part, taps_at):
+    for piece, c, r in (
+        (own_w, col, row), (near_w, side, row), (flip_w, col, flip), (slant_w, side, flip),
+        (anti_w, anti, row), (far_w, anti, flip),
+    ):
+        layer = 2 * c + r
+        pltpu.make_async_copy(piece, w_ref.at[layer], wsem.at[layer]).start()
+    for piece, c, r, part in (
+        (n2, across, row, core), (m2, across, row, other),
+        (n5, across, flip, core), (m5, across, flip, other),
+    ):
         layer = 2 * c + r
         start = pl.multiple_of(part * H, H)
-        pltpu.make_async_copy(
-            piece.at[pl.ds(first, H)], w_ref.at[layer, pl.ds(start, H)], wsem.at[layer]).start()
-        if taps_at is not None:
-            pltpu.make_async_copy(
-                piece.at[pl.ds(taps_at, TAPS)], traw_ref.at[layer], tsem.at[layer]).start()
-
-    for piece, c, r, part in (
-        (own_w, col, row, core), (near_w, side, row, core), (slant_w, side, flip, core),
-        (anti_w, anti, row, other), (far_w, anti, flip, other),
-    ):
-        bring(piece, 0, c, r, part, H)
-        bring(piece, PIECE, c, r, 1 - part, None)
-    for piece, mirror, c, r in (
-        (n3, m3, col, flip), (n2, m2, across, row), (n5, m5, across, flip),
-    ):
-        bring(piece, 0, c, r, core, H)
-        bring(mirror, 0, c, r, other, None)
+        pltpu.make_async_copy(piece, w_ref.at[layer, pl.ds(start, H)], wsem.at[layer]).start()
 
     for copy in inputs:
         copy.wait()
@@ -145,7 +120,6 @@
     gpad_ref[T + 8:, :] = edge
 
     def forward(l, carry):
-        pltpu.make_async_copy(traw_ref.at[l], traw_ref.at[l], tsem.at[l]).wait()
         pltpu.make_async_copy(w_ref.at[l], w_ref.at[l], wsem.at[l]).wait()
         raw = traw_ref[l].astype(F32)
         taps = raw[0:KER] + raw[KER:2 * KER] + raw[2 * KER:3 * KER]
@@ -180,8 +154,7 @@
         pay_ref[l, 0:T, :] = gb
         act = act_ref[l].astype(F32)
         share = jnp.where(core == 0, act[:, 0:H], act[:, H:])
-        pay_ref[l, T:T + T // 2, 0:H] = share[0:T // 2].astype(BF)
-        pay_ref[l, T:T + T // 2, H:] = share[T // 2:].astype(BF)
+        pay_ref[l, T:T + HT, :] = fold(share).astype(BF)
         grad_act = lax.dot_general(
             gb, w_ref[l], (((1,), (1,)), ((), ())), preferred_element_type=F32)
         grad_conv = grad_act * slope_ref[l]
@@ -193,7 +166,7 @@
         total = jnp.concatenate(rows, axis=0)
         hi = total.astype(BF).astype(F32)
         packed = jnp.concatenate([hi, total - hi, jnp.zeros((TAPS - 2 * KER, D), F32)], axis=0)
-        pay_ref[l, T + T // 2:, :] = packed.astype(BF)
+        pay_ref[l, T + HT:, :] = packed.astype(BF)
         grad_norm = taps[0:1] * gpad_ref[10:T + 10, :]
         for k in range(1, KER):
             grad_norm = grad_norm + taps[k:k + 1] * gpad_ref[10 - k:T + 10 - k, :]
@@ -282,40 +255,39 @@
     def to_core(a):
         return lax.ppermute(a, "c", [(0, 1), (1, 0)])
 
-    both, near, io = pl.pallas_call(
+    weight = pointwise[0]
+    packed, io = pl.pallas_call(
         prep_kernel,
         name="prep",
         out_shape=(
-            jax.ShapeDtypeStruct((PIECE + H, D), BF),
-            jax.ShapeDtypeStruct((PIECE, D), BF),
+            jax.ShapeDtypeStruct((L, TAPS, D), BF),
             jax.ShapeDtypeStruct((INROWS, FEAT + D), BF),
         ),
-        in_specs=[ANY, VMEM, ANY, ANY, SMEM],
-        out_specs=(ANY, ANY, ANY),
-        scratch_shapes=[
-            pltpu.VMEM((TAPS, D), BF),
-            pltpu.VMEM((INROWS - T, FEAT + D), BF),
-            pltpu.SemaphoreType.DMA((8,)),
-        ],
-    )(pointwise, jnp.transpose(kernel, (1, 0, 2)), features, targets, lengths)
-
-    beside, n3 = lax.optimization_barrier((along_x(both), along_z(near)))
-    io_other = to_core(io)
-    n2 = along_x(beside[:PIECE])
+        in_specs=[VMEM, VMEM, VMEM, SMEM],
+        out_specs=(VMEM, VMEM),
+    )(jnp.transpose(kernel, (1, 0, 2)), features, targets, lengths)
+
+    beside, flipped, taps, io_other = lax.optimization_barrier((
+        along_x(weight), along_z(weight),
+        lax.all_to_all(packed, ("x", "zl"), 0, 0), to_core(io),
+    ))
+    start = lax.axis_index("c") * H
+    n2 = along_x(lax.dynamic_slice_in_dim(beside, start, H, 0))
     slant = along_z(beside)
+    anti = to_core(beside)
+    n2, anti = lax.optimization_barrier((n2, anti))
     n5 = along_z(n2)
-    here = [both, beside, n3, n2, slant, n5]
-    there = [to_core(a) for a in (beside, n3, n2, slant, n5)]
+    here = [weight, beside, flipped, n2, slant, n5]
+    there = [anti] + [to_core(a) for a in (n2, slant, n5)]
 
     payload = pl.pallas_call(
         model_kernel,
         name="model",
         out_shape=jax.ShapeDtypeStruct((L, PAY, D), BF),
-        in_specs=[ANY, ANY, VMEM] + [ANY] * 11,
+        in_specs=[ANY, ANY, VMEM, VMEM] + [ANY] * 10,
         out_specs=VMEM,
         scratch_shapes=[
             pltpu.VMEM((L, D, D), BF),
-            pltpu.VMEM((L, TAPS, D), BF),
             pltpu.VMEM((L, 8, D), F32),
             pltpu.VMEM((L, T, D), F32),
             pltpu.VMEM((L, T, 128), F32),
@@ -326,11 +298,10 @@
             pltpu.VMEM((T, D), F32),
             pltpu.VMEM((2, INROWS, FEAT + D), BF),
             pltpu.SemaphoreType.DMA((L,)),
-            pltpu.SemaphoreType.DMA((L,)),
             pltpu.SemaphoreType.DMA((2,)),
         ],
         compiler_params=params(28),
-    )(io, io_other, front_weight, *here, *there)
+    )(io, io_other, front_weight, taps, *here, *there)
 
     received = lax.all_to_all(payload, ("x", "zl"), 0, 0)
 

time: 224 us -> 169 us (0.75)
  Pallas kernels: 77 us -> 18.4 us
  waiting for transfers between devices: 18.1 us -> 25 us
  blocking collectives: 79.4 us -> 76.9 us
    pallas_call x1, Pallas kernels: 60.6 us -> 1.87 us  [body(): pl.pallas_call(prep_kernel, name='prep', out_shape=(jax.ShapeDtypeStruct(...]
    all_to_all x0 -> x1, waiting for transfers between devices: none -> 5.03 us  [body(): lax.all_to_all(packed, ('x', 'zl'), 0, 0)]
    all_to_all x0 -> x1, starting transfers between devices: none -> 4.03 us  [body(): lax.all_to_all(packed, ('x', 'zl'), 0, 0)]
    ppermute x2, starting transfers between devices: 9.44 us -> 6.45 us  [along_x(): return lax.ppermute(a, ('c', 'x'), ring)]
    ppermute x7 -> x6, starting transfers between devices: 18.8 us -> 15.9 us  [to_core(): return lax.ppermute(a, 'c', [(0, 1), (1, 0)])]
    ppermute x7 -> x6, waiting for transfers between devices: 3.33 us -> 5.29 us  [to_core(): return lax.ppermute(a, 'c', [(0, 1), (1, 0)])]
  transfers between devices with their start and end apart: 12 -> 12, of which waited for: 4 -> 7; matrix products, arithmetic and copies ran while one was open for 0% -> 0% of each run, Pallas kernels for 0% -> 1%
where the time goes in v3:
time: 169 us; the launch traced here: 168 us
  blocking collectives  76.9 us (46%)
  starting transfers between devices  45.3 us (27%)
  waiting for transfers between devices  25 us (15%)
  Pallas kernels  18.4 us (11%)
    all_to_all x1, blocking collectives, body(): scattered = lax.all_to_all(parts, ('y', 'zh'), 0, 0)  28.4 us
    all_to_all x1, blocking collectives, body(): half = lax.all_to_all(mine, ('y', 'zh'), 0, 0)  27.3 us
    all_to_all x1, blocking collectives, body(): received = lax.all_to_all(payload, ('x', 'zl'), 0, 0)  21.3 us
    ppermute x3, starting transfers between devices, along_z(): return lax.ppermute(a, ('zh', 'c', 'zl'), pair)  19 us
    ppermute x6, starting transfers between devices, to_core(): return lax.ppermute(a, 'c', [(0, 1), (1, 0)])  15.9 us
    pallas_call x1, Pallas kernels, body(): pl.pallas_call(model_kernel, name='model', out_shape=jax.ShapeDtypeStruct...  14.6 us
    ppermute x2, waiting for transfers between devices, along_x(): return lax.ppermute(a, ('c', 'x'), ring)  9.09 us
    ppermute x2, starting transfers between devices, along_x(): return lax.ppermute(a, ('c', 'x'), ring)  6.45 us
  transfers between devices with their start and end apart: 12, of which 7 were waited for; matrix products, arithmetic and copies ran while one was open for 0% of the time, Pallas kernels for 1%

profile of v3, /device:TPU:9, one launch (start us, length us, event | category | flops | bytes accessed | tf_op | source)
XLA Modules:
  0.0 168.1 jit_solution(7384747689143460837)
XLA Ops:
  0.6 0.0 copy-start
  0.6 10.8 %collective-permute-start.1 = (bf16[768,768]{1,0:T(8,128)(2,1)}, bf16[768,768]{1,0:T(8,128)(2,1)S(1)}, u32[]{:S(2)}, u32[]{:S(2)}) collective-permute-start(bf16[768,768]{1,0:T(8,128)(2,1)} %bitcast.3), channel_id=1, source_target_pairs={{0,1},{1,0},{8,57},{9,24},{16,17},{17,16},{24,9},{25,40},{32,33},{... | collective-permute-start | bytes 3538952 | tf_op jit(solution)/shard_map/ppermute | solution.py:253
  11.4 4.4 %collective-permute-start = (bf16[768,768]{1,0:T(8,128)(2,1)}, bf16[768,768]{1,0:T(8,128)(2,1)S(1)}, u32[]{:S(2)}, u32[]{:S(2)}) collective-permute-start(bf16[768,768]{1,0:T(8,128)(2,1)} %bitcast.4), channel_id=1, source_target_pairs={{0,2},{2,4},{4,6},{6,0},{8,14},{10,8},{12,10},{14,12},{1,3},{3,5},... | collective-permute-start | bytes 3538952 | tf_op jit(solution)/shard_map/ppermute | solution.py:250
  15.8 1.9 %prep.1 = (bf16[8,16,768]{2,1,0:T(8,128)(2,1)}, bf16[80,1280]{1,0:T(8,128)(2,1)}) custom-call(f32[5,1,768]{2,1,0:T(1,128)} %bitcast.6, bf16[4,64,512]{2,1,0:T(8,128)(2,1)} %feat_ref.1, bf16[4,64,768]{2,1,0:T(8,128)(2,1)} %targ_ref.1, s32[4]{0:T(128)} %len_ref.1), custom_call_target="tpu_custom_call" | custom-call | tf_op jit(solution)/shard_map/prep/pallas_call | solution.py:259
  17.7 4.0 %all-to-all-start = ((bf16[8,16,768]{2,1,0:T(8,128)(2,1)}), bf16[8,16,768]{2,1,0:T(8,128)(2,1)}, u32[]{:S(2)}, u32[]{:S(2)}) async-start(bf16[8,16,768]{2,1,0:T(8,128)(2,1)} %get-tuple-element.13), calls=%async_computation | async-start | bytes 393216 | tf_op jit(solution)/shard_map/all_to_all | solution.py:272
  21.8 1.9 %collective-permute-start.2 = (bf16[80,1280]{1,0:T(8,128)(2,1)}, bf16[80,1280]{1,0:T(8,128)(2,1)S(1)}, u32[]{:S(2)}, u32[]{:S(2)}) collective-permute-start(bf16[80,1280]{1,0:T(8,128)(2,1)} %get-tuple-element.12.io_a_ref), channel_id=1, source_target_pairs={{0,8},{8,0},{1,9},{9,1},{2,10},{10,2},{3,11},{11,3},{4,12},{12,4},... | collective-permute-start | bytes 614408 | tf_op jit(solution)/shard_map/ppermute | solution.py:256
  23.7 1.6 collective-permute-done.2.io_b_ref
  25.3 0.0 copy-start.3
  25.3 0.7 copy-done.3
  26.0 5.0 %all-to-all-done.traw_ref = bf16[8,16,768]{2,1,0:T(8,128)(2,1)} async-done(((bf16[8,16,768]{2,1,0:T(8,128)(2,1)}), bf16[8,16,768]{2,1,0:T(8,128)(2,1)}, u32[]{:S(2)}, u32[]{:S(2)}) %all-to-all-start) | async-done | bytes 196640 | tf_op jit(solution)/shard_map/all_to_all | solution.py:272
  31.0 0.0 collective-permute-done.1.flip_w
  31.0 0.0 collective-permute-done.near_w
  31.0 1.9 %collective-permute-start.4 = (bf16[768,768]{1,0:T(8,128)(2,1)S(1)}, bf16[768,768]{1,0:T(8,128)(2,1)}, u32[]{:S(2)}, u32[]{:S(2)}) collective-permute-start(bf16[768,768]{1,0:T(8,128)(2,1)S(1)} %collective-permute-done.near_w), channel_id=1, source_target_pairs={{0,8},{8,0},{1,9},{9,1},{2,10},{10,2},{3,11},{11,3},{4,12},{12,4},... | collective-permute-start | bytes 3538952 | tf_op jit(solution)/shard_map/ppermute | solution.py:256
  32.9 6.3 %collective-permute-start.5 = (bf16[768,768]{1,0:T(8,128)(2,1)S(1)}, bf16[768,768]{1,0:T(8,128)(2,1)}, u32[]{:S(2)}, u32[]{:S(2)}) collective-permute-start(bf16[768,768]{1,0:T(8,128)(2,1)S(1)} %collective-permute-done.near_w), channel_id=1, source_target_pairs={{0,1},{1,0},{8,57},{9,24},{16,17},{17,16},{24,9},{25,40},{32,33},{... | collective-permute-start | bytes 3538952 | tf_op jit(solution)/shard_map/ppermute | solution.py:253
  39.2 0.0 copy-start.1
  39.2 0.0 copy-start.2
  39.3 2.1 %collective-permute-start.3 = (bf16[384,768]{1,0:T(8,128)(2,1)S(1)}, bf16[384,768]{1,0:T(8,128)(2,1)S(1)}, u32[]{:S(2)}, u32[]{:S(2)}) collective-permute-start(bf16[384,768]{1,0:T(8,128)(2,1)S(1)} %constant_dynamic-slice_fusion), channel_id=1, source_target_pairs={{0,2},{2,4},{4,6},{6,0},{8,14},{10,8},{12,10},{14,12},{1,3},{3,5},... | collective-permute-start | bytes 1769480 | tf_op jit(solution)/shard_map/ppermute | solution.py:250
  41.4 9.1 %collective-permute-done.3.n2 = bf16[384,768]{1,0:T(8,128)(2,1)S(1)} collective-permute-done((bf16[384,768]{1,0:T(8,128)(2,1)S(1)}, bf16[384,768]{1,0:T(8,128)(2,1)S(1)}, u32[]{:S(2)}, u32[]{:S(2)}) %collective-permute-start.3) | collective-permute-done | bytes 589856 | tf_op jit(solution)/shard_map/ppermute | solution.py:250
  50.5 0.0 collective-permute-done.4.anti_w
  50.5 1.9 %collective-permute-start.6 = (bf16[384,768]{1,0:T(8,128)(2,1)S(1)}, bf16[384,768]{1,0:T(8,128)(2,1)S(1)}, u32[]{:S(2)}, u32[]{:S(2)}) collective-permute-start(bf16[384,768]{1,0:T(8,128)(2,1)S(1)} %collective-permute-done.3.n2), channel_id=1, source_target_pairs={{0,1},{1,0},{8,57},{9,24},{16,17},{17,16},{24,9},{25,40},{32,33},{... | collective-permute-start | bytes 1769480 | tf_op jit(solution)/shard_map/ppermute | solution.py:253
  52.4 0.5 collective-permute-done.5.slant_w
  52.9 1.9 %collective-permute-start.8 = (bf16[768,768]{1,0:T(8,128)(2,1)}, bf16[768,768]{1,0:T(8,128)(2,1)S(1)}, u32[]{:S(2)}, u32[]{:S(2)}) collective-permute-start(bf16[768,768]{1,0:T(8,128)(2,1)} %collective-permute-done.5.slant_w), channel_id=1, source_target_pairs={{0,8},{8,0},{1,9},{9,1},{2,10},{10,2},{3,11},{11,3},{4,12},{12,4},... | collective-permute-start | bytes 3538952 | tf_op jit(solution)/shard_map/ppermute | solution.py:256
  54.8 2.4 %collective-permute-start.7 = (bf16[384,768]{1,0:T(8,128)(2,1)S(1)}, bf16[384,768]{1,0:T(8,128)(2,1)S(1)}, u32[]{:S(2)}, u32[]{:S(2)}) collective-permute-start(bf16[384,768]{1,0:T(8,128)(2,1)S(1)} %collective-permute-done.3.n2), channel_id=1, source_target_pairs={{0,8},{8,0},{1,9},{9,1},{2,10},{10,2},{3,11},{11,3},{4,12},{12,4},... | collective-permute-start | bytes 1769480 | tf_op jit(solution)/shard_map/ppermute | solution.py:256
  57.2 5.1 %collective-permute-done.6.n5 = bf16[384,768]{1,0:T(8,128)(2,1)S(1)} collective-permute-done((bf16[384,768]{1,0:T(8,128)(2,1)S(1)}, bf16[384,768]{1,0:T(8,128)(2,1)S(1)}, u32[]{:S(2)}, u32[]{:S(2)}) %collective-permute-start.6) | collective-permute-done | bytes 589856 | tf_op jit(solution)/shard_map/ppermute | solution.py:253
  62.3 1.9 %collective-permute-start.9 = (bf16[384,768]{1,0:T(8,128)(2,1)S(1)}, bf16[384,768]{1,0:T(8,128)(2,1)S(1)}, u32[]{:S(2)}, u32[]{:S(2)}) collective-permute-start(bf16[384,768]{1,0:T(8,128)(2,1)S(1)} %collective-permute-done.6.n5), channel_id=1, source_target_pairs={{0,8},{8,0},{1,9},{9,1},{2,10},{10,2},{3,11},{11,3},{4,12},{12,4},... | collective-permute-start | bytes 1769480 | tf_op jit(solution)/shard_map/ppermute | solution.py:256
  64.2 0.0 collective-permute-done.7.m2
  64.2 0.0 collective-permute-done.8.far_w
  64.2 1.9 %collective-permute-done.9.m5 = bf16[384,768]{1,0:T(8,128)(2,1)S(1)} collective-permute-done((bf16[384,768]{1,0:T(8,128)(2,1)S(1)}, bf16[384,768]{1,0:T(8,128)(2,1)S(1)}, u32[]{:S(2)}, u32[]{:S(2)}) %collective-permute-start.9) | collective-permute-done | bytes 589856 | tf_op jit(solution)/shard_map/ppermute | solution.py:256
  66.2 0.0 copy-done
  66.2 0.0 copy-done.1
  66.2 0.0 copy-done.2
  66.2 0.0 copy-start.4
  66.2 0.9 copy-done.4
  67.1 14.6 %model.1 = bf16[8,112,768]{2,1,0:T(8,128)(2,1)S(1)} custom-call(bf16[80,1280]{1,0:T(8,128)(2,1)S(1)} %copy-done.2, bf16[80,1280]{1,0:T(8,128)(2,1)S(1)} %copy-done.4, bf16[512,768]{1,0:T(8,128)(2,1)S(1)} %copy-done.1, bf16[8,16,768]{2,1,0:T(8,128)(2,1)} %all-to-all-done.traw_ref, bf16[768,768]{1,0:T(8,128)(2,1)S(1)} %bitcast.5, ...), custom_call_target="tpu_custom_call" | custom-call | tf_op jit(solution)/shard_map/model/pallas_call | solution.py:283
  81.8 21.3 %all_to_all.20.recv_ref = bf16[8,112,768]{2,1,0:T(8,128)(2,1)S(1)} all-to-all(bf16[8,112,768]{2,1,0:T(8,128)(2,1)S(1)} %model.1), channel_id=1, replica_groups=mesh['y'=8,'zh'=4,'c'=2,'x'=4,'zl'=2] {'x','zl'}, dimensions={0} | all-to-all | bytes 2752512 | tf_op jit(solution)/shard_map/all_to_all | solution.py:306
  103.0 0.6 grad.1
  103.6 28.4 %all_to_all.21.parts_ref = bf16[32,80,128]{2,1,0:T(8,128)(2,1)S(1)} all-to-all(bf16[32,80,128]{2,1,0:T(8,128)(2,1)S(1)} %grad.1), channel_id=1, replica_groups=mesh['y'=8,'zh'=4,'c'=2,'x'=4,'zl'=2] {'y','zh'}, dimensions={0} | all-to-all | bytes 1310720 | tf_op jit(solution)/shard_map/all_to_all | solution.py:323
  132.0 0.1 total.1
  132.1 27.3 %all_to_all.22.mine_ref = bf16[32,80,128]{2,1,0:T(8,128)(2,1)S(1)} all-to-all(bf16[32,80,128]{2,1,0:T(8,128)(2,1)S(1)} %total.1), channel_id=1, replica_groups=mesh['y'=8,'zh'=4,'c'=2,'x'=4,'zl'=2] {'y','zh'}, dimensions={0} | all-to-all | bytes 1310720 | tf_op jit(solution)/shard_map/all_to_all | solution.py:335
  159.4 5.8 %collective-permute-start.10 = (bf16[32,80,128]{2,1,0:T(8,128)(2,1)S(1)}, bf16[32,80,128]{2,1,0:T(8,128)(2,1)S(1)}, u32[]{:S(2)}, u32[]{:S(2)}) collective-permute-start(bf16[32,80,128]{2,1,0:T(8,128)(2,1)S(1)} %all_to_all.22.mine_ref), channel_id=1, source_target_pairs={{0,8},{8,0},{1,9},{9,1},{2,10},{10,2},{3,11},{11,3},{4,12},{12,4},... | collective-permute-start | bytes 1966088 | tf_op jit(solution)/shard_map/ppermute | solution.py:256
  165.2 1.7 %collective-permute-done.10.theirs_ref = bf16[32,80,128]{2,1,0:T(8,128)(2,1)S(1)} collective-permute-done((bf16[32,80,128]{2,1,0:T(8,128)(2,1)S(1)}, bf16[32,80,128]{2,1,0:T(8,128)(2,1)S(1)}, u32[]{:S(2)}, u32[]{:S(2)}) %collective-permute-start.10) | collective-permute-done | bytes 655392 | tf_op jit(solution)/shard_map/ppermute | solution.py:256
  166.9 1.2 place.1
  (1 shorter events, 0.0 us)
Async XLA Ops:
  0.6 65.6 %copy-start = (bf16[1,768,768]{2,1,0:T(8,128)(2,1)S(1)}, bf16[1,768,768]{2,1,0:T(8,128)(2,1)}, u32[]{:S(2)}) copy-start(bf16[1,768,768]{2,1,0:T(8,128)(2,1)} %param.9) | copy-start | bytes 3538948
  0.6 30.4 %collective-permute-start.1 = (bf16[768,768]{1,0:T(8,128)(2,1)}, bf16[768,768]{1,0:T(8,128)(2,1)S(1)}, u32[]{:S(2)}, u32[]{:S(2)}) collective-permute-start(bf16[768,768]{1,0:T(8,128)(2,1)} %bitcast.3), channel_id=1, source_target_pairs={{0,1},{1,0},{8,57},{9,24},{16,17},{17,16},{24,9},{25,40},{32,33},{... | collective-permute-start | bytes 3538952 | tf_op jit(solution)/shard_map/ppermute | solution.py:253
  11.4 19.6 %collective-permute-start = (bf16[768,768]{1,0:T(8,128)(2,1)}, bf16[768,768]{1,0:T(8,128)(2,1)S(1)}, u32[]{:S(2)}, u32[]{:S(2)}) collective-permute-start(bf16[768,768]{1,0:T(8,128)(2,1)} %bitcast.4), channel_id=1, source_target_pairs={{0,2},{2,4},{4,6},{6,0},{8,14},{10,8},{12,10},{14,12},{1,3},{3,5},... | collective-permute-start | bytes 3538952 | tf_op jit(solution)/shard_map/ppermute | solution.py:250
  17.7 13.3 %all-to-all-start = ((bf16[8,16,768]{2,1,0:T(8,128)(2,1)}), bf16[8,16,768]{2,1,0:T(8,128)(2,1)}, u32[]{:S(2)}, u32[]{:S(2)}) async-start(bf16[8,16,768]{2,1,0:T(8,128)(2,1)} %get-tuple-element.13), calls=%async_computation | async-start | bytes 393216 | tf_op jit(solution)/shard_map/all_to_all | solution.py:272
  21.8 3.6 %collective-permute-start.2 = (bf16[80,1280]{1,0:T(8,128)(2,1)}, bf16[80,1280]{1,0:T(8,128)(2,1)S(1)}, u32[]{:S(2)}, u32[]{:S(2)}) collective-permute-start(bf16[80,1280]{1,0:T(8,128)(2,1)} %get-tuple-element.12.io_a_ref), channel_id=1, source_target_pairs={{0,8},{8,0},{1,9},{9,1},{2,10},{10,2},{3,11},{11,3},{4,12},{12,4},... | collective-permute-start | bytes 614408 | tf_op jit(solution)/shard_map/ppermute | solution.py:256
  25.3 0.7 copy-start.3
  31.0 19.4 %collective-permute-start.4 = (bf16[768,768]{1,0:T(8,128)(2,1)S(1)}, bf16[768,768]{1,0:T(8,128)(2,1)}, u32[]{:S(2)}, u32[]{:S(2)}) collective-permute-start(bf16[768,768]{1,0:T(8,128)(2,1)S(1)} %collective-permute-done.near_w), channel_id=1, source_target_pairs={{0,8},{8,0},{1,9},{9,1},{2,10},{10,2},{3,11},{11,3},{4,12},{12,4},... | collective-permute-start | bytes 3538952 | tf_op jit(solution)/shard_map/ppermute | solution.py:256
  32.9 20.0 %collective-permute-start.5 = (bf16[768,768]{1,0:T(8,128)(2,1)S(1)}, bf16[768,768]{1,0:T(8,128)(2,1)}, u32[]{:S(2)}, u32[]{:S(2)}) collective-permute-start(bf16[768,768]{1,0:T(8,128)(2,1)S(1)} %collective-permute-done.near_w), channel_id=1, source_target_pairs={{0,1},{1,0},{8,57},{9,24},{16,17},{17,16},{24,9},{25,40},{32,33},{... | collective-permute-start | bytes 3538952 | tf_op jit(solution)/shard_map/ppermute | solution.py:253
  39.2 27.0 %copy-start.1 = (bf16[512,768]{1,0:T(8,128)(2,1)S(1)}, bf16[512,768]{1,0:T(8,128)(2,1)}, u32[]{:S(2)}) copy-start(bf16[512,768]{1,0:T(8,128)(2,1)} %front_ref.1) | copy-start | bytes 2359300
  39.2 27.0 %copy-start.2 = (bf16[80,1280]{1,0:T(8,128)(2,1)S(1)}, bf16[80,1280]{1,0:T(8,128)(2,1)}, u32[]{:S(2)}) copy-start(bf16[80,1280]{1,0:T(8,128)(2,1)} %get-tuple-element.12.io_a_ref) | copy-start | bytes 614404
  39.3 11.2 %collective-permute-start.3 = (bf16[384,768]{1,0:T(8,128)(2,1)S(1)}, bf16[384,768]{1,0:T(8,128)(2,1)S(1)}, u32[]{:S(2)}, u32[]{:S(2)}) collective-permute-start(bf16[384,768]{1,0:T(8,128)(2,1)S(1)} %constant_dynamic-slice_fusion), channel_id=1, source_target_pairs={{0,2},{2,4},{4,6},{6,0},{8,14},{10,8},{12,10},{14,12},{1,3},{3,5},... | collective-permute-start | bytes 1769480 | tf_op jit(solution)/shard_map/ppermute | solution.py:250
  50.5 11.8 %collective-permute-start.6 = (bf16[384,768]{1,0:T(8,128)(2,1)S(1)}, bf16[384,768]{1,0:T(8,128)(2,1)S(1)}, u32[]{:S(2)}, u32[]{:S(2)}) collective-permute-start(bf16[384,768]{1,0:T(8,128)(2,1)S(1)} %collective-permute-done.3.n2), channel_id=1, source_target_pairs={{0,1},{1,0},{8,57},{9,24},{16,17},{17,16},{24,9},{25,40},{32,33},{... | collective-permute-start | bytes 1769480 | tf_op jit(solution)/shard_map/ppermute | solution.py:253
  52.9 11.3 %collective-permute-start.8 = (bf16[768,768]{1,0:T(8,128)(2,1)}, bf16[768,768]{1,0:T(8,128)(2,1)S(1)}, u32[]{:S(2)}, u32[]{:S(2)}) collective-permute-start(bf16[768,768]{1,0:T(8,128)(2,1)} %collective-permute-done.5.slant_w), channel_id=1, source_target_pairs={{0,8},{8,0},{1,9},{9,1},{2,10},{10,2},{3,11},{11,3},{4,12},{12,4},... | collective-permute-start | bytes 3538952 | tf_op jit(solution)/shard_map/ppermute | solution.py:256
  54.8 9.4 %collective-permute-start.7 = (bf16[384,768]{1,0:T(8,128)(2,1)S(1)}, bf16[384,768]{1,0:T(8,128)(2,1)S(1)}, u32[]{:S(2)}, u32[]{:S(2)}) collective-permute-start(bf16[384,768]{1,0:T(8,128)(2,1)S(1)} %collective-permute-done.3.n2), channel_id=1, source_target_pairs={{0,8},{8,0},{1,9},{9,1},{2,10},{10,2},{3,11},{11,3},{4,12},{12,4},... | collective-permute-start | bytes 1769480 | tf_op jit(solution)/shard_map/ppermute | solution.py:256
  62.3 3.9 %collective-permute-start.9 = (bf16[384,768]{1,0:T(8,128)(2,1)S(1)}, bf16[384,768]{1,0:T(8,128)(2,1)S(1)}, u32[]{:S(2)}, u32[]{:S(2)}) collective-permute-start(bf16[384,768]{1,0:T(8,128)(2,1)S(1)} %collective-permute-done.6.n5), channel_id=1, source_target_pairs={{0,8},{8,0},{1,9},{9,1},{2,10},{10,2},{3,11},{11,3},{4,12},{12,4},... | collective-permute-start | bytes 1769480 | tf_op jit(solution)/shard_map/ppermute | solution.py:256
  66.2 0.9 copy-start.4
  159.4 7.5 %collective-permute-start.10 = (bf16[32,80,128]{2,1,0:T(8,128)(2,1)S(1)}, bf16[32,80,128]{2,1,0:T(8,128)(2,1)S(1)}, u32[]{:S(2)}, u32[]{:S(2)}) collective-permute-start(bf16[32,80,128]{2,1,0:T(8,128)(2,1)S(1)} %all_to_all.22.mine_ref), channel_id=1, source_target_pairs={{0,8},{8,0},{1,9},{9,1},{2,10},{10,2},{3,11},{11,3},{4,12},{12,4},... | collective-permute-start | bytes 1966088 | tf_op jit(solution)/shard_map/ppermute | solution.py:256

commit v4 on v2

--- a/solution.py
+++ b/solution.py
@@ -20,7 +20,8 @@
 TAPS = 16
 PIECE = H + TAPS
 INROWS = T + 16
-PAY = T + T // 2 + TAPS
+HT = T // 2
+PAY = T + HT + 8
 PEERS = 32
 CHUNK = 72
 CROWS = 80
@@ -50,8 +51,7 @@
 
 
 def prep_kernel(
-    w_ref, taps_ref, feat_ref, targ_ref, len_ref, both_ref, near_ref, io_ref,
-    packed_ref, count_ref, sem,
+    w_ref, taps_ref, feat_ref, targ_ref, len_ref, both_ref, io_ref, sem
 ):
     section, core = where_am_i()
     utt = lax.rem(section, 4)
@@ -62,7 +62,6 @@
         pltpu.make_async_copy(w_ref.at[0, pl.ds(theirs, H)], both_ref.at[pl.ds(PIECE, H)], sem.at[1]),
         pltpu.make_async_copy(
             feat_ref.at[utt], io_ref.at[pl.ds(0, T), pl.ds(0, FEAT)], sem.at[2]),
-        pltpu.make_async_copy(w_ref.at[0, pl.ds(mine, H)], near_ref.at[pl.ds(0, H)], sem.at[6]),
         pltpu.make_async_copy(
             targ_ref.at[utt], io_ref.at[pl.ds(0, T), pl.ds(FEAT, D)], sem.at[3]),
     ]
@@ -71,26 +70,33 @@
     taps = jnp.concatenate([taps_ref[k] for k in range(KER)], axis=0)
     hi, mid, low = split3(taps)
     packed = jnp.concatenate([hi, mid, low, jnp.zeros((1, D), F32)], axis=0)
-    packed_ref[...] = packed.astype(BF)
+    both_ref[H:PIECE, :] = packed.astype(BF)
     count = len_ref[utt].astype(F32)
-    count_ref[...] = jnp.full((INROWS - T, FEAT + D), count, F32).astype(BF)
-    late = [
-        pltpu.make_async_copy(packed_ref, both_ref.at[pl.ds(H, TAPS)], sem.at[4]),
-        pltpu.make_async_copy(packed_ref, near_ref.at[pl.ds(H, TAPS)], sem.at[7]),
-        pltpu.make_async_copy(count_ref, io_ref.at[pl.ds(T, INROWS - T)], sem.at[5]),
-    ]
-    for copy in late:
-        copy.start()
-    for copy in copies + late:
+    io_ref[T:, :] = jnp.full((INROWS - T, FEAT + D), count, F32).astype(BF)
+    for copy in copies:
         copy.wait()
 
 
+def front_kernel(io_a_ref, io_b_ref, front_ref, out_ref):
+    section, core = where_am_i()
+    own = core == lax.div(section, 4)
+    pick = jnp.where(own, 1.0, 0.0).astype(F32)
+    io = io_a_ref[...].astype(F32) * pick + io_b_ref[...].astype(F32) * (1.0 - pick)
+    out_ref[0:T, :] = jnp.dot(
+        io[0:T, 0:FEAT].astype(BF), front_ref[...], preferred_element_type=F32).astype(BF)
+    out_ref[T:, :] = io[:, FEAT:].astype(BF)
+
+
+def fold(x):
+    return jnp.concatenate([x[0:HT], x[HT:]], axis=1)
+
+
 def model_kernel(
-    io_a_ref, io_b_ref, front_ref,
-    own_w, near_w, n3, n2, slant_w, n5, anti_w, m3, m2, far_w, m5,
+    start_ref,
+    own_w, near_w, flip_w, n2, slant_w, n5, anti_w, m2, far_w, m5,
     pay_ref,
     w_ref, traw_ref, taps_ref, vals_ref, inv_ref, norm_ref, slope_ref, act_ref, gpad_ref, g_ref,
-    io_ref, wsem, tsem, isem,
+    wsem, tsem,
 ):
     section, core = where_am_i()
     col = lax.div(section, 2)
@@ -100,45 +106,31 @@
     anti = lax.rem(col + 1 + 2 * core, 4)
     across = lax.rem(col + 2, 4)
     flip = 1 - row
-    inputs = [
-        pltpu.make_async_copy(ref, io_ref.at[i], isem.at[i])
-        for i, ref in enumerate((io_a_ref, io_b_ref))
-    ]
-    for copy in inputs:
-        copy.start()
-
-    def bring(piece, first, c, r, part, taps_at):
+
+    def bring(piece, first, c, r, part, with_taps):
         layer = 2 * c + r
         start = pl.multiple_of(part * H, H)
         pltpu.make_async_copy(
             piece.at[pl.ds(first, H)], w_ref.at[layer, pl.ds(start, H)], wsem.at[layer]).start()
-        if taps_at is not None:
+        if with_taps:
             pltpu.make_async_copy(
-                piece.at[pl.ds(taps_at, TAPS)], traw_ref.at[layer], tsem.at[layer]).start()
+                piece.at[pl.ds(H, TAPS)], traw_ref.at[layer], tsem.at[layer]).start()
 
     for piece, c, r, part in (
-        (own_w, col, row, core), (near_w, side, row, core), (slant_w, side, flip, core),
-        (anti_w, anti, row, other), (far_w, anti, flip, other),
+        (own_w, col, row, core), (near_w, side, row, core), (flip_w, col, flip, core),
+        (slant_w, side, flip, core), (anti_w, anti, row, other), (far_w, anti, flip, other),
     ):
-        bring(piece, 0, c, r, part, H)
-        bring(piece, PIECE, c, r, 1 - part, None)
-    for piece, mirror, c, r in (
-        (n3, m3, col, flip), (n2, m2, across, row), (n5, m5, across, flip),
-    ):
-        bring(piece, 0, c, r, core, H)
-        bring(mirror, 0, c, r, other, None)
-
-    for copy in inputs:
-        copy.wait()
-    own = core == lax.div(section, 4)
-    pick = jnp.where(own, 1.0, 0.0).astype(F32)
-    io = io_ref[0].astype(F32) * pick + io_ref[1].astype(F32) * (1.0 - pick)
-    count = io[T:T + 1, 0:1]
-    target = io[0:T, FEAT:]
+        bring(piece, 0, c, r, part, True)
+        bring(piece, PIECE, c, r, 1 - part, False)
+    for piece, mirror, r in ((n2, m2, row), (n5, m5, flip)):
+        bring(piece, 0, across, r, core, True)
+        bring(mirror, 0, across, r, other, False)
+
+    count = start_ref[2 * T:, :].astype(F32)[0:1, 0:1]
+    target = start_ref[T:2 * T, :].astype(F32)
     frame = lax.broadcasted_iota(jnp.int32, (T, 1), 0).astype(F32)
     mask = jnp.where(frame < count, 1.0, 0.0).astype(F32)
-    hidden = jnp.dot(io[0:T, 0:FEAT].astype(BF), front_ref[...], preferred_element_type=F32)
-    g_ref[...] = hidden.astype(BF).astype(F32)
+    g_ref[...] = start_ref[0:T, :].astype(F32)
 
     edge = jnp.zeros((8, D), F32)
     gpad_ref[0:8, :] = edge
@@ -180,8 +172,7 @@
         pay_ref[l, 0:T, :] = gb
         act = act_ref[l].astype(F32)
         share = jnp.where(core == 0, act[:, 0:H], act[:, H:])
-        pay_ref[l, T:T + T // 2, 0:H] = share[0:T // 2].astype(BF)
-        pay_ref[l, T:T + T // 2, H:] = share[T // 2:].astype(BF)
+        pay_ref[l, T:T + HT, :] = fold(share).astype(BF)
         grad_act = lax.dot_general(
             gb, w_ref[l], (((1,), (1,)), ((), ())), preferred_element_type=F32)
         grad_conv = grad_act * slope_ref[l]
@@ -192,8 +183,9 @@
             rows.append(jnp.sum(grad_conv * norm_ref[l, 6 + k:T + 6 + k, :], axis=0, keepdims=True))
         total = jnp.concatenate(rows, axis=0)
         hi = total.astype(BF).astype(F32)
-        packed = jnp.concatenate([hi, total - hi, jnp.zeros((TAPS - 2 * KER, D), F32)], axis=0)
-        pay_ref[l, T + T // 2:, :] = packed.astype(BF)
+        part = jnp.where(core == 0, hi, total - hi)
+        packed = jnp.concatenate([part, jnp.zeros((8 - KER, D), F32)], axis=0)
+        pay_ref[l, T + HT:, :] = packed.astype(BF)
         grad_norm = taps[0:1] * gpad_ref[10:T + 10, :]
         for k in range(1, KER):
             grad_norm = grad_norm + taps[k:k + 1] * gpad_ref[10 - k:T + 10 - k, :]
@@ -220,7 +212,7 @@
     taps = recv_ref[0, T + half:, :].astype(F32)
     for i in range(1, L):
         taps = taps + recv_ref[i, T + half:, :].astype(F32)
-    total = taps[0:KER] + taps[KER:2 * KER]
+    total = taps[0:KER]
     hi = total.astype(BF).astype(F32)
     low = total - hi
     chunk_ref[CHUNK:, :] = jnp.zeros((CROWS - CHUNK, 128), F32)
@@ -258,7 +250,7 @@
                 flat_ref[b * H:(b + 1) * H, :].astype(BF))
     for j in range(KER * 6):
         k, b = divmod(j, 6)
-        pair = mine_ref[j, CHUNK:, :].astype(F32)
+        pair = mine_ref[j, CHUNK:, :].astype(F32) + theirs_ref[j, CHUNK:, :].astype(F32)
         taps_ref[k, :, b * 128:(b + 1) * 128] = pair[0:1] + pair[1:2]
 
 
@@ -282,36 +274,37 @@
     def to_core(a):
         return lax.ppermute(a, "c", [(0, 1), (1, 0)])
 
-    both, near, io = pl.pallas_call(
+    both, io = pl.pallas_call(
         prep_kernel,
         name="prep",
         out_shape=(
             jax.ShapeDtypeStruct((PIECE + H, D), BF),
-            jax.ShapeDtypeStruct((PIECE, D), BF),
             jax.ShapeDtypeStruct((INROWS, FEAT + D), BF),
         ),
         in_specs=[ANY, VMEM, ANY, ANY, SMEM],
-        out_specs=(ANY, ANY, ANY),
-        scratch_shapes=[
-            pltpu.VMEM((TAPS, D), BF),
-            pltpu.VMEM((INROWS - T, FEAT + D), BF),
-            pltpu.SemaphoreType.DMA((8,)),
-        ],
+        out_specs=(VMEM, VMEM),
+        scratch_shapes=[pltpu.SemaphoreType.DMA((4,))],
     )(pointwise, jnp.transpose(kernel, (1, 0, 2)), features, targets, lengths)
 
-    beside, n3 = lax.optimization_barrier((along_x(both), along_z(near)))
-    io_other = to_core(io)
+    begin = pl.pallas_call(
+        front_kernel,
+        name="front",
+        out_shape=jax.ShapeDtypeStruct((2 * T + INROWS - T, D), BF),
+        in_specs=[VMEM, VMEM, VMEM],
+        out_specs=VMEM,
+    )(io, to_core(io), front_weight)
+    beside, flipped, begin = lax.optimization_barrier((along_x(both), along_z(both), begin))
     n2 = along_x(beside[:PIECE])
     slant = along_z(beside)
     n5 = along_z(n2)
-    here = [both, beside, n3, n2, slant, n5]
-    there = [to_core(a) for a in (beside, n3, n2, slant, n5)]
+    here = [both, beside, flipped, n2, slant, n5]
+    there = [to_core(a) for a in (beside, n2, slant, n5)]
 
     payload = pl.pallas_call(
         model_kernel,
         name="model",
         out_shape=jax.ShapeDtypeStruct((L, PAY, D), BF),
-        in_specs=[ANY, ANY, VMEM] + [ANY] * 11,
+        in_specs=[VMEM] + [ANY] * 10,
         out_specs=VMEM,
         scratch_shapes=[
             pltpu.VMEM((L, D, D), BF),
@@ -324,13 +317,11 @@
             pltpu.VMEM((L, T, D), BF),
             pltpu.VMEM((T + 16, D), F32),
             pltpu.VMEM((T, D), F32),
-            pltpu.VMEM((2, INROWS, FEAT + D), BF),
             pltpu.SemaphoreType.DMA((L,)),
             pltpu.SemaphoreType.DMA((L,)),
-            pltpu.SemaphoreType.DMA((2,)),
         ],
         compiler_params=params(28),
-    )(io, io_other, front_weight, *here, *there)
+    )(begin, *here, *there)
 
     received = lax.all_to_all(payload, ("x", "zl"), 0, 0)
 

time: 224 us -> 164 us (0.73)
  Pallas kernels: 77 us -> 21 us
  starting transfers between devices: 46.7 us -> 43.1 us
  waiting for transfers between devices: 18.1 us -> 20.7 us
  blocking collectives: 79.4 us -> 77.1 us
    pallas_call x1, Pallas kernels: 60.6 us -> 3.26 us  [body(): pl.pallas_call(prep_kernel, name='prep', out_shape=(jax.ShapeDtypeStruct(...]
    ppermute x2, waiting for transfers between devices: 7.07 us -> 11 us  [along_x(): return lax.ppermute(a, ('c', 'x'), ring)]
    ppermute x3, waiting for transfers between devices: 7.74 us -> 4.34 us  [along_z(): return lax.ppermute(a, ('zh', 'c', 'zl'), pair)]
    pallas_call x0 -> x1, Pallas kernels: none -> 2.29 us  [body(): pl.pallas_call(front_kernel, name='front', out_shape=jax.ShapeDtypeStruct...]
    ppermute x7 -> x6, starting transfers between devices: 18.8 us -> 16.6 us  [to_core(): return lax.ppermute(a, 'c', [(0, 1), (1, 0)])]
    ppermute x7 -> x6, waiting for transfers between devices: 3.33 us -> 5.32 us  [to_core(): return lax.ppermute(a, 'c', [(0, 1), (1, 0)])]
  transfers between devices with their start and end apart: 12 -> 11, of which waited for: 4 -> 7; matrix products, arithmetic and copies ran while one was open for 0% -> 0% of each run, Pallas kernels for 0% -> 1%
where the time goes in v4:
time: 164 us; the launch traced here: 163 us
  blocking collectives  77.1 us (47%)
  starting transfers between devices  43.1 us (26%)
  Pallas kernels  21 us (13%)
  waiting for transfers between devices  20.7 us (13%)
    all_to_all x1, blocking collectives, body(): scattered = lax.all_to_all(parts, ('y', 'zh'), 0, 0)  28.9 us
    all_to_all x1, blocking collectives, body(): half = lax.all_to_all(mine, ('y', 'zh'), 0, 0)  26.4 us
    all_to_all x1, blocking collectives, body(): received = lax.all_to_all(payload, ('x', 'zl'), 0, 0)  21.7 us
    ppermute x3, starting transfers between devices, along_z(): return lax.ppermute(a, ('zh', 'c', 'zl'), pair)  17.1 us
    ppermute x6, starting transfers between devices, to_core(): return lax.ppermute(a, 'c', [(0, 1), (1, 0)])  16.6 us
    pallas_call x1, Pallas kernels, body(): pl.pallas_call(model_kernel, name='model', out_shape=jax.ShapeDtypeStruct...  13.6 us
    ppermute x2, waiting for transfers between devices, along_x(): return lax.ppermute(a, ('c', 'x'), ring)  11 us
    ppermute x2, starting transfers between devices, along_x(): return lax.ppermute(a, ('c', 'x'), ring)  9.31 us
  transfers between devices with their start and end apart: 11, of which 7 were waited for; matrix products, arithmetic and copies ran while one was open for 0% of the time, Pallas kernels for 1%

profile of v4, /device:TPU:9, one launch (start us, length us, event | category | flops | bytes accessed | tf_op | source)
XLA Modules:
  0.0 163.4 jit_solution(9451331606202558418)
XLA Ops:
  0.6 3.3 %prep.1 = (bf16[784,768]{1,0:T(8,128)(2,1)}, bf16[80,1280]{1,0:T(8,128)(2,1)}) custom-call(bf16[1,768,768]{2,1,0:T(8,128)(2,1)} %w_ref.1, f32[5,1,768]{2,1,0:T(1,128)} %bitcast.2, bf16[4,64,512]{2,1,0:T(8,128)(2,1)} %feat_ref.1, bf16[4,64,768]{2,1,0:T(8,128)(2,1)} %targ_ref.1, s32[4]{0:T(128)} %len_ref.1), custom_call_target="tpu_custom_call" | custom-call | tf_op jit(solution)/shard_map/prep/pallas_call | solution.py:277
  3.9 10.7 %collective-permute-start.1 = (bf16[784,768]{1,0:T(8,128)(2,1)}, bf16[784,768]{1,0:T(8,128)(2,1)}, u32[]{:S(2)}, u32[]{:S(2)}) collective-permute-start(bf16[784,768]{1,0:T(8,128)(2,1)} %get-tuple-element.9.own_w), channel_id=1, source_target_pairs={{0,1},{1,0},{8,57},{9,24},{16,17},{17,16},{24,9},{25,40},{32,33},{... | collective-permute-start | bytes 3612680 | tf_op jit(solution)/shard_map/ppermute | solution.py:272
  14.6 4.4 %collective-permute-start = (bf16[784,768]{1,0:T(8,128)(2,1)}, bf16[784,768]{1,0:T(8,128)(2,1)S(1)}, u32[]{:S(2)}, u32[]{:S(2)}) collective-permute-start(bf16[784,768]{1,0:T(8,128)(2,1)} %get-tuple-element.9.own_w), channel_id=1, source_target_pairs={{0,2},{2,4},{4,6},{6,0},{8,14},{10,8},{12,10},{14,12},{1,3},{3,5},... | collective-permute-start | bytes 3612680 | tf_op jit(solution)/shard_map/ppermute | solution.py:269
  19.0 0.0 copy-start
  19.0 2.1 %collective-permute-start.2 = (bf16[80,1280]{1,0:T(8,128)(2,1)}, bf16[80,1280]{1,0:T(8,128)(2,1)S(1)}, u32[]{:S(2)}, u32[]{:S(2)}) collective-permute-start(bf16[80,1280]{1,0:T(8,128)(2,1)} %get-tuple-element.10.io_a_ref), channel_id=1, source_target_pairs={{0,8},{8,0},{1,9},{9,1},{2,10},{10,2},{3,11},{11,3},{4,12},{12,4},... | collective-permute-start | bytes 614408 | tf_op jit(solution)/shard_map/ppermute | solution.py:275
  21.0 1.6 collective-permute-done.2.io_b_ref
  22.7 0.0 copy-start.2
  22.7 0.7 copy-done.2
  23.3 2.3 %front.1.start_ref = bf16[144,768]{1,0:T(8,128)(2,1)} custom-call(bf16[80,1280]{1,0:T(8,128)(2,1)} %get-tuple-element.10.io_a_ref, bf16[80,1280]{1,0:T(8,128)(2,1)} %copy-done.2, bf16[512,768]{1,0:T(8,128)(2,1)} %front_ref.1), custom_call_target="tpu_custom_call" | custom-call | tf_op jit(solution)/shard_map/front/pallas_call | solution.py:289
  25.6 0.0 copy-start.1
  25.6 3.1 %collective-permute-done.1.flip_w = bf16[784,768]{1,0:T(8,128)(2,1)} collective-permute-done((bf16[784,768]{1,0:T(8,128)(2,1)}, bf16[784,768]{1,0:T(8,128)(2,1)}, u32[]{:S(2)}, u32[]{:S(2)}) %collective-permute-start.1) | collective-permute-done | bytes 1204256 | tf_op jit(solution)/shard_map/ppermute | solution.py:272
  28.7 3.9 %collective-permute-done.near_w = bf16[784,768]{1,0:T(8,128)(2,1)S(1)} collective-permute-done((bf16[784,768]{1,0:T(8,128)(2,1)}, bf16[784,768]{1,0:T(8,128)(2,1)S(1)}, u32[]{:S(2)}, u32[]{:S(2)}) %collective-permute-start) | collective-permute-done | bytes 1204256 | tf_op jit(solution)/shard_map/ppermute | solution.py:269
  32.7 1.9 %collective-permute-start.4 = (bf16[784,768]{1,0:T(8,128)(2,1)S(1)}, bf16[784,768]{1,0:T(8,128)(2,1)S(1)}, u32[]{:S(2)}, u32[]{:S(2)}) collective-permute-start(bf16[784,768]{1,0:T(8,128)(2,1)S(1)} %collective-permute-done.near_w), channel_id=1, source_target_pairs={{0,1},{1,0},{8,57},{9,24},{16,17},{17,16},{24,9},{25,40},{32,33},{... | collective-permute-start | bytes 3612680 | tf_op jit(solution)/shard_map/ppermute | solution.py:272
  34.6 4.9 %collective-permute-start.3 = (bf16[400,768]{1,0:T(8,128)(2,1)S(1)}, bf16[400,768]{1,0:T(8,128)(2,1)S(1)}, u32[]{:S(2)}, u32[]{:S(2)}) collective-permute-start(bf16[400,768]{1,0:T(8,128)(2,1)S(1)} %slice.3), channel_id=1, source_target_pairs={{0,2},{2,4},{4,6},{6,0},{8,14},{10,8},{12,10},{14,12},{1,3},{3,5},... | collective-permute-start | bytes 1843208 | tf_op jit(solution)/shard_map/ppermute | solution.py:269
  39.6 7.1 %collective-permute-done.3.n2 = bf16[400,768]{1,0:T(8,128)(2,1)S(1)} collective-permute-done((bf16[400,768]{1,0:T(8,128)(2,1)S(1)}, bf16[400,768]{1,0:T(8,128)(2,1)S(1)}, u32[]{:S(2)}, u32[]{:S(2)}) %collective-permute-start.3) | collective-permute-done | bytes 614432 | tf_op jit(solution)/shard_map/ppermute | solution.py:269
  46.6 4.6 %collective-permute-start.5 = (bf16[400,768]{1,0:T(8,128)(2,1)S(1)}, bf16[400,768]{1,0:T(8,128)(2,1)S(1)}, u32[]{:S(2)}, u32[]{:S(2)}) collective-permute-start(bf16[400,768]{1,0:T(8,128)(2,1)S(1)} %collective-permute-done.3.n2), channel_id=1, source_target_pairs={{0,1},{1,0},{8,57},{9,24},{16,17},{17,16},{24,9},{25,40},{32,33},{... | collective-permute-start | bytes 1843208 | tf_op jit(solution)/shard_map/ppermute | solution.py:272
  51.2 1.9 %collective-permute-start.6 = (bf16[784,768]{1,0:T(8,128)(2,1)S(1)}, bf16[784,768]{1,0:T(8,128)(2,1)S(1)}, u32[]{:S(2)}, u32[]{:S(2)}) collective-permute-start(bf16[784,768]{1,0:T(8,128)(2,1)S(1)} %collective-permute-done.near_w), channel_id=1, source_target_pairs={{0,8},{8,0},{1,9},{9,1},{2,10},{10,2},{3,11},{11,3},{4,12},{12,4},... | collective-permute-start | bytes 3612680 | tf_op jit(solution)/shard_map/ppermute | solution.py:275
  53.1 0.0 collective-permute-done.4.slant_w
  53.1 2.4 %collective-permute-start.8 = (bf16[784,768]{1,0:T(8,128)(2,1)S(1)}, bf16[784,768]{1,0:T(8,128)(2,1)S(1)}, u32[]{:S(2)}, u32[]{:S(2)}) collective-permute-start(bf16[784,768]{1,0:T(8,128)(2,1)S(1)} %collective-permute-done.4.slant_w), channel_id=1, source_target_pairs={{0,8},{8,0},{1,9},{9,1},{2,10},{10,2},{3,11},{11,3},{4,12},{12,4},... | collective-permute-start | bytes 3612680 | tf_op jit(solution)/shard_map/ppermute | solution.py:275
  55.6 1.9 %collective-permute-start.7 = (bf16[400,768]{1,0:T(8,128)(2,1)S(1)}, bf16[400,768]{1,0:T(8,128)(2,1)S(1)}, u32[]{:S(2)}, u32[]{:S(2)}) collective-permute-start(bf16[400,768]{1,0:T(8,128)(2,1)S(1)} %collective-permute-done.3.n2), channel_id=1, source_target_pairs={{0,8},{8,0},{1,9},{9,1},{2,10},{10,2},{3,11},{11,3},{4,12},{12,4},... | collective-permute-start | bytes 1843208 | tf_op jit(solution)/shard_map/ppermute | solution.py:275
  57.5 1.2 collective-permute-done.5.n5
  58.7 1.9 %collective-permute-start.9 = (bf16[400,768]{1,0:T(8,128)(2,1)S(1)}, bf16[400,768]{1,0:T(8,128)(2,1)S(1)}, u32[]{:S(2)}, u32[]{:S(2)}) collective-permute-start(bf16[400,768]{1,0:T(8,128)(2,1)S(1)} %collective-permute-done.5.n5), channel_id=1, source_target_pairs={{0,8},{8,0},{1,9},{9,1},{2,10},{10,2},{3,11},{11,3},{4,12},{12,4},... | collective-permute-start | bytes 1843208 | tf_op jit(solution)/shard_map/ppermute | solution.py:275
  60.6 0.0 collective-permute-done.6.anti_w
  60.7 0.0 collective-permute-done.7.m2
  60.7 2.0 %collective-permute-done.9.m5 = bf16[400,768]{1,0:T(8,128)(2,1)S(1)} collective-permute-done((bf16[400,768]{1,0:T(8,128)(2,1)S(1)}, bf16[400,768]{1,0:T(8,128)(2,1)S(1)}, u32[]{:S(2)}, u32[]{:S(2)}) %collective-permute-start.9) | collective-permute-done | bytes 614432 | tf_op jit(solution)/shard_map/ppermute | solution.py:275
  62.6 0.0 collective-permute-done.8.far_w
  62.6 0.0 copy-done
  62.7 0.0 copy-done.1
  62.7 13.6 %model.1 = bf16[8,104,768]{2,1,0:T(8,128)(2,1)S(1)} custom-call(bf16[144,768]{1,0:T(8,128)(2,1)S(1)} %copy-done.1, bf16[784,768]{1,0:T(8,128)(2,1)S(1)} %copy-done, bf16[784,768]{1,0:T(8,128)(2,1)S(1)} %collective-permute-done.near_w, bf16[784,768]{1,0:T(8,128)(2,1)} %collective-permute-done.1.flip_w, bf16[400,768]{1,0:T(8,128)(2,1)S(1)} %collective-permute-done.3.n2, ...), custom_call_target="tpu_custom_call" | custom-call | tf_op jit(solution)/shard_map/model/pallas_call | solution.py:303
  76.3 21.7 %all_to_all.15.recv_ref = bf16[8,104,768]{2,1,0:T(8,128)(2,1)S(1)} all-to-all(bf16[8,104,768]{2,1,0:T(8,128)(2,1)S(1)} %model.1), channel_id=1, replica_groups=mesh['y'=8,'zh'=4,'c'=2,'x'=4,'zl'=2] {'x','zl'}, dimensions={0} | all-to-all | bytes 2555904 | tf_op jit(solution)/shard_map/all_to_all | solution.py:326
  98.0 0.6 grad.1
  98.6 28.9 %all_to_all.16.parts_ref = bf16[32,80,128]{2,1,0:T(8,128)(2,1)S(1)} all-to-all(bf16[32,80,128]{2,1,0:T(8,128)(2,1)S(1)} %grad.1), channel_id=1, replica_groups=mesh['y'=8,'zh'=4,'c'=2,'x'=4,'zl'=2] {'y','zh'}, dimensions={0} | all-to-all | bytes 1310720 | tf_op jit(solution)/shard_map/all_to_all | solution.py:343
  127.5 0.1 total.1
  127.6 26.4 %all_to_all.17.mine_ref = bf16[32,80,128]{2,1,0:T(8,128)(2,1)S(1)} all-to-all(bf16[32,80,128]{2,1,0:T(8,128)(2,1)S(1)} %total.1), channel_id=1, replica_groups=mesh['y'=8,'zh'=4,'c'=2,'x'=4,'zl'=2] {'y','zh'}, dimensions={0} | all-to-all | bytes 1310720 | tf_op jit(solution)/shard_map/all_to_all | solution.py:355
  154.0 6.4 %collective-permute-start.10 = (bf16[32,80,128]{2,1,0:T(8,128)(2,1)S(1)}, bf16[32,80,128]{2,1,0:T(8,128)(2,1)S(1)}, u32[]{:S(2)}, u32[]{:S(2)}) collective-permute-start(bf16[32,80,128]{2,1,0:T(8,128)(2,1)S(1)} %all_to_all.17.mine_ref), channel_id=1, source_target_pairs={{0,8},{8,0},{1,9},{9,1},{2,10},{10,2},{3,11},{11,3},{4,12},{12,4},... | collective-permute-start | bytes 1966088 | tf_op jit(solution)/shard_map/ppermute | solution.py:275
  160.5 1.7 %collective-permute-done.10.theirs_ref = bf16[32,80,128]{2,1,0:T(8,128)(2,1)S(1)} collective-permute-done((bf16[32,80,128]{2,1,0:T(8,128)(2,1)S(1)}, bf16[32,80,128]{2,1,0:T(8,128)(2,1)S(1)}, u32[]{:S(2)}, u32[]{:S(2)}) %collective-permute-start.10) | collective-permute-done | bytes 655392 | tf_op jit(solution)/shard_map/ppermute | solution.py:275
  162.2 1.2 place.1
  (1 shorter events, 0.0 us)
Async XLA Ops:
  3.9 24.8 %collective-permute-start.1 = (bf16[784,768]{1,0:T(8,128)(2,1)}, bf16[784,768]{1,0:T(8,128)(2,1)}, u32[]{:S(2)}, u32[]{:S(2)}) collective-permute-start(bf16[784,768]{1,0:T(8,128)(2,1)} %get-tuple-element.9.own_w), channel_id=1, source_target_pairs={{0,1},{1,0},{8,57},{9,24},{16,17},{17,16},{24,9},{25,40},{32,33},{... | collective-permute-start | bytes 3612680 | tf_op jit(solution)/shard_map/ppermute | solution.py:272
  14.6 18.1 %collective-permute-start = (bf16[784,768]{1,0:T(8,128)(2,1)}, bf16[784,768]{1,0:T(8,128)(2,1)S(1)}, u32[]{:S(2)}, u32[]{:S(2)}) collective-permute-start(bf16[784,768]{1,0:T(8,128)(2,1)} %get-tuple-element.9.own_w), channel_id=1, source_target_pairs={{0,2},{2,4},{4,6},{6,0},{8,14},{10,8},{12,10},{14,12},{1,3},{3,5},... | collective-permute-start | bytes 3612680 | tf_op jit(solution)/shard_map/ppermute | solution.py:269
  19.0 43.7 %copy-start = (bf16[784,768]{1,0:T(8,128)(2,1)S(1)}, bf16[784,768]{1,0:T(8,128)(2,1)}, u32[]{:S(2)}) copy-start(bf16[784,768]{1,0:T(8,128)(2,1)} %get-tuple-element.9.own_w) | copy-start | bytes 3612676
  19.0 3.7 %collective-permute-start.2 = (bf16[80,1280]{1,0:T(8,128)(2,1)}, bf16[80,1280]{1,0:T(8,128)(2,1)S(1)}, u32[]{:S(2)}, u32[]{:S(2)}) collective-permute-start(bf16[80,1280]{1,0:T(8,128)(2,1)} %get-tuple-element.10.io_a_ref), channel_id=1, source_target_pairs={{0,8},{8,0},{1,9},{9,1},{2,10},{10,2},{3,11},{11,3},{4,12},{12,4},... | collective-permute-start | bytes 614408 | tf_op jit(solution)/shard_map/ppermute | solution.py:275
  22.7 0.7 copy-start.2
  25.6 37.0 %copy-start.1 = (bf16[144,768]{1,0:T(8,128)(2,1)S(1)}, bf16[144,768]{1,0:T(8,128)(2,1)}, u32[]{:S(2)}) copy-start(bf16[144,768]{1,0:T(8,128)(2,1)} %front.1.start_ref) | copy-start | bytes 663556
  32.7 20.5 %collective-permute-start.4 = (bf16[784,768]{1,0:T(8,128)(2,1)S(1)}, bf16[784,768]{1,0:T(8,128)(2,1)S(1)}, u32[]{:S(2)}, u32[]{:S(2)}) collective-permute-start(bf16[784,768]{1,0:T(8,128)(2,1)S(1)} %collective-permute-done.near_w), channel_id=1, source_target_pairs={{0,1},{1,0},{8,57},{9,24},{16,17},{17,16},{24,9},{25,40},{32,33},{... | collective-permute-start | bytes 3612680 | tf_op jit(solution)/shard_map/ppermute | solution.py:272
  34.6 12.0 %collective-permute-start.3 = (bf16[400,768]{1,0:T(8,128)(2,1)S(1)}, bf16[400,768]{1,0:T(8,128)(2,1)S(1)}, u32[]{:S(2)}, u32[]{:S(2)}) collective-permute-start(bf16[400,768]{1,0:T(8,128)(2,1)S(1)} %slice.3), channel_id=1, source_target_pairs={{0,2},{2,4},{4,6},{6,0},{8,14},{10,8},{12,10},{14,12},{1,3},{3,5},... | collective-permute-start | bytes 1843208 | tf_op jit(solution)/shard_map/ppermute | solution.py:269
  46.6 12.1 %collective-permute-start.5 = (bf16[400,768]{1,0:T(8,128)(2,1)S(1)}, bf16[400,768]{1,0:T(8,128)(2,1)S(1)}, u32[]{:S(2)}, u32[]{:S(2)}) collective-permute-start(bf16[400,768]{1,0:T(8,128)(2,1)S(1)} %collective-permute-done.3.n2), channel_id=1, source_target_pairs={{0,1},{1,0},{8,57},{9,24},{16,17},{17,16},{24,9},{25,40},{32,33},{... | collective-permute-start | bytes 1843208 | tf_op jit(solution)/shard_map/ppermute | solution.py:272
  51.2 9.4 %collective-permute-start.6 = (bf16[784,768]{1,0:T(8,128)(2,1)S(1)}, bf16[784,768]{1,0:T(8,128)(2,1)S(1)}, u32[]{:S(2)}, u32[]{:S(2)}) collective-permute-start(bf16[784,768]{1,0:T(8,128)(2,1)S(1)} %collective-permute-done.near_w), channel_id=1, source_target_pairs={{0,8},{8,0},{1,9},{9,1},{2,10},{10,2},{3,11},{11,3},{4,12},{12,4},... | collective-permute-start | bytes 3612680 | tf_op jit(solution)/shard_map/ppermute | solution.py:275
  53.1 9.5 %collective-permute-start.8 = (bf16[784,768]{1,0:T(8,128)(2,1)S(1)}, bf16[784,768]{1,0:T(8,128)(2,1)S(1)}, u32[]{:S(2)}, u32[]{:S(2)}) collective-permute-start(bf16[784,768]{1,0:T(8,128)(2,1)S(1)} %collective-permute-done.4.slant_w), channel_id=1, source_target_pairs={{0,8},{8,0},{1,9},{9,1},{2,10},{10,2},{3,11},{11,3},{4,12},{12,4},... | collective-permute-start | bytes 3612680 | tf_op jit(solution)/shard_map/ppermute | solution.py:275
  55.6 5.1 %collective-permute-start.7 = (bf16[400,768]{1,0:T(8,128)(2,1)S(1)}, bf16[400,768]{1,0:T(8,128)(2,1)S(1)}, u32[]{:S(2)}, u32[]{:S(2)}) collective-permute-start(bf16[400,768]{1,0:T(8,128)(2,1)S(1)} %collective-permute-done.3.n2), channel_id=1, source_target_pairs={{0,8},{8,0},{1,9},{9,1},{2,10},{10,2},{3,11},{11,3},{4,12},{12,4},... | collective-permute-start | bytes 1843208 | tf_op jit(solution)/shard_map/ppermute | solution.py:275
  58.7 3.9 %collective-permute-start.9 = (bf16[400,768]{1,0:T(8,128)(2,1)S(1)}, bf16[400,768]{1,0:T(8,128)(2,1)S(1)}, u32[]{:S(2)}, u32[]{:S(2)}) collective-permute-start(bf16[400,768]{1,0:T(8,128)(2,1)S(1)} %collective-permute-done.5.n5), channel_id=1, source_target_pairs={{0,8},{8,0},{1,9},{9,1},{2,10},{10,2},{3,11},{11,3},{4,12},{12,4},... | collective-permute-start | bytes 1843208 | tf_op jit(solution)/shard_map/ppermute | solution.py:275
  154.0 8.1 %collective-permute-start.10 = (bf16[32,80,128]{2,1,0:T(8,128)(2,1)S(1)}, bf16[32,80,128]{2,1,0:T(8,128)(2,1)S(1)}, u32[]{:S(2)}, u32[]{:S(2)}) collective-permute-start(bf16[32,80,128]{2,1,0:T(8,128)(2,1)S(1)} %all_to_all.17.mine_ref), channel_id=1, source_target_pairs={{0,8},{8,0},{1,9},{9,1},{2,10},{10,2},{3,11},{11,3},{4,12},{12,4},... | collective-permute-start | bytes 1966088 | tf_op jit(solution)/shard_map/ppermute | solution.py:275

commit v5 on v4

--- a/solution.py
+++ b/solution.py
@@ -18,7 +18,8 @@
 T = 64
 L = 8
 TAPS = 16
-PIECE = H + TAPS
+NEAR = H + TAPS
+FAR = H + 2 * TAPS
 INROWS = T + 16
 HT = T // 2
 PAY = T + HT + 8
@@ -50,16 +51,14 @@
     return section, lax.axis_index("c")
 
 
-def prep_kernel(
-    w_ref, taps_ref, feat_ref, targ_ref, len_ref, both_ref, io_ref, sem
-):
+def prep_kernel(w_ref, taps_ref, feat_ref, targ_ref, len_ref, near_ref, far_ref, io_ref, sem):
     section, core = where_am_i()
     utt = lax.rem(section, 4)
     mine = pl.multiple_of(core * H, H)
     theirs = pl.multiple_of((1 - core) * H, H)
     copies = [
-        pltpu.make_async_copy(w_ref.at[0, pl.ds(mine, H)], both_ref.at[pl.ds(0, H)], sem.at[0]),
-        pltpu.make_async_copy(w_ref.at[0, pl.ds(theirs, H)], both_ref.at[pl.ds(PIECE, H)], sem.at[1]),
+        pltpu.make_async_copy(w_ref.at[0, pl.ds(mine, H)], near_ref.at[pl.ds(0, H)], sem.at[0]),
+        pltpu.make_async_copy(w_ref.at[0, pl.ds(theirs, H)], far_ref.at[pl.ds(0, H)], sem.at[1]),
         pltpu.make_async_copy(
             feat_ref.at[utt], io_ref.at[pl.ds(0, T), pl.ds(0, FEAT)], sem.at[2]),
         pltpu.make_async_copy(
@@ -69,8 +68,10 @@
         copy.start()
     taps = jnp.concatenate([taps_ref[k] for k in range(KER)], axis=0)
     hi, mid, low = split3(taps)
-    packed = jnp.concatenate([hi, mid, low, jnp.zeros((1, D), F32)], axis=0)
-    both_ref[H:PIECE, :] = packed.astype(BF)
+    packed = jnp.concatenate([hi, mid, low, jnp.zeros((1, D), F32)], axis=0).astype(BF)
+    near_ref[H:, :] = packed
+    far_ref[H:NEAR, :] = packed
+    far_ref[NEAR:, :] = packed
     count = len_ref[utt].astype(F32)
     io_ref[T:, :] = jnp.full((INROWS - T, FEAT + D), count, F32).astype(BF)
     for copy in copies:
@@ -93,7 +94,7 @@
 
 def model_kernel(
     start_ref,
-    own_w, near_w, flip_w, n2, slant_w, n5, anti_w, m2, far_w, m5,
+    n0, f0, n1, f1, n2, n3, n4, f4, n5, m1, g1, m2, m3, m4, g4, m5,
     pay_ref,
     w_ref, traw_ref, taps_ref, vals_ref, inv_ref, norm_ref, slope_ref, act_ref, gpad_ref, g_ref,
     wsem, tsem,
@@ -107,24 +108,24 @@
     across = lax.rem(col + 2, 4)
     flip = 1 - row
 
-    def bring(piece, first, c, r, part, with_taps):
+    def bring(piece, c, r, part, with_taps):
         layer = 2 * c + r
         start = pl.multiple_of(part * H, H)
         pltpu.make_async_copy(
-            piece.at[pl.ds(first, H)], w_ref.at[layer, pl.ds(start, H)], wsem.at[layer]).start()
+            piece.at[pl.ds(0, H)], w_ref.at[layer, pl.ds(start, H)], wsem.at[layer]).start()
         if with_taps:
             pltpu.make_async_copy(
                 piece.at[pl.ds(H, TAPS)], traw_ref.at[layer], tsem.at[layer]).start()
 
-    for piece, c, r, part in (
-        (own_w, col, row, core), (near_w, side, row, core), (flip_w, col, flip, core),
-        (slant_w, side, flip, core), (anti_w, anti, row, other), (far_w, anti, flip, other),
+    for near, far, c, r, part in (
+        (n0, f0, col, row, core), (n1, f1, side, row, core), (n4, f4, side, flip, core),
+        (m1, g1, anti, row, other), (m4, g4, anti, flip, other),
     ):
-        bring(piece, 0, c, r, part, True)
-        bring(piece, PIECE, c, r, 1 - part, False)
-    for piece, mirror, r in ((n2, m2, row), (n5, m5, flip)):
-        bring(piece, 0, across, r, core, True)
-        bring(mirror, 0, across, r, other, False)
+        bring(near, c, r, part, False)
+        bring(far, c, r, 1 - part, True)
+    for near, mirror, c, r in ((n2, m2, across, row), (n3, m3, col, flip), (n5, m5, across, flip)):
+        bring(near, c, r, core, True)
+        bring(mirror, c, r, other, False)
 
     count = start_ref[2 * T:, :].astype(F32)[0:1, 0:1]
     target = start_ref[T:2 * T, :].astype(F32)
@@ -161,7 +162,7 @@
         g_ref[...] = out.astype(BF).astype(F32)
         return carry
 
-    lax.fori_loop(0, L, forward, 0)
+    lax.fori_loop(0, L, forward, 0, unroll=True)
 
     g_ref[...] = ((g_ref[...] - target) * mask / count).astype(BF).astype(F32)
 
@@ -196,7 +197,7 @@
         g_ref[...] = (g + (inv * grad_norm - vals * (inv * inv * inv * mean))).astype(BF).astype(F32)
         return carry
 
-    lax.fori_loop(0, L, backward, 0)
+    lax.fori_loop(0, L, backward, 0, unroll=True)
 
 
 def grad_kernel(recv_ref, out_ref, act_ref, flat_ref, row_ref, chunk_ref):
@@ -274,18 +275,18 @@
     def to_core(a):
         return lax.ppermute(a, "c", [(0, 1), (1, 0)])
 
-    both, io = pl.pallas_call(
+    near, far, io = pl.pallas_call(
         prep_kernel,
         name="prep",
         out_shape=(
-            jax.ShapeDtypeStruct((PIECE + H, D), BF),
+            jax.ShapeDtypeStruct((NEAR, D), BF),
+            jax.ShapeDtypeStruct((FAR, D), BF),
             jax.ShapeDtypeStruct((INROWS, FEAT + D), BF),
         ),
         in_specs=[ANY, VMEM, ANY, ANY, SMEM],
-        out_specs=(VMEM, VMEM),
+        out_specs=(VMEM, VMEM, VMEM),
         scratch_shapes=[pltpu.SemaphoreType.DMA((4,))],
     )(pointwise, jnp.transpose(kernel, (1, 0, 2)), features, targets, lengths)
-
     begin = pl.pallas_call(
         front_kernel,
         name="front",
@@ -293,18 +294,23 @@
         in_specs=[VMEM, VMEM, VMEM],
         out_specs=VMEM,
     )(io, to_core(io), front_weight)
-    beside, flipped, begin = lax.optimization_barrier((along_x(both), along_z(both), begin))
-    n2 = along_x(beside[:PIECE])
-    slant = along_z(beside)
+
+    n1, n3, begin = lax.optimization_barrier((along_x(near), along_z(near), begin))
+    f1 = along_x(far)
+    n2 = along_x(n1)
+    n4 = along_z(n1)
+    f4 = along_z(f1)
+    m1, m3 = to_core(n1[:H]), to_core(n3[:H])
+    n2, n4, m1, m3 = lax.optimization_barrier((n2, n4, m1, m3))
     n5 = along_z(n2)
-    here = [both, beside, flipped, n2, slant, n5]
-    there = [to_core(a) for a in (beside, n2, slant, n5)]
+    here = [near, far, n1, f1, n2, n3, n4, f4, n5]
+    there = [m1, to_core(f1), to_core(n2), m3, to_core(n4), to_core(f4), to_core(n5)]
 
     payload = pl.pallas_call(
         model_kernel,
         name="model",
         out_shape=jax.ShapeDtypeStruct((L, PAY, D), BF),
-        in_specs=[VMEM] + [ANY] * 10,
+        in_specs=[VMEM] + [ANY] * 16,
         out_specs=VMEM,
         scratch_shapes=[
             pltpu.VMEM((L, D, D), BF),

time: 164 us -> 159 us (0.970)
  waiting for transfers between devices: 20.7 us -> 6.38 us
  starting transfers between devices: 43.1 us -> 55.2 us
  blocking collectives: 77.1 us -> 74.9 us
    ppermute x2 -> x3, waiting for transfers between devices: 11 us -> 0.01 us  [along_x(): return lax.ppermute(a, ('c', 'x'), ring)]
    ppermute x6 -> x9, starting transfers between devices: 16.6 us -> 23.7 us  [to_core(): return lax.ppermute(a, 'c', [(0, 1), (1, 0)])]
    ppermute x3 -> x4, starting transfers between devices: 17.1 us -> 21 us  [along_z(): return lax.ppermute(a, ('zh', 'c', 'zl'), pair)]
    ppermute x6 -> x9, waiting for transfers between devices: 5.32 us -> 3.5 us  [to_core(): return lax.ppermute(a, 'c', [(0, 1), (1, 0)])]
    ppermute x3 -> x4, waiting for transfers between devices: 4.34 us -> 2.87 us  [along_z(): return lax.ppermute(a, ('zh', 'c', 'zl'), pair)]
    ppermute x2 -> x3, starting transfers between devices: 9.31 us -> 10.5 us  [along_x(): return lax.ppermute(a, ('c', 'x'), ring)]
  transfers between devices with their start and end apart: 11 -> 16, of which waited for: 7 -> 4; matrix products, arithmetic and copies ran while one was open for 0% -> 0% of each run, Pallas kernels for 1% -> 1%
where the time goes in v5:
time: 159 us
  blocking collectives  74.9 us (47%)
  starting transfers between devices  55.2 us (35%)
  Pallas kernels  20.4 us (13%)
  waiting for transfers between devices  6.38 us (4%)
    all_to_all x1, blocking collectives, body(): scattered = lax.all_to_all(parts, ('y', 'zh'), 0, 0)  27.6 us
    all_to_all x1, blocking collectives, body(): half = lax.all_to_all(mine, ('y', 'zh'), 0, 0)  26.3 us
    ppermute x9, starting transfers between devices, to_core(): return lax.ppermute(a, 'c', [(0, 1), (1, 0)])  23.7 us
    all_to_all x1, blocking collectives, body(): received = lax.all_to_all(payload, ('x', 'zl'), 0, 0)  21 us
    ppermute x4, starting transfers between devices, along_z(): return lax.ppermute(a, ('zh', 'c', 'zl'), pair)  21 us
    pallas_call x1, Pallas kernels, body(): pl.pallas_call(model_kernel, name='model', out_shape=jax.ShapeDtypeStruct...  13 us
    ppermute x3, starting transfers between devices, along_x(): return lax.ppermute(a, ('c', 'x'), ring)  10.5 us
    ppermute x9, waiting for transfers between devices, to_core(): return lax.ppermute(a, 'c', [(0, 1), (1, 0)])  3.5 us
  transfers between devices with their start and end apart: 16, of which 4 were waited for; matrix products, arithmetic and copies ran while one was open for 0% of the time, Pallas kernels for 1%

profile of v5, /device:TPU:9, one launch (start us, length us, event | category | flops | bytes accessed | tf_op | source)
XLA Modules:
  0.0 158.5 jit_solution(17439385051849084088)
XLA Ops:
  0.6 3.2 %prep.1 = (bf16[400,768]{1,0:T(8,128)(2,1)}, bf16[416,768]{1,0:T(8,128)(2,1)}, bf16[80,1280]{1,0:T(8,128)(2,1)}) custom-call(bf16[1,768,768]{2,1,0:T(8,128)(2,1)} %w_ref.1, f32[5,1,768]{2,1,0:T(1,128)} %bitcast.2, bf16[4,64,512]{2,1,0:T(8,128)(2,1)} %feat_ref.1, bf16[4,64,768]{2,1,0:T(8,128)(2,1)} %targ_ref.1, s32[4]{0:T(128)} %len_ref.1), custom_call_target="tpu_custom_call" | custom-call | tf_op jit(solution)/shard_map/prep/pallas_call | solution.py:278
  3.9 10.7 %collective-permute-start.1 = (bf16[400,768]{1,0:T(8,128)(2,1)}, bf16[400,768]{1,0:T(8,128)(2,1)S(1)}, u32[]{:S(2)}, u32[]{:S(2)}) collective-permute-start(bf16[400,768]{1,0:T(8,128)(2,1)} %get-tuple-element.14.n0), channel_id=1, source_target_pairs={{0,1},{1,0},{8,57},{9,24},{16,17},{17,16},{24,9},{25,40},{32,33},{... | collective-permute-start | bytes 1843208 | tf_op jit(solution)/shard_map/ppermute | solution.py:273
  14.5 4.4 %collective-permute-start = (bf16[400,768]{1,0:T(8,128)(2,1)}, bf16[400,768]{1,0:T(8,128)(2,1)S(1)}, u32[]{:S(2)}, u32[]{:S(2)}) collective-permute-start(bf16[400,768]{1,0:T(8,128)(2,1)} %get-tuple-element.14.n0), channel_id=1, source_target_pairs={{0,2},{2,4},{4,6},{6,0},{8,14},{10,8},{12,10},{14,12},{1,3},{3,5},... | collective-permute-start | bytes 1843208 | tf_op jit(solution)/shard_map/ppermute | solution.py:270
  18.9 1.9 %collective-permute-start.2 = (bf16[80,1280]{1,0:T(8,128)(2,1)}, bf16[80,1280]{1,0:T(8,128)(2,1)S(1)}, u32[]{:S(2)}, u32[]{:S(2)}) collective-permute-start(bf16[80,1280]{1,0:T(8,128)(2,1)} %get-tuple-element.15.io_a_ref), channel_id=1, source_target_pairs={{0,8},{8,0},{1,9},{9,1},{2,10},{10,2},{3,11},{11,3},{4,12},{12,4},... | collective-permute-start | bytes 614408 | tf_op jit(solution)/shard_map/ppermute | solution.py:276
  20.9 2.5 %collective-permute-start.3 = (bf16[416,768]{1,0:T(8,128)(2,1)}, bf16[416,768]{1,0:T(8,128)(2,1)S(1)}, u32[]{:S(2)}, u32[]{:S(2)}) collective-permute-start(bf16[416,768]{1,0:T(8,128)(2,1)} %get-tuple-element.17.f0), channel_id=1, source_target_pairs={{0,2},{2,4},{4,6},{6,0},{8,14},{10,8},{12,10},{14,12},{1,3},{3,5},... | collective-permute-start | bytes 1916936 | tf_op jit(solution)/shard_map/ppermute | solution.py:270
  23.3 0.0 collective-permute-done.2.io_b_ref
  23.3 0.0 copy-start.3
  23.3 0.7 copy-done.3
  24.0 2.3 %front.1.start_ref = bf16[144,768]{1,0:T(8,128)(2,1)} custom-call(bf16[80,1280]{1,0:T(8,128)(2,1)} %get-tuple-element.15.io_a_ref, bf16[80,1280]{1,0:T(8,128)(2,1)} %copy-done.3, bf16[512,768]{1,0:T(8,128)(2,1)} %front_ref.1), custom_call_target="tpu_custom_call" | custom-call | tf_op jit(solution)/shard_map/front/pallas_call | solution.py:290
  26.3 0.0 copy-start
  26.3 0.0 copy-start.1
  26.3 0.0 copy-start.2
  26.3 0.0 collective-permute-done.1.n3
  26.3 0.0 collective-permute-done.n1
  26.3 3.2 %collective-permute-start.5 = (bf16[400,768]{1,0:T(8,128)(2,1)S(1)}, bf16[400,768]{1,0:T(8,128)(2,1)S(1)}, u32[]{:S(2)}, u32[]{:S(2)}) collective-permute-start(bf16[400,768]{1,0:T(8,128)(2,1)S(1)} %collective-permute-done.n1), channel_id=1, source_target_pairs={{0,1},{1,0},{8,57},{9,24},{16,17},{17,16},{24,9},{25,40},{32,33},{... | collective-permute-start | bytes 1843208 | tf_op jit(solution)/shard_map/ppermute | solution.py:273
  29.5 3.6 %collective-permute-start.4 = (bf16[400,768]{1,0:T(8,128)(2,1)S(1)}, bf16[400,768]{1,0:T(8,128)(2,1)S(1)}, u32[]{:S(2)}, u32[]{:S(2)}) collective-permute-start(bf16[400,768]{1,0:T(8,128)(2,1)S(1)} %collective-permute-done.n1), channel_id=1, source_target_pairs={{0,2},{2,4},{4,6},{6,0},{8,14},{10,8},{12,10},{14,12},{1,3},{3,5},... | collective-permute-start | bytes 1843208 | tf_op jit(solution)/shard_map/ppermute | solution.py:270
  33.2 1.9 %collective-permute-start.6 = (bf16[384,768]{1,0:T(8,128)(2,1)S(1)}, bf16[384,768]{1,0:T(8,128)(2,1)S(1)}, u32[]{:S(2)}, u32[]{:S(2)}) collective-permute-start(bf16[384,768]{1,0:T(8,128)(2,1)S(1)} %slice.6), channel_id=1, source_target_pairs={{0,8},{8,0},{1,9},{9,1},{2,10},{10,2},{3,11},{11,3},{4,12},{12,4},... | collective-permute-start | bytes 1769480 | tf_op jit(solution)/shard_map/ppermute | solution.py:276
  35.2 2.4 %collective-permute-start.7 = (bf16[384,768]{1,0:T(8,128)(2,1)S(1)}, bf16[384,768]{1,0:T(8,128)(2,1)S(1)}, u32[]{:S(2)}, u32[]{:S(2)}) collective-permute-start(bf16[384,768]{1,0:T(8,128)(2,1)S(1)} %slice.7), channel_id=1, source_target_pairs={{0,8},{8,0},{1,9},{9,1},{2,10},{10,2},{3,11},{11,3},{4,12},{12,4},... | collective-permute-start | bytes 1769480 | tf_op jit(solution)/shard_map/ppermute | solution.py:276
  37.6 0.0 collective-permute-done.3.f1
  37.6 4.6 %collective-permute-start.8 = (bf16[416,768]{1,0:T(8,128)(2,1)S(1)}, bf16[416,768]{1,0:T(8,128)(2,1)S(1)}, u32[]{:S(2)}, u32[]{:S(2)}) collective-permute-start(bf16[416,768]{1,0:T(8,128)(2,1)S(1)} %collective-permute-done.3.f1), channel_id=1, source_target_pairs={{0,1},{1,0},{8,57},{9,24},{16,17},{17,16},{24,9},{25,40},{32,33},{... | collective-permute-start | bytes 1916936 | tf_op jit(solution)/shard_map/ppermute | solution.py:273
  42.2 0.0 collective-permute-done.6.m1
  42.2 0.0 collective-permute-done.7.m3
  42.2 0.0 collective-permute-done.5.n4
  42.2 0.0 collective-permute-done.4.n2
  42.2 2.6 %collective-permute-start.9 = (bf16[400,768]{1,0:T(8,128)(2,1)S(1)}, bf16[400,768]{1,0:T(8,128)(2,1)S(1)}, u32[]{:S(2)}, u32[]{:S(2)}) collective-permute-start(bf16[400,768]{1,0:T(8,128)(2,1)S(1)} %collective-permute-done.4.n2), channel_id=1, source_target_pairs={{0,1},{1,0},{8,57},{9,24},{16,17},{17,16},{24,9},{25,40},{32,33},{... | collective-permute-start | bytes 1843208 | tf_op jit(solution)/shard_map/ppermute | solution.py:273
  44.8 2.6 %collective-permute-start.10 = (bf16[416,768]{1,0:T(8,128)(2,1)S(1)}, bf16[416,768]{1,0:T(8,128)(2,1)S(1)}, u32[]{:S(2)}, u32[]{:S(2)}) collective-permute-start(bf16[416,768]{1,0:T(8,128)(2,1)S(1)} %collective-permute-done.3.f1), channel_id=1, source_target_pairs={{0,8},{8,0},{1,9},{9,1},{2,10},{10,2},{3,11},{11,3},{4,12},{12,4},... | collective-permute-start | bytes 1916936 | tf_op jit(solution)/shard_map/ppermute | solution.py:276
  47.4 2.5 %collective-permute-done.8.f4 = bf16[416,768]{1,0:T(8,128)(2,1)S(1)} collective-permute-done((bf16[416,768]{1,0:T(8,128)(2,1)S(1)}, bf16[416,768]{1,0:T(8,128)(2,1)S(1)}, u32[]{:S(2)}, u32[]{:S(2)}) %collective-permute-start.8) | collective-permute-done | bytes 639008 | tf_op jit(solution)/shard_map/ppermute | solution.py:273
  50.0 1.9 %collective-permute-start.13 = (bf16[416,768]{1,0:T(8,128)(2,1)S(1)}, bf16[416,768]{1,0:T(8,128)(2,1)S(1)}, u32[]{:S(2)}, u32[]{:S(2)}) collective-permute-start(bf16[416,768]{1,0:T(8,128)(2,1)S(1)} %collective-permute-done.8.f4), channel_id=1, source_target_pairs={{0,8},{8,0},{1,9},{9,1},{2,10},{10,2},{3,11},{11,3},{4,12},{12,4},... | collective-permute-start | bytes 1916936 | tf_op jit(solution)/shard_map/ppermute | solution.py:276
  51.9 2.4 %collective-permute-start.12 = (bf16[400,768]{1,0:T(8,128)(2,1)S(1)}, bf16[400,768]{1,0:T(8,128)(2,1)S(1)}, u32[]{:S(2)}, u32[]{:S(2)}) collective-permute-start(bf16[400,768]{1,0:T(8,128)(2,1)S(1)} %collective-permute-done.5.n4), channel_id=1, source_target_pairs={{0,8},{8,0},{1,9},{9,1},{2,10},{10,2},{3,11},{11,3},{4,12},{12,4},... | collective-permute-start | bytes 1843208 | tf_op jit(solution)/shard_map/ppermute | solution.py:276
  54.3 1.9 %collective-permute-start.11 = (bf16[400,768]{1,0:T(8,128)(2,1)S(1)}, bf16[400,768]{1,0:T(8,128)(2,1)S(1)}, u32[]{:S(2)}, u32[]{:S(2)}) collective-permute-start(bf16[400,768]{1,0:T(8,128)(2,1)S(1)} %collective-permute-done.4.n2), channel_id=1, source_target_pairs={{0,8},{8,0},{1,9},{9,1},{2,10},{10,2},{3,11},{11,3},{4,12},{12,4},... | collective-permute-start | bytes 1843208 | tf_op jit(solution)/shard_map/ppermute | solution.py:276
  56.2 0.3 collective-permute-done.9.n5
  56.5 2.1 %collective-permute-start.14 = (bf16[400,768]{1,0:T(8,128)(2,1)S(1)}, bf16[400,768]{1,0:T(8,128)(2,1)S(1)}, u32[]{:S(2)}, u32[]{:S(2)}) collective-permute-start(bf16[400,768]{1,0:T(8,128)(2,1)S(1)} %collective-permute-done.9.n5), channel_id=1, source_target_pairs={{0,8},{8,0},{1,9},{9,1},{2,10},{10,2},{3,11},{11,3},{4,12},{12,4},... | collective-permute-start | bytes 1843208 | tf_op jit(solution)/shard_map/ppermute | solution.py:276
  58.7 0.0 collective-permute-done.10.g1
  58.7 0.0 collective-permute-done.12.m4
  58.7 0.0 collective-permute-done.11.m2
  58.7 0.0 collective-permute-done.13.g4
  58.7 1.8 %collective-permute-done.14.m5 = bf16[400,768]{1,0:T(8,128)(2,1)S(1)} collective-permute-done((bf16[400,768]{1,0:T(8,128)(2,1)S(1)}, bf16[400,768]{1,0:T(8,128)(2,1)S(1)}, u32[]{:S(2)}, u32[]{:S(2)}) %collective-permute-start.14) | collective-permute-done | bytes 614432 | tf_op jit(solution)/shard_map/ppermute | solution.py:276
  60.5 0.0 copy-done
  60.5 0.0 copy-done.1
  60.5 0.0 copy-done.2
  60.5 13.0 %model.1 = bf16[8,104,768]{2,1,0:T(8,128)(2,1)S(1)} custom-call(bf16[144,768]{1,0:T(8,128)(2,1)S(1)} %copy-done, bf16[400,768]{1,0:T(8,128)(2,1)S(1)} %copy-done.2, bf16[416,768]{1,0:T(8,128)(2,1)S(1)} %copy-done.1, bf16[400,768]{1,0:T(8,128)(2,1)S(1)} %collective-permute-done.n1, bf16[416,768]{1,0:T(8,128)(2,1)S(1)} %collective-permute-done.3.f1, ...), custom_call_target="tpu_custom_call" | custom-call | tf_op jit(solution)/shard_map/model/pallas_call | solution.py:309
  73.5 21.0 %all_to_all.15.recv_ref = bf16[8,104,768]{2,1,0:T(8,128)(2,1)S(1)} all-to-all(bf16[8,104,768]{2,1,0:T(8,128)(2,1)S(1)} %model.1), channel_id=1, replica_groups=mesh['y'=8,'zh'=4,'c'=2,'x'=4,'zl'=2] {'x','zl'}, dimensions={0} | all-to-all | bytes 2555904 | tf_op jit(solution)/shard_map/all_to_all | solution.py:332
  94.5 0.6 grad.1
  95.1 27.6 %all_to_all.16.parts_ref = bf16[32,80,128]{2,1,0:T(8,128)(2,1)S(1)} all-to-all(bf16[32,80,128]{2,1,0:T(8,128)(2,1)S(1)} %grad.1), channel_id=1, replica_groups=mesh['y'=8,'zh'=4,'c'=2,'x'=4,'zl'=2] {'y','zh'}, dimensions={0} | all-to-all | bytes 1310720 | tf_op jit(solution)/shard_map/all_to_all | solution.py:349
  122.7 0.1 total.1
  122.8 26.3 %all_to_all.17.mine_ref = bf16[32,80,128]{2,1,0:T(8,128)(2,1)S(1)} all-to-all(bf16[32,80,128]{2,1,0:T(8,128)(2,1)S(1)} %total.1), channel_id=1, replica_groups=mesh['y'=8,'zh'=4,'c'=2,'x'=4,'zl'=2] {'y','zh'}, dimensions={0} | all-to-all | bytes 1310720 | tf_op jit(solution)/shard_map/all_to_all | solution.py:361
  149.1 6.5 %collective-permute-start.15 = (bf16[32,80,128]{2,1,0:T(8,128)(2,1)S(1)}, bf16[32,80,128]{2,1,0:T(8,128)(2,1)S(1)}, u32[]{:S(2)}, u32[]{:S(2)}) collective-permute-start(bf16[32,80,128]{2,1,0:T(8,128)(2,1)S(1)} %all_to_all.17.mine_ref), channel_id=1, source_target_pairs={{0,8},{8,0},{1,9},{9,1},{2,10},{10,2},{3,11},{11,3},{4,12},{12,4},... | collective-permute-start | bytes 1966088 | tf_op jit(solution)/shard_map/ppermute | solution.py:276
  155.6 1.7 %collective-permute-done.15.theirs_ref = bf16[32,80,128]{2,1,0:T(8,128)(2,1)S(1)} collective-permute-done((bf16[32,80,128]{2,1,0:T(8,128)(2,1)S(1)}, bf16[32,80,128]{2,1,0:T(8,128)(2,1)S(1)}, u32[]{:S(2)}, u32[]{:S(2)}) %collective-permute-start.15) | collective-permute-done | bytes 655392 | tf_op jit(solution)/shard_map/ppermute | solution.py:276
  157.3 1.2 place.1
  (2 shorter events, 0.1 us)
Async XLA Ops:
  3.9 22.4 %collective-permute-start.1 = (bf16[400,768]{1,0:T(8,128)(2,1)}, bf16[400,768]{1,0:T(8,128)(2,1)S(1)}, u32[]{:S(2)}, u32[]{:S(2)}) collective-permute-start(bf16[400,768]{1,0:T(8,128)(2,1)} %get-tuple-element.14.n0), channel_id=1, source_target_pairs={{0,1},{1,0},{8,57},{9,24},{16,17},{17,16},{24,9},{25,40},{32,33},{... | collective-permute-start | bytes 1843208 | tf_op jit(solution)/shard_map/ppermute | solution.py:273
  14.5 11.8 %collective-permute-start = (bf16[400,768]{1,0:T(8,128)(2,1)}, bf16[400,768]{1,0:T(8,128)(2,1)S(1)}, u32[]{:S(2)}, u32[]{:S(2)}) collective-permute-start(bf16[400,768]{1,0:T(8,128)(2,1)} %get-tuple-element.14.n0), channel_id=1, source_target_pairs={{0,2},{2,4},{4,6},{6,0},{8,14},{10,8},{12,10},{14,12},{1,3},{3,5},... | collective-permute-start | bytes 1843208 | tf_op jit(solution)/shard_map/ppermute | solution.py:270
  18.9 4.4 %collective-permute-start.2 = (bf16[80,1280]{1,0:T(8,128)(2,1)}, bf16[80,1280]{1,0:T(8,128)(2,1)S(1)}, u32[]{:S(2)}, u32[]{:S(2)}) collective-permute-start(bf16[80,1280]{1,0:T(8,128)(2,1)} %get-tuple-element.15.io_a_ref), channel_id=1, source_target_pairs={{0,8},{8,0},{1,9},{9,1},{2,10},{10,2},{3,11},{11,3},{4,12},{12,4},... | collective-permute-start | bytes 614408 | tf_op jit(solution)/shard_map/ppermute | solution.py:276
  20.9 16.7 %collective-permute-start.3 = (bf16[416,768]{1,0:T(8,128)(2,1)}, bf16[416,768]{1,0:T(8,128)(2,1)S(1)}, u32[]{:S(2)}, u32[]{:S(2)}) collective-permute-start(bf16[416,768]{1,0:T(8,128)(2,1)} %get-tuple-element.17.f0), channel_id=1, source_target_pairs={{0,2},{2,4},{4,6},{6,0},{8,14},{10,8},{12,10},{14,12},{1,3},{3,5},... | collective-permute-start | bytes 1916936 | tf_op jit(solution)/shard_map/ppermute | solution.py:270
  23.3 0.7 copy-start.3
  26.3 34.2 %copy-start = (bf16[144,768]{1,0:T(8,128)(2,1)S(1)}, bf16[144,768]{1,0:T(8,128)(2,1)}, u32[]{:S(2)}) copy-start(bf16[144,768]{1,0:T(8,128)(2,1)} %front.1.start_ref) | copy-start | bytes 663556
  26.3 34.2 %copy-start.1 = (bf16[416,768]{1,0:T(8,128)(2,1)S(1)}, bf16[416,768]{1,0:T(8,128)(2,1)}, u32[]{:S(2)}) copy-start(bf16[416,768]{1,0:T(8,128)(2,1)} %get-tuple-element.17.f0) | copy-start | bytes 1916932
  26.3 34.2 %copy-start.2 = (bf16[400,768]{1,0:T(8,128)(2,1)S(1)}, bf16[400,768]{1,0:T(8,128)(2,1)}, u32[]{:S(2)}) copy-start(bf16[400,768]{1,0:T(8,128)(2,1)} %get-tuple-element.14.n0) | copy-start | bytes 1843204
  26.3 15.9 %collective-permute-start.5 = (bf16[400,768]{1,0:T(8,128)(2,1)S(1)}, bf16[400,768]{1,0:T(8,128)(2,1)S(1)}, u32[]{:S(2)}, u32[]{:S(2)}) collective-permute-start(bf16[400,768]{1,0:T(8,128)(2,1)S(1)} %collective-permute-done.n1), channel_id=1, source_target_pairs={{0,1},{1,0},{8,57},{9,24},{16,17},{17,16},{24,9},{25,40},{32,33},{... | collective-permute-start | bytes 1843208 | tf_op jit(solution)/shard_map/ppermute | solution.py:273
  29.5 12.7 %collective-permute-start.4 = (bf16[400,768]{1,0:T(8,128)(2,1)S(1)}, bf16[400,768]{1,0:T(8,128)(2,1)S(1)}, u32[]{:S(2)}, u32[]{:S(2)}) collective-permute-start(bf16[400,768]{1,0:T(8,128)(2,1)S(1)} %collective-permute-done.n1), channel_id=1, source_target_pairs={{0,2},{2,4},{4,6},{6,0},{8,14},{10,8},{12,10},{14,12},{1,3},{3,5},... | collective-permute-start | bytes 1843208 | tf_op jit(solution)/shard_map/ppermute | solution.py:270
  33.2 8.9 %collective-permute-start.6 = (bf16[384,768]{1,0:T(8,128)(2,1)S(1)}, bf16[384,768]{1,0:T(8,128)(2,1)S(1)}, u32[]{:S(2)}, u32[]{:S(2)}) collective-permute-start(bf16[384,768]{1,0:T(8,128)(2,1)S(1)} %slice.6), channel_id=1, source_target_pairs={{0,8},{8,0},{1,9},{9,1},{2,10},{10,2},{3,11},{11,3},{4,12},{12,4},... | collective-permute-start | bytes 1769480 | tf_op jit(solution)/shard_map/ppermute | solution.py:276
  35.2 7.0 %collective-permute-start.7 = (bf16[384,768]{1,0:T(8,128)(2,1)S(1)}, bf16[384,768]{1,0:T(8,128)(2,1)S(1)}, u32[]{:S(2)}, u32[]{:S(2)}) collective-permute-start(bf16[384,768]{1,0:T(8,128)(2,1)S(1)} %slice.7), channel_id=1, source_target_pairs={{0,8},{8,0},{1,9},{9,1},{2,10},{10,2},{3,11},{11,3},{4,12},{12,4},... | collective-permute-start | bytes 1769480 | tf_op jit(solution)/shard_map/ppermute | solution.py:276
  37.6 12.4 %collective-permute-start.8 = (bf16[416,768]{1,0:T(8,128)(2,1)S(1)}, bf16[416,768]{1,0:T(8,128)(2,1)S(1)}, u32[]{:S(2)}, u32[]{:S(2)}) collective-permute-start(bf16[416,768]{1,0:T(8,128)(2,1)S(1)} %collective-permute-done.3.f1), channel_id=1, source_target_pairs={{0,1},{1,0},{8,57},{9,24},{16,17},{17,16},{24,9},{25,40},{32,33},{... | collective-permute-start | bytes 1916936 | tf_op jit(solution)/shard_map/ppermute | solution.py:273
  42.2 14.3 %collective-permute-start.9 = (bf16[400,768]{1,0:T(8,128)(2,1)S(1)}, bf16[400,768]{1,0:T(8,128)(2,1)S(1)}, u32[]{:S(2)}, u32[]{:S(2)}) collective-permute-start(bf16[400,768]{1,0:T(8,128)(2,1)S(1)} %collective-permute-done.4.n2), channel_id=1, source_target_pairs={{0,1},{1,0},{8,57},{9,24},{16,17},{17,16},{24,9},{25,40},{32,33},{... | collective-permute-start | bytes 1843208 | tf_op jit(solution)/shard_map/ppermute | solution.py:273
  44.8 13.9 %collective-permute-start.10 = (bf16[416,768]{1,0:T(8,128)(2,1)S(1)}, bf16[416,768]{1,0:T(8,128)(2,1)S(1)}, u32[]{:S(2)}, u32[]{:S(2)}) collective-permute-start(bf16[416,768]{1,0:T(8,128)(2,1)S(1)} %collective-permute-done.3.f1), channel_id=1, source_target_pairs={{0,8},{8,0},{1,9},{9,1},{2,10},{10,2},{3,11},{11,3},{4,12},{12,4},... | collective-permute-start | bytes 1916936 | tf_op jit(solution)/shard_map/ppermute | solution.py:276
  50.0 8.7 %collective-permute-start.13 = (bf16[416,768]{1,0:T(8,128)(2,1)S(1)}, bf16[416,768]{1,0:T(8,128)(2,1)S(1)}, u32[]{:S(2)}, u32[]{:S(2)}) collective-permute-start(bf16[416,768]{1,0:T(8,128)(2,1)S(1)} %collective-permute-done.8.f4), channel_id=1, source_target_pairs={{0,8},{8,0},{1,9},{9,1},{2,10},{10,2},{3,11},{11,3},{4,12},{12,4},... | collective-permute-start | bytes 1916936 | tf_op jit(solution)/shard_map/ppermute | solution.py:276
  51.9 6.8 %collective-permute-start.12 = (bf16[400,768]{1,0:T(8,128)(2,1)S(1)}, bf16[400,768]{1,0:T(8,128)(2,1)S(1)}, u32[]{:S(2)}, u32[]{:S(2)}) collective-permute-start(bf16[400,768]{1,0:T(8,128)(2,1)S(1)} %collective-permute-done.5.n4), channel_id=1, source_target_pairs={{0,8},{8,0},{1,9},{9,1},{2,10},{10,2},{3,11},{11,3},{4,12},{12,4},... | collective-permute-start | bytes 1843208 | tf_op jit(solution)/shard_map/ppermute | solution.py:276
  54.3 4.4 %collective-permute-start.11 = (bf16[400,768]{1,0:T(8,128)(2,1)S(1)}, bf16[400,768]{1,0:T(8,128)(2,1)S(1)}, u32[]{:S(2)}, u32[]{:S(2)}) collective-permute-start(bf16[400,768]{1,0:T(8,128)(2,1)S(1)} %collective-permute-done.4.n2), channel_id=1, source_target_pairs={{0,8},{8,0},{1,9},{9,1},{2,10},{10,2},{3,11},{11,3},{4,12},{12,4},... | collective-permute-start | bytes 1843208 | tf_op jit(solution)/shard_map/ppermute | solution.py:276
  56.5 3.9 %collective-permute-start.14 = (bf16[400,768]{1,0:T(8,128)(2,1)S(1)}, bf16[400,768]{1,0:T(8,128)(2,1)S(1)}, u32[]{:S(2)}, u32[]{:S(2)}) collective-permute-start(bf16[400,768]{1,0:T(8,128)(2,1)S(1)} %collective-permute-done.9.n5), channel_id=1, source_target_pairs={{0,8},{8,0},{1,9},{9,1},{2,10},{10,2},{3,11},{11,3},{4,12},{12,4},... | collective-permute-start | bytes 1843208 | tf_op jit(solution)/shard_map/ppermute | solution.py:276
  149.1 8.2 %collective-permute-start.15 = (bf16[32,80,128]{2,1,0:T(8,128)(2,1)S(1)}, bf16[32,80,128]{2,1,0:T(8,128)(2,1)S(1)}, u32[]{:S(2)}, u32[]{:S(2)}) collective-permute-start(bf16[32,80,128]{2,1,0:T(8,128)(2,1)S(1)} %all_to_all.17.mine_ref), channel_id=1, source_target_pairs={{0,8},{8,0},{1,9},{9,1},{2,10},{10,2},{3,11},{11,3},{4,12},{12,4},... | collective-permute-start | bytes 1966088 | tf_op jit(solution)/shard_map/ppermute | solution.py:276

commit v6 on v5

--- a/solution.py
+++ b/solution.py
@@ -18,7 +18,7 @@
 T = 64
 L = 8
 TAPS = 16
-NEAR = H + TAPS
+NEAR = H + TAPS + 8
 FAR = H + 2 * TAPS
 INROWS = T + 16
 HT = T // 2
@@ -69,9 +69,10 @@
     taps = jnp.concatenate([taps_ref[k] for k in range(KER)], axis=0)
     hi, mid, low = split3(taps)
     packed = jnp.concatenate([hi, mid, low, jnp.zeros((1, D), F32)], axis=0).astype(BF)
-    near_ref[H:, :] = packed
-    far_ref[H:NEAR, :] = packed
-    far_ref[NEAR:, :] = packed
+    near_ref[H:H + TAPS, :] = packed
+    near_ref[H + TAPS:, :] = jnp.zeros((NEAR - H - TAPS, D), BF)
+    far_ref[H:H + TAPS, :] = packed
+    far_ref[H + TAPS:, :] = packed
     count = len_ref[utt].astype(F32)
     io_ref[T:, :] = jnp.full((INROWS - T, FEAT + D), count, F32).astype(BF)
     for copy in copies:
@@ -88,15 +89,11 @@
     out_ref[T:, :] = io[:, FEAT:].astype(BF)
 
 
-def fold(x):
-    return jnp.concatenate([x[0:HT], x[HT:]], axis=1)
-
-
 def model_kernel(
     start_ref,
     n0, f0, n1, f1, n2, n3, n4, f4, n5, m1, g1, m2, m3, m4, g4, m5,
     pay_ref,
-    w_ref, traw_ref, taps_ref, vals_ref, inv_ref, norm_ref, slope_ref, act_ref, gpad_ref, g_ref,
+    w_ref, traw_ref, taps_ref, inv_ref, norm_ref, slope_ref, act_ref, gpad_ref, g_ref,
     wsem, tsem,
 ):
     section, core = where_am_i()
@@ -119,10 +116,13 @@
 
     for near, far, c, r, part in (
         (n0, f0, col, row, core), (n1, f1, side, row, core), (n4, f4, side, flip, core),
-        (m1, g1, anti, row, other), (m4, g4, anti, flip, other),
     ):
         bring(near, c, r, part, False)
         bring(far, c, r, 1 - part, True)
+    bring(m1, anti, row, other, False)
+    bring(g1, anti, row, core, True)
+    bring(m4, anti, flip, other, True)
+    bring(g4, anti, flip, core, False)
     for near, mirror, c, r in ((n2, m2, across, row), (n3, m3, col, flip), (n5, m5, across, flip)):
         bring(near, c, r, core, True)
         bring(mirror, c, r, other, False)
@@ -145,8 +145,7 @@
         taps_ref[l, 0:KER, :] = taps
         vals = g_ref[...]
         inv = lax.rsqrt(jnp.mean(vals * vals, axis=-1, keepdims=True) + EPS)
-        norm = vals * inv * mask
-        vals_ref[l] = vals
+        norm = vals * (inv * mask)
         inv_ref[l] = jnp.broadcast_to(inv, (T, 128))
         norm_ref[l, 0:8, :] = edge
         norm_ref[l, T + 8:, :] = edge
@@ -166,14 +165,15 @@
 
     g_ref[...] = ((g_ref[...] - target) * mask / count).astype(BF).astype(F32)
 
+    share = pl.multiple_of(core * H, H)
+
     def backward(i, carry):
         l = L - 1 - i
         g = g_ref[...]
         gb = g.astype(BF)
         pay_ref[l, 0:T, :] = gb
-        act = act_ref[l].astype(F32)
-        share = jnp.where(core == 0, act[:, 0:H], act[:, H:])
-        pay_ref[l, T:T + HT, :] = fold(share).astype(BF)
+        pay_ref[l, T:T + HT, 0:H] = act_ref[l, 0:HT, pl.ds(share, H)]
+        pay_ref[l, T:T + HT, H:] = act_ref[l, HT:, pl.ds(share, H)]
         grad_act = lax.dot_general(
             gb, w_ref[l], (((1,), (1,)), ((), ())), preferred_element_type=F32)
         grad_conv = grad_act * slope_ref[l]
@@ -191,10 +191,10 @@
         for k in range(1, KER):
             grad_norm = grad_norm + taps[k:k + 1] * gpad_ref[10 - k:T + 10 - k, :]
         grad_norm = grad_norm * mask
-        vals = vals_ref[l]
         inv = inv_ref[l][:, 0:1]
-        mean = jnp.mean(grad_norm * vals, axis=-1, keepdims=True)
-        g_ref[...] = (g + (inv * grad_norm - vals * (inv * inv * inv * mean))).astype(BF).astype(F32)
+        norm = norm_ref[l, 8:T + 8, :]
+        mean = jnp.mean(grad_norm * norm, axis=-1, keepdims=True)
+        g_ref[...] = (g + inv * (grad_norm - norm * mean)).astype(BF).astype(F32)
         return carry
 
     lax.fori_loop(0, L, backward, 0, unroll=True)
@@ -298,13 +298,15 @@
     n1, n3, begin = lax.optimization_barrier((along_x(near), along_z(near), begin))
     f1 = along_x(far)
     n2 = along_x(n1)
-    n4 = along_z(n1)
+    n4 = along_z(n1[:H + TAPS])
     f4 = along_z(f1)
     m1, m3 = to_core(n1[:H]), to_core(n3[:H])
     n2, n4, m1, m3 = lax.optimization_barrier((n2, n4, m1, m3))
-    n5 = along_z(n2)
+    n5 = along_z(n2[:H + TAPS])
+    g1, m2, m4 = to_core(f1[:H + TAPS]), to_core(n2[:H + TAPS]), to_core(n4)
+    g4, m5 = to_core(f4[:H + 8]), to_core(n5[:H])
     here = [near, far, n1, f1, n2, n3, n4, f4, n5]
-    there = [m1, to_core(f1), to_core(n2), m3, to_core(n4), to_core(f4), to_core(n5)]
+    there = [m1, g1, m2, m3, m4, g4, m5]
 
     payload = pl.pallas_call(
         model_kernel,
@@ -316,7 +318,6 @@
             pltpu.VMEM((L, D, D), BF),
             pltpu.VMEM((L, TAPS, D), BF),
             pltpu.VMEM((L, 8, D), F32),
-            pltpu.VMEM((L, T, D), F32),
             pltpu.VMEM((L, T, 128), F32),
             pltpu.VMEM((L, T + 16, D), F32),
             pltpu.VMEM((L, T, D), F32),

time: 159 us -> 159 us (level)
    ppermute x4, starting transfers between devices: 21 us -> 19.1 us  [along_z(): return lax.ppermute(a, ('zh', 'c', 'zl'), pair)]
  transfers between devices with their start and end apart: 16 -> 16, of which waited for: 4 -> 5; matrix products, arithmetic and copies ran while one was open for 0% -> 0% of each run, Pallas kernels for 1% -> 1%
where the time goes in v6:
time: 159 us
  blocking collectives  74.8 us (47%)
  starting transfers between devices  54.1 us (34%)
  Pallas kernels  20.4 us (13%)
  waiting for transfers between devices  7.41 us (5%)
    all_to_all x1, blocking collectives, body(): scattered = lax.all_to_all(parts, ('y', 'zh'), 0, 0)  27.9 us
    all_to_all x1, blocking collectives, body(): half = lax.all_to_all(mine, ('y', 'zh'), 0, 0)  26.4 us
    ppermute x9, starting transfers between devices, to_core(): return lax.ppermute(a, 'c', [(0, 1), (1, 0)])  23.3 us
    all_to_all x1, blocking collectives, body(): received = lax.all_to_all(payload, ('x', 'zl'), 0, 0)  20.5 us
    ppermute x4, starting transfers between devices, along_z(): return lax.ppermute(a, ('zh', 'c', 'zl'), pair)  19.1 us
    pallas_call x1, Pallas kernels, body(): pl.pallas_call(model_kernel, name='model', out_shape=jax.ShapeDtypeStruct...  13.1 us
    ppermute x3, starting transfers between devices, along_x(): return lax.ppermute(a, ('c', 'x'), ring)  11.8 us
    ppermute x9, waiting for transfers between devices, to_core(): return lax.ppermute(a, 'c', [(0, 1), (1, 0)])  3.65 us
  transfers between devices with their start and end apart: 16, of which 5 were waited for; matrix products, arithmetic and copies ran while one was open for 0% of the time, Pallas kernels for 1%

profile of v6, /device:TPU:9, one launch (start us, length us, event | category | flops | bytes accessed | tf_op | source)
XLA Modules:
  0.0 158.7 jit_solution(8235838268995814558)
XLA Ops:
  0.6 3.2 %prep.1 = (bf16[408,768]{1,0:T(8,128)(2,1)}, bf16[416,768]{1,0:T(8,128)(2,1)}, bf16[80,1280]{1,0:T(8,128)(2,1)}) custom-call(bf16[1,768,768]{2,1,0:T(8,128)(2,1)} %w_ref.1, f32[5,1,768]{2,1,0:T(1,128)} %bitcast.2, bf16[4,64,512]{2,1,0:T(8,128)(2,1)} %feat_ref.1, bf16[4,64,768]{2,1,0:T(8,128)(2,1)} %targ_ref.1, s32[4]{0:T(128)} %len_ref.1), custom_call_target="tpu_custom_call" | custom-call | tf_op jit(solution)/shard_map/prep/pallas_call | solution.py:278
  3.9 10.7 %collective-permute-start.1 = (bf16[408,768]{1,0:T(8,128)(2,1)}, bf16[408,768]{1,0:T(8,128)(2,1)S(1)}, u32[]{:S(2)}, u32[]{:S(2)}) collective-permute-start(bf16[408,768]{1,0:T(8,128)(2,1)} %get-tuple-element.14.n0), channel_id=1, source_target_pairs={{0,1},{1,0},{8,57},{9,24},{16,17},{17,16},{24,9},{25,40},{32,33},{... | collective-permute-start | bytes 1880072 | tf_op jit(solution)/shard_map/ppermute | solution.py:273
  14.5 4.4 %collective-permute-start = (bf16[408,768]{1,0:T(8,128)(2,1)}, bf16[408,768]{1,0:T(8,128)(2,1)S(1)}, u32[]{:S(2)}, u32[]{:S(2)}) collective-permute-start(bf16[408,768]{1,0:T(8,128)(2,1)} %get-tuple-element.14.n0), channel_id=1, source_target_pairs={{0,2},{2,4},{4,6},{6,0},{8,14},{10,8},{12,10},{14,12},{1,3},{3,5},... | collective-permute-start | bytes 1880072 | tf_op jit(solution)/shard_map/ppermute | solution.py:270
  18.9 1.9 %collective-permute-start.2 = (bf16[80,1280]{1,0:T(8,128)(2,1)}, bf16[80,1280]{1,0:T(8,128)(2,1)S(1)}, u32[]{:S(2)}, u32[]{:S(2)}) collective-permute-start(bf16[80,1280]{1,0:T(8,128)(2,1)} %get-tuple-element.15.io_a_ref), channel_id=1, source_target_pairs={{0,8},{8,0},{1,9},{9,1},{2,10},{10,2},{3,11},{11,3},{4,12},{12,4},... | collective-permute-start | bytes 614408 | tf_op jit(solution)/shard_map/ppermute | solution.py:276
  20.9 2.5 %collective-permute-start.3 = (bf16[416,768]{1,0:T(8,128)(2,1)}, bf16[416,768]{1,0:T(8,128)(2,1)S(1)}, u32[]{:S(2)}, u32[]{:S(2)}) collective-permute-start(bf16[416,768]{1,0:T(8,128)(2,1)} %get-tuple-element.17.f0), channel_id=1, source_target_pairs={{0,2},{2,4},{4,6},{6,0},{8,14},{10,8},{12,10},{14,12},{1,3},{3,5},... | collective-permute-start | bytes 1916936 | tf_op jit(solution)/shard_map/ppermute | solution.py:270
  23.3 0.0 collective-permute-done.2.io_b_ref
  23.3 0.0 copy-start.3
  23.3 0.7 copy-done.3
  24.0 2.3 %front.1.start_ref = bf16[144,768]{1,0:T(8,128)(2,1)} custom-call(bf16[80,1280]{1,0:T(8,128)(2,1)} %get-tuple-element.15.io_a_ref, bf16[80,1280]{1,0:T(8,128)(2,1)} %copy-done.3, bf16[512,768]{1,0:T(8,128)(2,1)} %front_ref.1), custom_call_target="tpu_custom_call" | custom-call | tf_op jit(solution)/shard_map/front/pallas_call | solution.py:290
  26.3 0.0 collective-permute-done.1.n3
  26.3 0.1 collective-permute-done.n1
  26.4 4.9 %collective-permute-start.4 = (bf16[408,768]{1,0:T(8,128)(2,1)S(1)}, bf16[408,768]{1,0:T(8,128)(2,1)S(1)}, u32[]{:S(2)}, u32[]{:S(2)}) collective-permute-start(bf16[408,768]{1,0:T(8,128)(2,1)S(1)} %collective-permute-done.n1), channel_id=1, source_target_pairs={{0,2},{2,4},{4,6},{6,0},{8,14},{10,8},{12,10},{14,12},{1,3},{3,5},... | collective-permute-start | bytes 1880072 | tf_op jit(solution)/shard_map/ppermute | solution.py:270
  31.4 1.9 %collective-permute-start.5 = (bf16[400,768]{1,0:T(8,128)(2,1)S(1)}, bf16[400,768]{1,0:T(8,128)(2,1)S(1)}, u32[]{:S(2)}, u32[]{:S(2)}) collective-permute-start(bf16[400,768]{1,0:T(8,128)(2,1)S(1)} %slice.22), channel_id=1, source_target_pairs={{0,1},{1,0},{8,57},{9,24},{16,17},{17,16},{24,9},{25,40},{32,33},{... | collective-permute-start | bytes 1843208 | tf_op jit(solution)/shard_map/ppermute | solution.py:273
  33.4 1.9 %collective-permute-start.6 = (bf16[384,768]{1,0:T(8,128)(2,1)S(1)}, bf16[384,768]{1,0:T(8,128)(2,1)S(1)}, u32[]{:S(2)}, u32[]{:S(2)}) collective-permute-start(bf16[384,768]{1,0:T(8,128)(2,1)S(1)} %slice.23), channel_id=1, source_target_pairs={{0,8},{8,0},{1,9},{9,1},{2,10},{10,2},{3,11},{11,3},{4,12},{12,4},... | collective-permute-start | bytes 1769480 | tf_op jit(solution)/shard_map/ppermute | solution.py:276
  35.4 2.4 %collective-permute-start.7 = (bf16[384,768]{1,0:T(8,128)(2,1)S(1)}, bf16[384,768]{1,0:T(8,128)(2,1)S(1)}, u32[]{:S(2)}, u32[]{:S(2)}) collective-permute-start(bf16[384,768]{1,0:T(8,128)(2,1)S(1)} %slice.24), channel_id=1, source_target_pairs={{0,8},{8,0},{1,9},{9,1},{2,10},{10,2},{3,11},{11,3},{4,12},{12,4},... | collective-permute-start | bytes 1769480 | tf_op jit(solution)/shard_map/ppermute | solution.py:276
  37.8 0.0 collective-permute-done.3.f1
  37.8 4.6 %collective-permute-start.8 = (bf16[416,768]{1,0:T(8,128)(2,1)S(1)}, bf16[416,768]{1,0:T(8,128)(2,1)S(1)}, u32[]{:S(2)}, u32[]{:S(2)}) collective-permute-start(bf16[416,768]{1,0:T(8,128)(2,1)S(1)} %collective-permute-done.3.f1), channel_id=1, source_target_pairs={{0,1},{1,0},{8,57},{9,24},{16,17},{17,16},{24,9},{25,40},{32,33},{... | collective-permute-start | bytes 1916936 | tf_op jit(solution)/shard_map/ppermute | solution.py:273
  42.4 0.0 collective-permute-done.6.m1
  42.4 0.0 collective-permute-done.7.m3
  42.4 1.1 collective-permute-done.5.n4
  43.5 0.0 collective-permute-done.4.n2
  43.6 1.9 %collective-permute-start.9 = (bf16[400,768]{1,0:T(8,128)(2,1)S(1)}, bf16[400,768]{1,0:T(8,128)(2,1)S(1)}, u32[]{:S(2)}, u32[]{:S(2)}) collective-permute-start(bf16[400,768]{1,0:T(8,128)(2,1)S(1)} %slice.25), channel_id=1, source_target_pairs={{0,1},{1,0},{8,57},{9,24},{16,17},{17,16},{24,9},{25,40},{32,33},{... | collective-permute-start | bytes 1843208 | tf_op jit(solution)/shard_map/ppermute | solution.py:273
  45.5 0.0 copy-start
  45.5 0.0 copy-start.1
  45.6 0.0 copy-start.2
  45.6 2.1 %collective-permute-start.10 = (bf16[400,768]{1,0:T(8,128)(2,1)S(1)}, bf16[400,768]{1,0:T(8,128)(2,1)S(1)}, u32[]{:S(2)}, u32[]{:S(2)}) collective-permute-start(bf16[400,768]{1,0:T(8,128)(2,1)S(1)} %slice.29), channel_id=1, source_target_pairs={{0,8},{8,0},{1,9},{9,1},{2,10},{10,2},{3,11},{11,3},{4,12},{12,4},... | collective-permute-start | bytes 1843208 | tf_op jit(solution)/shard_map/ppermute | solution.py:276
  47.6 2.4 %collective-permute-start.11 = (bf16[400,768]{1,0:T(8,128)(2,1)S(1)}, bf16[400,768]{1,0:T(8,128)(2,1)S(1)}, u32[]{:S(2)}, u32[]{:S(2)}) collective-permute-start(bf16[400,768]{1,0:T(8,128)(2,1)S(1)} %slice.25), channel_id=1, source_target_pairs={{0,8},{8,0},{1,9},{9,1},{2,10},{10,2},{3,11},{11,3},{4,12},{12,4},... | collective-permute-start | bytes 1843208 | tf_op jit(solution)/shard_map/ppermute | solution.py:276
  50.0 1.9 %collective-permute-start.12 = (bf16[400,768]{1,0:T(8,128)(2,1)S(1)}, bf16[400,768]{1,0:T(8,128)(2,1)S(1)}, u32[]{:S(2)}, u32[]{:S(2)}) collective-permute-start(bf16[400,768]{1,0:T(8,128)(2,1)S(1)} %collective-permute-done.5.n4), channel_id=1, source_target_pairs={{0,8},{8,0},{1,9},{9,1},{2,10},{10,2},{3,11},{11,3},{4,12},{12,4},... | collective-permute-start | bytes 1843208 | tf_op jit(solution)/shard_map/ppermute | solution.py:276
  52.0 0.0 collective-permute-done.8.f4
  52.0 2.4 %collective-permute-start.13 = (bf16[392,768]{1,0:T(8,128)(2,1)S(1)}, bf16[392,768]{1,0:T(8,128)(2,1)S(1)}, u32[]{:S(2)}, u32[]{:S(2)}) collective-permute-start(bf16[392,768]{1,0:T(8,128)(2,1)S(1)} %slice.30), channel_id=1, source_target_pairs={{0,8},{8,0},{1,9},{9,1},{2,10},{10,2},{3,11},{11,3},{4,12},{12,4},... | collective-permute-start | bytes 1806344 | tf_op jit(solution)/shard_map/ppermute | solution.py:276
  54.4 2.5 %collective-permute-done.9.n5 = bf16[400,768]{1,0:T(8,128)(2,1)S(1)} collective-permute-done((bf16[400,768]{1,0:T(8,128)(2,1)S(1)}, bf16[400,768]{1,0:T(8,128)(2,1)S(1)}, u32[]{:S(2)}, u32[]{:S(2)}) %collective-permute-start.9) | collective-permute-done | bytes 614432 | tf_op jit(solution)/shard_map/ppermute | solution.py:273
  57.0 1.9 %collective-permute-start.14 = (bf16[384,768]{1,0:T(8,128)(2,1)S(1)}, bf16[384,768]{1,0:T(8,128)(2,1)S(1)}, u32[]{:S(2)}, u32[]{:S(2)}) collective-permute-start(bf16[384,768]{1,0:T(8,128)(2,1)S(1)} %slice.31), channel_id=1, source_target_pairs={{0,8},{8,0},{1,9},{9,1},{2,10},{10,2},{3,11},{11,3},{4,12},{12,4},... | collective-permute-start | bytes 1769480 | tf_op jit(solution)/shard_map/ppermute | solution.py:276
  58.9 0.0 collective-permute-done.10.g1
  58.9 0.0 collective-permute-done.11.m2
  58.9 0.0 collective-permute-done.12.m4
  58.9 0.0 collective-permute-done.13.g4
  59.0 1.9 %collective-permute-done.14.m5 = bf16[384,768]{1,0:T(8,128)(2,1)S(1)} collective-permute-done((bf16[384,768]{1,0:T(8,128)(2,1)S(1)}, bf16[384,768]{1,0:T(8,128)(2,1)S(1)}, u32[]{:S(2)}, u32[]{:S(2)}) %collective-permute-start.14) | collective-permute-done | bytes 589856 | tf_op jit(solution)/shard_map/ppermute | solution.py:276
  60.9 0.0 copy-done
  60.9 0.0 copy-done.1
  60.9 0.0 copy-done.2
  60.9 13.1 %model.1 = bf16[8,104,768]{2,1,0:T(8,128)(2,1)S(1)} custom-call(bf16[144,768]{1,0:T(8,128)(2,1)S(1)} %copy-done, bf16[408,768]{1,0:T(8,128)(2,1)S(1)} %copy-done.2, bf16[416,768]{1,0:T(8,128)(2,1)S(1)} %copy-done.1, bf16[408,768]{1,0:T(8,128)(2,1)S(1)} %collective-permute-done.n1, bf16[416,768]{1,0:T(8,128)(2,1)S(1)} %collective-permute-done.3.f1, ...), custom_call_target="tpu_custom_call" | custom-call | tf_op jit(solution)/shard_map/model/pallas_call | solution.py:311
  74.0 20.5 %all_to_all.15.recv_ref = bf16[8,104,768]{2,1,0:T(8,128)(2,1)S(1)} all-to-all(bf16[8,104,768]{2,1,0:T(8,128)(2,1)S(1)} %model.1), channel_id=1, replica_groups=mesh['y'=8,'zh'=4,'c'=2,'x'=4,'zl'=2] {'x','zl'}, dimensions={0} | all-to-all | bytes 2555904 | tf_op jit(solution)/shard_map/all_to_all | solution.py:333
  94.5 0.6 grad.1
  95.1 27.9 %all_to_all.16.parts_ref = bf16[32,80,128]{2,1,0:T(8,128)(2,1)S(1)} all-to-all(bf16[32,80,128]{2,1,0:T(8,128)(2,1)S(1)} %grad.1), channel_id=1, replica_groups=mesh['y'=8,'zh'=4,'c'=2,'x'=4,'zl'=2] {'y','zh'}, dimensions={0} | all-to-all | bytes 1310720 | tf_op jit(solution)/shard_map/all_to_all | solution.py:350
  122.9 0.1 total.1
  123.1 26.4 %all_to_all.17.mine_ref = bf16[32,80,128]{2,1,0:T(8,128)(2,1)S(1)} all-to-all(bf16[32,80,128]{2,1,0:T(8,128)(2,1)S(1)} %total.1), channel_id=1, replica_groups=mesh['y'=8,'zh'=4,'c'=2,'x'=4,'zl'=2] {'y','zh'}, dimensions={0} | all-to-all | bytes 1310720 | tf_op jit(solution)/shard_map/all_to_all | solution.py:362
  149.5 6.3 %collective-permute-start.15 = (bf16[32,80,128]{2,1,0:T(8,128)(2,1)S(1)}, bf16[32,80,128]{2,1,0:T(8,128)(2,1)S(1)}, u32[]{:S(2)}, u32[]{:S(2)}) collective-permute-start(bf16[32,80,128]{2,1,0:T(8,128)(2,1)S(1)} %all_to_all.17.mine_ref), channel_id=1, source_target_pairs={{0,8},{8,0},{1,9},{9,1},{2,10},{10,2},{3,11},{11,3},{4,12},{12,4},... | collective-permute-start | bytes 1966088 | tf_op jit(solution)/shard_map/ppermute | solution.py:276
  155.8 1.7 %collective-permute-done.15.theirs_ref = bf16[32,80,128]{2,1,0:T(8,128)(2,1)S(1)} collective-permute-done((bf16[32,80,128]{2,1,0:T(8,128)(2,1)S(1)}, bf16[32,80,128]{2,1,0:T(8,128)(2,1)S(1)}, u32[]{:S(2)}, u32[]{:S(2)}) %collective-permute-start.15) | collective-permute-done | bytes 655392 | tf_op jit(solution)/shard_map/ppermute | solution.py:276
  157.5 1.2 place.1
  (7 shorter events, 0.3 us)
Async XLA Ops:
  3.9 22.4 %collective-permute-start.1 = (bf16[408,768]{1,0:T(8,128)(2,1)}, bf16[408,768]{1,0:T(8,128)(2,1)S(1)}, u32[]{:S(2)}, u32[]{:S(2)}) collective-permute-start(bf16[408,768]{1,0:T(8,128)(2,1)} %get-tuple-element.14.n0), channel_id=1, source_target_pairs={{0,1},{1,0},{8,57},{9,24},{16,17},{17,16},{24,9},{25,40},{32,33},{... | collective-permute-start | bytes 1880072 | tf_op jit(solution)/shard_map/ppermute | solution.py:273
  14.5 11.9 %collective-permute-start = (bf16[408,768]{1,0:T(8,128)(2,1)}, bf16[408,768]{1,0:T(8,128)(2,1)S(1)}, u32[]{:S(2)}, u32[]{:S(2)}) collective-permute-start(bf16[408,768]{1,0:T(8,128)(2,1)} %get-tuple-element.14.n0), channel_id=1, source_target_pairs={{0,2},{2,4},{4,6},{6,0},{8,14},{10,8},{12,10},{14,12},{1,3},{3,5},... | collective-permute-start | bytes 1880072 | tf_op jit(solution)/shard_map/ppermute | solution.py:270
  18.9 4.4 %collective-permute-start.2 = (bf16[80,1280]{1,0:T(8,128)(2,1)}, bf16[80,1280]{1,0:T(8,128)(2,1)S(1)}, u32[]{:S(2)}, u32[]{:S(2)}) collective-permute-start(bf16[80,1280]{1,0:T(8,128)(2,1)} %get-tuple-element.15.io_a_ref), channel_id=1, source_target_pairs={{0,8},{8,0},{1,9},{9,1},{2,10},{10,2},{3,11},{11,3},{4,12},{12,4},... | collective-permute-start | bytes 614408 | tf_op jit(solution)/shard_map/ppermute | solution.py:276
  20.9 16.9 %collective-permute-start.3 = (bf16[416,768]{1,0:T(8,128)(2,1)}, bf16[416,768]{1,0:T(8,128)(2,1)S(1)}, u32[]{:S(2)}, u32[]{:S(2)}) collective-permute-start(bf16[416,768]{1,0:T(8,128)(2,1)} %get-tuple-element.17.f0), channel_id=1, source_target_pairs={{0,2},{2,4},{4,6},{6,0},{8,14},{10,8},{12,10},{14,12},{1,3},{3,5},... | collective-permute-start | bytes 1916936 | tf_op jit(solution)/shard_map/ppermute | solution.py:270
  23.3 0.7 copy-start.3
  26.4 17.1 %collective-permute-start.4 = (bf16[408,768]{1,0:T(8,128)(2,1)S(1)}, bf16[408,768]{1,0:T(8,128)(2,1)S(1)}, u32[]{:S(2)}, u32[]{:S(2)}) collective-permute-start(bf16[408,768]{1,0:T(8,128)(2,1)S(1)} %collective-permute-done.n1), channel_id=1, source_target_pairs={{0,2},{2,4},{4,6},{6,0},{8,14},{10,8},{12,10},{14,12},{1,3},{3,5},... | collective-permute-start | bytes 1880072 | tf_op jit(solution)/shard_map/ppermute | solution.py:270
  31.4 12.1 %collective-permute-start.5 = (bf16[400,768]{1,0:T(8,128)(2,1)S(1)}, bf16[400,768]{1,0:T(8,128)(2,1)S(1)}, u32[]{:S(2)}, u32[]{:S(2)}) collective-permute-start(bf16[400,768]{1,0:T(8,128)(2,1)S(1)} %slice.22), channel_id=1, source_target_pairs={{0,1},{1,0},{8,57},{9,24},{16,17},{17,16},{24,9},{25,40},{32,33},{... | collective-permute-start | bytes 1843208 | tf_op jit(solution)/shard_map/ppermute | solution.py:273
  33.4 8.9 %collective-permute-start.6 = (bf16[384,768]{1,0:T(8,128)(2,1)S(1)}, bf16[384,768]{1,0:T(8,128)(2,1)S(1)}, u32[]{:S(2)}, u32[]{:S(2)}) collective-permute-start(bf16[384,768]{1,0:T(8,128)(2,1)S(1)} %slice.23), channel_id=1, source_target_pairs={{0,8},{8,0},{1,9},{9,1},{2,10},{10,2},{3,11},{11,3},{4,12},{12,4},... | collective-permute-start | bytes 1769480 | tf_op jit(solution)/shard_map/ppermute | solution.py:276
  35.4 7.0 %collective-permute-start.7 = (bf16[384,768]{1,0:T(8,128)(2,1)S(1)}, bf16[384,768]{1,0:T(8,128)(2,1)S(1)}, u32[]{:S(2)}, u32[]{:S(2)}) collective-permute-start(bf16[384,768]{1,0:T(8,128)(2,1)S(1)} %slice.24), channel_id=1, source_target_pairs={{0,8},{8,0},{1,9},{9,1},{2,10},{10,2},{3,11},{11,3},{4,12},{12,4},... | collective-permute-start | bytes 1769480 | tf_op jit(solution)/shard_map/ppermute | solution.py:276
  37.8 14.2 %collective-permute-start.8 = (bf16[416,768]{1,0:T(8,128)(2,1)S(1)}, bf16[416,768]{1,0:T(8,128)(2,1)S(1)}, u32[]{:S(2)}, u32[]{:S(2)}) collective-permute-start(bf16[416,768]{1,0:T(8,128)(2,1)S(1)} %collective-permute-done.3.f1), channel_id=1, source_target_pairs={{0,1},{1,0},{8,57},{9,24},{16,17},{17,16},{24,9},{25,40},{32,33},{... | collective-permute-start | bytes 1916936 | tf_op jit(solution)/shard_map/ppermute | solution.py:273
  43.6 13.4 %collective-permute-start.9 = (bf16[400,768]{1,0:T(8,128)(2,1)S(1)}, bf16[400,768]{1,0:T(8,128)(2,1)S(1)}, u32[]{:S(2)}, u32[]{:S(2)}) collective-permute-start(bf16[400,768]{1,0:T(8,128)(2,1)S(1)} %slice.25), channel_id=1, source_target_pairs={{0,1},{1,0},{8,57},{9,24},{16,17},{17,16},{24,9},{25,40},{32,33},{... | collective-permute-start | bytes 1843208 | tf_op jit(solution)/shard_map/ppermute | solution.py:273
  45.5 15.3 %copy-start = (bf16[144,768]{1,0:T(8,128)(2,1)S(1)}, bf16[144,768]{1,0:T(8,128)(2,1)}, u32[]{:S(2)}) copy-start(bf16[144,768]{1,0:T(8,128)(2,1)} %front.1.start_ref) | copy-start | bytes 663556
  45.5 15.3 %copy-start.1 = (bf16[416,768]{1,0:T(8,128)(2,1)S(1)}, bf16[416,768]{1,0:T(8,128)(2,1)}, u32[]{:S(2)}) copy-start(bf16[416,768]{1,0:T(8,128)(2,1)} %get-tuple-element.17.f0) | copy-start | bytes 1916932
  45.6 15.3 %copy-start.2 = (bf16[408,768]{1,0:T(8,128)(2,1)S(1)}, bf16[408,768]{1,0:T(8,128)(2,1)}, u32[]{:S(2)}) copy-start(bf16[408,768]{1,0:T(8,128)(2,1)} %get-tuple-element.14.n0) | copy-start | bytes 1880068
  45.6 13.3 %collective-permute-start.10 = (bf16[400,768]{1,0:T(8,128)(2,1)S(1)}, bf16[400,768]{1,0:T(8,128)(2,1)S(1)}, u32[]{:S(2)}, u32[]{:S(2)}) collective-permute-start(bf16[400,768]{1,0:T(8,128)(2,1)S(1)} %slice.29), channel_id=1, source_target_pairs={{0,8},{8,0},{1,9},{9,1},{2,10},{10,2},{3,11},{11,3},{4,12},{12,4},... | collective-permute-start | bytes 1843208 | tf_op jit(solution)/shard_map/ppermute | solution.py:276
  47.6 11.3 %collective-permute-start.11 = (bf16[400,768]{1,0:T(8,128)(2,1)S(1)}, bf16[400,768]{1,0:T(8,128)(2,1)S(1)}, u32[]{:S(2)}, u32[]{:S(2)}) collective-permute-start(bf16[400,768]{1,0:T(8,128)(2,1)S(1)} %slice.25), channel_id=1, source_target_pairs={{0,8},{8,0},{1,9},{9,1},{2,10},{10,2},{3,11},{11,3},{4,12},{12,4},... | collective-permute-start | bytes 1843208 | tf_op jit(solution)/shard_map/ppermute | solution.py:276
  50.0 8.9 %collective-permute-start.12 = (bf16[400,768]{1,0:T(8,128)(2,1)S(1)}, bf16[400,768]{1,0:T(8,128)(2,1)S(1)}, u32[]{:S(2)}, u32[]{:S(2)}) collective-permute-start(bf16[400,768]{1,0:T(8,128)(2,1)S(1)} %collective-permute-done.5.n4), channel_id=1, source_target_pairs={{0,8},{8,0},{1,9},{9,1},{2,10},{10,2},{3,11},{11,3},{4,12},{12,4},... | collective-permute-start | bytes 1843208 | tf_op jit(solution)/shard_map/ppermute | solution.py:276
  52.0 6.9 %collective-permute-start.13 = (bf16[392,768]{1,0:T(8,128)(2,1)S(1)}, bf16[392,768]{1,0:T(8,128)(2,1)S(1)}, u32[]{:S(2)}, u32[]{:S(2)}) collective-permute-start(bf16[392,768]{1,0:T(8,128)(2,1)S(1)} %slice.30), channel_id=1, source_target_pairs={{0,8},{8,0},{1,9},{9,1},{2,10},{10,2},{3,11},{11,3},{4,12},{12,4},... | collective-permute-start | bytes 1806344 | tf_op jit(solution)/shard_map/ppermute | solution.py:276
  57.0 3.9 %collective-permute-start.14 = (bf16[384,768]{1,0:T(8,128)(2,1)S(1)}, bf16[384,768]{1,0:T(8,128)(2,1)S(1)}, u32[]{:S(2)}, u32[]{:S(2)}) collective-permute-start(bf16[384,768]{1,0:T(8,128)(2,1)S(1)} %slice.31), channel_id=1, source_target_pairs={{0,8},{8,0},{1,9},{9,1},{2,10},{10,2},{3,11},{11,3},{4,12},{12,4},... | collective-permute-start | bytes 1769480 | tf_op jit(solution)/shard_map/ppermute | solution.py:276
  149.5 8.0 %collective-permute-start.15 = (bf16[32,80,128]{2,1,0:T(8,128)(2,1)S(1)}, bf16[32,80,128]{2,1,0:T(8,128)(2,1)S(1)}, u32[]{:S(2)}, u32[]{:S(2)}) collective-permute-start(bf16[32,80,128]{2,1,0:T(8,128)(2,1)S(1)} %all_to_all.17.mine_ref), channel_id=1, source_target_pairs={{0,8},{8,0},{1,9},{9,1},{2,10},{10,2},{3,11},{11,3},{4,12},{12,4},... | collective-permute-start | bytes 1966088 | tf_op jit(solution)/shard_map/ppermute | solution.py:276

commit v7 on v6

--- a/solution.py
+++ b/solution.py
@@ -20,9 +20,9 @@
 TAPS = 16
 NEAR = H + TAPS + 8
 FAR = H + 2 * TAPS
-INROWS = T + 16
-HT = T // 2
-PAY = T + HT + 8
+START = 2 * T + 16
+PAY = T + 8
+ROWS = H * 6
 PEERS = 32
 CHUNK = 72
 CROWS = 80
@@ -51,18 +51,13 @@
     return section, lax.axis_index("c")
 
 
-def prep_kernel(w_ref, taps_ref, feat_ref, targ_ref, len_ref, near_ref, far_ref, io_ref, sem):
-    section, core = where_am_i()
-    utt = lax.rem(section, 4)
+def prep_kernel(w_ref, taps_ref, near_ref, far_ref, sem):
+    _, core = where_am_i()
     mine = pl.multiple_of(core * H, H)
     theirs = pl.multiple_of((1 - core) * H, H)
     copies = [
         pltpu.make_async_copy(w_ref.at[0, pl.ds(mine, H)], near_ref.at[pl.ds(0, H)], sem.at[0]),
         pltpu.make_async_copy(w_ref.at[0, pl.ds(theirs, H)], far_ref.at[pl.ds(0, H)], sem.at[1]),
-        pltpu.make_async_copy(
-            feat_ref.at[utt], io_ref.at[pl.ds(0, T), pl.ds(0, FEAT)], sem.at[2]),
-        pltpu.make_async_copy(
-            targ_ref.at[utt], io_ref.at[pl.ds(0, T), pl.ds(FEAT, D)], sem.at[3]),
     ]
     for copy in copies:
         copy.start()
@@ -73,25 +68,23 @@
     near_ref[H + TAPS:, :] = jnp.zeros((NEAR - H - TAPS, D), BF)
     far_ref[H:H + TAPS, :] = packed
     far_ref[H + TAPS:, :] = packed
-    count = len_ref[utt].astype(F32)
-    io_ref[T:, :] = jnp.full((INROWS - T, FEAT + D), count, F32).astype(BF)
     for copy in copies:
         copy.wait()
 
 
-def front_kernel(io_a_ref, io_b_ref, front_ref, out_ref):
-    section, core = where_am_i()
-    own = core == lax.div(section, 4)
-    pick = jnp.where(own, 1.0, 0.0).astype(F32)
-    io = io_a_ref[...].astype(F32) * pick + io_b_ref[...].astype(F32) * (1.0 - pick)
+def front_kernel(feat_ref, front_ref, targ_ref, len_ref, out_ref):
+    section, _ = where_am_i()
+    utt = lax.rem(section, 4)
     out_ref[0:T, :] = jnp.dot(
-        io[0:T, 0:FEAT].astype(BF), front_ref[...], preferred_element_type=F32).astype(BF)
-    out_ref[T:, :] = io[:, FEAT:].astype(BF)
+        feat_ref[utt], front_ref[...], preferred_element_type=F32).astype(BF)
+    out_ref[T:2 * T, :] = targ_ref[utt]
+    count = len_ref[utt].astype(F32)
+    out_ref[2 * T:, :] = jnp.full((START - 2 * T, D), count, F32).astype(BF)
 
 
 def model_kernel(
     start_ref,
-    n0, f0, n1, f1, n2, n3, n4, f4, n5, m1, g1, m2, m3, m4, g4, m5,
+    n0, f0, n1, f1, n2, n3, f3, n4, f4, n5, m1, g1, m2, m4, g4, m5,
     pay_ref,
     w_ref, traw_ref, taps_ref, inv_ref, norm_ref, slope_ref, act_ref, gpad_ref, g_ref,
     wsem, tsem,
@@ -115,7 +108,8 @@
                 piece.at[pl.ds(H, TAPS)], traw_ref.at[layer], tsem.at[layer]).start()
 
     for near, far, c, r, part in (
-        (n0, f0, col, row, core), (n1, f1, side, row, core), (n4, f4, side, flip, core),
+        (n0, f0, col, row, core), (n1, f1, side, row, core),
+        (n3, f3, col, flip, core), (n4, f4, side, flip, core),
     ):
         bring(near, c, r, part, False)
         bring(far, c, r, 1 - part, True)
@@ -123,9 +117,9 @@
     bring(g1, anti, row, core, True)
     bring(m4, anti, flip, other, True)
     bring(g4, anti, flip, core, False)
-    for near, mirror, c, r in ((n2, m2, across, row), (n3, m3, col, flip), (n5, m5, across, flip)):
-        bring(near, c, r, core, True)
-        bring(mirror, c, r, other, False)
+    for near, mirror, r in ((n2, m2, row), (n5, m5, flip)):
+        bring(near, across, r, core, True)
+        bring(mirror, across, r, other, False)
 
     count = start_ref[2 * T:, :].astype(F32)[0:1, 0:1]
     target = start_ref[T:2 * T, :].astype(F32)
@@ -165,15 +159,13 @@
 
     g_ref[...] = ((g_ref[...] - target) * mask / count).astype(BF).astype(F32)
 
-    share = pl.multiple_of(core * H, H)
+    first = section < 4
 
     def backward(i, carry):
         l = L - 1 - i
         g = g_ref[...]
         gb = g.astype(BF)
-        pay_ref[l, 0:T, :] = gb
-        pay_ref[l, T:T + HT, 0:H] = act_ref[l, 0:HT, pl.ds(share, H)]
-        pay_ref[l, T:T + HT, H:] = act_ref[l, HT:, pl.ds(share, H)]
+        pay_ref[l, 0:T, :] = jnp.where(first, act_ref[l].astype(F32), g).astype(BF)
         grad_act = lax.dot_general(
             gb, w_ref[l], (((1,), (1,)), ((), ())), preferred_element_type=F32)
         grad_conv = grad_act * slope_ref[l]
@@ -184,9 +176,9 @@
             rows.append(jnp.sum(grad_conv * norm_ref[l, 6 + k:T + 6 + k, :], axis=0, keepdims=True))
         total = jnp.concatenate(rows, axis=0)
         hi = total.astype(BF).astype(F32)
-        part = jnp.where(core == 0, hi, total - hi)
+        part = jnp.where(first, hi, total - hi)
         packed = jnp.concatenate([part, jnp.zeros((8 - KER, D), F32)], axis=0)
-        pay_ref[l, T + HT:, :] = packed.astype(BF)
+        pay_ref[l, T:, :] = packed.astype(BF)
         grad_norm = taps[0:1] * gpad_ref[10:T + 10, :]
         for k in range(1, KER):
             grad_norm = grad_norm + taps[k:k + 1] * gpad_ref[10 - k:T + 10 - k, :]
@@ -200,23 +192,29 @@
     lax.fori_loop(0, L, backward, 0, unroll=True)
 
 
-def grad_kernel(recv_ref, out_ref, act_ref, flat_ref, row_ref, chunk_ref):
-    half = T // 2
-    for i in range(L):
-        act_ref[i * T:i * T + half, :] = recv_ref[i, T:T + half, 0:H]
-        act_ref[i * T + half:(i + 1) * T, :] = recv_ref[i, T:T + half, H:]
-    g = recv_ref[:, 0:T, :].reshape(L * T, D)
-    grad = lax.dot_general(
-        act_ref[...], g, (((0,), (0,)), ((), ())), preferred_element_type=F32)
+def half_product(recv_ref, part, out_ref):
+    start = pl.multiple_of(part * H, H)
+    act = recv_ref[0:4, 0:T, pl.ds(start, H)].reshape(4 * T, H)
+    cot = recv_ref[4:8, 0:T, :].reshape(4 * T, D)
+    grad = lax.dot_general(act, cot, (((0,), (0,)), ((), ())), preferred_element_type=F32)
     for b in range(D // 128):
-        flat_ref[b * H:(b + 1) * H, :] = grad[:, b * 128:(b + 1) * 128]
-    taps = recv_ref[0, T + half:, :].astype(F32)
+        out_ref[b * H:(b + 1) * H, :] = grad[:, b * 128:(b + 1) * 128].astype(out_ref.dtype)
+
+
+def lend_kernel(recv_ref, out_ref):
+    half_product(recv_ref, 1 - lax.axis_index("c"), out_ref)
+
+
+def grad_kernel(recv_ref, lent_ref, out_ref, flat_ref, chunk_ref):
+    half_product(recv_ref, lax.axis_index("c"), flat_ref)
+    taps = recv_ref[0, T:, :].astype(F32)
     for i in range(1, L):
-        taps = taps + recv_ref[i, T + half:, :].astype(F32)
+        taps = taps + recv_ref[i, T:, :].astype(F32)
     total = taps[0:KER]
     hi = total.astype(BF).astype(F32)
     low = total - hi
     chunk_ref[CHUNK:, :] = jnp.zeros((CROWS - CHUNK, 128), F32)
+    flat_ref[...] = flat_ref[...] + lent_ref[...].astype(F32)
     for j in range(PEERS):
         chunk_ref[0:CHUNK, :] = flat_ref[j * CHUNK:(j + 1) * CHUNK, :]
         if j < KER * 6:
@@ -275,38 +273,34 @@
     def to_core(a):
         return lax.ppermute(a, "c", [(0, 1), (1, 0)])
 
-    near, far, io = pl.pallas_call(
+    near, far = pl.pallas_call(
         prep_kernel,
         name="prep",
-        out_shape=(
-            jax.ShapeDtypeStruct((NEAR, D), BF),
-            jax.ShapeDtypeStruct((FAR, D), BF),
-            jax.ShapeDtypeStruct((INROWS, FEAT + D), BF),
-        ),
-        in_specs=[ANY, VMEM, ANY, ANY, SMEM],
-        out_specs=(VMEM, VMEM, VMEM),
-        scratch_shapes=[pltpu.SemaphoreType.DMA((4,))],
-    )(pointwise, jnp.transpose(kernel, (1, 0, 2)), features, targets, lengths)
+        out_shape=(jax.ShapeDtypeStruct((NEAR, D), BF), jax.ShapeDtypeStruct((FAR, D), BF)),
+        in_specs=[ANY, VMEM],
+        out_specs=(VMEM, VMEM),
+        scratch_shapes=[pltpu.SemaphoreType.DMA((2,))],
+    )(pointwise, jnp.transpose(kernel, (1, 0, 2)))
     begin = pl.pallas_call(
         front_kernel,
         name="front",
-        out_shape=jax.ShapeDtypeStruct((2 * T + INROWS - T, D), BF),
-        in_specs=[VMEM, VMEM, VMEM],
-        out_specs=VMEM,
-    )(io, to_core(io), front_weight)
+        out_shape=jax.ShapeDtypeStruct((START, D), BF),
+        in_specs=[VMEM, VMEM, VMEM, SMEM],
+        out_specs=VMEM,
+    )(features, front_weight, targets, lengths)
 
     n1, n3, begin = lax.optimization_barrier((along_x(near), along_z(near), begin))
-    f1 = along_x(far)
+    f1, f3 = along_x(far), along_z(far)
     n2 = along_x(n1)
     n4 = along_z(n1[:H + TAPS])
-    f4 = along_z(f1)
-    m1, m3 = to_core(n1[:H]), to_core(n3[:H])
-    n2, n4, m1, m3 = lax.optimization_barrier((n2, n4, m1, m3))
+    f4 = along_x(f3)
+    m1 = to_core(n1[:H])
+    n2, n4, m1, f1 = lax.optimization_barrier((n2, n4, m1, f1))
     n5 = along_z(n2[:H + TAPS])
     g1, m2, m4 = to_core(f1[:H + TAPS]), to_core(n2[:H + TAPS]), to_core(n4)
     g4, m5 = to_core(f4[:H + 8]), to_core(n5[:H])
-    here = [near, far, n1, f1, n2, n3, n4, f4, n5]
-    there = [m1, g1, m2, m3, m4, g4, m5]
+    here = [near, far, n1, f1, n2, n3, f3, n4, f4, n5]
+    there = [m1, g1, m2, m4, g4, m5]
 
     payload = pl.pallas_call(
         model_kernel,
@@ -332,20 +326,23 @@
 
     received = lax.all_to_all(payload, ("x", "zl"), 0, 0)
 
+    lend = pl.pallas_call(
+        lend_kernel,
+        name="lend",
+        out_shape=jax.ShapeDtypeStruct((ROWS, 128), BF),
+        in_specs=[VMEM],
+        out_specs=VMEM,
+        compiler_params=params(24),
+    )(received)
     parts = pl.pallas_call(
         grad_kernel,
         name="grad",
         out_shape=jax.ShapeDtypeStruct((PEERS, CROWS, 128), BF),
-        in_specs=[VMEM],
-        out_specs=VMEM,
-        scratch_shapes=[
-            pltpu.VMEM((L * T, H), BF),
-            pltpu.VMEM((H * 6, 128), F32),
-            pltpu.VMEM((8, D), F32),
-            pltpu.VMEM((CROWS, 128), F32),
-        ],
+        in_specs=[VMEM, VMEM],
+        out_specs=VMEM,
+        scratch_shapes=[pltpu.VMEM((ROWS, 128), F32), pltpu.VMEM((CROWS, 128), F32)],
         compiler_params=params(24),
-    )(received)
+    )(received, to_core(lend))
 
     scattered = lax.all_to_all(parts, ("y", "zh"), 0, 0)
 

time: 159 us -> 159 us (level)
  waiting for transfers between devices: 7.41 us -> 13.9 us
  blocking collectives: 74.8 us -> 71 us
  starting transfers between devices: 54.1 us -> 51.6 us
    all_to_all x1, blocking collectives: 20.5 us -> 16.3 us  [body(): received = lax.all_to_all(payload, ('x', 'zl'), 0, 0)]
    ppermute x4, waiting for transfers between devices: 3.62 us -> 7.74 us  [along_z(): return lax.ppermute(a, ('zh', 'c', 'zl'), pair)]
    ppermute x4, starting transfers between devices: 19.1 us -> 16.4 us  [along_z(): return lax.ppermute(a, ('zh', 'c', 'zl'), pair)]
    ppermute x3 -> x4, starting transfers between devices: 11.8 us -> 13.7 us  [along_x(): return lax.ppermute(a, ('c', 'x'), ring)]
    ppermute x9 -> x8, starting transfers between devices: 23.3 us -> 21.5 us  [to_core(): return lax.ppermute(a, 'c', [(0, 1), (1, 0)])]
    ppermute x9 -> x8, waiting for transfers between devices: 3.65 us -> 5.27 us  [to_core(): return lax.ppermute(a, 'c', [(0, 1), (1, 0)])]
  transfers between devices with their start and end apart: 16 -> 16, of which waited for: 5 -> 6; matrix products, arithmetic and copies ran while one was open for 0% -> 0% of each run, Pallas kernels for 1% -> 1%
where the time goes in v7:
time: 159 us; the launch traced here: 158 us
  blocking collectives  71 us (45%)
  starting transfers between devices  51.6 us (32%)
  Pallas kernels  20.4 us (13%)
  waiting for transfers between devices  13.9 us (9%)
    all_to_all x1, blocking collectives, body(): scattered = lax.all_to_all(parts, ('y', 'zh'), 0, 0)  29.2 us
    all_to_all x1, blocking collectives, body(): half = lax.all_to_all(mine, ('y', 'zh'), 0, 0)  25.5 us
    ppermute x8, starting transfers between devices, to_core(): return lax.ppermute(a, 'c', [(0, 1), (1, 0)])  21.5 us
    ppermute x4, starting transfers between devices, along_z(): return lax.ppermute(a, ('zh', 'c', 'zl'), pair)  16.4 us
    all_to_all x1, blocking collectives, body(): received = lax.all_to_all(payload, ('x', 'zl'), 0, 0)  16.3 us
    ppermute x4, starting transfers between devices, along_x(): return lax.ppermute(a, ('c', 'x'), ring)  13.7 us
    pallas_call x1, Pallas kernels, body(): pl.pallas_call(model_kernel, name='model', out_shape=jax.ShapeDtypeStruct...  13 us
    ppermute x4, waiting for transfers between devices, along_z(): return lax.ppermute(a, ('zh', 'c', 'zl'), pair)  7.74 us
  transfers between devices with their start and end apart: 16, of which 6 were waited for; matrix products, arithmetic and copies ran while one was open for 0% of the time, Pallas kernels for 1%

profile of v7, /device:TPU:9, one launch (start us, length us, event | category | flops | bytes accessed | tf_op | source)
XLA Modules:
  0.0 158.0 jit_solution(4271325530726071921)
XLA Ops:
  0.6 3.0 %prep.1 = (bf16[408,768]{1,0:T(8,128)(2,1)}, bf16[416,768]{1,0:T(8,128)(2,1)}) custom-call(bf16[1,768,768]{2,1,0:T(8,128)(2,1)} %w_ref.1, f32[5,1,768]{2,1,0:T(1,128)} %bitcast.2), custom_call_target="tpu_custom_call" | custom-call | tf_op jit(solution)/shard_map/prep/pallas_call | solution.py:276
  3.7 10.7 %collective-permute-start.1 = (bf16[408,768]{1,0:T(8,128)(2,1)}, bf16[408,768]{1,0:T(8,128)(2,1)S(1)}, u32[]{:S(2)}, u32[]{:S(2)}) collective-permute-start(bf16[408,768]{1,0:T(8,128)(2,1)} %get-tuple-element.13.n0), channel_id=1, source_target_pairs={{0,1},{1,0},{8,57},{9,24},{16,17},{17,16},{24,9},{25,40},{32,33},{... | collective-permute-start | bytes 1880072 | tf_op jit(solution)/shard_map/ppermute | solution.py:271
  14.3 4.4 %collective-permute-start = (bf16[408,768]{1,0:T(8,128)(2,1)}, bf16[408,768]{1,0:T(8,128)(2,1)S(1)}, u32[]{:S(2)}, u32[]{:S(2)}) collective-permute-start(bf16[408,768]{1,0:T(8,128)(2,1)} %get-tuple-element.13.n0), channel_id=1, source_target_pairs={{0,2},{2,4},{4,6},{6,0},{8,14},{10,8},{12,10},{14,12},{1,3},{3,5},... | collective-permute-start | bytes 1880072 | tf_op jit(solution)/shard_map/ppermute | solution.py:268
  18.7 1.9 %collective-permute-start.6 = (bf16[416,768]{1,0:T(8,128)(2,1)}, bf16[416,768]{1,0:T(8,128)(2,1)S(1)}, u32[]{:S(2)}, u32[]{:S(2)}) collective-permute-start(bf16[416,768]{1,0:T(8,128)(2,1)} %get-tuple-element.15.f0), channel_id=1, source_target_pairs={{0,1},{1,0},{8,57},{9,24},{16,17},{17,16},{24,9},{25,40},{32,33},{... | collective-permute-start | bytes 1916936 | tf_op jit(solution)/shard_map/ppermute | solution.py:271
  20.7 2.5 %collective-permute-start.5 = (bf16[416,768]{1,0:T(8,128)(2,1)}, bf16[416,768]{1,0:T(8,128)(2,1)S(1)}, u32[]{:S(2)}, u32[]{:S(2)}) collective-permute-start(bf16[416,768]{1,0:T(8,128)(2,1)} %get-tuple-element.15.f0), channel_id=1, source_target_pairs={{0,2},{2,4},{4,6},{6,0},{8,14},{10,8},{12,10},{14,12},{1,3},{3,5},... | collective-permute-start | bytes 1916936 | tf_op jit(solution)/shard_map/ppermute | solution.py:268
  23.1 2.3 %front.1.start_ref = bf16[144,768]{1,0:T(8,128)(2,1)} custom-call(bf16[4,64,512]{2,1,0:T(8,128)(2,1)} %feat_ref.1, bf16[512,768]{1,0:T(8,128)(2,1)} %front_ref.1, bf16[4,64,768]{2,1,0:T(8,128)(2,1)} %targ_ref.1, s32[4]{0:T(128)} %len_ref.1), custom_call_target="tpu_custom_call" | custom-call | tf_op jit(solution)/shard_map/front/pallas_call | solution.py:284
  25.4 0.0 collective-permute-done.1.n3
  25.4 0.9 collective-permute-done.n1
  26.2 4.9 %collective-permute-start.2 = (bf16[408,768]{1,0:T(8,128)(2,1)S(1)}, bf16[408,768]{1,0:T(8,128)(2,1)S(1)}, u32[]{:S(2)}, u32[]{:S(2)}) collective-permute-start(bf16[408,768]{1,0:T(8,128)(2,1)S(1)} %collective-permute-done.n1), channel_id=1, source_target_pairs={{0,2},{2,4},{4,6},{6,0},{8,14},{10,8},{12,10},{14,12},{1,3},{3,5},... | collective-permute-start | bytes 1880072 | tf_op jit(solution)/shard_map/ppermute | solution.py:268
  31.2 1.9 %collective-permute-start.3 = (bf16[400,768]{1,0:T(8,128)(2,1)S(1)}, bf16[400,768]{1,0:T(8,128)(2,1)S(1)}, u32[]{:S(2)}, u32[]{:S(2)}) collective-permute-start(bf16[400,768]{1,0:T(8,128)(2,1)S(1)} %slice.19), channel_id=1, source_target_pairs={{0,1},{1,0},{8,57},{9,24},{16,17},{17,16},{24,9},{25,40},{32,33},{... | collective-permute-start | bytes 1843208 | tf_op jit(solution)/shard_map/ppermute | solution.py:271
  33.2 1.9 %collective-permute-start.4 = (bf16[384,768]{1,0:T(8,128)(2,1)S(1)}, bf16[384,768]{1,0:T(8,128)(2,1)S(1)}, u32[]{:S(2)}, u32[]{:S(2)}) collective-permute-start(bf16[384,768]{1,0:T(8,128)(2,1)S(1)} %slice.20), channel_id=1, source_target_pairs={{0,8},{8,0},{1,9},{9,1},{2,10},{10,2},{3,11},{11,3},{4,12},{12,4},... | collective-permute-start | bytes 1769480 | tf_op jit(solution)/shard_map/ppermute | solution.py:274
  35.1 0.0 collective-permute-done.6.f3
  35.1 1.9 %collective-permute-start.7 = (bf16[416,768]{1,0:T(8,128)(2,1)S(1)}, bf16[416,768]{1,0:T(8,128)(2,1)S(1)}, u32[]{:S(2)}, u32[]{:S(2)}) collective-permute-start(bf16[416,768]{1,0:T(8,128)(2,1)S(1)} %collective-permute-done.6.f3), channel_id=1, source_target_pairs={{0,2},{2,4},{4,6},{6,0},{8,14},{10,8},{12,10},{14,12},{1,3},{3,5},... | collective-permute-start | bytes 1916936 | tf_op jit(solution)/shard_map/ppermute | solution.py:268
  37.1 0.0 collective-permute-done.5.f1
  37.1 0.0 collective-permute-done.4.m1
  37.1 6.5 %collective-permute-done.3.n4 = bf16[400,768]{1,0:T(8,128)(2,1)S(1)} collective-permute-done((bf16[400,768]{1,0:T(8,128)(2,1)S(1)}, bf16[400,768]{1,0:T(8,128)(2,1)S(1)}, u32[]{:S(2)}, u32[]{:S(2)}) %collective-permute-start.3) | collective-permute-done | bytes 614432 | tf_op jit(solution)/shard_map/ppermute | solution.py:271
  43.6 0.0 collective-permute-done.2.n2
  43.7 1.9 %collective-permute-start.8 = (bf16[400,768]{1,0:T(8,128)(2,1)S(1)}, bf16[400,768]{1,0:T(8,128)(2,1)S(1)}, u32[]{:S(2)}, u32[]{:S(2)}) collective-permute-start(bf16[400,768]{1,0:T(8,128)(2,1)S(1)} %slice.21), channel_id=1, source_target_pairs={{0,1},{1,0},{8,57},{9,24},{16,17},{17,16},{24,9},{25,40},{32,33},{... | collective-permute-start | bytes 1843208 | tf_op jit(solution)/shard_map/ppermute | solution.py:271
  45.6 1.9 %collective-permute-start.10 = (bf16[400,768]{1,0:T(8,128)(2,1)S(1)}, bf16[400,768]{1,0:T(8,128)(2,1)S(1)}, u32[]{:S(2)}, u32[]{:S(2)}) collective-permute-start(bf16[400,768]{1,0:T(8,128)(2,1)S(1)} %slice.21), channel_id=1, source_target_pairs={{0,8},{8,0},{1,9},{9,1},{2,10},{10,2},{3,11},{11,3},{4,12},{12,4},... | collective-permute-start | bytes 1843208 | tf_op jit(solution)/shard_map/ppermute | solution.py:274
  47.6 0.0 copy-start
  47.6 0.0 copy-start.1
  47.6 0.0 copy-start.2
  47.6 2.5 %collective-permute-start.9 = (bf16[400,768]{1,0:T(8,128)(2,1)S(1)}, bf16[400,768]{1,0:T(8,128)(2,1)S(1)}, u32[]{:S(2)}, u32[]{:S(2)}) collective-permute-start(bf16[400,768]{1,0:T(8,128)(2,1)S(1)} %slice.22), channel_id=1, source_target_pairs={{0,8},{8,0},{1,9},{9,1},{2,10},{10,2},{3,11},{11,3},{4,12},{12,4},... | collective-permute-start | bytes 1843208 | tf_op jit(solution)/shard_map/ppermute | solution.py:274
  50.1 1.9 %collective-permute-start.11 = (bf16[400,768]{1,0:T(8,128)(2,1)S(1)}, bf16[400,768]{1,0:T(8,128)(2,1)S(1)}, u32[]{:S(2)}, u32[]{:S(2)}) collective-permute-start(bf16[400,768]{1,0:T(8,128)(2,1)S(1)} %collective-permute-done.3.n4), channel_id=1, source_target_pairs={{0,8},{8,0},{1,9},{9,1},{2,10},{10,2},{3,11},{11,3},{4,12},{12,4},... | collective-permute-start | bytes 1843208 | tf_op jit(solution)/shard_map/ppermute | solution.py:274
  52.1 0.0 collective-permute-done.7.f4
  52.1 2.4 %collective-permute-start.12 = (bf16[392,768]{1,0:T(8,128)(2,1)S(1)}, bf16[392,768]{1,0:T(8,128)(2,1)S(1)}, u32[]{:S(2)}, u32[]{:S(2)}) collective-permute-start(bf16[392,768]{1,0:T(8,128)(2,1)S(1)} %slice.25), channel_id=1, source_target_pairs={{0,8},{8,0},{1,9},{9,1},{2,10},{10,2},{3,11},{11,3},{4,12},{12,4},... | collective-permute-start | bytes 1806344 | tf_op jit(solution)/shard_map/ppermute | solution.py:274
  54.5 1.2 collective-permute-done.8.n5
  55.8 1.9 %collective-permute-start.13 = (bf16[384,768]{1,0:T(8,128)(2,1)S(1)}, bf16[384,768]{1,0:T(8,128)(2,1)S(1)}, u32[]{:S(2)}, u32[]{:S(2)}) collective-permute-start(bf16[384,768]{1,0:T(8,128)(2,1)S(1)} %slice.26), channel_id=1, source_target_pairs={{0,8},{8,0},{1,9},{9,1},{2,10},{10,2},{3,11},{11,3},{4,12},{12,4},... | collective-permute-start | bytes 1769480 | tf_op jit(solution)/shard_map/ppermute | solution.py:274
  57.7 0.0 collective-permute-done.9.g1
  57.7 0.0 collective-permute-done.10.m2
  57.8 0.0 collective-permute-done.11.m4
  57.8 0.0 collective-permute-done.12.g4
  57.8 1.9 %collective-permute-done.13.m5 = bf16[384,768]{1,0:T(8,128)(2,1)S(1)} collective-permute-done((bf16[384,768]{1,0:T(8,128)(2,1)S(1)}, bf16[384,768]{1,0:T(8,128)(2,1)S(1)}, u32[]{:S(2)}, u32[]{:S(2)}) %collective-permute-start.13) | collective-permute-done | bytes 589856 | tf_op jit(solution)/shard_map/ppermute | solution.py:274
  59.7 0.0 copy-done
  59.7 0.0 copy-done.1
  59.7 0.0 copy-done.2
  59.7 13.0 %model.1 = bf16[8,72,768]{2,1,0:T(8,128)(2,1)S(1)} custom-call(bf16[144,768]{1,0:T(8,128)(2,1)S(1)} %copy-done, bf16[408,768]{1,0:T(8,128)(2,1)S(1)} %copy-done.2, bf16[416,768]{1,0:T(8,128)(2,1)S(1)} %copy-done.1, bf16[408,768]{1,0:T(8,128)(2,1)S(1)} %collective-permute-done.n1, bf16[416,768]{1,0:T(8,128)(2,1)S(1)} %collective-permute-done.5.f1, ...), custom_call_target="tpu_custom_call" | custom-call | tf_op jit(solution)/shard_map/model/pallas_call | solution.py:305
  72.8 16.3 %all_to_all.15.recv_ref = bf16[8,72,768]{2,1,0:T(8,128)(2,1)S(1)} all-to-all(bf16[8,72,768]{2,1,0:T(8,128)(2,1)S(1)} %model.1), channel_id=1, replica_groups=mesh['y'=8,'zh'=4,'c'=2,'x'=4,'zl'=2] {'x','zl'}, dimensions={0} | all-to-all | bytes 1769472 | tf_op jit(solution)/shard_map/all_to_all | solution.py:327
  89.1 0.4 lend.1
  89.5 3.0 %collective-permute-start.14 = (bf16[2304,128]{1,0:T(8,128)(2,1)S(1)}, bf16[2304,128]{1,0:T(8,128)(2,1)S(1)}, u32[]{:S(2)}, u32[]{:S(2)}) collective-permute-start(bf16[2304,128]{1,0:T(8,128)(2,1)S(1)} %lend.1), channel_id=1, source_target_pairs={{0,8},{8,0},{1,9},{9,1},{2,10},{10,2},{3,11},{11,3},{4,12},{12,4},... | collective-permute-start | bytes 1769480 | tf_op jit(solution)/shard_map/ppermute | solution.py:274
  92.5 1.6 %collective-permute-done.14.lent_ref = bf16[2304,128]{1,0:T(8,128)(2,1)S(1)} collective-permute-done((bf16[2304,128]{1,0:T(8,128)(2,1)S(1)}, bf16[2304,128]{1,0:T(8,128)(2,1)S(1)}, u32[]{:S(2)}, u32[]{:S(2)}) %collective-permute-start.14) | collective-permute-done | bytes 589856 | tf_op jit(solution)/shard_map/ppermute | solution.py:274
  94.1 0.4 grad.1
  94.5 29.2 %all_to_all.16.parts_ref = bf16[32,80,128]{2,1,0:T(8,128)(2,1)S(1)} all-to-all(bf16[32,80,128]{2,1,0:T(8,128)(2,1)S(1)} %grad.1), channel_id=1, replica_groups=mesh['y'=8,'zh'=4,'c'=2,'x'=4,'zl'=2] {'y','zh'}, dimensions={0} | all-to-all | bytes 1310720 | tf_op jit(solution)/shard_map/all_to_all | solution.py:347
  123.7 0.1 total.1
  123.8 25.5 %all_to_all.17.mine_ref = bf16[32,80,128]{2,1,0:T(8,128)(2,1)S(1)} all-to-all(bf16[32,80,128]{2,1,0:T(8,128)(2,1)S(1)} %total.1), channel_id=1, replica_groups=mesh['y'=8,'zh'=4,'c'=2,'x'=4,'zl'=2] {'y','zh'}, dimensions={0} | all-to-all | bytes 1310720 | tf_op jit(solution)/shard_map/all_to_all | solution.py:359
  149.3 5.8 %collective-permute-start.15 = (bf16[32,80,128]{2,1,0:T(8,128)(2,1)S(1)}, bf16[32,80,128]{2,1,0:T(8,128)(2,1)S(1)}, u32[]{:S(2)}, u32[]{:S(2)}) collective-permute-start(bf16[32,80,128]{2,1,0:T(8,128)(2,1)S(1)} %all_to_all.17.mine_ref), channel_id=1, source_target_pairs={{0,8},{8,0},{1,9},{9,1},{2,10},{10,2},{3,11},{11,3},{4,12},{12,4},... | collective-permute-start | bytes 1966088 | tf_op jit(solution)/shard_map/ppermute | solution.py:274
  155.1 1.7 %collective-permute-done.15.theirs_ref = bf16[32,80,128]{2,1,0:T(8,128)(2,1)S(1)} collective-permute-done((bf16[32,80,128]{2,1,0:T(8,128)(2,1)S(1)}, bf16[32,80,128]{2,1,0:T(8,128)(2,1)S(1)}, u32[]{:S(2)}, u32[]{:S(2)}) %collective-permute-start.15) | collective-permute-done | bytes 655392 | tf_op jit(solution)/shard_map/ppermute | solution.py:274
  156.8 1.2 place.1
  (6 shorter events, 0.2 us)
Async XLA Ops:
  3.7 21.7 %collective-permute-start.1 = (bf16[408,768]{1,0:T(8,128)(2,1)}, bf16[408,768]{1,0:T(8,128)(2,1)S(1)}, u32[]{:S(2)}, u32[]{:S(2)}) collective-permute-start(bf16[408,768]{1,0:T(8,128)(2,1)} %get-tuple-element.13.n0), channel_id=1, source_target_pairs={{0,1},{1,0},{8,57},{9,24},{16,17},{17,16},{24,9},{25,40},{32,33},{... | collective-permute-start | bytes 1880072 | tf_op jit(solution)/shard_map/ppermute | solution.py:271
  14.3 11.9 %collective-permute-start = (bf16[408,768]{1,0:T(8,128)(2,1)}, bf16[408,768]{1,0:T(8,128)(2,1)S(1)}, u32[]{:S(2)}, u32[]{:S(2)}) collective-permute-start(bf16[408,768]{1,0:T(8,128)(2,1)} %get-tuple-element.13.n0), channel_id=1, source_target_pairs={{0,2},{2,4},{4,6},{6,0},{8,14},{10,8},{12,10},{14,12},{1,3},{3,5},... | collective-permute-start | bytes 1880072 | tf_op jit(solution)/shard_map/ppermute | solution.py:268
  18.7 16.4 %collective-permute-start.6 = (bf16[416,768]{1,0:T(8,128)(2,1)}, bf16[416,768]{1,0:T(8,128)(2,1)S(1)}, u32[]{:S(2)}, u32[]{:S(2)}) collective-permute-start(bf16[416,768]{1,0:T(8,128)(2,1)} %get-tuple-element.15.f0), channel_id=1, source_target_pairs={{0,1},{1,0},{8,57},{9,24},{16,17},{17,16},{24,9},{25,40},{32,33},{... | collective-permute-start | bytes 1916936 | tf_op jit(solution)/shard_map/ppermute | solution.py:271
  20.7 16.4 %collective-permute-start.5 = (bf16[416,768]{1,0:T(8,128)(2,1)}, bf16[416,768]{1,0:T(8,128)(2,1)S(1)}, u32[]{:S(2)}, u32[]{:S(2)}) collective-permute-start(bf16[416,768]{1,0:T(8,128)(2,1)} %get-tuple-element.15.f0), channel_id=1, source_target_pairs={{0,2},{2,4},{4,6},{6,0},{8,14},{10,8},{12,10},{14,12},{1,3},{3,5},... | collective-permute-start | bytes 1916936 | tf_op jit(solution)/shard_map/ppermute | solution.py:268
  26.2 17.4 %collective-permute-start.2 = (bf16[408,768]{1,0:T(8,128)(2,1)S(1)}, bf16[408,768]{1,0:T(8,128)(2,1)S(1)}, u32[]{:S(2)}, u32[]{:S(2)}) collective-permute-start(bf16[408,768]{1,0:T(8,128)(2,1)S(1)} %collective-permute-done.n1), channel_id=1, source_target_pairs={{0,2},{2,4},{4,6},{6,0},{8,14},{10,8},{12,10},{14,12},{1,3},{3,5},... | collective-permute-start | bytes 1880072 | tf_op jit(solution)/shard_map/ppermute | solution.py:268
  31.2 12.4 %collective-permute-start.3 = (bf16[400,768]{1,0:T(8,128)(2,1)S(1)}, bf16[400,768]{1,0:T(8,128)(2,1)S(1)}, u32[]{:S(2)}, u32[]{:S(2)}) collective-permute-start(bf16[400,768]{1,0:T(8,128)(2,1)S(1)} %slice.19), channel_id=1, source_target_pairs={{0,1},{1,0},{8,57},{9,24},{16,17},{17,16},{24,9},{25,40},{32,33},{... | collective-permute-start | bytes 1843208 | tf_op jit(solution)/shard_map/ppermute | solution.py:271
  33.2 3.9 %collective-permute-start.4 = (bf16[384,768]{1,0:T(8,128)(2,1)S(1)}, bf16[384,768]{1,0:T(8,128)(2,1)S(1)}, u32[]{:S(2)}, u32[]{:S(2)}) collective-permute-start(bf16[384,768]{1,0:T(8,128)(2,1)S(1)} %slice.20), channel_id=1, source_target_pairs={{0,8},{8,0},{1,9},{9,1},{2,10},{10,2},{3,11},{11,3},{4,12},{12,4},... | collective-permute-start | bytes 1769480 | tf_op jit(solution)/shard_map/ppermute | solution.py:274
  35.1 16.9 %collective-permute-start.7 = (bf16[416,768]{1,0:T(8,128)(2,1)S(1)}, bf16[416,768]{1,0:T(8,128)(2,1)S(1)}, u32[]{:S(2)}, u32[]{:S(2)}) collective-permute-start(bf16[416,768]{1,0:T(8,128)(2,1)S(1)} %collective-permute-done.6.f3), channel_id=1, source_target_pairs={{0,2},{2,4},{4,6},{6,0},{8,14},{10,8},{12,10},{14,12},{1,3},{3,5},... | collective-permute-start | bytes 1916936 | tf_op jit(solution)/shard_map/ppermute | solution.py:268
  43.7 12.1 %collective-permute-start.8 = (bf16[400,768]{1,0:T(8,128)(2,1)S(1)}, bf16[400,768]{1,0:T(8,128)(2,1)S(1)}, u32[]{:S(2)}, u32[]{:S(2)}) collective-permute-start(bf16[400,768]{1,0:T(8,128)(2,1)S(1)} %slice.21), channel_id=1, source_target_pairs={{0,1},{1,0},{8,57},{9,24},{16,17},{17,16},{24,9},{25,40},{32,33},{... | collective-permute-start | bytes 1843208 | tf_op jit(solution)/shard_map/ppermute | solution.py:271
  45.6 12.2 %collective-permute-start.10 = (bf16[400,768]{1,0:T(8,128)(2,1)S(1)}, bf16[400,768]{1,0:T(8,128)(2,1)S(1)}, u32[]{:S(2)}, u32[]{:S(2)}) collective-permute-start(bf16[400,768]{1,0:T(8,128)(2,1)S(1)} %slice.21), channel_id=1, source_target_pairs={{0,8},{8,0},{1,9},{9,1},{2,10},{10,2},{3,11},{11,3},{4,12},{12,4},... | collective-permute-start | bytes 1843208 | tf_op jit(solution)/shard_map/ppermute | solution.py:274
  47.6 12.1 %copy-start = (bf16[144,768]{1,0:T(8,128)(2,1)S(1)}, bf16[144,768]{1,0:T(8,128)(2,1)}, u32[]{:S(2)}) copy-start(bf16[144,768]{1,0:T(8,128)(2,1)} %front.1.start_ref) | copy-start | bytes 663556
  47.6 12.1 %copy-start.1 = (bf16[416,768]{1,0:T(8,128)(2,1)S(1)}, bf16[416,768]{1,0:T(8,128)(2,1)}, u32[]{:S(2)}) copy-start(bf16[416,768]{1,0:T(8,128)(2,1)} %get-tuple-element.15.f0) | copy-start | bytes 1916932
  47.6 12.1 %copy-start.2 = (bf16[408,768]{1,0:T(8,128)(2,1)S(1)}, bf16[408,768]{1,0:T(8,128)(2,1)}, u32[]{:S(2)}) copy-start(bf16[408,768]{1,0:T(8,128)(2,1)} %get-tuple-element.13.n0) | copy-start | bytes 1880068
  47.6 10.1 %collective-permute-start.9 = (bf16[400,768]{1,0:T(8,128)(2,1)S(1)}, bf16[400,768]{1,0:T(8,128)(2,1)S(1)}, u32[]{:S(2)}, u32[]{:S(2)}) collective-permute-start(bf16[400,768]{1,0:T(8,128)(2,1)S(1)} %slice.22), channel_id=1, source_target_pairs={{0,8},{8,0},{1,9},{9,1},{2,10},{10,2},{3,11},{11,3},{4,12},{12,4},... | collective-permute-start | bytes 1843208 | tf_op jit(solution)/shard_map/ppermute | solution.py:274
  50.1 7.6 %collective-permute-start.11 = (bf16[400,768]{1,0:T(8,128)(2,1)S(1)}, bf16[400,768]{1,0:T(8,128)(2,1)S(1)}, u32[]{:S(2)}, u32[]{:S(2)}) collective-permute-start(bf16[400,768]{1,0:T(8,128)(2,1)S(1)} %collective-permute-done.3.n4), channel_id=1, source_target_pairs={{0,8},{8,0},{1,9},{9,1},{2,10},{10,2},{3,11},{11,3},{4,12},{12,4},... | collective-permute-start | bytes 1843208 | tf_op jit(solution)/shard_map/ppermute | solution.py:274
  52.1 5.6 %collective-permute-start.12 = (bf16[392,768]{1,0:T(8,128)(2,1)S(1)}, bf16[392,768]{1,0:T(8,128)(2,1)S(1)}, u32[]{:S(2)}, u32[]{:S(2)}) collective-permute-start(bf16[392,768]{1,0:T(8,128)(2,1)S(1)} %slice.25), channel_id=1, source_target_pairs={{0,8},{8,0},{1,9},{9,1},{2,10},{10,2},{3,11},{11,3},{4,12},{12,4},... | collective-permute-start | bytes 1806344 | tf_op jit(solution)/shard_map/ppermute | solution.py:274
  55.8 3.9 %collective-permute-start.13 = (bf16[384,768]{1,0:T(8,128)(2,1)S(1)}, bf16[384,768]{1,0:T(8,128)(2,1)S(1)}, u32[]{:S(2)}, u32[]{:S(2)}) collective-permute-start(bf16[384,768]{1,0:T(8,128)(2,1)S(1)} %slice.26), channel_id=1, source_target_pairs={{0,8},{8,0},{1,9},{9,1},{2,10},{10,2},{3,11},{11,3},{4,12},{12,4},... | collective-permute-start | bytes 1769480 | tf_op jit(solution)/shard_map/ppermute | solution.py:274
  89.5 4.6 %collective-permute-start.14 = (bf16[2304,128]{1,0:T(8,128)(2,1)S(1)}, bf16[2304,128]{1,0:T(8,128)(2,1)S(1)}, u32[]{:S(2)}, u32[]{:S(2)}) collective-permute-start(bf16[2304,128]{1,0:T(8,128)(2,1)S(1)} %lend.1), channel_id=1, source_target_pairs={{0,8},{8,0},{1,9},{9,1},{2,10},{10,2},{3,11},{11,3},{4,12},{12,4},... | collective-permute-start | bytes 1769480 | tf_op jit(solution)/shard_map/ppermute | solution.py:274
  149.3 7.5 %collective-permute-start.15 = (bf16[32,80,128]{2,1,0:T(8,128)(2,1)S(1)}, bf16[32,80,128]{2,1,0:T(8,128)(2,1)S(1)}, u32[]{:S(2)}, u32[]{:S(2)}) collective-permute-start(bf16[32,80,128]{2,1,0:T(8,128)(2,1)S(1)} %all_to_all.17.mine_ref), channel_id=1, source_target_pairs={{0,8},{8,0},{1,9},{9,1},{2,10},{10,2},{3,11},{11,3},{4,12},{12,4},... | collective-permute-start | bytes 1966088 | tf_op jit(solution)/shard_map/ppermute | solution.py:274

commit v8 on v7

--- a/solution.py
+++ b/solution.py
@@ -1,3 +1,4 @@
+import functools
 import itertools
 
 import jax
@@ -27,6 +28,7 @@
 CHUNK = 72
 CROWS = 80
 MIB = 1024 * 1024
+BLOCKS = [slice(i, i + H) for i in range(0, D, H)]
 
 VMEM = pl.BlockSpec(memory_space=pltpu.VMEM)
 ANY = pl.BlockSpec(memory_space=pl.ANY)
@@ -51,25 +53,17 @@
     return section, lax.axis_index("c")
 
 
-def prep_kernel(w_ref, taps_ref, near_ref, far_ref, sem):
-    _, core = where_am_i()
-    mine = pl.multiple_of(core * H, H)
-    theirs = pl.multiple_of((1 - core) * H, H)
-    copies = [
-        pltpu.make_async_copy(w_ref.at[0, pl.ds(mine, H)], near_ref.at[pl.ds(0, H)], sem.at[0]),
-        pltpu.make_async_copy(w_ref.at[0, pl.ds(theirs, H)], far_ref.at[pl.ds(0, H)], sem.at[1]),
-    ]
-    for copy in copies:
-        copy.start()
+def prep_kernel(far, w_ref, taps_ref, out_ref, sem):
+    core = lax.axis_index("c")
+    part = pl.multiple_of((1 - core if far else core) * H, H)
+    copy = pltpu.make_async_copy(w_ref.at[0, pl.ds(part, H)], out_ref.at[pl.ds(0, H)], sem)
+    copy.start()
     taps = jnp.concatenate([taps_ref[k] for k in range(KER)], axis=0)
     hi, mid, low = split3(taps)
     packed = jnp.concatenate([hi, mid, low, jnp.zeros((1, D), F32)], axis=0).astype(BF)
-    near_ref[H:H + TAPS, :] = packed
-    near_ref[H + TAPS:, :] = jnp.zeros((NEAR - H - TAPS, D), BF)
-    far_ref[H:H + TAPS, :] = packed
-    far_ref[H + TAPS:, :] = packed
-    for copy in copies:
-        copy.wait()
+    out_ref[H:H + TAPS, :] = packed
+    out_ref[H + TAPS:, :] = jnp.zeros((out_ref.shape[0] - H - TAPS, D), BF)
+    copy.wait()
 
 
 def front_kernel(feat_ref, front_ref, targ_ref, len_ref, out_ref):
@@ -84,7 +78,7 @@
 
 def model_kernel(
     start_ref,
-    n0, f0, n1, f1, n2, n3, f3, n4, f4, n5, m1, g1, m2, m4, g4, m5,
+    n0, f0, n1, f1, n2, n3, f3, n4, f4, n5, m1, m2, g4, m5,
     pay_ref,
     w_ref, traw_ref, taps_ref, inv_ref, norm_ref, slope_ref, act_ref, gpad_ref, g_ref,
     wsem, tsem,
@@ -98,28 +92,28 @@
     across = lax.rem(col + 2, 4)
     flip = 1 - row
 
-    def bring(piece, c, r, part, with_taps):
+    def bring(piece, first, c, r, part, taps_at):
         layer = 2 * c + r
         start = pl.multiple_of(part * H, H)
         pltpu.make_async_copy(
-            piece.at[pl.ds(0, H)], w_ref.at[layer, pl.ds(start, H)], wsem.at[layer]).start()
-        if with_taps:
+            piece.at[pl.ds(first, H)], w_ref.at[layer, pl.ds(start, H)], wsem.at[layer]).start()
+        if taps_at is not None:
             pltpu.make_async_copy(
-                piece.at[pl.ds(H, TAPS)], traw_ref.at[layer], tsem.at[layer]).start()
-
-    for near, far, c, r, part in (
-        (n0, f0, col, row, core), (n1, f1, side, row, core),
-        (n3, f3, col, flip, core), (n4, f4, side, flip, core),
+                piece.at[pl.ds(taps_at, TAPS)], traw_ref.at[layer], tsem.at[layer]).start()
+
+    for near, far, c, r in (
+        (n0, f0, col, row), (n1, f1, side, row), (n3, f3, col, flip), (n4, f4, side, flip),
     ):
-        bring(near, c, r, part, False)
-        bring(far, c, r, 1 - part, True)
-    bring(m1, anti, row, other, False)
-    bring(g1, anti, row, core, True)
-    bring(m4, anti, flip, other, True)
-    bring(g4, anti, flip, core, False)
-    for near, mirror, r in ((n2, m2, row), (n5, m5, flip)):
-        bring(near, across, r, core, True)
-        bring(mirror, across, r, other, False)
+        bring(near, 0, c, r, core, H)
+        bring(far, 0, c, r, other, None)
+    bring(m1, 0, anti, row, other, H)
+    bring(m1, H + TAPS, anti, row, core, None)
+    bring(m2, H, anti, flip, other, 2 * H)
+    bring(g4, 0, anti, flip, core, None)
+    bring(n2, 0, across, row, core, H)
+    bring(m2, 0, across, row, other, None)
+    bring(n5, 0, across, flip, core, H)
+    bring(m5, 0, across, flip, other, None)
 
     count = start_ref[2 * T:, :].astype(F32)[0:1, 0:1]
     target = start_ref[T:2 * T, :].astype(F32)
@@ -139,19 +133,21 @@
         taps_ref[l, 0:KER, :] = taps
         vals = g_ref[...]
         inv = lax.rsqrt(jnp.mean(vals * vals, axis=-1, keepdims=True) + EPS)
-        norm = vals * (inv * mask)
         inv_ref[l] = jnp.broadcast_to(inv, (T, 128))
+        scale = inv * mask
         norm_ref[l, 0:8, :] = edge
         norm_ref[l, T + 8:, :] = edge
-        norm_ref[l, 8:T + 8, :] = norm
-        conv = taps[0:1] * norm_ref[l, 6:T + 6, :]
-        for k in range(1, KER):
-            conv = conv + taps[k:k + 1] * norm_ref[l, 6 + k:T + 6 + k, :]
-        sig = jax.nn.sigmoid(conv)
-        act = (conv * sig).astype(BF)
-        slope_ref[l] = sig * (1.0 + conv * (1.0 - sig))
-        act_ref[l] = act
-        out = vals + jnp.dot(act, w_ref[l], preferred_element_type=F32)
+        out = vals
+        for block in BLOCKS:
+            norm_ref[l, 8:T + 8, block] = vals[:, block] * scale
+            conv = taps[0:1, block] * norm_ref[l, 6:T + 6, block]
+            for k in range(1, KER):
+                conv = conv + taps[k:k + 1, block] * norm_ref[l, 6 + k:T + 6 + k, block]
+            sig = jax.nn.sigmoid(conv)
+            act = (conv * sig).astype(BF)
+            slope_ref[l, :, block] = sig * (1.0 + conv * (1.0 - sig))
+            act_ref[l, :, block] = act
+            out = out + jnp.dot(act, w_ref[l, block, :], preferred_element_type=F32)
         g_ref[...] = out.astype(BF).astype(F32)
         return carry
 
@@ -166,27 +162,35 @@
         g = g_ref[...]
         gb = g.astype(BF)
         pay_ref[l, 0:T, :] = jnp.where(first, act_ref[l].astype(F32), g).astype(BF)
-        grad_act = lax.dot_general(
-            gb, w_ref[l], (((1,), (1,)), ((), ())), preferred_element_type=F32)
-        grad_conv = grad_act * slope_ref[l]
-        gpad_ref[8:T + 8, :] = grad_conv
+        inv = inv_ref[l][:, 0:1]
         taps = taps_ref[l, 0:KER, :]
-        rows = []
-        for k in range(KER):
-            rows.append(jnp.sum(grad_conv * norm_ref[l, 6 + k:T + 6 + k, :], axis=0, keepdims=True))
-        total = jnp.concatenate(rows, axis=0)
-        hi = total.astype(BF).astype(F32)
-        part = jnp.where(first, hi, total - hi)
-        packed = jnp.concatenate([part, jnp.zeros((8 - KER, D), F32)], axis=0)
-        pay_ref[l, T:, :] = packed.astype(BF)
-        grad_norm = taps[0:1] * gpad_ref[10:T + 10, :]
-        for k in range(1, KER):
-            grad_norm = grad_norm + taps[k:k + 1] * gpad_ref[10 - k:T + 10 - k, :]
-        grad_norm = grad_norm * mask
-        inv = inv_ref[l][:, 0:1]
-        norm = norm_ref[l, 8:T + 8, :]
-        mean = jnp.mean(grad_norm * norm, axis=-1, keepdims=True)
-        g_ref[...] = (g + inv * (grad_norm - norm * mean)).astype(BF).astype(F32)
+        grads, mean = [], 0.0
+        for block in BLOCKS:
+            grad_act = lax.dot_general(
+                gb, w_ref[l, block, :], (((1,), (1,)), ((), ())), preferred_element_type=F32)
+            grad_conv = grad_act * slope_ref[l, :, block]
+            gpad_ref[8:T + 8, block] = grad_conv
+            rows = []
+            for k in range(KER):
+                rows.append(jnp.sum(
+                    grad_conv * norm_ref[l, 6 + k:T + 6 + k, block], axis=0, keepdims=True))
+            total = jnp.concatenate(rows, axis=0)
+            hi = total.astype(BF).astype(F32)
+            part = jnp.where(first, hi, total - hi)
+            part = jnp.concatenate([part, jnp.zeros((8 - KER, part.shape[1]), F32)], axis=0)
+            pay_ref[l, T:, block] = part.astype(BF)
+            grad_norm = taps[0:1, block] * gpad_ref[10:T + 10, block]
+            for k in range(1, KER):
+                grad_norm = grad_norm + taps[k:k + 1, block] * gpad_ref[10 - k:T + 10 - k, block]
+            grad_norm = grad_norm * mask
+            grads.append(grad_norm)
+            mean = mean + jnp.sum(
+                grad_norm * norm_ref[l, 8:T + 8, block], axis=-1, keepdims=True)
+        mean = mean * (1.0 / D)
+        for block, grad_norm in zip(BLOCKS, grads):
+            norm = norm_ref[l, 8:T + 8, block]
+            g_ref[:, block] = (
+                g[:, block] + inv * (grad_norm - norm * mean)).astype(BF).astype(F32)
         return carry
 
     lax.fori_loop(0, L, backward, 0, unroll=True)
@@ -273,14 +277,19 @@
     def to_core(a):
         return lax.ppermute(a, "c", [(0, 1), (1, 0)])
 
-    near, far = pl.pallas_call(
-        prep_kernel,
-        name="prep",
-        out_shape=(jax.ShapeDtypeStruct((NEAR, D), BF), jax.ShapeDtypeStruct((FAR, D), BF)),
-        in_specs=[ANY, VMEM],
-        out_specs=(VMEM, VMEM),
-        scratch_shapes=[pltpu.SemaphoreType.DMA((2,))],
-    )(pointwise, jnp.transpose(kernel, (1, 0, 2)))
+    flat_taps = jnp.transpose(kernel, (1, 0, 2))
+
+    def prepare(far, rows):
+        return pl.pallas_call(
+            functools.partial(prep_kernel, far),
+            name="far" if far else "near",
+            out_shape=jax.ShapeDtypeStruct((rows, D), BF),
+            in_specs=[ANY, VMEM],
+            out_specs=VMEM,
+            scratch_shapes=[pltpu.SemaphoreType.DMA],
+        )(pointwise, flat_taps)
+
+    near, far = prepare(False, NEAR), prepare(True, FAR)
     begin = pl.pallas_call(
         front_kernel,
         name="front",
@@ -294,19 +303,19 @@
     n2 = along_x(n1)
     n4 = along_z(n1[:H + TAPS])
     f4 = along_x(f3)
-    m1 = to_core(n1[:H])
-    n2, n4, m1, f1 = lax.optimization_barrier((n2, n4, m1, f1))
-    n5 = along_z(n2[:H + TAPS])
-    g1, m2, m4 = to_core(f1[:H + TAPS]), to_core(n2[:H + TAPS]), to_core(n4)
+    n2, n4, f1 = lax.optimization_barrier((n2, n4, f1))
+    n5 = along_z(n2)
+    m1 = to_core(jnp.concatenate([n1[:H + TAPS], f1[:H]], axis=0))
+    m2 = to_core(jnp.concatenate([n2[:H], n4], axis=0))
     g4, m5 = to_core(f4[:H + 8]), to_core(n5[:H])
     here = [near, far, n1, f1, n2, n3, f3, n4, f4, n5]
-    there = [m1, g1, m2, m4, g4, m5]
+    there = [m1, m2, g4, m5]
 
     payload = pl.pallas_call(
         model_kernel,
         name="model",
         out_shape=jax.ShapeDtypeStruct((L, PAY, D), BF),
-        in_specs=[VMEM] + [ANY] * 16,
+        in_specs=[VMEM] + [ANY] * 14,
         out_specs=VMEM,
         scratch_shapes=[
             pltpu.VMEM((L, D, D), BF),

time: 159 us -> 159 us (level)
  blocking collectives: 71 us -> 73.2 us
  waiting for transfers between devices: 13.9 us -> 11.8 us
    ppermute x4, starting transfers between devices: 16.4 us -> 21.7 us  [along_z(): return lax.ppermute(a, ('zh', 'c', 'zl'), pair)]
    ppermute x8 -> x6, starting transfers between devices: 21.5 us -> 17.4 us  [to_core(): return lax.ppermute(a, 'c', [(0, 1), (1, 0)])]
    ppermute x4, starting transfers between devices: 13.7 us -> 11.2 us  [along_x(): return lax.ppermute(a, ('c', 'x'), ring)]
    pallas_call x1 -> x2, Pallas kernels: 3.02 us -> 5.27 us  [prepare(): pl.pallas_call(functools.partial(prep_kernel, far), name='far' if far els...]
    all_to_all x1, blocking collectives: 29.2 us -> 30.8 us  [body(): scattered = lax.all_to_all(parts, ('y', 'zh'), 0, 0)]
    ppermute x8 -> x6, waiting for transfers between devices: 5.27 us -> 5.26 us  [to_core(): return lax.ppermute(a, 'c', [(0, 1), (1, 0)])]
  transfers between devices with their start and end apart: 16 -> 14, of which waited for: 6 -> 5; matrix products, arithmetic and copies ran while one was open for 0% -> 0% of each run, Pallas kernels for 1% -> 3%
where the time goes in v8:
time: 159 us; the launch traced here: 158 us
  blocking collectives  73.2 us (46%)
  starting transfers between devices  50.2 us (32%)
  Pallas kernels  21.6 us (14%)
  waiting for transfers between devices  11.8 us (7%)
    all_to_all x1, blocking collectives, body(): scattered = lax.all_to_all(parts, ('y', 'zh'), 0, 0)  30.8 us
    all_to_all x1, blocking collectives, body(): half = lax.all_to_all(mine, ('y', 'zh'), 0, 0)  25.4 us
    ppermute x4, starting transfers between devices, along_z(): return lax.ppermute(a, ('zh', 'c', 'zl'), pair)  21.7 us
    ppermute x6, starting transfers between devices, to_core(): return lax.ppermute(a, 'c', [(0, 1), (1, 0)])  17.4 us
    all_to_all x1, blocking collectives, body(): received = lax.all_to_all(payload, ('x', 'zl'), 0, 0)  17 us
    pallas_call x1, Pallas kernels, body(): pl.pallas_call(model_kernel, name='model', out_shape=jax.ShapeDtypeStruct...  12 us
    ppermute x4, starting transfers between devices, along_x(): return lax.ppermute(a, ('c', 'x'), ring)  11.2 us
    ppermute x4, waiting for transfers between devices, along_z(): return lax.ppermute(a, ('zh', 'c', 'zl'), pair)  6.57 us
  transfers between devices with their start and end apart: 14, of which 5 were waited for; matrix products, arithmetic and copies ran while one was open for 0% of the time, Pallas kernels for 3%

profile of v8, /device:TPU:9, one launch (start us, length us, event | category | flops | bytes accessed | tf_op | source)
XLA Modules:
  0.0 158.2 jit_solution(2298863282281285163)
XLA Ops:
  0.6 2.6 %near.1.n0 = bf16[408,768]{1,0:T(8,128)(2,1)} custom-call(bf16[1,768,768]{2,1,0:T(8,128)(2,1)} %w_ref.3, f32[5,1,768]{2,1,0:T(1,128)} %bitcast.2), custom_call_target="tpu_custom_call" | custom-call | tf_op jit(solution)/shard_map/near/pallas_call | solution.py:283
  3.3 4.4 %collective-permute-start = (bf16[408,768]{1,0:T(8,128)(2,1)}, bf16[408,768]{1,0:T(8,128)(2,1)S(1)}, u32[]{:S(2)}, u32[]{:S(2)}) collective-permute-start(bf16[408,768]{1,0:T(8,128)(2,1)} %near.1.n0), channel_id=1, source_target_pairs={{0,2},{2,4},{4,6},{6,0},{8,14},{10,8},{12,10},{14,12},{1,3},{3,5},... | collective-permute-start | bytes 1880072 | tf_op jit(solution)/shard_map/ppermute | solution.py:272
  7.7 10.7 %collective-permute-start.1 = (bf16[408,768]{1,0:T(8,128)(2,1)}, bf16[408,768]{1,0:T(8,128)(2,1)S(1)}, u32[]{:S(2)}, u32[]{:S(2)}) collective-permute-start(bf16[408,768]{1,0:T(8,128)(2,1)} %near.1.n0), channel_id=1, source_target_pairs={{0,1},{1,0},{8,57},{9,24},{16,17},{17,16},{24,9},{25,40},{32,33},{... | collective-permute-start | bytes 1880072 | tf_op jit(solution)/shard_map/ppermute | solution.py:275
  18.3 2.6 %far.1.f0 = bf16[416,768]{1,0:T(8,128)(2,1)} custom-call(bf16[1,768,768]{2,1,0:T(8,128)(2,1)} %w_ref.3, f32[5,1,768]{2,1,0:T(1,128)} %bitcast.3), custom_call_target="tpu_custom_call" | custom-call | tf_op jit(solution)/shard_map/far/pallas_call | solution.py:283
  21.0 1.9 %collective-permute-start.5 = (bf16[416,768]{1,0:T(8,128)(2,1)}, bf16[416,768]{1,0:T(8,128)(2,1)S(1)}, u32[]{:S(2)}, u32[]{:S(2)}) collective-permute-start(bf16[416,768]{1,0:T(8,128)(2,1)} %far.1.f0), channel_id=1, source_target_pairs={{0,1},{1,0},{8,57},{9,24},{16,17},{17,16},{24,9},{25,40},{32,33},{... | collective-permute-start | bytes 1916936 | tf_op jit(solution)/shard_map/ppermute | solution.py:275
  22.9 2.5 %collective-permute-start.4 = (bf16[416,768]{1,0:T(8,128)(2,1)}, bf16[416,768]{1,0:T(8,128)(2,1)S(1)}, u32[]{:S(2)}, u32[]{:S(2)}) collective-permute-start(bf16[416,768]{1,0:T(8,128)(2,1)} %far.1.f0), channel_id=1, source_target_pairs={{0,2},{2,4},{4,6},{6,0},{8,14},{10,8},{12,10},{14,12},{1,3},{3,5},... | collective-permute-start | bytes 1916936 | tf_op jit(solution)/shard_map/ppermute | solution.py:272
  25.4 2.3 %front.1.start_ref = bf16[144,768]{1,0:T(8,128)(2,1)} custom-call(bf16[4,64,512]{2,1,0:T(8,128)(2,1)} %feat_ref.1, bf16[512,768]{1,0:T(8,128)(2,1)} %front_ref.1, bf16[4,64,768]{2,1,0:T(8,128)(2,1)} %targ_ref.1, s32[4]{0:T(128)} %len_ref.1), custom_call_target="tpu_custom_call" | custom-call | tf_op jit(solution)/shard_map/front/pallas_call | solution.py:293
  27.7 0.0 collective-permute-done.n1
  27.7 0.0 collective-permute-done.1.n3
  27.7 2.2 %collective-permute-start.2 = (bf16[408,768]{1,0:T(8,128)(2,1)S(1)}, bf16[408,768]{1,0:T(8,128)(2,1)S(1)}, u32[]{:S(2)}, u32[]{:S(2)}) collective-permute-start(bf16[408,768]{1,0:T(8,128)(2,1)S(1)} %collective-permute-done.n1), channel_id=1, source_target_pairs={{0,2},{2,4},{4,6},{6,0},{8,14},{10,8},{12,10},{14,12},{1,3},{3,5},... | collective-permute-start | bytes 1880072 | tf_op jit(solution)/shard_map/ppermute | solution.py:272
  29.9 4.6 %collective-permute-start.3 = (bf16[400,768]{1,0:T(8,128)(2,1)S(1)}, bf16[400,768]{1,0:T(8,128)(2,1)S(1)}, u32[]{:S(2)}, u32[]{:S(2)}) collective-permute-start(bf16[400,768]{1,0:T(8,128)(2,1)S(1)} %slice.16), channel_id=1, source_target_pairs={{0,1},{1,0},{8,57},{9,24},{16,17},{17,16},{24,9},{25,40},{32,33},{... | collective-permute-start | bytes 1843208 | tf_op jit(solution)/shard_map/ppermute | solution.py:275
  34.5 0.0 collective-permute-done.5.f3
  34.5 2.2 %collective-permute-start.6 = (bf16[416,768]{1,0:T(8,128)(2,1)S(1)}, bf16[416,768]{1,0:T(8,128)(2,1)S(1)}, u32[]{:S(2)}, u32[]{:S(2)}) collective-permute-start(bf16[416,768]{1,0:T(8,128)(2,1)S(1)} %collective-permute-done.5.f3), channel_id=1, source_target_pairs={{0,2},{2,4},{4,6},{6,0},{8,14},{10,8},{12,10},{14,12},{1,3},{3,5},... | collective-permute-start | bytes 1916936 | tf_op jit(solution)/shard_map/ppermute | solution.py:272
  36.6 0.0 collective-permute-done.4.f1
  36.7 5.6 %collective-permute-done.3.n4 = bf16[400,768]{1,0:T(8,128)(2,1)S(1)} collective-permute-done((bf16[400,768]{1,0:T(8,128)(2,1)S(1)}, bf16[400,768]{1,0:T(8,128)(2,1)S(1)}, u32[]{:S(2)}, u32[]{:S(2)}) %collective-permute-start.3) | collective-permute-done | bytes 614432 | tf_op jit(solution)/shard_map/ppermute | solution.py:275
  42.3 0.0 collective-permute-done.2.n2
  42.3 4.6 %collective-permute-start.7 = (bf16[408,768]{1,0:T(8,128)(2,1)S(1)}, bf16[408,768]{1,0:T(8,128)(2,1)S(1)}, u32[]{:S(2)}, u32[]{:S(2)}) collective-permute-start(bf16[408,768]{1,0:T(8,128)(2,1)S(1)} %collective-permute-done.2.n2), channel_id=1, source_target_pairs={{0,1},{1,0},{8,57},{9,24},{16,17},{17,16},{24,9},{25,40},{32,33},{... | collective-permute-start | bytes 1880072 | tf_op jit(solution)/shard_map/ppermute | solution.py:275
  46.9 0.1 pad_maximum_fusion.1
  47.0 1.9 %collective-permute-start.9 = (bf16[784,768]{1,0:T(8,128)(2,1)S(1)}, bf16[784,768]{1,0:T(8,128)(2,1)S(1)}, u32[]{:S(2)}, u32[]{:S(2)}) collective-permute-start(bf16[784,768]{1,0:T(8,128)(2,1)S(1)} %pad_maximum_fusion.1), channel_id=1, source_target_pairs={{0,8},{8,0},{1,9},{9,1},{2,10},{10,2},{3,11},{11,3},{4,12},{12,4},... | collective-permute-start | bytes 3612680 | tf_op jit(solution)/shard_map/ppermute | solution.py:278
  49.0 0.1 pad_maximum_fusion
  49.1 0.0 copy-start
  49.1 0.0 copy-start.1
  49.1 0.0 copy-start.2
  49.1 2.5 %collective-permute-start.8 = (bf16[784,768]{1,0:T(8,128)(2,1)S(1)}, bf16[784,768]{1,0:T(8,128)(2,1)S(1)}, u32[]{:S(2)}, u32[]{:S(2)}) collective-permute-start(bf16[784,768]{1,0:T(8,128)(2,1)S(1)} %pad_maximum_fusion), channel_id=1, source_target_pairs={{0,8},{8,0},{1,9},{9,1},{2,10},{10,2},{3,11},{11,3},{4,12},{12,4},... | collective-permute-start | bytes 3612680 | tf_op jit(solution)/shard_map/ppermute | solution.py:278
  51.6 0.0 collective-permute-done.6.f4
  51.7 1.9 %collective-permute-start.10 = (bf16[392,768]{1,0:T(8,128)(2,1)S(1)}, bf16[392,768]{1,0:T(8,128)(2,1)S(1)}, u32[]{:S(2)}, u32[]{:S(2)}) collective-permute-start(bf16[392,768]{1,0:T(8,128)(2,1)S(1)} %slice.21), channel_id=1, source_target_pairs={{0,8},{8,0},{1,9},{9,1},{2,10},{10,2},{3,11},{11,3},{4,12},{12,4},... | collective-permute-start | bytes 1806344 | tf_op jit(solution)/shard_map/ppermute | solution.py:278
  53.6 0.9 collective-permute-done.7.n5
  54.6 1.9 %collective-permute-start.11 = (bf16[384,768]{1,0:T(8,128)(2,1)S(1)}, bf16[384,768]{1,0:T(8,128)(2,1)S(1)}, u32[]{:S(2)}, u32[]{:S(2)}) collective-permute-start(bf16[384,768]{1,0:T(8,128)(2,1)S(1)} %slice.22), channel_id=1, source_target_pairs={{0,8},{8,0},{1,9},{9,1},{2,10},{10,2},{3,11},{11,3},{4,12},{12,4},... | collective-permute-start | bytes 1769480 | tf_op jit(solution)/shard_map/ppermute | solution.py:278
  56.5 0.0 collective-permute-done.10.g4
  56.5 0.0 collective-permute-done.9.m2
  56.6 0.0 collective-permute-done.8.m1
  56.6 1.9 %collective-permute-done.11.m5 = bf16[384,768]{1,0:T(8,128)(2,1)S(1)} collective-permute-done((bf16[384,768]{1,0:T(8,128)(2,1)S(1)}, bf16[384,768]{1,0:T(8,128)(2,1)S(1)}, u32[]{:S(2)}, u32[]{:S(2)}) %collective-permute-start.11) | collective-permute-done | bytes 589856 | tf_op jit(solution)/shard_map/ppermute | solution.py:278
  58.5 0.0 copy-done
  58.5 0.0 copy-done.1
  58.5 0.0 copy-done.2
  58.5 12.0 %model.1 = bf16[8,72,768]{2,1,0:T(8,128)(2,1)S(1)} custom-call(bf16[144,768]{1,0:T(8,128)(2,1)S(1)} %copy-done.2, bf16[408,768]{1,0:T(8,128)(2,1)S(1)} %copy-done.1, bf16[416,768]{1,0:T(8,128)(2,1)S(1)} %copy-done, bf16[408,768]{1,0:T(8,128)(2,1)S(1)} %collective-permute-done.n1, bf16[416,768]{1,0:T(8,128)(2,1)S(1)} %collective-permute-done.4.f1, ...), custom_call_target="tpu_custom_call" | custom-call | tf_op jit(solution)/shard_map/model/pallas_call | solution.py:314
  70.5 17.0 %all_to_all.15.recv_ref = bf16[8,72,768]{2,1,0:T(8,128)(2,1)S(1)} all-to-all(bf16[8,72,768]{2,1,0:T(8,128)(2,1)S(1)} %model.1), channel_id=1, replica_groups=mesh['y'=8,'zh'=4,'c'=2,'x'=4,'zl'=2] {'x','zl'}, dimensions={0} | all-to-all | bytes 1769472 | tf_op jit(solution)/shard_map/all_to_all | solution.py:336
  87.5 0.4 lend.1
  87.9 3.2 %collective-permute-start.12 = (bf16[2304,128]{1,0:T(8,128)(2,1)S(1)}, bf16[2304,128]{1,0:T(8,128)(2,1)S(1)}, u32[]{:S(2)}, u32[]{:S(2)}) collective-permute-start(bf16[2304,128]{1,0:T(8,128)(2,1)S(1)} %lend.1), channel_id=1, source_target_pairs={{0,8},{8,0},{1,9},{9,1},{2,10},{10,2},{3,11},{11,3},{4,12},{12,4},... | collective-permute-start | bytes 1769480 | tf_op jit(solution)/shard_map/ppermute | solution.py:278
  91.1 1.6 %collective-permute-done.12.lent_ref = bf16[2304,128]{1,0:T(8,128)(2,1)S(1)} collective-permute-done((bf16[2304,128]{1,0:T(8,128)(2,1)S(1)}, bf16[2304,128]{1,0:T(8,128)(2,1)S(1)}, u32[]{:S(2)}, u32[]{:S(2)}) %collective-permute-start.12) | collective-permute-done | bytes 589856 | tf_op jit(solution)/shard_map/ppermute | solution.py:278
  92.7 0.4 grad.1
  93.1 30.8 %all_to_all.16.parts_ref = bf16[32,80,128]{2,1,0:T(8,128)(2,1)S(1)} all-to-all(bf16[32,80,128]{2,1,0:T(8,128)(2,1)S(1)} %grad.1), channel_id=1, replica_groups=mesh['y'=8,'zh'=4,'c'=2,'x'=4,'zl'=2] {'y','zh'}, dimensions={0} | all-to-all | bytes 1310720 | tf_op jit(solution)/shard_map/all_to_all | solution.py:356
  123.9 0.1 total.1
  124.1 25.4 %all_to_all.17.mine_ref = bf16[32,80,128]{2,1,0:T(8,128)(2,1)S(1)} all-to-all(bf16[32,80,128]{2,1,0:T(8,128)(2,1)S(1)} %total.1), channel_id=1, replica_groups=mesh['y'=8,'zh'=4,'c'=2,'x'=4,'zl'=2] {'y','zh'}, dimensions={0} | all-to-all | bytes 1310720 | tf_op jit(solution)/shard_map/all_to_all | solution.py:368
  149.5 5.8 %collective-permute-start.13 = (bf16[32,80,128]{2,1,0:T(8,128)(2,1)S(1)}, bf16[32,80,128]{2,1,0:T(8,128)(2,1)S(1)}, u32[]{:S(2)}, u32[]{:S(2)}) collective-permute-start(bf16[32,80,128]{2,1,0:T(8,128)(2,1)S(1)} %all_to_all.17.mine_ref), channel_id=1, source_target_pairs={{0,8},{8,0},{1,9},{9,1},{2,10},{10,2},{3,11},{11,3},{4,12},{12,4},... | collective-permute-start | bytes 1966088 | tf_op jit(solution)/shard_map/ppermute | solution.py:278
  155.3 1.7 %collective-permute-done.13.theirs_ref = bf16[32,80,128]{2,1,0:T(8,128)(2,1)S(1)} collective-permute-done((bf16[32,80,128]{2,1,0:T(8,128)(2,1)S(1)}, bf16[32,80,128]{2,1,0:T(8,128)(2,1)S(1)}, u32[]{:S(2)}, u32[]{:S(2)}) %collective-permute-start.13) | collective-permute-done | bytes 655392 | tf_op jit(solution)/shard_map/ppermute | solution.py:278
  157.0 1.2 place.1
  (5 shorter events, 0.2 us)
Async XLA Ops:
  3.3 24.4 %collective-permute-start = (bf16[408,768]{1,0:T(8,128)(2,1)}, bf16[408,768]{1,0:T(8,128)(2,1)S(1)}, u32[]{:S(2)}, u32[]{:S(2)}) collective-permute-start(bf16[408,768]{1,0:T(8,128)(2,1)} %near.1.n0), channel_id=1, source_target_pairs={{0,2},{2,4},{4,6},{6,0},{8,14},{10,8},{12,10},{14,12},{1,3},{3,5},... | collective-permute-start | bytes 1880072 | tf_op jit(solution)/shard_map/ppermute | solution.py:272
  7.7 20.0 %collective-permute-start.1 = (bf16[408,768]{1,0:T(8,128)(2,1)}, bf16[408,768]{1,0:T(8,128)(2,1)S(1)}, u32[]{:S(2)}, u32[]{:S(2)}) collective-permute-start(bf16[408,768]{1,0:T(8,128)(2,1)} %near.1.n0), channel_id=1, source_target_pairs={{0,1},{1,0},{8,57},{9,24},{16,17},{17,16},{24,9},{25,40},{32,33},{... | collective-permute-start | bytes 1880072 | tf_op jit(solution)/shard_map/ppermute | solution.py:275
  21.0 13.5 %collective-permute-start.5 = (bf16[416,768]{1,0:T(8,128)(2,1)}, bf16[416,768]{1,0:T(8,128)(2,1)S(1)}, u32[]{:S(2)}, u32[]{:S(2)}) collective-permute-start(bf16[416,768]{1,0:T(8,128)(2,1)} %far.1.f0), channel_id=1, source_target_pairs={{0,1},{1,0},{8,57},{9,24},{16,17},{17,16},{24,9},{25,40},{32,33},{... | collective-permute-start | bytes 1916936 | tf_op jit(solution)/shard_map/ppermute | solution.py:275
  22.9 13.7 %collective-permute-start.4 = (bf16[416,768]{1,0:T(8,128)(2,1)}, bf16[416,768]{1,0:T(8,128)(2,1)S(1)}, u32[]{:S(2)}, u32[]{:S(2)}) collective-permute-start(bf16[416,768]{1,0:T(8,128)(2,1)} %far.1.f0), channel_id=1, source_target_pairs={{0,2},{2,4},{4,6},{6,0},{8,14},{10,8},{12,10},{14,12},{1,3},{3,5},... | collective-permute-start | bytes 1916936 | tf_op jit(solution)/shard_map/ppermute | solution.py:272
  27.7 14.6 %collective-permute-start.2 = (bf16[408,768]{1,0:T(8,128)(2,1)S(1)}, bf16[408,768]{1,0:T(8,128)(2,1)S(1)}, u32[]{:S(2)}, u32[]{:S(2)}) collective-permute-start(bf16[408,768]{1,0:T(8,128)(2,1)S(1)} %collective-permute-done.n1), channel_id=1, source_target_pairs={{0,2},{2,4},{4,6},{6,0},{8,14},{10,8},{12,10},{14,12},{1,3},{3,5},... | collective-permute-start | bytes 1880072 | tf_op jit(solution)/shard_map/ppermute | solution.py:272
  29.9 12.4 %collective-permute-start.3 = (bf16[400,768]{1,0:T(8,128)(2,1)S(1)}, bf16[400,768]{1,0:T(8,128)(2,1)S(1)}, u32[]{:S(2)}, u32[]{:S(2)}) collective-permute-start(bf16[400,768]{1,0:T(8,128)(2,1)S(1)} %slice.16), channel_id=1, source_target_pairs={{0,1},{1,0},{8,57},{9,24},{16,17},{17,16},{24,9},{25,40},{32,33},{... | collective-permute-start | bytes 1843208 | tf_op jit(solution)/shard_map/ppermute | solution.py:275
  34.5 17.2 %collective-permute-start.6 = (bf16[416,768]{1,0:T(8,128)(2,1)S(1)}, bf16[416,768]{1,0:T(8,128)(2,1)S(1)}, u32[]{:S(2)}, u32[]{:S(2)}) collective-permute-start(bf16[416,768]{1,0:T(8,128)(2,1)S(1)} %collective-permute-done.5.f3), channel_id=1, source_target_pairs={{0,2},{2,4},{4,6},{6,0},{8,14},{10,8},{12,10},{14,12},{1,3},{3,5},... | collective-permute-start | bytes 1916936 | tf_op jit(solution)/shard_map/ppermute | solution.py:272
  42.3 12.2 %collective-permute-start.7 = (bf16[408,768]{1,0:T(8,128)(2,1)S(1)}, bf16[408,768]{1,0:T(8,128)(2,1)S(1)}, u32[]{:S(2)}, u32[]{:S(2)}) collective-permute-start(bf16[408,768]{1,0:T(8,128)(2,1)S(1)} %collective-permute-done.2.n2), channel_id=1, source_target_pairs={{0,1},{1,0},{8,57},{9,24},{16,17},{17,16},{24,9},{25,40},{32,33},{... | collective-permute-start | bytes 1880072 | tf_op jit(solution)/shard_map/ppermute | solution.py:275
  47.0 9.5 %collective-permute-start.9 = (bf16[784,768]{1,0:T(8,128)(2,1)S(1)}, bf16[784,768]{1,0:T(8,128)(2,1)S(1)}, u32[]{:S(2)}, u32[]{:S(2)}) collective-permute-start(bf16[784,768]{1,0:T(8,128)(2,1)S(1)} %pad_maximum_fusion.1), channel_id=1, source_target_pairs={{0,8},{8,0},{1,9},{9,1},{2,10},{10,2},{3,11},{11,3},{4,12},{12,4},... | collective-permute-start | bytes 3612680 | tf_op jit(solution)/shard_map/ppermute | solution.py:278
  49.1 9.4 %copy-start = (bf16[416,768]{1,0:T(8,128)(2,1)S(1)}, bf16[416,768]{1,0:T(8,128)(2,1)}, u32[]{:S(2)}) copy-start(bf16[416,768]{1,0:T(8,128)(2,1)} %far.1.f0) | copy-start | bytes 1916932
  49.1 9.4 %copy-start.1 = (bf16[408,768]{1,0:T(8,128)(2,1)S(1)}, bf16[408,768]{1,0:T(8,128)(2,1)}, u32[]{:S(2)}) copy-start(bf16[408,768]{1,0:T(8,128)(2,1)} %near.1.n0) | copy-start | bytes 1880068
  49.1 9.4 %copy-start.2 = (bf16[144,768]{1,0:T(8,128)(2,1)S(1)}, bf16[144,768]{1,0:T(8,128)(2,1)}, u32[]{:S(2)}) copy-start(bf16[144,768]{1,0:T(8,128)(2,1)} %front.1.start_ref) | copy-start | bytes 663556
  49.1 7.5 %collective-permute-start.8 = (bf16[784,768]{1,0:T(8,128)(2,1)S(1)}, bf16[784,768]{1,0:T(8,128)(2,1)S(1)}, u32[]{:S(2)}, u32[]{:S(2)}) collective-permute-start(bf16[784,768]{1,0:T(8,128)(2,1)S(1)} %pad_maximum_fusion), channel_id=1, source_target_pairs={{0,8},{8,0},{1,9},{9,1},{2,10},{10,2},{3,11},{11,3},{4,12},{12,4},... | collective-permute-start | bytes 3612680 | tf_op jit(solution)/shard_map/ppermute | solution.py:278
  51.7 4.8 %collective-permute-start.10 = (bf16[392,768]{1,0:T(8,128)(2,1)S(1)}, bf16[392,768]{1,0:T(8,128)(2,1)S(1)}, u32[]{:S(2)}, u32[]{:S(2)}) collective-permute-start(bf16[392,768]{1,0:T(8,128)(2,1)S(1)} %slice.21), channel_id=1, source_target_pairs={{0,8},{8,0},{1,9},{9,1},{2,10},{10,2},{3,11},{11,3},{4,12},{12,4},... | collective-permute-start | bytes 1806344 | tf_op jit(solution)/shard_map/ppermute | solution.py:278
  54.6 3.9 %collective-permute-start.11 = (bf16[384,768]{1,0:T(8,128)(2,1)S(1)}, bf16[384,768]{1,0:T(8,128)(2,1)S(1)}, u32[]{:S(2)}, u32[]{:S(2)}) collective-permute-start(bf16[384,768]{1,0:T(8,128)(2,1)S(1)} %slice.22), channel_id=1, source_target_pairs={{0,8},{8,0},{1,9},{9,1},{2,10},{10,2},{3,11},{11,3},{4,12},{12,4},... | collective-permute-start | bytes 1769480 | tf_op jit(solution)/shard_map/ppermute | solution.py:278
  87.9 4.8 %collective-permute-start.12 = (bf16[2304,128]{1,0:T(8,128)(2,1)S(1)}, bf16[2304,128]{1,0:T(8,128)(2,1)S(1)}, u32[]{:S(2)}, u32[]{:S(2)}) collective-permute-start(bf16[2304,128]{1,0:T(8,128)(2,1)S(1)} %lend.1), channel_id=1, source_target_pairs={{0,8},{8,0},{1,9},{9,1},{2,10},{10,2},{3,11},{11,3},{4,12},{12,4},... | collective-permute-start | bytes 1769480 | tf_op jit(solution)/shard_map/ppermute | solution.py:278
  149.5 7.5 %collective-permute-start.13 = (bf16[32,80,128]{2,1,0:T(8,128)(2,1)S(1)}, bf16[32,80,128]{2,1,0:T(8,128)(2,1)S(1)}, u32[]{:S(2)}, u32[]{:S(2)}) collective-permute-start(bf16[32,80,128]{2,1,0:T(8,128)(2,1)S(1)} %all_to_all.17.mine_ref), channel_id=1, source_target_pairs={{0,8},{8,0},{1,9},{9,1},{2,10},{10,2},{3,11},{11,3},{4,12},{12,4},... | collective-permute-start | bytes 1966088 | tf_op jit(solution)/shard_map/ppermute | solution.py:278

commit v9 on v8

--- a/solution.py
+++ b/solution.py
@@ -6,7 +6,7 @@
 from jax import lax
 from jax.experimental import pallas as pl
 from jax.experimental.pallas import tpu as pltpu
-from jax.sharding import Mesh, PartitionSpec as P
+from jax.sharding import PartitionSpec as P
 
 EPS = 1e-06
 BF = jnp.bfloat16
@@ -48,13 +48,16 @@
     return hi, mid, rest - mid
 
 
+def which_core():
+    return lax.rem(lax.axis_index("dp"), 2)
+
+
 def where_am_i():
-    section = 2 * lax.axis_index("x") + lax.axis_index("zl")
-    return section, lax.axis_index("c")
+    return lax.axis_index("section"), which_core()
 
 
 def prep_kernel(far, w_ref, taps_ref, out_ref, sem):
-    core = lax.axis_index("c")
+    core = which_core()
     part = pl.multiple_of((1 - core if far else core) * H, H)
     copy = pltpu.make_async_copy(w_ref.at[0, pl.ds(part, H)], out_ref.at[pl.ds(0, H)], sem)
     copy.start()
@@ -206,11 +209,11 @@
 
 
 def lend_kernel(recv_ref, out_ref):
-    half_product(recv_ref, 1 - lax.axis_index("c"), out_ref)
+    half_product(recv_ref, 1 - which_core(), out_ref)
 
 
 def grad_kernel(recv_ref, lent_ref, out_ref, flat_ref, chunk_ref):
-    half_product(recv_ref, lax.axis_index("c"), flat_ref)
+    half_product(recv_ref, which_core(), flat_ref)
     taps = recv_ref[0, T:, :].astype(F32)
     for i in range(1, L):
         taps = taps + recv_ref[i, T:, :].astype(F32)
@@ -243,7 +246,7 @@
 
 
 def place_kernel(mine_ref, theirs_ref, grad_ref, taps_ref, flat_ref):
-    core = lax.axis_index("c")
+    core = which_core()
     for ref, which in ((mine_ref, core), (theirs_ref, 1 - core)):
         start = pl.multiple_of(which * H, H)
         for j in range(PEERS):
@@ -262,20 +265,26 @@
 
 
 def body(features, lengths, front_weight, pointwise, kernel, targets):
-    ring = route((2, 4), lambda c, x: (c, (x + 1 if c == 0 else x - 1) % 4))
+    ring = route(
+        (8, 4, 2, 4, 2), lambda y, h, c, x, z: (y, h, c, (x + 1 if c == 0 else x - 1) % 4, z))
     pair = route(
-        (4, 2, 2),
-        lambda h, c, z: (h, c, 1 - z) if c == 0 else ((h + 2 * z - 1) % 4, c, 1 - z),
+        (8, 4, 2, 4, 2),
+        lambda y, h, c, x, z: (y, h if c == 0 else (h + 2 * z - 1) % 4, c, x, 1 - z),
     )
+    swap = route((8, 4, 2), lambda y, h, c: (y, h, 1 - c))
+    cores = [list(range(c, 64, 2)) for c in range(2)]
 
     def along_x(a):
-        return lax.ppermute(a, ("c", "x"), ring)
+        return lax.ppermute(a, ("dp", "section"), ring)
 
     def along_z(a):
-        return lax.ppermute(a, ("zh", "c", "zl"), pair)
+        return lax.ppermute(a, ("dp", "section"), pair)
 
     def to_core(a):
-        return lax.ppermute(a, "c", [(0, 1), (1, 0)])
+        return lax.ppermute(a, "dp", swap)
+
+    def to_chips(a):
+        return lax.all_to_all(a, "dp", 0, 0, axis_index_groups=cores)
 
     flat_taps = jnp.transpose(kernel, (1, 0, 2))
 
@@ -333,7 +342,8 @@
         compiler_params=params(28),
     )(begin, *here, *there)
 
-    received = lax.all_to_all(payload, ("x", "zl"), 0, 0)
+    received = lax.all_to_all(
+        payload, "section", 0, 0, axis_index_groups=[list(range(L))])
 
     lend = pl.pallas_call(
         lend_kernel,
@@ -353,7 +363,7 @@
         compiler_params=params(24),
     )(received, to_core(lend))
 
-    scattered = lax.all_to_all(parts, ("y", "zh"), 0, 0)
+    scattered = to_chips(parts)
 
     mine = pl.pallas_call(
         sum_kernel,
@@ -365,7 +375,7 @@
         compiler_params=params(16),
     )(scattered)
 
-    half = lax.all_to_all(mine, ("y", "zh"), 0, 0)
+    half = to_chips(mine)
     other_half = to_core(half)
 
     grads, tap_grads = pl.pallas_call(
@@ -384,12 +394,10 @@
 
 
 def solution(mesh):
-    fine = Mesh(mesh.devices.reshape(8, 4, 2, 4, 2), ("y", "zh", "c", "x", "zl"))
-    dp = ("y", "zh", "c")
-    section = ("x", "zl")
+    dp, section = "dp", "section"
     return jax.shard_map(
         body,
-        mesh=fine,
+        mesh=mesh,
         in_specs=(
             P(dp, None, None),
             P(dp),

time: 159 us -> 159 us (level)
  no operation moved by 1% of the time
where the time goes in v9:
time: 159 us; the launch traced here: 158 us
  blocking collectives  73.2 us (46%)
  starting transfers between devices  50.2 us (32%)
  Pallas kernels  21.7 us (14%)
  waiting for transfers between devices  11.8 us (7%)
    all_to_all x2, blocking collectives, to_chips(): return lax.all_to_all(a, 'dp', 0, 0, axis_index_groups=cores)  56.2 us
    ppermute x4, starting transfers between devices, along_z(): return lax.ppermute(a, ('dp', 'section'), pair)  21.7 us
    ppermute x6, starting transfers between devices, to_core(): return lax.ppermute(a, 'dp', swap)  17.3 us
    all_to_all x1, blocking collectives, body(): lax.all_to_all(payload, 'section', 0, 0, axis_index_groups=[list(range(L))])  17 us
    pallas_call x1, Pallas kernels, body(): pl.pallas_call(model_kernel, name='model', out_shape=jax.ShapeDtypeStruct...  12 us
    ppermute x4, starting transfers between devices, along_x(): return lax.ppermute(a, ('dp', 'section'), ring)  11.2 us
    ppermute x4, waiting for transfers between devices, along_z(): return lax.ppermute(a, ('dp', 'section'), pair)  6.57 us
    pallas_call x2, Pallas kernels, prepare(): pl.pallas_call(functools.partial(prep_kernel, far), name='far' if far els...  5.28 us
  transfers between devices with their start and end apart: 14, of which 5 were waited for; matrix products, arithmetic and copies ran while one was open for 0% of the time, Pallas kernels for 3%

profile of v9, /device:TPU:9, one launch (start us, length us, event | category | flops | bytes accessed | tf_op | source)
XLA Modules:
  0.0 158.2 jit_solution(13200537836192334769)
XLA Ops:
  0.6 2.6 %near.1.n0 = bf16[408,768]{1,0:T(8,128)(2,1)} custom-call(bf16[1,768,768]{2,1,0:T(8,128)(2,1)} %w_ref.3, f32[5,1,768]{2,1,0:T(1,128)} %bitcast.2), custom_call_target="tpu_custom_call" | custom-call | tf_op jit(solution)/shard_map/near/pallas_call | solution.py:292
  3.3 4.4 %collective-permute-start = (bf16[408,768]{1,0:T(8,128)(2,1)}, bf16[408,768]{1,0:T(8,128)(2,1)S(1)}, u32[]{:S(2)}, u32[]{:S(2)}) collective-permute-start(bf16[408,768]{1,0:T(8,128)(2,1)} %near.1.n0), channel_id=1, source_target_pairs={{0,2},{1,3},{2,4},{3,5},{4,6},{5,7},{6,0},{7,1},{8,14},{9,15},{10,... | collective-permute-start | bytes 1880072 | tf_op jit(solution)/shard_map/ppermute | solution.py:278
  7.7 10.7 %collective-permute-start.1 = (bf16[408,768]{1,0:T(8,128)(2,1)}, bf16[408,768]{1,0:T(8,128)(2,1)S(1)}, u32[]{:S(2)}, u32[]{:S(2)}) collective-permute-start(bf16[408,768]{1,0:T(8,128)(2,1)} %near.1.n0), channel_id=1, source_target_pairs={{0,1},{1,0},{2,3},{3,2},{4,5},{5,4},{6,7},{7,6},{8,57},{9,24},{10,... | collective-permute-start | bytes 1880072 | tf_op jit(solution)/shard_map/ppermute | solution.py:281
  18.4 2.6 %far.1.f0 = bf16[416,768]{1,0:T(8,128)(2,1)} custom-call(bf16[1,768,768]{2,1,0:T(8,128)(2,1)} %w_ref.3, f32[5,1,768]{2,1,0:T(1,128)} %bitcast.3), custom_call_target="tpu_custom_call" | custom-call | tf_op jit(solution)/shard_map/far/pallas_call | solution.py:292
  21.0 1.9 %collective-permute-start.5 = (bf16[416,768]{1,0:T(8,128)(2,1)}, bf16[416,768]{1,0:T(8,128)(2,1)S(1)}, u32[]{:S(2)}, u32[]{:S(2)}) collective-permute-start(bf16[416,768]{1,0:T(8,128)(2,1)} %far.1.f0), channel_id=1, source_target_pairs={{0,1},{1,0},{2,3},{3,2},{4,5},{5,4},{6,7},{7,6},{8,57},{9,24},{10,... | collective-permute-start | bytes 1916936 | tf_op jit(solution)/shard_map/ppermute | solution.py:281
  22.9 2.5 %collective-permute-start.4 = (bf16[416,768]{1,0:T(8,128)(2,1)}, bf16[416,768]{1,0:T(8,128)(2,1)S(1)}, u32[]{:S(2)}, u32[]{:S(2)}) collective-permute-start(bf16[416,768]{1,0:T(8,128)(2,1)} %far.1.f0), channel_id=1, source_target_pairs={{0,2},{1,3},{2,4},{3,5},{4,6},{5,7},{6,0},{7,1},{8,14},{9,15},{10,... | collective-permute-start | bytes 1916936 | tf_op jit(solution)/shard_map/ppermute | solution.py:278
  25.4 2.3 %front.1.start_ref = bf16[144,768]{1,0:T(8,128)(2,1)} custom-call(bf16[4,64,512]{2,1,0:T(8,128)(2,1)} %feat_ref.1, bf16[512,768]{1,0:T(8,128)(2,1)} %front_ref.1, bf16[4,64,768]{2,1,0:T(8,128)(2,1)} %targ_ref.1, s32[4]{0:T(128)} %len_ref.1), custom_call_target="tpu_custom_call" | custom-call | tf_op jit(solution)/shard_map/front/pallas_call | solution.py:302
  27.7 0.0 collective-permute-done.n1
  27.7 0.0 collective-permute-done.1.n3
  27.7 2.2 %collective-permute-start.2 = (bf16[408,768]{1,0:T(8,128)(2,1)S(1)}, bf16[408,768]{1,0:T(8,128)(2,1)S(1)}, u32[]{:S(2)}, u32[]{:S(2)}) collective-permute-start(bf16[408,768]{1,0:T(8,128)(2,1)S(1)} %collective-permute-done.n1), channel_id=1, source_target_pairs={{0,2},{1,3},{2,4},{3,5},{4,6},{5,7},{6,0},{7,1},{8,14},{9,15},{10,... | collective-permute-start | bytes 1880072 | tf_op jit(solution)/shard_map/ppermute | solution.py:278
  29.9 4.6 %collective-permute-start.3 = (bf16[400,768]{1,0:T(8,128)(2,1)S(1)}, bf16[400,768]{1,0:T(8,128)(2,1)S(1)}, u32[]{:S(2)}, u32[]{:S(2)}) collective-permute-start(bf16[400,768]{1,0:T(8,128)(2,1)S(1)} %slice.16), channel_id=1, source_target_pairs={{0,1},{1,0},{2,3},{3,2},{4,5},{5,4},{6,7},{7,6},{8,57},{9,24},{10,... | collective-permute-start | bytes 1843208 | tf_op jit(solution)/shard_map/ppermute | solution.py:281
  34.5 0.0 collective-permute-done.5.f3
  34.5 2.2 %collective-permute-start.6 = (bf16[416,768]{1,0:T(8,128)(2,1)S(1)}, bf16[416,768]{1,0:T(8,128)(2,1)S(1)}, u32[]{:S(2)}, u32[]{:S(2)}) collective-permute-start(bf16[416,768]{1,0:T(8,128)(2,1)S(1)} %collective-permute-done.5.f3), channel_id=1, source_target_pairs={{0,2},{1,3},{2,4},{3,5},{4,6},{5,7},{6,0},{7,1},{8,14},{9,15},{10,... | collective-permute-start | bytes 1916936 | tf_op jit(solution)/shard_map/ppermute | solution.py:278
  36.6 0.0 collective-permute-done.4.f1
  36.7 5.6 %collective-permute-done.3.n4 = bf16[400,768]{1,0:T(8,128)(2,1)S(1)} collective-permute-done((bf16[400,768]{1,0:T(8,128)(2,1)S(1)}, bf16[400,768]{1,0:T(8,128)(2,1)S(1)}, u32[]{:S(2)}, u32[]{:S(2)}) %collective-permute-start.3) | collective-permute-done | bytes 614432 | tf_op jit(solution)/shard_map/ppermute | solution.py:281
  42.3 0.0 collective-permute-done.2.n2
  42.3 4.6 %collective-permute-start.7 = (bf16[408,768]{1,0:T(8,128)(2,1)S(1)}, bf16[408,768]{1,0:T(8,128)(2,1)S(1)}, u32[]{:S(2)}, u32[]{:S(2)}) collective-permute-start(bf16[408,768]{1,0:T(8,128)(2,1)S(1)} %collective-permute-done.2.n2), channel_id=1, source_target_pairs={{0,1},{1,0},{2,3},{3,2},{4,5},{5,4},{6,7},{7,6},{8,57},{9,24},{10,... | collective-permute-start | bytes 1880072 | tf_op jit(solution)/shard_map/ppermute | solution.py:281
  46.9 0.1 pad_maximum_fusion.1
  47.0 1.9 %collective-permute-start.9 = (bf16[784,768]{1,0:T(8,128)(2,1)S(1)}, bf16[784,768]{1,0:T(8,128)(2,1)S(1)}, u32[]{:S(2)}, u32[]{:S(2)}) collective-permute-start(bf16[784,768]{1,0:T(8,128)(2,1)S(1)} %pad_maximum_fusion.1), channel_id=1, source_target_pairs={{0,8},{8,0},{16,24},{24,16},{32,40},{40,32},{48,56},{56,48},{64,72... | collective-permute-start | bytes 3612680 | tf_op jit(solution)/shard_map/ppermute | solution.py:284
  49.0 0.1 pad_maximum_fusion
  49.1 0.0 copy-start
  49.1 0.0 copy-start.1
  49.1 0.0 copy-start.2
  49.1 2.5 %collective-permute-start.8 = (bf16[784,768]{1,0:T(8,128)(2,1)S(1)}, bf16[784,768]{1,0:T(8,128)(2,1)S(1)}, u32[]{:S(2)}, u32[]{:S(2)}) collective-permute-start(bf16[784,768]{1,0:T(8,128)(2,1)S(1)} %pad_maximum_fusion), channel_id=1, source_target_pairs={{0,8},{8,0},{16,24},{24,16},{32,40},{40,32},{48,56},{56,48},{64,72... | collective-permute-start | bytes 3612680 | tf_op jit(solution)/shard_map/ppermute | solution.py:284
  51.6 0.0 collective-permute-done.6.f4
  51.7 1.9 %collective-permute-start.10 = (bf16[392,768]{1,0:T(8,128)(2,1)S(1)}, bf16[392,768]{1,0:T(8,128)(2,1)S(1)}, u32[]{:S(2)}, u32[]{:S(2)}) collective-permute-start(bf16[392,768]{1,0:T(8,128)(2,1)S(1)} %slice.21), channel_id=1, source_target_pairs={{0,8},{8,0},{16,24},{24,16},{32,40},{40,32},{48,56},{56,48},{64,72... | collective-permute-start | bytes 1806344 | tf_op jit(solution)/shard_map/ppermute | solution.py:284
  53.6 0.9 collective-permute-done.7.n5
  54.6 1.9 %collective-permute-start.11 = (bf16[384,768]{1,0:T(8,128)(2,1)S(1)}, bf16[384,768]{1,0:T(8,128)(2,1)S(1)}, u32[]{:S(2)}, u32[]{:S(2)}) collective-permute-start(bf16[384,768]{1,0:T(8,128)(2,1)S(1)} %slice.22), channel_id=1, source_target_pairs={{0,8},{8,0},{16,24},{24,16},{32,40},{40,32},{48,56},{56,48},{64,72... | collective-permute-start | bytes 1769480 | tf_op jit(solution)/shard_map/ppermute | solution.py:284
  56.5 0.0 collective-permute-done.10.g4
  56.5 0.0 collective-permute-done.9.m2
  56.6 0.0 collective-permute-done.8.m1
  56.6 1.9 %collective-permute-done.11.m5 = bf16[384,768]{1,0:T(8,128)(2,1)S(1)} collective-permute-done((bf16[384,768]{1,0:T(8,128)(2,1)S(1)}, bf16[384,768]{1,0:T(8,128)(2,1)S(1)}, u32[]{:S(2)}, u32[]{:S(2)}) %collective-permute-start.11) | collective-permute-done | bytes 589856 | tf_op jit(solution)/shard_map/ppermute | solution.py:284
  58.5 0.0 copy-done
  58.5 0.0 copy-done.1
  58.5 0.0 copy-done.2
  58.5 12.0 %model.1 = bf16[8,72,768]{2,1,0:T(8,128)(2,1)S(1)} custom-call(bf16[144,768]{1,0:T(8,128)(2,1)S(1)} %copy-done.2, bf16[408,768]{1,0:T(8,128)(2,1)S(1)} %copy-done.1, bf16[416,768]{1,0:T(8,128)(2,1)S(1)} %copy-done, bf16[408,768]{1,0:T(8,128)(2,1)S(1)} %collective-permute-done.n1, bf16[416,768]{1,0:T(8,128)(2,1)S(1)} %collective-permute-done.4.f1, ...), custom_call_target="tpu_custom_call" | custom-call | tf_op jit(solution)/shard_map/model/pallas_call | solution.py:323
  70.5 17.0 %all_to_all.15.recv_ref = bf16[8,72,768]{2,1,0:T(8,128)(2,1)S(1)} all-to-all(bf16[8,72,768]{2,1,0:T(8,128)(2,1)S(1)} %model.1), channel_id=1, replica_groups={{0,1,2,3,4,5,6,7},{8,9,10,11,12,13,14,15},{16,17,18,19,20,21,22,23},{24..., dimensions={0} | all-to-all | bytes 1769472 | tf_op jit(solution)/shard_map/all_to_all | solution.py:345
  87.5 0.4 lend.1
  87.9 3.2 %collective-permute-start.12 = (bf16[2304,128]{1,0:T(8,128)(2,1)S(1)}, bf16[2304,128]{1,0:T(8,128)(2,1)S(1)}, u32[]{:S(2)}, u32[]{:S(2)}) collective-permute-start(bf16[2304,128]{1,0:T(8,128)(2,1)S(1)} %lend.1), channel_id=1, source_target_pairs={{0,8},{8,0},{16,24},{24,16},{32,40},{40,32},{48,56},{56,48},{64,72... | collective-permute-start | bytes 1769480 | tf_op jit(solution)/shard_map/ppermute | solution.py:284
  91.1 1.6 %collective-permute-done.12.lent_ref = bf16[2304,128]{1,0:T(8,128)(2,1)S(1)} collective-permute-done((bf16[2304,128]{1,0:T(8,128)(2,1)S(1)}, bf16[2304,128]{1,0:T(8,128)(2,1)S(1)}, u32[]{:S(2)}, u32[]{:S(2)}) %collective-permute-start.12) | collective-permute-done | bytes 589856 | tf_op jit(solution)/shard_map/ppermute | solution.py:284
  92.7 0.4 grad.1
  93.1 30.8 %all_to_all.16.parts_ref = bf16[32,80,128]{2,1,0:T(8,128)(2,1)S(1)} all-to-all(bf16[32,80,128]{2,1,0:T(8,128)(2,1)S(1)} %grad.1), channel_id=1, replica_groups={{0,16,32,48,64,80,96,112,128,144,160,176,192,208,224,240,256,272,288,30..., dimensions={0} | all-to-all | bytes 1310720 | tf_op jit(solution)/shard_map/all_to_all | solution.py:287
  123.9 0.1 total.1
  124.1 25.4 %all_to_all.17.mine_ref = bf16[32,80,128]{2,1,0:T(8,128)(2,1)S(1)} all-to-all(bf16[32,80,128]{2,1,0:T(8,128)(2,1)S(1)} %total.1), channel_id=1, replica_groups={{0,16,32,48,64,80,96,112,128,144,160,176,192,208,224,240,256,272,288,30..., dimensions={0} | all-to-all | bytes 1310720 | tf_op jit(solution)/shard_map/all_to_all | solution.py:287
  149.5 5.8 %collective-permute-start.13 = (bf16[32,80,128]{2,1,0:T(8,128)(2,1)S(1)}, bf16[32,80,128]{2,1,0:T(8,128)(2,1)S(1)}, u32[]{:S(2)}, u32[]{:S(2)}) collective-permute-start(bf16[32,80,128]{2,1,0:T(8,128)(2,1)S(1)} %all_to_all.17.mine_ref), channel_id=1, source_target_pairs={{0,8},{8,0},{16,24},{24,16},{32,40},{40,32},{48,56},{56,48},{64,72... | collective-permute-start | bytes 1966088 | tf_op jit(solution)/shard_map/ppermute | solution.py:284
  155.3 1.7 %collective-permute-done.13.theirs_ref = bf16[32,80,128]{2,1,0:T(8,128)(2,1)S(1)} collective-permute-done((bf16[32,80,128]{2,1,0:T(8,128)(2,1)S(1)}, bf16[32,80,128]{2,1,0:T(8,128)(2,1)S(1)}, u32[]{:S(2)}, u32[]{:S(2)}) %collective-permute-start.13) | collective-permute-done | bytes 655392 | tf_op jit(solution)/shard_map/ppermute | solution.py:284
  157.0 1.2 place.1
  (5 shorter events, 0.2 us)
Async XLA Ops:
  3.3 24.4 %collective-permute-start = (bf16[408,768]{1,0:T(8,128)(2,1)}, bf16[408,768]{1,0:T(8,128)(2,1)S(1)}, u32[]{:S(2)}, u32[]{:S(2)}) collective-permute-start(bf16[408,768]{1,0:T(8,128)(2,1)} %near.1.n0), channel_id=1, source_target_pairs={{0,2},{1,3},{2,4},{3,5},{4,6},{5,7},{6,0},{7,1},{8,14},{9,15},{10,... | collective-permute-start | bytes 1880072 | tf_op jit(solution)/shard_map/ppermute | solution.py:278
  7.7 20.0 %collective-permute-start.1 = (bf16[408,768]{1,0:T(8,128)(2,1)}, bf16[408,768]{1,0:T(8,128)(2,1)S(1)}, u32[]{:S(2)}, u32[]{:S(2)}) collective-permute-start(bf16[408,768]{1,0:T(8,128)(2,1)} %near.1.n0), channel_id=1, source_target_pairs={{0,1},{1,0},{2,3},{3,2},{4,5},{5,4},{6,7},{7,6},{8,57},{9,24},{10,... | collective-permute-start | bytes 1880072 | tf_op jit(solution)/shard_map/ppermute | solution.py:281
  21.0 13.5 %collective-permute-start.5 = (bf16[416,768]{1,0:T(8,128)(2,1)}, bf16[416,768]{1,0:T(8,128)(2,1)S(1)}, u32[]{:S(2)}, u32[]{:S(2)}) collective-permute-start(bf16[416,768]{1,0:T(8,128)(2,1)} %far.1.f0), channel_id=1, source_target_pairs={{0,1},{1,0},{2,3},{3,2},{4,5},{5,4},{6,7},{7,6},{8,57},{9,24},{10,... | collective-permute-start | bytes 1916936 | tf_op jit(solution)/shard_map/ppermute | solution.py:281
  22.9 13.7 %collective-permute-start.4 = (bf16[416,768]{1,0:T(8,128)(2,1)}, bf16[416,768]{1,0:T(8,128)(2,1)S(1)}, u32[]{:S(2)}, u32[]{:S(2)}) collective-permute-start(bf16[416,768]{1,0:T(8,128)(2,1)} %far.1.f0), channel_id=1, source_target_pairs={{0,2},{1,3},{2,4},{3,5},{4,6},{5,7},{6,0},{7,1},{8,14},{9,15},{10,... | collective-permute-start | bytes 1916936 | tf_op jit(solution)/shard_map/ppermute | solution.py:278
  27.7 14.6 %collective-permute-start.2 = (bf16[408,768]{1,0:T(8,128)(2,1)S(1)}, bf16[408,768]{1,0:T(8,128)(2,1)S(1)}, u32[]{:S(2)}, u32[]{:S(2)}) collective-permute-start(bf16[408,768]{1,0:T(8,128)(2,1)S(1)} %collective-permute-done.n1), channel_id=1, source_target_pairs={{0,2},{1,3},{2,4},{3,5},{4,6},{5,7},{6,0},{7,1},{8,14},{9,15},{10,... | collective-permute-start | bytes 1880072 | tf_op jit(solution)/shard_map/ppermute | solution.py:278
  29.9 12.4 %collective-permute-start.3 = (bf16[400,768]{1,0:T(8,128)(2,1)S(1)}, bf16[400,768]{1,0:T(8,128)(2,1)S(1)}, u32[]{:S(2)}, u32[]{:S(2)}) collective-permute-start(bf16[400,768]{1,0:T(8,128)(2,1)S(1)} %slice.16), channel_id=1, source_target_pairs={{0,1},{1,0},{2,3},{3,2},{4,5},{5,4},{6,7},{7,6},{8,57},{9,24},{10,... | collective-permute-start | bytes 1843208 | tf_op jit(solution)/shard_map/ppermute | solution.py:281
  34.5 17.2 %collective-permute-start.6 = (bf16[416,768]{1,0:T(8,128)(2,1)S(1)}, bf16[416,768]{1,0:T(8,128)(2,1)S(1)}, u32[]{:S(2)}, u32[]{:S(2)}) collective-permute-start(bf16[416,768]{1,0:T(8,128)(2,1)S(1)} %collective-permute-done.5.f3), channel_id=1, source_target_pairs={{0,2},{1,3},{2,4},{3,5},{4,6},{5,7},{6,0},{7,1},{8,14},{9,15},{10,... | collective-permute-start | bytes 1916936 | tf_op jit(solution)/shard_map/ppermute | solution.py:278
  42.3 12.2 %collective-permute-start.7 = (bf16[408,768]{1,0:T(8,128)(2,1)S(1)}, bf16[408,768]{1,0:T(8,128)(2,1)S(1)}, u32[]{:S(2)}, u32[]{:S(2)}) collective-permute-start(bf16[408,768]{1,0:T(8,128)(2,1)S(1)} %collective-permute-done.2.n2), channel_id=1, source_target_pairs={{0,1},{1,0},{2,3},{3,2},{4,5},{5,4},{6,7},{7,6},{8,57},{9,24},{10,... | collective-permute-start | bytes 1880072 | tf_op jit(solution)/shard_map/ppermute | solution.py:281
  47.0 9.6 %collective-permute-start.9 = (bf16[784,768]{1,0:T(8,128)(2,1)S(1)}, bf16[784,768]{1,0:T(8,128)(2,1)S(1)}, u32[]{:S(2)}, u32[]{:S(2)}) collective-permute-start(bf16[784,768]{1,0:T(8,128)(2,1)S(1)} %pad_maximum_fusion.1), channel_id=1, source_target_pairs={{0,8},{8,0},{16,24},{24,16},{32,40},{40,32},{48,56},{56,48},{64,72... | collective-permute-start | bytes 3612680 | tf_op jit(solution)/shard_map/ppermute | solution.py:284
  49.1 9.4 %copy-start = (bf16[416,768]{1,0:T(8,128)(2,1)S(1)}, bf16[416,768]{1,0:T(8,128)(2,1)}, u32[]{:S(2)}) copy-start(bf16[416,768]{1,0:T(8,128)(2,1)} %far.1.f0) | copy-start | bytes 1916932
  49.1 9.4 %copy-start.1 = (bf16[408,768]{1,0:T(8,128)(2,1)S(1)}, bf16[408,768]{1,0:T(8,128)(2,1)}, u32[]{:S(2)}) copy-start(bf16[408,768]{1,0:T(8,128)(2,1)} %near.1.n0) | copy-start | bytes 1880068
  49.1 9.4 %copy-start.2 = (bf16[144,768]{1,0:T(8,128)(2,1)S(1)}, bf16[144,768]{1,0:T(8,128)(2,1)}, u32[]{:S(2)}) copy-start(bf16[144,768]{1,0:T(8,128)(2,1)} %front.1.start_ref) | copy-start | bytes 663556
  49.1 7.5 %collective-permute-start.8 = (bf16[784,768]{1,0:T(8,128)(2,1)S(1)}, bf16[784,768]{1,0:T(8,128)(2,1)S(1)}, u32[]{:S(2)}, u32[]{:S(2)}) collective-permute-start(bf16[784,768]{1,0:T(8,128)(2,1)S(1)} %pad_maximum_fusion), channel_id=1, source_target_pairs={{0,8},{8,0},{16,24},{24,16},{32,40},{40,32},{48,56},{56,48},{64,72... | collective-permute-start | bytes 3612680 | tf_op jit(solution)/shard_map/ppermute | solution.py:284
  51.7 4.8 %collective-permute-start.10 = (bf16[392,768]{1,0:T(8,128)(2,1)S(1)}, bf16[392,768]{1,0:T(8,128)(2,1)S(1)}, u32[]{:S(2)}, u32[]{:S(2)}) collective-permute-start(bf16[392,768]{1,0:T(8,128)(2,1)S(1)} %slice.21), channel_id=1, source_target_pairs={{0,8},{8,0},{16,24},{24,16},{32,40},{40,32},{48,56},{56,48},{64,72... | collective-permute-start | bytes 1806344 | tf_op jit(solution)/shard_map/ppermute | solution.py:284
  54.6 3.9 %collective-permute-start.11 = (bf16[384,768]{1,0:T(8,128)(2,1)S(1)}, bf16[384,768]{1,0:T(8,128)(2,1)S(1)}, u32[]{:S(2)}, u32[]{:S(2)}) collective-permute-start(bf16[384,768]{1,0:T(8,128)(2,1)S(1)} %slice.22), channel_id=1, source_target_pairs={{0,8},{8,0},{16,24},{24,16},{32,40},{40,32},{48,56},{56,48},{64,72... | collective-permute-start | bytes 1769480 | tf_op jit(solution)/shard_map/ppermute | solution.py:284
  87.9 4.8 %collective-permute-start.12 = (bf16[2304,128]{1,0:T(8,128)(2,1)S(1)}, bf16[2304,128]{1,0:T(8,128)(2,1)S(1)}, u32[]{:S(2)}, u32[]{:S(2)}) collective-permute-start(bf16[2304,128]{1,0:T(8,128)(2,1)S(1)} %lend.1), channel_id=1, source_target_pairs={{0,8},{8,0},{16,24},{24,16},{32,40},{40,32},{48,56},{56,48},{64,72... | collective-permute-start | bytes 1769480 | tf_op jit(solution)/shard_map/ppermute | solution.py:284
  149.5 7.5 %collective-permute-start.13 = (bf16[32,80,128]{2,1,0:T(8,128)(2,1)S(1)}, bf16[32,80,128]{2,1,0:T(8,128)(2,1)S(1)}, u32[]{:S(2)}, u32[]{:S(2)}) collective-permute-start(bf16[32,80,128]{2,1,0:T(8,128)(2,1)S(1)} %all_to_all.17.mine_ref), channel_id=1, source_target_pairs={{0,8},{8,0},{16,24},{24,16},{32,40},{40,32},{48,56},{56,48},{64,72... | collective-permute-start | bytes 1966088 | tf_op jit(solution)/shard_map/ppermute | solution.py:284

commit v10 on v8

--- a/solution.py
+++ b/solution.py
@@ -66,14 +66,22 @@
     copy.wait()
 
 
-def front_kernel(feat_ref, front_ref, targ_ref, len_ref, out_ref):
+def front_kernel(feat_ref, front_ref, targ_ref, len_ref, out_ref, input_ref, weight_ref, sem):
     section, _ = where_am_i()
     utt = lax.rem(section, 4)
-    out_ref[0:T, :] = jnp.dot(
-        feat_ref[utt], front_ref[...], preferred_element_type=F32).astype(BF)
-    out_ref[T:2 * T, :] = targ_ref[utt]
+    copies = [
+        pltpu.make_async_copy(front_ref, weight_ref, sem.at[0]),
+        pltpu.make_async_copy(feat_ref.at[utt], input_ref, sem.at[1]),
+        pltpu.make_async_copy(targ_ref.at[utt], out_ref.at[pl.ds(T, T)], sem.at[2]),
+    ]
+    for copy in copies:
+        copy.start()
     count = len_ref[utt].astype(F32)
     out_ref[2 * T:, :] = jnp.full((START - 2 * T, D), count, F32).astype(BF)
+    for copy in copies:
+        copy.wait()
+    out_ref[0:T, :] = jnp.dot(
+        input_ref[...], weight_ref[...], preferred_element_type=F32).astype(BF)
 
 
 def model_kernel(
@@ -294,8 +302,13 @@
         front_kernel,
         name="front",
         out_shape=jax.ShapeDtypeStruct((START, D), BF),
-        in_specs=[VMEM, VMEM, VMEM, SMEM],
+        in_specs=[ANY, ANY, ANY, SMEM],
         out_specs=VMEM,
+        scratch_shapes=[
+            pltpu.VMEM((T, FEAT), BF),
+            pltpu.VMEM((FEAT, D), BF),
+            pltpu.SemaphoreType.DMA((3,)),
+        ],
     )(features, front_weight, targets, lengths)
 
     n1, n3, begin = lax.optimization_barrier((along_x(near), along_z(near), begin))

time: 159 us -> 160 us (level)
  no operation moved by 1% of the time
where the time goes in v10:
time: 160 us; the launch traced here: 159 us
  blocking collectives  73.2 us (46%)
  starting transfers between devices  50.2 us (31%)
  Pallas kernels  22.2 us (14%)
  waiting for transfers between devices  11.8 us (7%)
    all_to_all x1, blocking collectives, body(): scattered = lax.all_to_all(parts, ('y', 'zh'), 0, 0)  30.8 us
    all_to_all x1, blocking collectives, body(): half = lax.all_to_all(mine, ('y', 'zh'), 0, 0)  25.4 us
    ppermute x4, starting transfers between devices, along_z(): return lax.ppermute(a, ('zh', 'c', 'zl'), pair)  21.7 us
    ppermute x6, starting transfers between devices, to_core(): return lax.ppermute(a, 'c', [(0, 1), (1, 0)])  17.3 us
    all_to_all x1, blocking collectives, body(): received = lax.all_to_all(payload, ('x', 'zl'), 0, 0)  17 us
    pallas_call x1, Pallas kernels, body(): pl.pallas_call(model_kernel, name='model', out_shape=jax.ShapeDtypeStruct...  12 us
    ppermute x4, starting transfers between devices, along_x(): return lax.ppermute(a, ('c', 'x'), ring)  11.2 us
    ppermute x4, waiting for transfers between devices, along_z(): return lax.ppermute(a, ('zh', 'c', 'zl'), pair)  6.57 us
  transfers between devices with their start and end apart: 14, of which 5 were waited for; matrix products, arithmetic and copies ran while one was open for 0% of the time, Pallas kernels for 3%

profile of v10, /device:TPU:9, one launch (start us, length us, event | category | flops | bytes accessed | tf_op | source)
XLA Modules:
  0.0 158.7 jit_solution(8156685345130445781)
XLA Ops:
  0.6 2.6 %near.1.n0 = bf16[408,768]{1,0:T(8,128)(2,1)} custom-call(bf16[1,768,768]{2,1,0:T(8,128)(2,1)} %w_ref.3, f32[5,1,768]{2,1,0:T(1,128)} %bitcast.2), custom_call_target="tpu_custom_call" | custom-call | tf_op jit(solution)/shard_map/near/pallas_call | solution.py:291
  3.3 4.4 %collective-permute-start = (bf16[408,768]{1,0:T(8,128)(2,1)}, bf16[408,768]{1,0:T(8,128)(2,1)S(1)}, u32[]{:S(2)}, u32[]{:S(2)}) collective-permute-start(bf16[408,768]{1,0:T(8,128)(2,1)} %near.1.n0), channel_id=1, source_target_pairs={{0,2},{2,4},{4,6},{6,0},{8,14},{10,8},{12,10},{14,12},{1,3},{3,5},... | collective-permute-start | bytes 1880072 | tf_op jit(solution)/shard_map/ppermute | solution.py:280
  7.7 10.7 %collective-permute-start.1 = (bf16[408,768]{1,0:T(8,128)(2,1)}, bf16[408,768]{1,0:T(8,128)(2,1)S(1)}, u32[]{:S(2)}, u32[]{:S(2)}) collective-permute-start(bf16[408,768]{1,0:T(8,128)(2,1)} %near.1.n0), channel_id=1, source_target_pairs={{0,1},{1,0},{8,57},{9,24},{16,17},{17,16},{24,9},{25,40},{32,33},{... | collective-permute-start | bytes 1880072 | tf_op jit(solution)/shard_map/ppermute | solution.py:283
  18.3 2.6 %far.1.f0 = bf16[416,768]{1,0:T(8,128)(2,1)} custom-call(bf16[1,768,768]{2,1,0:T(8,128)(2,1)} %w_ref.3, f32[5,1,768]{2,1,0:T(1,128)} %bitcast.3), custom_call_target="tpu_custom_call" | custom-call | tf_op jit(solution)/shard_map/far/pallas_call | solution.py:291
  21.0 1.9 %collective-permute-start.5 = (bf16[416,768]{1,0:T(8,128)(2,1)}, bf16[416,768]{1,0:T(8,128)(2,1)S(1)}, u32[]{:S(2)}, u32[]{:S(2)}) collective-permute-start(bf16[416,768]{1,0:T(8,128)(2,1)} %far.1.f0), channel_id=1, source_target_pairs={{0,1},{1,0},{8,57},{9,24},{16,17},{17,16},{24,9},{25,40},{32,33},{... | collective-permute-start | bytes 1916936 | tf_op jit(solution)/shard_map/ppermute | solution.py:283
  22.9 2.5 %collective-permute-start.4 = (bf16[416,768]{1,0:T(8,128)(2,1)}, bf16[416,768]{1,0:T(8,128)(2,1)S(1)}, u32[]{:S(2)}, u32[]{:S(2)}) collective-permute-start(bf16[416,768]{1,0:T(8,128)(2,1)} %far.1.f0), channel_id=1, source_target_pairs={{0,2},{2,4},{4,6},{6,0},{8,14},{10,8},{12,10},{14,12},{1,3},{3,5},... | collective-permute-start | bytes 1916936 | tf_op jit(solution)/shard_map/ppermute | solution.py:280
  25.4 2.8 %front.1.start_ref = bf16[144,768]{1,0:T(8,128)(2,1)} custom-call(bf16[4,64,512]{2,1,0:T(8,128)(2,1)} %feat_ref.1, bf16[512,768]{1,0:T(8,128)(2,1)} %front_ref.1, bf16[4,64,768]{2,1,0:T(8,128)(2,1)} %targ_ref.1, s32[4]{0:T(128)} %len_ref.1), custom_call_target="tpu_custom_call" | custom-call | tf_op jit(solution)/shard_map/front/pallas_call | solution.py:301
  28.2 0.0 collective-permute-done.n1
  28.2 0.0 collective-permute-done.1.n3
  28.2 2.2 %collective-permute-start.2 = (bf16[408,768]{1,0:T(8,128)(2,1)S(1)}, bf16[408,768]{1,0:T(8,128)(2,1)S(1)}, u32[]{:S(2)}, u32[]{:S(2)}) collective-permute-start(bf16[408,768]{1,0:T(8,128)(2,1)S(1)} %collective-permute-done.n1), channel_id=1, source_target_pairs={{0,2},{2,4},{4,6},{6,0},{8,14},{10,8},{12,10},{14,12},{1,3},{3,5},... | collective-permute-start | bytes 1880072 | tf_op jit(solution)/shard_map/ppermute | solution.py:280
  30.4 4.6 %collective-permute-start.3 = (bf16[400,768]{1,0:T(8,128)(2,1)S(1)}, bf16[400,768]{1,0:T(8,128)(2,1)S(1)}, u32[]{:S(2)}, u32[]{:S(2)}) collective-permute-start(bf16[400,768]{1,0:T(8,128)(2,1)S(1)} %slice.16), channel_id=1, source_target_pairs={{0,1},{1,0},{8,57},{9,24},{16,17},{17,16},{24,9},{25,40},{32,33},{... | collective-permute-start | bytes 1843208 | tf_op jit(solution)/shard_map/ppermute | solution.py:283
  35.0 0.0 collective-permute-done.5.f3
  35.0 2.2 %collective-permute-start.6 = (bf16[416,768]{1,0:T(8,128)(2,1)S(1)}, bf16[416,768]{1,0:T(8,128)(2,1)S(1)}, u32[]{:S(2)}, u32[]{:S(2)}) collective-permute-start(bf16[416,768]{1,0:T(8,128)(2,1)S(1)} %collective-permute-done.5.f3), channel_id=1, source_target_pairs={{0,2},{2,4},{4,6},{6,0},{8,14},{10,8},{12,10},{14,12},{1,3},{3,5},... | collective-permute-start | bytes 1916936 | tf_op jit(solution)/shard_map/ppermute | solution.py:280
  37.2 0.0 collective-permute-done.4.f1
  37.2 5.6 %collective-permute-done.3.n4 = bf16[400,768]{1,0:T(8,128)(2,1)S(1)} collective-permute-done((bf16[400,768]{1,0:T(8,128)(2,1)S(1)}, bf16[400,768]{1,0:T(8,128)(2,1)S(1)}, u32[]{:S(2)}, u32[]{:S(2)}) %collective-permute-start.3) | collective-permute-done | bytes 614432 | tf_op jit(solution)/shard_map/ppermute | solution.py:283
  42.8 0.0 collective-permute-done.2.n2
  42.9 4.6 %collective-permute-start.7 = (bf16[408,768]{1,0:T(8,128)(2,1)S(1)}, bf16[408,768]{1,0:T(8,128)(2,1)S(1)}, u32[]{:S(2)}, u32[]{:S(2)}) collective-permute-start(bf16[408,768]{1,0:T(8,128)(2,1)S(1)} %collective-permute-done.2.n2), channel_id=1, source_target_pairs={{0,1},{1,0},{8,57},{9,24},{16,17},{17,16},{24,9},{25,40},{32,33},{... | collective-permute-start | bytes 1880072 | tf_op jit(solution)/shard_map/ppermute | solution.py:283
  47.4 0.1 pad_maximum_fusion.1
  47.5 1.9 %collective-permute-start.9 = (bf16[784,768]{1,0:T(8,128)(2,1)S(1)}, bf16[784,768]{1,0:T(8,128)(2,1)S(1)}, u32[]{:S(2)}, u32[]{:S(2)}) collective-permute-start(bf16[784,768]{1,0:T(8,128)(2,1)S(1)} %pad_maximum_fusion.1), channel_id=1, source_target_pairs={{0,8},{8,0},{1,9},{9,1},{2,10},{10,2},{3,11},{11,3},{4,12},{12,4},... | collective-permute-start | bytes 3612680 | tf_op jit(solution)/shard_map/ppermute | solution.py:286
  49.5 0.1 pad_maximum_fusion
  49.6 0.0 copy-start
  49.6 0.0 copy-start.1
  49.6 0.0 copy-start.2
  49.6 2.5 %collective-permute-start.8 = (bf16[784,768]{1,0:T(8,128)(2,1)S(1)}, bf16[784,768]{1,0:T(8,128)(2,1)S(1)}, u32[]{:S(2)}, u32[]{:S(2)}) collective-permute-start(bf16[784,768]{1,0:T(8,128)(2,1)S(1)} %pad_maximum_fusion), channel_id=1, source_target_pairs={{0,8},{8,0},{1,9},{9,1},{2,10},{10,2},{3,11},{11,3},{4,12},{12,4},... | collective-permute-start | bytes 3612680 | tf_op jit(solution)/shard_map/ppermute | solution.py:286
  52.2 0.0 collective-permute-done.6.f4
  52.2 1.9 %collective-permute-start.10 = (bf16[392,768]{1,0:T(8,128)(2,1)S(1)}, bf16[392,768]{1,0:T(8,128)(2,1)S(1)}, u32[]{:S(2)}, u32[]{:S(2)}) collective-permute-start(bf16[392,768]{1,0:T(8,128)(2,1)S(1)} %slice.21), channel_id=1, source_target_pairs={{0,8},{8,0},{1,9},{9,1},{2,10},{10,2},{3,11},{11,3},{4,12},{12,4},... | collective-permute-start | bytes 1806344 | tf_op jit(solution)/shard_map/ppermute | solution.py:286
  54.2 0.9 collective-permute-done.7.n5
  55.1 1.9 %collective-permute-start.11 = (bf16[384,768]{1,0:T(8,128)(2,1)S(1)}, bf16[384,768]{1,0:T(8,128)(2,1)S(1)}, u32[]{:S(2)}, u32[]{:S(2)}) collective-permute-start(bf16[384,768]{1,0:T(8,128)(2,1)S(1)} %slice.22), channel_id=1, source_target_pairs={{0,8},{8,0},{1,9},{9,1},{2,10},{10,2},{3,11},{11,3},{4,12},{12,4},... | collective-permute-start | bytes 1769480 | tf_op jit(solution)/shard_map/ppermute | solution.py:286
  57.1 0.0 collective-permute-done.10.g4
  57.1 0.0 collective-permute-done.9.m2
  57.1 0.0 collective-permute-done.8.m1
  57.1 1.9 %collective-permute-done.11.m5 = bf16[384,768]{1,0:T(8,128)(2,1)S(1)} collective-permute-done((bf16[384,768]{1,0:T(8,128)(2,1)S(1)}, bf16[384,768]{1,0:T(8,128)(2,1)S(1)}, u32[]{:S(2)}, u32[]{:S(2)}) %collective-permute-start.11) | collective-permute-done | bytes 589856 | tf_op jit(solution)/shard_map/ppermute | solution.py:286
  59.0 0.0 copy-done
  59.0 0.0 copy-done.1
  59.0 0.0 copy-done.2
  59.1 12.0 %model.1 = bf16[8,72,768]{2,1,0:T(8,128)(2,1)S(1)} custom-call(bf16[144,768]{1,0:T(8,128)(2,1)S(1)} %copy-done.2, bf16[408,768]{1,0:T(8,128)(2,1)S(1)} %copy-done.1, bf16[416,768]{1,0:T(8,128)(2,1)S(1)} %copy-done, bf16[408,768]{1,0:T(8,128)(2,1)S(1)} %collective-permute-done.n1, bf16[416,768]{1,0:T(8,128)(2,1)S(1)} %collective-permute-done.4.f1, ...), custom_call_target="tpu_custom_call" | custom-call | tf_op jit(solution)/shard_map/model/pallas_call | solution.py:327
  71.1 17.0 %all_to_all.15.recv_ref = bf16[8,72,768]{2,1,0:T(8,128)(2,1)S(1)} all-to-all(bf16[8,72,768]{2,1,0:T(8,128)(2,1)S(1)} %model.1), channel_id=1, replica_groups=mesh['y'=8,'zh'=4,'c'=2,'x'=4,'zl'=2] {'x','zl'}, dimensions={0} | all-to-all | bytes 1769472 | tf_op jit(solution)/shard_map/all_to_all | solution.py:349
  88.0 0.4 lend.1
  88.4 3.2 %collective-permute-start.12 = (bf16[2304,128]{1,0:T(8,128)(2,1)S(1)}, bf16[2304,128]{1,0:T(8,128)(2,1)S(1)}, u32[]{:S(2)}, u32[]{:S(2)}) collective-permute-start(bf16[2304,128]{1,0:T(8,128)(2,1)S(1)} %lend.1), channel_id=1, source_target_pairs={{0,8},{8,0},{1,9},{9,1},{2,10},{10,2},{3,11},{11,3},{4,12},{12,4},... | collective-permute-start | bytes 1769480 | tf_op jit(solution)/shard_map/ppermute | solution.py:286
  91.6 1.6 %collective-permute-done.12.lent_ref = bf16[2304,128]{1,0:T(8,128)(2,1)S(1)} collective-permute-done((bf16[2304,128]{1,0:T(8,128)(2,1)S(1)}, bf16[2304,128]{1,0:T(8,128)(2,1)S(1)}, u32[]{:S(2)}, u32[]{:S(2)}) %collective-permute-start.12) | collective-permute-done | bytes 589856 | tf_op jit(solution)/shard_map/ppermute | solution.py:286
  93.2 0.4 grad.1
  93.7 30.8 %all_to_all.16.parts_ref = bf16[32,80,128]{2,1,0:T(8,128)(2,1)S(1)} all-to-all(bf16[32,80,128]{2,1,0:T(8,128)(2,1)S(1)} %grad.1), channel_id=1, replica_groups=mesh['y'=8,'zh'=4,'c'=2,'x'=4,'zl'=2] {'y','zh'}, dimensions={0} | all-to-all | bytes 1310720 | tf_op jit(solution)/shard_map/all_to_all | solution.py:369
  124.5 0.1 total.1
  124.6 25.4 %all_to_all.17.mine_ref = bf16[32,80,128]{2,1,0:T(8,128)(2,1)S(1)} all-to-all(bf16[32,80,128]{2,1,0:T(8,128)(2,1)S(1)} %total.1), channel_id=1, replica_groups=mesh['y'=8,'zh'=4,'c'=2,'x'=4,'zl'=2] {'y','zh'}, dimensions={0} | all-to-all | bytes 1310720 | tf_op jit(solution)/shard_map/all_to_all | solution.py:381
  150.0 5.8 %collective-permute-start.13 = (bf16[32,80,128]{2,1,0:T(8,128)(2,1)S(1)}, bf16[32,80,128]{2,1,0:T(8,128)(2,1)S(1)}, u32[]{:S(2)}, u32[]{:S(2)}) collective-permute-start(bf16[32,80,128]{2,1,0:T(8,128)(2,1)S(1)} %all_to_all.17.mine_ref), channel_id=1, source_target_pairs={{0,8},{8,0},{1,9},{9,1},{2,10},{10,2},{3,11},{11,3},{4,12},{12,4},... | collective-permute-start | bytes 1966088 | tf_op jit(solution)/shard_map/ppermute | solution.py:286
  155.8 1.7 %collective-permute-done.13.theirs_ref = bf16[32,80,128]{2,1,0:T(8,128)(2,1)S(1)} collective-permute-done((bf16[32,80,128]{2,1,0:T(8,128)(2,1)S(1)}, bf16[32,80,128]{2,1,0:T(8,128)(2,1)S(1)}, u32[]{:S(2)}, u32[]{:S(2)}) %collective-permute-start.13) | collective-permute-done | bytes 655392 | tf_op jit(solution)/shard_map/ppermute | solution.py:286
  157.5 1.2 place.1
  (5 shorter events, 0.2 us)
Async XLA Ops:
  3.3 24.9 %collective-permute-start = (bf16[408,768]{1,0:T(8,128)(2,1)}, bf16[408,768]{1,0:T(8,128)(2,1)S(1)}, u32[]{:S(2)}, u32[]{:S(2)}) collective-permute-start(bf16[408,768]{1,0:T(8,128)(2,1)} %near.1.n0), channel_id=1, source_target_pairs={{0,2},{2,4},{4,6},{6,0},{8,14},{10,8},{12,10},{14,12},{1,3},{3,5},... | collective-permute-start | bytes 1880072 | tf_op jit(solution)/shard_map/ppermute | solution.py:280
  7.7 20.5 %collective-permute-start.1 = (bf16[408,768]{1,0:T(8,128)(2,1)}, bf16[408,768]{1,0:T(8,128)(2,1)S(1)}, u32[]{:S(2)}, u32[]{:S(2)}) collective-permute-start(bf16[408,768]{1,0:T(8,128)(2,1)} %near.1.n0), channel_id=1, source_target_pairs={{0,1},{1,0},{8,57},{9,24},{16,17},{17,16},{24,9},{25,40},{32,33},{... | collective-permute-start | bytes 1880072 | tf_op jit(solution)/shard_map/ppermute | solution.py:283
  21.0 14.0 %collective-permute-start.5 = (bf16[416,768]{1,0:T(8,128)(2,1)}, bf16[416,768]{1,0:T(8,128)(2,1)S(1)}, u32[]{:S(2)}, u32[]{:S(2)}) collective-permute-start(bf16[416,768]{1,0:T(8,128)(2,1)} %far.1.f0), channel_id=1, source_target_pairs={{0,1},{1,0},{8,57},{9,24},{16,17},{17,16},{24,9},{25,40},{32,33},{... | collective-permute-start | bytes 1916936 | tf_op jit(solution)/shard_map/ppermute | solution.py:283
  22.9 14.3 %collective-permute-start.4 = (bf16[416,768]{1,0:T(8,128)(2,1)}, bf16[416,768]{1,0:T(8,128)(2,1)S(1)}, u32[]{:S(2)}, u32[]{:S(2)}) collective-permute-start(bf16[416,768]{1,0:T(8,128)(2,1)} %far.1.f0), channel_id=1, source_target_pairs={{0,2},{2,4},{4,6},{6,0},{8,14},{10,8},{12,10},{14,12},{1,3},{3,5},... | collective-permute-start | bytes 1916936 | tf_op jit(solution)/shard_map/ppermute | solution.py:280
  28.2 14.6 %collective-permute-start.2 = (bf16[408,768]{1,0:T(8,128)(2,1)S(1)}, bf16[408,768]{1,0:T(8,128)(2,1)S(1)}, u32[]{:S(2)}, u32[]{:S(2)}) collective-permute-start(bf16[408,768]{1,0:T(8,128)(2,1)S(1)} %collective-permute-done.n1), channel_id=1, source_target_pairs={{0,2},{2,4},{4,6},{6,0},{8,14},{10,8},{12,10},{14,12},{1,3},{3,5},... | collective-permute-start | bytes 1880072 | tf_op jit(solution)/shard_map/ppermute | solution.py:280
  30.4 12.4 %collective-permute-start.3 = (bf16[400,768]{1,0:T(8,128)(2,1)S(1)}, bf16[400,768]{1,0:T(8,128)(2,1)S(1)}, u32[]{:S(2)}, u32[]{:S(2)}) collective-permute-start(bf16[400,768]{1,0:T(8,128)(2,1)S(1)} %slice.16), channel_id=1, source_target_pairs={{0,1},{1,0},{8,57},{9,24},{16,17},{17,16},{24,9},{25,40},{32,33},{... | collective-permute-start | bytes 1843208 | tf_op jit(solution)/shard_map/ppermute | solution.py:283
  35.0 17.2 %collective-permute-start.6 = (bf16[416,768]{1,0:T(8,128)(2,1)S(1)}, bf16[416,768]{1,0:T(8,128)(2,1)S(1)}, u32[]{:S(2)}, u32[]{:S(2)}) collective-permute-start(bf16[416,768]{1,0:T(8,128)(2,1)S(1)} %collective-permute-done.5.f3), channel_id=1, source_target_pairs={{0,2},{2,4},{4,6},{6,0},{8,14},{10,8},{12,10},{14,12},{1,3},{3,5},... | collective-permute-start | bytes 1916936 | tf_op jit(solution)/shard_map/ppermute | solution.py:280
  42.9 12.2 %collective-permute-start.7 = (bf16[408,768]{1,0:T(8,128)(2,1)S(1)}, bf16[408,768]{1,0:T(8,128)(2,1)S(1)}, u32[]{:S(2)}, u32[]{:S(2)}) collective-permute-start(bf16[408,768]{1,0:T(8,128)(2,1)S(1)} %collective-permute-done.2.n2), channel_id=1, source_target_pairs={{0,1},{1,0},{8,57},{9,24},{16,17},{17,16},{24,9},{25,40},{32,33},{... | collective-permute-start | bytes 1880072 | tf_op jit(solution)/shard_map/ppermute | solution.py:283
  47.5 9.5 %collective-permute-start.9 = (bf16[784,768]{1,0:T(8,128)(2,1)S(1)}, bf16[784,768]{1,0:T(8,128)(2,1)S(1)}, u32[]{:S(2)}, u32[]{:S(2)}) collective-permute-start(bf16[784,768]{1,0:T(8,128)(2,1)S(1)} %pad_maximum_fusion.1), channel_id=1, source_target_pairs={{0,8},{8,0},{1,9},{9,1},{2,10},{10,2},{3,11},{11,3},{4,12},{12,4},... | collective-permute-start | bytes 3612680 | tf_op jit(solution)/shard_map/ppermute | solution.py:286
  49.6 9.4 %copy-start = (bf16[416,768]{1,0:T(8,128)(2,1)S(1)}, bf16[416,768]{1,0:T(8,128)(2,1)}, u32[]{:S(2)}) copy-start(bf16[416,768]{1,0:T(8,128)(2,1)} %far.1.f0) | copy-start | bytes 1916932
  49.6 9.4 %copy-start.1 = (bf16[408,768]{1,0:T(8,128)(2,1)S(1)}, bf16[408,768]{1,0:T(8,128)(2,1)}, u32[]{:S(2)}) copy-start(bf16[408,768]{1,0:T(8,128)(2,1)} %near.1.n0) | copy-start | bytes 1880068
  49.6 9.4 %copy-start.2 = (bf16[144,768]{1,0:T(8,128)(2,1)S(1)}, bf16[144,768]{1,0:T(8,128)(2,1)}, u32[]{:S(2)}) copy-start(bf16[144,768]{1,0:T(8,128)(2,1)} %front.1.start_ref) | copy-start | bytes 663556
  49.6 7.5 %collective-permute-start.8 = (bf16[784,768]{1,0:T(8,128)(2,1)S(1)}, bf16[784,768]{1,0:T(8,128)(2,1)S(1)}, u32[]{:S(2)}, u32[]{:S(2)}) collective-permute-start(bf16[784,768]{1,0:T(8,128)(2,1)S(1)} %pad_maximum_fusion), channel_id=1, source_target_pairs={{0,8},{8,0},{1,9},{9,1},{2,10},{10,2},{3,11},{11,3},{4,12},{12,4},... | collective-permute-start | bytes 3612680 | tf_op jit(solution)/shard_map/ppermute | solution.py:286
  52.2 4.8 %collective-permute-start.10 = (bf16[392,768]{1,0:T(8,128)(2,1)S(1)}, bf16[392,768]{1,0:T(8,128)(2,1)S(1)}, u32[]{:S(2)}, u32[]{:S(2)}) collective-permute-start(bf16[392,768]{1,0:T(8,128)(2,1)S(1)} %slice.21), channel_id=1, source_target_pairs={{0,8},{8,0},{1,9},{9,1},{2,10},{10,2},{3,11},{11,3},{4,12},{12,4},... | collective-permute-start | bytes 1806344 | tf_op jit(solution)/shard_map/ppermute | solution.py:286
  55.1 3.9 %collective-permute-start.11 = (bf16[384,768]{1,0:T(8,128)(2,1)S(1)}, bf16[384,768]{1,0:T(8,128)(2,1)S(1)}, u32[]{:S(2)}, u32[]{:S(2)}) collective-permute-start(bf16[384,768]{1,0:T(8,128)(2,1)S(1)} %slice.22), channel_id=1, source_target_pairs={{0,8},{8,0},{1,9},{9,1},{2,10},{10,2},{3,11},{11,3},{4,12},{12,4},... | collective-permute-start | bytes 1769480 | tf_op jit(solution)/shard_map/ppermute | solution.py:286
  88.4 4.8 %collective-permute-start.12 = (bf16[2304,128]{1,0:T(8,128)(2,1)S(1)}, bf16[2304,128]{1,0:T(8,128)(2,1)S(1)}, u32[]{:S(2)}, u32[]{:S(2)}) collective-permute-start(bf16[2304,128]{1,0:T(8,128)(2,1)S(1)} %lend.1), channel_id=1, source_target_pairs={{0,8},{8,0},{1,9},{9,1},{2,10},{10,2},{3,11},{11,3},{4,12},{12,4},... | collective-permute-start | bytes 1769480 | tf_op jit(solution)/shard_map/ppermute | solution.py:286
  150.0 7.5 %collective-permute-start.13 = (bf16[32,80,128]{2,1,0:T(8,128)(2,1)S(1)}, bf16[32,80,128]{2,1,0:T(8,128)(2,1)S(1)}, u32[]{:S(2)}, u32[]{:S(2)}) collective-permute-start(bf16[32,80,128]{2,1,0:T(8,128)(2,1)S(1)} %all_to_all.17.mine_ref), channel_id=1, source_target_pairs={{0,8},{8,0},{1,9},{9,1},{2,10},{10,2},{3,11},{11,3},{4,12},{12,4},... | collective-permute-start | bytes 1966088 | tf_op jit(solution)/shard_map/ppermute | solution.py:286

commit v11 on v8

--- a/solution.py
+++ b/solution.py
@@ -1,4 +1,3 @@
-import functools
 import itertools
 
 import jax
@@ -53,17 +52,25 @@
     return section, lax.axis_index("c")
 
 
-def prep_kernel(far, w_ref, taps_ref, out_ref, sem):
-    core = lax.axis_index("c")
-    part = pl.multiple_of((1 - core if far else core) * H, H)
-    copy = pltpu.make_async_copy(w_ref.at[0, pl.ds(part, H)], out_ref.at[pl.ds(0, H)], sem)
-    copy.start()
+def prep_kernel(w_ref, taps_ref, near_ref, far_ref, sem):
+    _, core = where_am_i()
+    mine = pl.multiple_of(core * H, H)
+    theirs = pl.multiple_of((1 - core) * H, H)
+    copies = [
+        pltpu.make_async_copy(w_ref.at[0, pl.ds(mine, H)], near_ref.at[pl.ds(0, H)], sem.at[0]),
+        pltpu.make_async_copy(w_ref.at[0, pl.ds(theirs, H)], far_ref.at[pl.ds(0, H)], sem.at[1]),
+    ]
+    for copy in copies:
+        copy.start()
     taps = jnp.concatenate([taps_ref[k] for k in range(KER)], axis=0)
     hi, mid, low = split3(taps)
     packed = jnp.concatenate([hi, mid, low, jnp.zeros((1, D), F32)], axis=0).astype(BF)
-    out_ref[H:H + TAPS, :] = packed
-    out_ref[H + TAPS:, :] = jnp.zeros((out_ref.shape[0] - H - TAPS, D), BF)
-    copy.wait()
+    near_ref[H:H + TAPS, :] = packed
+    near_ref[H + TAPS:, :] = jnp.zeros((NEAR - H - TAPS, D), BF)
+    far_ref[H:H + TAPS, :] = packed
+    far_ref[H + TAPS:, :] = packed
+    for copy in copies:
+        copy.wait()
 
 
 def front_kernel(feat_ref, front_ref, targ_ref, len_ref, out_ref):
@@ -277,19 +284,14 @@
     def to_core(a):
         return lax.ppermute(a, "c", [(0, 1), (1, 0)])
 
-    flat_taps = jnp.transpose(kernel, (1, 0, 2))
-
-    def prepare(far, rows):
-        return pl.pallas_call(
-            functools.partial(prep_kernel, far),
-            name="far" if far else "near",
-            out_shape=jax.ShapeDtypeStruct((rows, D), BF),
-            in_specs=[ANY, VMEM],
-            out_specs=VMEM,
-            scratch_shapes=[pltpu.SemaphoreType.DMA],
-        )(pointwise, flat_taps)
-
-    near, far = prepare(False, NEAR), prepare(True, FAR)
+    near, far = pl.pallas_call(
+        prep_kernel,
+        name="prep",
+        out_shape=(jax.ShapeDtypeStruct((NEAR, D), BF), jax.ShapeDtypeStruct((FAR, D), BF)),
+        in_specs=[ANY, VMEM],
+        out_specs=(VMEM, VMEM),
+        scratch_shapes=[pltpu.SemaphoreType.DMA((2,))],
+    )(pointwise, jnp.transpose(kernel, (1, 0, 2)))
     begin = pl.pallas_call(
         front_kernel,
         name="front",

time: 159 us -> 157 us (0.987)
  Pallas kernels: 21.6 us -> 19.4 us
    pallas_call x2 -> x1, Pallas kernels: 5.27 us -> 3.02 us  [body(): pl.pallas_call(prep_kernel, name='prep', out_shape=(jax.ShapeDtypeStruct(...]
  transfers between devices with their start and end apart: 14 -> 14, of which waited for: 5 -> 7; matrix products, arithmetic and copies ran while one was open for 0% -> 0% of each run, Pallas kernels for 3% -> 1%
where the time goes in v11:
time: 157 us; the launch traced here: 156 us
  blocking collectives  72.5 us (46%)
  starting transfers between devices  50.3 us (32%)
  Pallas kernels  19.4 us (12%)
  waiting for transfers between devices  13 us (8%)
    all_to_all x1, blocking collectives, body(): scattered = lax.all_to_all(parts, ('y', 'zh'), 0, 0)  30.7 us
    all_to_all x1, blocking collectives, body(): half = lax.all_to_all(mine, ('y', 'zh'), 0, 0)  25.4 us
    ppermute x4, starting transfers between devices, along_z(): return lax.ppermute(a, ('zh', 'c', 'zl'), pair)  22 us
    ppermute x6, starting transfers between devices, to_core(): return lax.ppermute(a, 'c', [(0, 1), (1, 0)])  17.1 us
    all_to_all x1, blocking collectives, body(): received = lax.all_to_all(payload, ('x', 'zl'), 0, 0)  16.3 us
    pallas_call x1, Pallas kernels, body(): pl.pallas_call(model_kernel, name='model', out_shape=jax.ShapeDtypeStruct...  12 us
    ppermute x4, starting transfers between devices, along_x(): return lax.ppermute(a, ('c', 'x'), ring)  11.1 us
    ppermute x4, waiting for transfers between devices, along_z(): return lax.ppermute(a, ('zh', 'c', 'zl'), pair)  7.78 us
  transfers between devices with their start and end apart: 14, of which 7 were waited for; matrix products, arithmetic and copies ran while one was open for 0% of the time, Pallas kernels for 1%

profile of v11, /device:TPU:9, one launch (start us, length us, event | category | flops | bytes accessed | tf_op | source)
XLA Modules:
  0.0 156.5 jit_solution(14678074528685812592)
XLA Ops:
  0.6 3.0 %prep.1 = (bf16[408,768]{1,0:T(8,128)(2,1)}, bf16[416,768]{1,0:T(8,128)(2,1)}) custom-call(bf16[1,768,768]{2,1,0:T(8,128)(2,1)} %w_ref.1, f32[5,1,768]{2,1,0:T(1,128)} %bitcast.2), custom_call_target="tpu_custom_call" | custom-call | tf_op jit(solution)/shard_map/prep/pallas_call | solution.py:287
  3.7 4.4 %collective-permute-start = (bf16[408,768]{1,0:T(8,128)(2,1)}, bf16[408,768]{1,0:T(8,128)(2,1)S(1)}, u32[]{:S(2)}, u32[]{:S(2)}) collective-permute-start(bf16[408,768]{1,0:T(8,128)(2,1)} %get-tuple-element.12.n0), channel_id=1, source_target_pairs={{0,2},{2,4},{4,6},{6,0},{8,14},{10,8},{12,10},{14,12},{1,3},{3,5},... | collective-permute-start | bytes 1880072 | tf_op jit(solution)/shard_map/ppermute | solution.py:279
  8.1 10.7 %collective-permute-start.1 = (bf16[408,768]{1,0:T(8,128)(2,1)}, bf16[408,768]{1,0:T(8,128)(2,1)S(1)}, u32[]{:S(2)}, u32[]{:S(2)}) collective-permute-start(bf16[408,768]{1,0:T(8,128)(2,1)} %get-tuple-element.12.n0), channel_id=1, source_target_pairs={{0,1},{1,0},{8,57},{9,24},{16,17},{17,16},{24,9},{25,40},{32,33},{... | collective-permute-start | bytes 1880072 | tf_op jit(solution)/shard_map/ppermute | solution.py:282
  18.7 1.9 %collective-permute-start.5 = (bf16[416,768]{1,0:T(8,128)(2,1)}, bf16[416,768]{1,0:T(8,128)(2,1)S(1)}, u32[]{:S(2)}, u32[]{:S(2)}) collective-permute-start(bf16[416,768]{1,0:T(8,128)(2,1)} %get-tuple-element.14.f0), channel_id=1, source_target_pairs={{0,1},{1,0},{8,57},{9,24},{16,17},{17,16},{24,9},{25,40},{32,33},{... | collective-permute-start | bytes 1916936 | tf_op jit(solution)/shard_map/ppermute | solution.py:282
  20.7 2.5 %collective-permute-start.4 = (bf16[416,768]{1,0:T(8,128)(2,1)}, bf16[416,768]{1,0:T(8,128)(2,1)S(1)}, u32[]{:S(2)}, u32[]{:S(2)}) collective-permute-start(bf16[416,768]{1,0:T(8,128)(2,1)} %get-tuple-element.14.f0), channel_id=1, source_target_pairs={{0,2},{2,4},{4,6},{6,0},{8,14},{10,8},{12,10},{14,12},{1,3},{3,5},... | collective-permute-start | bytes 1916936 | tf_op jit(solution)/shard_map/ppermute | solution.py:279
  23.1 2.3 %front.1.start_ref = bf16[144,768]{1,0:T(8,128)(2,1)} custom-call(bf16[4,64,512]{2,1,0:T(8,128)(2,1)} %feat_ref.1, bf16[512,768]{1,0:T(8,128)(2,1)} %front_ref.1, bf16[4,64,768]{2,1,0:T(8,128)(2,1)} %targ_ref.1, s32[4]{0:T(128)} %len_ref.1), custom_call_target="tpu_custom_call" | custom-call | tf_op jit(solution)/shard_map/front/pallas_call | solution.py:295
  25.4 0.0 collective-permute-done.n1
  25.4 1.5 collective-permute-done.1.n3
  26.9 2.2 %collective-permute-start.2 = (bf16[408,768]{1,0:T(8,128)(2,1)S(1)}, bf16[408,768]{1,0:T(8,128)(2,1)S(1)}, u32[]{:S(2)}, u32[]{:S(2)}) collective-permute-start(bf16[408,768]{1,0:T(8,128)(2,1)S(1)} %collective-permute-done.n1), channel_id=1, source_target_pairs={{0,2},{2,4},{4,6},{6,0},{8,14},{10,8},{12,10},{14,12},{1,3},{3,5},... | collective-permute-start | bytes 1880072 | tf_op jit(solution)/shard_map/ppermute | solution.py:279
  29.1 4.6 %collective-permute-start.3 = (bf16[400,768]{1,0:T(8,128)(2,1)S(1)}, bf16[400,768]{1,0:T(8,128)(2,1)S(1)}, u32[]{:S(2)}, u32[]{:S(2)}) collective-permute-start(bf16[400,768]{1,0:T(8,128)(2,1)S(1)} %slice.16), channel_id=1, source_target_pairs={{0,1},{1,0},{8,57},{9,24},{16,17},{17,16},{24,9},{25,40},{32,33},{... | collective-permute-start | bytes 1843208 | tf_op jit(solution)/shard_map/ppermute | solution.py:282
  33.7 0.1 collective-permute-done.5.f3
  33.7 2.2 %collective-permute-start.6 = (bf16[416,768]{1,0:T(8,128)(2,1)S(1)}, bf16[416,768]{1,0:T(8,128)(2,1)S(1)}, u32[]{:S(2)}, u32[]{:S(2)}) collective-permute-start(bf16[416,768]{1,0:T(8,128)(2,1)S(1)} %collective-permute-done.5.f3), channel_id=1, source_target_pairs={{0,2},{2,4},{4,6},{6,0},{8,14},{10,8},{12,10},{14,12},{1,3},{3,5},... | collective-permute-start | bytes 1916936 | tf_op jit(solution)/shard_map/ppermute | solution.py:279
  35.9 0.0 collective-permute-done.4.f1
  35.9 5.3 %collective-permute-done.3.n4 = bf16[400,768]{1,0:T(8,128)(2,1)S(1)} collective-permute-done((bf16[400,768]{1,0:T(8,128)(2,1)S(1)}, bf16[400,768]{1,0:T(8,128)(2,1)S(1)}, u32[]{:S(2)}, u32[]{:S(2)}) %collective-permute-start.3) | collective-permute-done | bytes 614432 | tf_op jit(solution)/shard_map/ppermute | solution.py:282
  41.2 0.0 collective-permute-done.2.n2
  41.2 4.9 %collective-permute-start.7 = (bf16[408,768]{1,0:T(8,128)(2,1)S(1)}, bf16[408,768]{1,0:T(8,128)(2,1)S(1)}, u32[]{:S(2)}, u32[]{:S(2)}) collective-permute-start(bf16[408,768]{1,0:T(8,128)(2,1)S(1)} %collective-permute-done.2.n2), channel_id=1, source_target_pairs={{0,1},{1,0},{8,57},{9,24},{16,17},{17,16},{24,9},{25,40},{32,33},{... | collective-permute-start | bytes 1880072 | tf_op jit(solution)/shard_map/ppermute | solution.py:282
  46.1 0.1 pad_maximum_fusion.1
  46.2 1.9 %collective-permute-start.9 = (bf16[784,768]{1,0:T(8,128)(2,1)S(1)}, bf16[784,768]{1,0:T(8,128)(2,1)S(1)}, u32[]{:S(2)}, u32[]{:S(2)}) collective-permute-start(bf16[784,768]{1,0:T(8,128)(2,1)S(1)} %pad_maximum_fusion.1), channel_id=1, source_target_pairs={{0,8},{8,0},{1,9},{9,1},{2,10},{10,2},{3,11},{11,3},{4,12},{12,4},... | collective-permute-start | bytes 3612680 | tf_op jit(solution)/shard_map/ppermute | solution.py:285
  48.2 0.1 pad_maximum_fusion
  48.3 0.0 copy-start
  48.3 0.0 copy-start.1
  48.3 0.0 copy-start.2
  48.3 2.5 %collective-permute-start.8 = (bf16[784,768]{1,0:T(8,128)(2,1)S(1)}, bf16[784,768]{1,0:T(8,128)(2,1)S(1)}, u32[]{:S(2)}, u32[]{:S(2)}) collective-permute-start(bf16[784,768]{1,0:T(8,128)(2,1)S(1)} %pad_maximum_fusion), channel_id=1, source_target_pairs={{0,8},{8,0},{1,9},{9,1},{2,10},{10,2},{3,11},{11,3},{4,12},{12,4},... | collective-permute-start | bytes 3612680 | tf_op jit(solution)/shard_map/ppermute | solution.py:285
  50.9 0.0 collective-permute-done.6.f4
  50.9 1.9 %collective-permute-start.10 = (bf16[392,768]{1,0:T(8,128)(2,1)S(1)}, bf16[392,768]{1,0:T(8,128)(2,1)S(1)}, u32[]{:S(2)}, u32[]{:S(2)}) collective-permute-start(bf16[392,768]{1,0:T(8,128)(2,1)S(1)} %slice.21), channel_id=1, source_target_pairs={{0,8},{8,0},{1,9},{9,1},{2,10},{10,2},{3,11},{11,3},{4,12},{12,4},... | collective-permute-start | bytes 1806344 | tf_op jit(solution)/shard_map/ppermute | solution.py:285
  52.8 0.9 collective-permute-done.7.n5
  53.8 1.9 %collective-permute-start.11 = (bf16[384,768]{1,0:T(8,128)(2,1)S(1)}, bf16[384,768]{1,0:T(8,128)(2,1)S(1)}, u32[]{:S(2)}, u32[]{:S(2)}) collective-permute-start(bf16[384,768]{1,0:T(8,128)(2,1)S(1)} %slice.22), channel_id=1, source_target_pairs={{0,8},{8,0},{1,9},{9,1},{2,10},{10,2},{3,11},{11,3},{4,12},{12,4},... | collective-permute-start | bytes 1769480 | tf_op jit(solution)/shard_map/ppermute | solution.py:285
  55.7 0.0 collective-permute-done.10.g4
  55.8 0.0 collective-permute-done.9.m2
  55.8 0.0 collective-permute-done.8.m1
  55.8 1.9 %collective-permute-done.11.m5 = bf16[384,768]{1,0:T(8,128)(2,1)S(1)} collective-permute-done((bf16[384,768]{1,0:T(8,128)(2,1)S(1)}, bf16[384,768]{1,0:T(8,128)(2,1)S(1)}, u32[]{:S(2)}, u32[]{:S(2)}) %collective-permute-start.11) | collective-permute-done | bytes 589856 | tf_op jit(solution)/shard_map/ppermute | solution.py:285
  57.7 0.0 copy-done
  57.7 0.0 copy-done.1
  57.7 0.0 copy-done.2
  57.7 12.0 %model.1 = bf16[8,72,768]{2,1,0:T(8,128)(2,1)S(1)} custom-call(bf16[144,768]{1,0:T(8,128)(2,1)S(1)} %copy-done, bf16[408,768]{1,0:T(8,128)(2,1)S(1)} %copy-done.2, bf16[416,768]{1,0:T(8,128)(2,1)S(1)} %copy-done.1, bf16[408,768]{1,0:T(8,128)(2,1)S(1)} %collective-permute-done.n1, bf16[416,768]{1,0:T(8,128)(2,1)S(1)} %collective-permute-done.4.f1, ...), custom_call_target="tpu_custom_call" | custom-call | tf_op jit(solution)/shard_map/model/pallas_call | solution.py:316
  69.7 16.3 %all_to_all.15.recv_ref = bf16[8,72,768]{2,1,0:T(8,128)(2,1)S(1)} all-to-all(bf16[8,72,768]{2,1,0:T(8,128)(2,1)S(1)} %model.1), channel_id=1, replica_groups=mesh['y'=8,'zh'=4,'c'=2,'x'=4,'zl'=2] {'x','zl'}, dimensions={0} | all-to-all | bytes 1769472 | tf_op jit(solution)/shard_map/all_to_all | solution.py:338
  86.1 0.4 lend.1
  86.5 3.0 %collective-permute-start.12 = (bf16[2304,128]{1,0:T(8,128)(2,1)S(1)}, bf16[2304,128]{1,0:T(8,128)(2,1)S(1)}, u32[]{:S(2)}, u32[]{:S(2)}) collective-permute-start(bf16[2304,128]{1,0:T(8,128)(2,1)S(1)} %lend.1), channel_id=1, source_target_pairs={{0,8},{8,0},{1,9},{9,1},{2,10},{10,2},{3,11},{11,3},{4,12},{12,4},... | collective-permute-start | bytes 1769480 | tf_op jit(solution)/shard_map/ppermute | solution.py:285
  89.5 1.6 %collective-permute-done.12.lent_ref = bf16[2304,128]{1,0:T(8,128)(2,1)S(1)} collective-permute-done((bf16[2304,128]{1,0:T(8,128)(2,1)S(1)}, bf16[2304,128]{1,0:T(8,128)(2,1)S(1)}, u32[]{:S(2)}, u32[]{:S(2)}) %collective-permute-start.12) | collective-permute-done | bytes 589856 | tf_op jit(solution)/shard_map/ppermute | solution.py:285
  91.1 0.4 grad.1
  91.5 30.7 %all_to_all.16.parts_ref = bf16[32,80,128]{2,1,0:T(8,128)(2,1)S(1)} all-to-all(bf16[32,80,128]{2,1,0:T(8,128)(2,1)S(1)} %grad.1), channel_id=1, replica_groups=mesh['y'=8,'zh'=4,'c'=2,'x'=4,'zl'=2] {'y','zh'}, dimensions={0} | all-to-all | bytes 1310720 | tf_op jit(solution)/shard_map/all_to_all | solution.py:358
  122.2 0.1 total.1
  122.3 25.4 %all_to_all.17.mine_ref = bf16[32,80,128]{2,1,0:T(8,128)(2,1)S(1)} all-to-all(bf16[32,80,128]{2,1,0:T(8,128)(2,1)S(1)} %total.1), channel_id=1, replica_groups=mesh['y'=8,'zh'=4,'c'=2,'x'=4,'zl'=2] {'y','zh'}, dimensions={0} | all-to-all | bytes 1310720 | tf_op jit(solution)/shard_map/all_to_all | solution.py:370
  147.8 5.8 %collective-permute-start.13 = (bf16[32,80,128]{2,1,0:T(8,128)(2,1)S(1)}, bf16[32,80,128]{2,1,0:T(8,128)(2,1)S(1)}, u32[]{:S(2)}, u32[]{:S(2)}) collective-permute-start(bf16[32,80,128]{2,1,0:T(8,128)(2,1)S(1)} %all_to_all.17.mine_ref), channel_id=1, source_target_pairs={{0,8},{8,0},{1,9},{9,1},{2,10},{10,2},{3,11},{11,3},{4,12},{12,4},... | collective-permute-start | bytes 1966088 | tf_op jit(solution)/shard_map/ppermute | solution.py:285
  153.6 1.7 %collective-permute-done.13.theirs_ref = bf16[32,80,128]{2,1,0:T(8,128)(2,1)S(1)} collective-permute-done((bf16[32,80,128]{2,1,0:T(8,128)(2,1)S(1)}, bf16[32,80,128]{2,1,0:T(8,128)(2,1)S(1)}, u32[]{:S(2)}, u32[]{:S(2)}) %collective-permute-start.13) | collective-permute-done | bytes 655392 | tf_op jit(solution)/shard_map/ppermute | solution.py:285
  155.3 1.2 place.1
  (5 shorter events, 0.2 us)
Async XLA Ops:
  3.7 21.7 %collective-permute-start = (bf16[408,768]{1,0:T(8,128)(2,1)}, bf16[408,768]{1,0:T(8,128)(2,1)S(1)}, u32[]{:S(2)}, u32[]{:S(2)}) collective-permute-start(bf16[408,768]{1,0:T(8,128)(2,1)} %get-tuple-element.12.n0), channel_id=1, source_target_pairs={{0,2},{2,4},{4,6},{6,0},{8,14},{10,8},{12,10},{14,12},{1,3},{3,5},... | collective-permute-start | bytes 1880072 | tf_op jit(solution)/shard_map/ppermute | solution.py:279
  8.1 18.8 %collective-permute-start.1 = (bf16[408,768]{1,0:T(8,128)(2,1)}, bf16[408,768]{1,0:T(8,128)(2,1)S(1)}, u32[]{:S(2)}, u32[]{:S(2)}) collective-permute-start(bf16[408,768]{1,0:T(8,128)(2,1)} %get-tuple-element.12.n0), channel_id=1, source_target_pairs={{0,1},{1,0},{8,57},{9,24},{16,17},{17,16},{24,9},{25,40},{32,33},{... | collective-permute-start | bytes 1880072 | tf_op jit(solution)/shard_map/ppermute | solution.py:282
  18.7 15.0 %collective-permute-start.5 = (bf16[416,768]{1,0:T(8,128)(2,1)}, bf16[416,768]{1,0:T(8,128)(2,1)S(1)}, u32[]{:S(2)}, u32[]{:S(2)}) collective-permute-start(bf16[416,768]{1,0:T(8,128)(2,1)} %get-tuple-element.14.f0), channel_id=1, source_target_pairs={{0,1},{1,0},{8,57},{9,24},{16,17},{17,16},{24,9},{25,40},{32,33},{... | collective-permute-start | bytes 1916936 | tf_op jit(solution)/shard_map/ppermute | solution.py:282
  20.7 15.2 %collective-permute-start.4 = (bf16[416,768]{1,0:T(8,128)(2,1)}, bf16[416,768]{1,0:T(8,128)(2,1)S(1)}, u32[]{:S(2)}, u32[]{:S(2)}) collective-permute-start(bf16[416,768]{1,0:T(8,128)(2,1)} %get-tuple-element.14.f0), channel_id=1, source_target_pairs={{0,2},{2,4},{4,6},{6,0},{8,14},{10,8},{12,10},{14,12},{1,3},{3,5},... | collective-permute-start | bytes 1916936 | tf_op jit(solution)/shard_map/ppermute | solution.py:279
  26.9 14.3 %collective-permute-start.2 = (bf16[408,768]{1,0:T(8,128)(2,1)S(1)}, bf16[408,768]{1,0:T(8,128)(2,1)S(1)}, u32[]{:S(2)}, u32[]{:S(2)}) collective-permute-start(bf16[408,768]{1,0:T(8,128)(2,1)S(1)} %collective-permute-done.n1), channel_id=1, source_target_pairs={{0,2},{2,4},{4,6},{6,0},{8,14},{10,8},{12,10},{14,12},{1,3},{3,5},... | collective-permute-start | bytes 1880072 | tf_op jit(solution)/shard_map/ppermute | solution.py:279
  29.1 12.1 %collective-permute-start.3 = (bf16[400,768]{1,0:T(8,128)(2,1)S(1)}, bf16[400,768]{1,0:T(8,128)(2,1)S(1)}, u32[]{:S(2)}, u32[]{:S(2)}) collective-permute-start(bf16[400,768]{1,0:T(8,128)(2,1)S(1)} %slice.16), channel_id=1, source_target_pairs={{0,1},{1,0},{8,57},{9,24},{16,17},{17,16},{24,9},{25,40},{32,33},{... | collective-permute-start | bytes 1843208 | tf_op jit(solution)/shard_map/ppermute | solution.py:282
  33.7 17.1 %collective-permute-start.6 = (bf16[416,768]{1,0:T(8,128)(2,1)S(1)}, bf16[416,768]{1,0:T(8,128)(2,1)S(1)}, u32[]{:S(2)}, u32[]{:S(2)}) collective-permute-start(bf16[416,768]{1,0:T(8,128)(2,1)S(1)} %collective-permute-done.5.f3), channel_id=1, source_target_pairs={{0,2},{2,4},{4,6},{6,0},{8,14},{10,8},{12,10},{14,12},{1,3},{3,5},... | collective-permute-start | bytes 1916936 | tf_op jit(solution)/shard_map/ppermute | solution.py:279
  41.2 12.5 %collective-permute-start.7 = (bf16[408,768]{1,0:T(8,128)(2,1)S(1)}, bf16[408,768]{1,0:T(8,128)(2,1)S(1)}, u32[]{:S(2)}, u32[]{:S(2)}) collective-permute-start(bf16[408,768]{1,0:T(8,128)(2,1)S(1)} %collective-permute-done.2.n2), channel_id=1, source_target_pairs={{0,1},{1,0},{8,57},{9,24},{16,17},{17,16},{24,9},{25,40},{32,33},{... | collective-permute-start | bytes 1880072 | tf_op jit(solution)/shard_map/ppermute | solution.py:282
  46.2 9.5 %collective-permute-start.9 = (bf16[784,768]{1,0:T(8,128)(2,1)S(1)}, bf16[784,768]{1,0:T(8,128)(2,1)S(1)}, u32[]{:S(2)}, u32[]{:S(2)}) collective-permute-start(bf16[784,768]{1,0:T(8,128)(2,1)S(1)} %pad_maximum_fusion.1), channel_id=1, source_target_pairs={{0,8},{8,0},{1,9},{9,1},{2,10},{10,2},{3,11},{11,3},{4,12},{12,4},... | collective-permute-start | bytes 3612680 | tf_op jit(solution)/shard_map/ppermute | solution.py:285
  48.3 9.4 %copy-start = (bf16[144,768]{1,0:T(8,128)(2,1)S(1)}, bf16[144,768]{1,0:T(8,128)(2,1)}, u32[]{:S(2)}) copy-start(bf16[144,768]{1,0:T(8,128)(2,1)} %front.1.start_ref) | copy-start | bytes 663556
  48.3 9.4 %copy-start.1 = (bf16[416,768]{1,0:T(8,128)(2,1)S(1)}, bf16[416,768]{1,0:T(8,128)(2,1)}, u32[]{:S(2)}) copy-start(bf16[416,768]{1,0:T(8,128)(2,1)} %get-tuple-element.14.f0) | copy-start | bytes 1916932
  48.3 9.4 %copy-start.2 = (bf16[408,768]{1,0:T(8,128)(2,1)S(1)}, bf16[408,768]{1,0:T(8,128)(2,1)}, u32[]{:S(2)}) copy-start(bf16[408,768]{1,0:T(8,128)(2,1)} %get-tuple-element.12.n0) | copy-start | bytes 1880068
  48.3 7.5 %collective-permute-start.8 = (bf16[784,768]{1,0:T(8,128)(2,1)S(1)}, bf16[784,768]{1,0:T(8,128)(2,1)S(1)}, u32[]{:S(2)}, u32[]{:S(2)}) collective-permute-start(bf16[784,768]{1,0:T(8,128)(2,1)S(1)} %pad_maximum_fusion), channel_id=1, source_target_pairs={{0,8},{8,0},{1,9},{9,1},{2,10},{10,2},{3,11},{11,3},{4,12},{12,4},... | collective-permute-start | bytes 3612680 | tf_op jit(solution)/shard_map/ppermute | solution.py:285
  50.9 4.8 %collective-permute-start.10 = (bf16[392,768]{1,0:T(8,128)(2,1)S(1)}, bf16[392,768]{1,0:T(8,128)(2,1)S(1)}, u32[]{:S(2)}, u32[]{:S(2)}) collective-permute-start(bf16[392,768]{1,0:T(8,128)(2,1)S(1)} %slice.21), channel_id=1, source_target_pairs={{0,8},{8,0},{1,9},{9,1},{2,10},{10,2},{3,11},{11,3},{4,12},{12,4},... | collective-permute-start | bytes 1806344 | tf_op jit(solution)/shard_map/ppermute | solution.py:285
  53.8 3.9 %collective-permute-start.11 = (bf16[384,768]{1,0:T(8,128)(2,1)S(1)}, bf16[384,768]{1,0:T(8,128)(2,1)S(1)}, u32[]{:S(2)}, u32[]{:S(2)}) collective-permute-start(bf16[384,768]{1,0:T(8,128)(2,1)S(1)} %slice.22), channel_id=1, source_target_pairs={{0,8},{8,0},{1,9},{9,1},{2,10},{10,2},{3,11},{11,3},{4,12},{12,4},... | collective-permute-start | bytes 1769480 | tf_op jit(solution)/shard_map/ppermute | solution.py:285
  86.5 4.6 %collective-permute-start.12 = (bf16[2304,128]{1,0:T(8,128)(2,1)S(1)}, bf16[2304,128]{1,0:T(8,128)(2,1)S(1)}, u32[]{:S(2)}, u32[]{:S(2)}) collective-permute-start(bf16[2304,128]{1,0:T(8,128)(2,1)S(1)} %lend.1), channel_id=1, source_target_pairs={{0,8},{8,0},{1,9},{9,1},{2,10},{10,2},{3,11},{11,3},{4,12},{12,4},... | collective-permute-start | bytes 1769480 | tf_op jit(solution)/shard_map/ppermute | solution.py:285
  147.8 7.5 %collective-permute-start.13 = (bf16[32,80,128]{2,1,0:T(8,128)(2,1)S(1)}, bf16[32,80,128]{2,1,0:T(8,128)(2,1)S(1)}, u32[]{:S(2)}, u32[]{:S(2)}) collective-permute-start(bf16[32,80,128]{2,1,0:T(8,128)(2,1)S(1)} %all_to_all.17.mine_ref), channel_id=1, source_target_pairs={{0,8},{8,0},{1,9},{9,1},{2,10},{10,2},{3,11},{11,3},{4,12},{12,4},... | collective-permute-start | bytes 1966088 | tf_op jit(solution)/shard_map/ppermute | solution.py:285
